TPU v7x, 32 devices: a whole 2x2x4 slice. The times are simulated.
32 devices in a mesh: groups: 2 (over y), tok: 4 (over z), lay: 2 (over x), head: 2 (over core).
Axes of the slice: x: 2, y: 2, z: 4, core: 2. Of those that a mesh axis runs over, the one named last changes fastest.
Arguments:
- keys: float32 [2, 4096, 1024], P('lay', ('groups', 'tok'), 'head'), parts along dimension 1, may hold values from -80 to 80, as said below
- values: float32 [2, 4096, 1024], P('lay', ('groups', 'tok'), 'head'), parts along dimension 1, may hold values from -24 to 24
- queries: float32 [2, 32, 8192], P('lay', 'groups', 'head'), parts along dimension 1, may hold values from -620 to 620, as said below
- start_block: float32 [4096, 256], P(('groups', 'tok')), parts along dimension 0, may hold values from -6 to 6
- lengths: int32 [32], P('groups'), parts along dimension 0, may hold values from 1 to 2048, as said below
Outputs:
- attended: float32 [2, 32, 2, 4096], P('lay', 'groups', 'head', 'tok'), parts along dimension 1
There are 2 independent parts, one for each index of `groups`. A program takes and returns all parts, laid end to end along the dimension named above; each array names one. Nothing has to cross between parts.
Inputs may be any that keep to these rules, and one draw needn't show every extreme that they name: keys lie within this range. queries lie within this range. `lengths`: the longest row covers all 2048 tokens.
All inputs are finite; a program needn't handle non-finite values.
Results may differ from a plain program's by a relative error of at most 0.0003.
Values sent between devices are 32-bit elements; how exact they have to be, the bound alone decides.
No kernel may reach another device: no remote copies, remote signals or barrier semaphores. Data moves between devices by JAX's collectives and lax.ppermute only.
A program may use at most 64 MiB of HBM per device.

v0:
```python
import functools
import math

import jax
import jax.numpy as jnp
from jax import lax
from jax.experimental import pallas as pl
from jax.experimental.pallas import tpu as pltpu
from jax.sharding import PartitionSpec as P

KVH = 8
HD = 128
QH = 64
ITERS = 2

NEG = -1e30
HIGHEST = lax.Precision.HIGHEST


def product(left, right, dims):
    return lax.dot_general(
        left, right, (dims, ((), ())), precision=HIGHEST, preferred_element_type=jnp.float32
    )


def diagonal_inverse(tile, step=8):
    size = tile.shape[0]
    rows = lax.broadcasted_iota(jnp.int32, (size, 2 * size), 0)
    cols = lax.broadcasted_iota(jnp.int32, (size, 2 * size), 1)
    state = jnp.concatenate([tile, jnp.zeros_like(tile)], axis=1)
    state = state + jnp.where(cols == rows + size, 1.0, 0.0)
    done = []
    for start in range(0, size, step):
        col = [
            jnp.broadcast_to(state[:, start + i : start + i + 1], state.shape) for i in range(step)
        ]
        row = [state[i : i + 1, :] for i in range(step)]
        state = state[step:]
        for i in range(step):
            pivot = col[i][i : i + 1, :]
            inverse = 1.0 / pivot
            for k in range(i + 1, step):
                ratio = col[i][k : k + 1, :] * inverse
                row[k] = row[k] - ratio * row[i]
                col[k] = col[k] - ratio * col[i]
            if start + step < size:
                state = state - col[i][step:] * (row[i] * inverse)
            done.append(row[i] * lax.rsqrt(pivot))
    return jnp.concatenate(done)[:, size:]


def vmem(*shape):
    return jax.ShapeDtypeStruct(shape, jnp.float32)


def call(kernel, out_shape, *args, scratch=(), flops=0):
    spec = pl.BlockSpec(memory_space=pltpu.VMEM)
    single = not isinstance(out_shape, (tuple, list))
    moved = sum(4 * math.prod(a.shape) for a in (*args, *((out_shape,) if single else out_shape)))
    return pl.pallas_call(
        kernel,
        out_shape=out_shape,
        in_specs=[spec] * len(args),
        out_specs=spec if single else [spec] * len(out_shape),
        scratch_shapes=[pltpu.VMEM(s, jnp.float32) for s in scratch],
        compiler_params=pltpu.CompilerParams(vmem_limit_bytes=40 << 20),
        cost_estimate=pl.CostEstimate(flops=flops, bytes_accessed=moved, transcendentals=0),
    )(*args)


def factor_kernel(own_ref, *refs):
    *part_refs, out_ref, gram_ref, tile_ref, panel_ref = refs
    part_refs = (own_ref, *part_refs)
    if len(part_refs) == 1:
        gram_ref[...] = own_ref[...]
    else:
        lay, head = lax.axis_index("lay"), lax.axis_index("head")
        rows = own_ref.shape[0]
        for i, ref in enumerate(part_refs):
            at = (2 * (head ^ (i // 2)) + (lay ^ (i % 2))) * rows
            gram_ref[pl.ds(pl.multiple_of(at, rows), rows), :] = ref[...]
    half = tile_ref.shape[0]
    low, high = pl.ds(0, half), pl.ds(half, half)

    @pl.loop(0, 2)
    def _(i):
        here = pl.ds(pl.multiple_of(i * half, half), half)
        tile_ref[...] = diagonal_inverse(gram_ref[here, here])
        out_ref[here, here] = tile_ref[...]

        @pl.when(i == 0)
        def _():
            panel = product(tile_ref[...], gram_ref[low, high], ((1,), (0,)))
            gram_ref[high, high] = gram_ref[high, high] - product(panel, panel, ((0,), (0,)))
            panel_ref[...] = product(panel, tile_ref[...], ((0,), (0,)))
            out_ref[low, high] = jnp.zeros((half, half), jnp.float32)

        @pl.when(i == 1)
        def _():
            out_ref[high, low] = -product(tile_ref[...], panel_ref[...], ((1,), (0,)))


def inverse_factor(*parts):
    rank = parts[0].shape[1]
    half = rank // 2
    return call(
        factor_kernel,
        vmem(rank, rank),
        *parts,
        scratch=[(rank, rank), (half, half), (half, half)],
        flops=10_000_000_000,
    )


def distances(axis):
    size = lax.axis_size(axis)
    return [1 << i for i in range(size.bit_length() - 1)]


def side(axis, distance):
    return lax.axis_index(axis) // distance % 2


def swap(x, axis, distance):
    pairs = [(i, i ^ distance) for i in range(lax.axis_size(axis))]
    return lax.ppermute(x, axis, pairs)


def halve(x, axis, distance):
    half = x.shape[0] // 2
    mine = side(axis, distance)
    keep = lax.dynamic_slice_in_dim(x, mine * half, half, 0)
    send = lax.dynamic_slice_in_dim(x, (1 - mine) * half, half, 0)
    return keep + swap(send, axis, distance)


def double(x, axis, distance):
    other = swap(x, axis, distance)
    first = side(axis, distance) == 0
    return jnp.concatenate([jnp.where(first, x, other), jnp.where(first, other, x)])


def summed_rows(x, hops):
    for hop in hops:
        x = halve(x, *hop)
    for hop in reversed(hops):
        x = double(x, *hop)
    return x


def spread_body(keys, values, queries, start_block, lengths):
    _, tok_dev, kv_dev = keys.shape
    keys, values = keys[0], values[0]
    rank = start_block.shape[1]
    rows = queries.shape[1]
    local_heads = queries.shape[2] // HD
    group = QH // KVH
    kv_local = kv_dev // HD
    tok_hops = [("tok", d) for d in distances("tok")]
    wide_hops = [("head", d) for d in distances("head")] + [("lay", d) for d in distances("lay")]

    def whole_gram(block):
        share = rank
        at = 0
        for axis, distance in reversed(wide_hops):
            share //= 2
            at = at + side(axis, distance) * share
        part = lax.dynamic_slice_in_dim(block, at, share, 1)
        gram = product(part, block, ((0,), (0,)))
        for hop in tok_hops:
            gram = gram + swap(gram, *hop)
        for hop in wide_hops:
            gram = double(gram, *hop)
        return gram

    def project(block):
        return summed_rows(product(keys, block, ((0,), (0,))), tok_hops)

    def mix(coef):
        return summed_rows(product(keys, coef, ((1,), (0,))), wide_hops)

    block = start_block
    for step in range(ITERS):
        lower = inverse_factor(whole_gram(block))
        block = product(mix(project(block)), lower, ((1,), (1,)))
    lower = inverse_factor(whole_gram(block))
    coef = product(project(block), lower, ((1,), (1,)))
    basis = product(block, lower, ((1,), (1,)))

    quer = queries.reshape(rows, kv_local, group, HD)
    factor = coef.reshape(kv_local, HD, rank)
    reduced = jnp.einsum("bgid,gdr->gibr", quer, factor, precision=HIGHEST) / math.sqrt(HD)
    reduced = reduced.reshape(kv_local, group * rows, rank)
    scores = jnp.einsum("tr,gxr->tgx", basis, reduced, precision=HIGHEST)
    position = lax.axis_index("tok") * tok_dev + jnp.arange(tok_dev, dtype=jnp.int32)
    valid = position[:, None] < lengths[None, :]
    valid = jnp.tile(valid, (1, group))[:, None, :]
    peak = jnp.max(jnp.where(valid, scores, NEG), axis=0)
    weight = jnp.where(valid, jnp.exp(scores - peak[None]), 0.0)
    total = jnp.sum(weight, axis=0)
    vals = values.reshape(tok_dev, kv_local, HD)
    summed = jnp.einsum("tgx,tgd->gxd", weight, vals, precision=HIGHEST)
    peak = peak.reshape(local_heads, rows)
    total = total.reshape(local_heads, rows)
    summed = summed.reshape(local_heads, rows, HD)

    share = local_heads // lax.axis_size("tok")
    peak, total, summed = jax.tree.map(
        lambda a: a.reshape((-1, share) + a.shape[1:]), (peak, total, summed)
    )

    def pack(part):
        top, tot, acc = part
        blank = jnp.zeros(top.shape[:-1] + (HD - 2 * rows,), jnp.float32)
        extra = jnp.concatenate([top, tot, blank], axis=-1).reshape(-1, HD)
        return jnp.concatenate([acc.reshape(-1, HD), extra])

    def unpack(buffer, like):
        count = like[0].shape[0] * share
        extra = buffer[count * rows :]
        return (
            extra[:, :rows].reshape(like[0].shape),
            extra[:, rows : 2 * rows].reshape(like[0].shape),
            buffer[: count * rows].reshape(like[2].shape),
        )

    state = (peak, total, summed)
    for hop in tok_hops:
        mine = side(*hop)
        pairs = jax.tree.map(lambda a: a.reshape((-1, 2) + a.shape[1:]), state)
        keep = jax.tree.map(lambda a: lax.dynamic_index_in_dim(a, mine, 1, False), pairs)
        send = jax.tree.map(lambda a: lax.dynamic_index_in_dim(a, 1 - mine, 1, False), pairs)
        got = unpack(swap(pack(send), *hop), keep)
        top = jnp.maximum(keep[0], got[0])
        one, two = jnp.exp(keep[0] - top), jnp.exp(got[0] - top)
        state = (
            top,
            keep[1] * one + got[1] * two,
            keep[2] * one[..., None] + got[2] * two[..., None],
        )
    result = state[2][0] / state[1][0][..., None]
    return result.transpose(1, 0, 2).reshape(1, rows, 1, share * HD)


def pair_sides():
    return side("tok", 1), side("tok", 2), lax.axis_index("lay"), lax.axis_index("head")


def lanes(index, size=HD):
    return pl.ds(pl.multiple_of(index * size, size), size)


def share_of(scratch_ref, out_ref):
    rows = out_ref.shape[0]
    out_ref[...] = scratch_ref[lanes(lax.axis_index("lay"), rows), :]


def start_kernel(
    keys_ref, block_ref, keep_ref, send_ref, kept_ref, sent_ref, gram_ref, scratch_ref
):
    mine, _, _, head = pair_sides()
    half = block_ref.shape[1] // 2

    @pl.loop(0, 2)
    def _(i):
        at = lanes(i)
        kept_ref[:, at] = keys_ref[:, lanes(2 * i + mine)]
        sent_ref[:, at] = keys_ref[:, lanes(2 * i + 1 - mine)]

    send_ref[...] = product(sent_ref[...], block_ref[...], ((0,), (0,)))
    keep_ref[...] = product(kept_ref[...], block_ref[...], ((0,), (0,)))
    scratch_ref[...] = product(block_ref[:, lanes(head, half)], block_ref[...], ((0,), (0,)))
    share_of(scratch_ref, gram_ref)


def mix_kernel(own_ref, other_ref, first_ref, second_ref, keep_ref, send_ref, coef_ref):
    mine, _, _, head = pair_sides()
    coef_ref[...] = first_ref[...] + second_ref[...]
    half = own_ref.shape[0] // 2
    for keys_ref, piece in ((own_ref, mine), (other_ref, 1 - mine)):
        to = lanes(piece, half)

        @pl.loop(0, 2)
        def _(i):
            term = product(keys_ref[lanes(i, half), :], coef_ref[...], ((1,), (0,)))

            @pl.when(i == head)
            def _():
                keep_ref[to, :] = term

            @pl.when(i != head)
            def _():
                send_ref[to, :] = term


def streams_kernel(first_ref, second_ref, a_keep, a_send, b_keep, b_send):
    mine, _, lay, _ = pair_sides()
    half = first_ref.shape[0] // 2
    quarter, eighth = half // 2, half // 4

    def rows(piece, at, count):
        here = pl.ds(pl.multiple_of(piece * half + at, count), count)
        return first_ref[here, :] + second_ref[here, :]

    for piece in range(2):
        to = pl.ds(piece * eighth, eighth)
        a_keep[to, :] = rows(piece, lay * eighth, eighth)
        a_send[to, :] = rows(piece, (1 - lay) * eighth, eighth)
    b_keep[...] = rows(mine, quarter, quarter)
    b_send[...] = rows(1 - mine, quarter, quarter)


def summed_streams(keep, send, lower):
    got = swap(send, "head", 1)
    quarter = vmem(keep.shape[0] // 4, keep.shape[1])
    a_keep, a_send, b_keep, b_send = call(streams_kernel, [quarter] * 4, keep, got)
    a = a_keep + swap(a_send, "lay", 1)
    b = b_keep + swap(b_send, "tok", 1)
    a, b = a + swap(a, "tok", 1), b + swap(b, "lay", 1)
    a = after(a, lower)
    stack = jnp.concatenate([a, swap(a, "lay", 1), b, swap(b, "tok", 1)])
    return stack, swap(stack, "head", 1)


def block_kernel(
    own_ref, other_ref, near_ref, far_ref, lower_ref, block_ref, proj_ref, gram_ref, whole_ref, scratch_ref
):
    mine, _, lay, head = pair_sides()
    count = near_ref.shape[0] // 4
    half, eighth = count // 2, count // 2
    piece_rows = near_ref.shape[0]
    for ref, owner in ((near_ref, head), (far_ref, 1 - head)):
        for i in range(2):
            for piece in range(2):
                place = (piece ^ mine) * piece_rows + owner * (piece_rows // 2)
                to = place + (lay ^ i) * half
                whole_ref[pl.ds(pl.multiple_of(to, half), half), :] = ref[
                    pl.ds(i * count + piece * half, half), :
                ]
            place = i * piece_rows + owner * (piece_rows // 2) + count
            whole_ref[pl.ds(pl.multiple_of(place, count), count), :] = ref[
                pl.ds((2 + i) * count, count), :
            ]
    columns = scratch_ref.shape[0]
    proj_ref[...] = jnp.zeros(proj_ref.shape, jnp.float32)
    scratch_ref[...] = jnp.zeros(scratch_ref.shape, jnp.float32)
    for i, keys_ref in enumerate((own_ref, other_ref)):

        @pl.loop(0, 2)
        def _(k):
            rows = piece_rows // 2
            here = pl.ds(pl.multiple_of(i * piece_rows + k * rows, rows), rows)
            block_ref[here, :] = product(whole_ref[here, :], lower_ref[...], ((1,), (1,)))
            block = block_ref[here, :]
            proj_ref[...] += product(keys_ref[lanes(k, rows), :], block, ((0,), (0,)))
            scratch_ref[...] += product(block_ref[here, lanes(head, columns)], block, ((0,), (0,)))

    share_of(scratch_ref, gram_ref)


def attend_kernel(
    query_ref,
    block_ref,
    first_ref,
    second_ref,
    lower_ref,
    own_ref,
    low_ref,
    high_ref,
    length_ref,
    keep_ref,
    send_ref,
    basis_ref,
    score_ref,
):
    mine, upper, _, _ = pair_sides()
    group = QH // KVH
    tokens = own_ref.shape[0]
    width = score_ref.shape[1]

    @pl.loop(0, 4)
    def _(i):
        here = lanes(i, tokens // 2)
        basis_ref[here, :] = product(block_ref[here, :], lower_ref[...], ((1,), (1,)))

    first = lax.axis_index("tok") * tokens
    second = (lax.axis_index("tok") ^ 1) * tokens
    at = lax.broadcasted_iota(jnp.int32, (2 * tokens, width), 0)
    valid = jnp.where(at < tokens, first + at, second + at - tokens) < length_ref[...]

    @pl.loop(0, 2)
    def _(which):
        local = lanes(which)
        coef = product(first_ref[local, :] + second_ref[local, :], lower_ref[...], ((1,), (1,)))
        quer = jnp.concatenate(
            [query_ref[:, lanes((2 * which + mine) * group + i)] for i in range(group)]
        )
        reduced = product(quer, coef, ((1,), (0,))) / math.sqrt(HD)
        score_ref[...] = product(basis_ref[...], reduced, ((1,), (1,)))
        peak = jnp.max(jnp.where(valid, score_ref[...], NEG), axis=0, keepdims=True)
        weight = jnp.where(valid, jnp.exp(score_ref[...] - peak), 0.0)
        total = jnp.sum(weight, axis=0, keepdims=True)
        other = jnp.where(which == 0, low_ref[...], high_ref[...])
        acc = product(own_ref[:, local], weight[:tokens], ((0,), (0,))) + product(
            other, weight[tokens:], ((0,), (0,))
        )

        def give(ref):
            ref[pl.ds(0, HD), :] = acc
            ref[pl.ds(HD, 8), :] = jnp.broadcast_to(peak, (8, width))
            ref[pl.ds(HD + 8, 8), :] = jnp.broadcast_to(total, (8, width))

        pl.when(which == upper)(lambda: give(keep_ref))
        pl.when(which != upper)(lambda: give(send_ref))


def merge_kernel(first_ref, second_ref, out_ref):
    rows = out_ref.shape[0]
    top = jnp.maximum(first_ref[pl.ds(HD, 1), :], second_ref[pl.ds(HD, 1), :])
    one = jnp.exp(first_ref[pl.ds(HD, 1), :] - top)
    two = jnp.exp(second_ref[pl.ds(HD, 1), :] - top)
    total = first_ref[pl.ds(HD + 8, 1), :] * one + second_ref[pl.ds(HD + 8, 1), :] * two
    acc = first_ref[pl.ds(0, HD), :] * one + second_ref[pl.ds(0, HD), :] * two
    result = (acc / total).T
    for i in range(QH // KVH):
        out_ref[:, pl.ds(i * HD, HD)] = result[i * rows : (i + 1) * rows, :]


def gathered(share):
    beside = swap(share, "lay", 1)
    return share, beside, swap(share, "head", 1), swap(beside, "head", 1)


def after(x, *others):
    return lax.optimization_barrier((x, *others))[0]


def split_kernel(values_ref, kept_ref, first_ref, second_ref):
    mine, _, _, _ = pair_sides()
    for i, ref in enumerate((first_ref, second_ref)):
        kept_ref[:, pl.ds(i * HD, HD)] = values_ref[:, lanes(2 * i + mine)]
        ref[...] = values_ref[:, lanes(2 * i + 1 - mine)]


def paired_body(keys, values, queries, start_block, lengths):
    _, tokens, width = keys.shape
    keys, values, queries = keys[0], values[0], queries[0]
    rank = start_block.shape[1]
    rows = queries.shape[0]
    half, share = width // 2, rank // 4

    keep, send, keys_own, keys_send, gram = call(
        start_kernel,
        [vmem(half, rank)] * 2 + [vmem(tokens, half)] * 2 + [vmem(share, rank)],
        keys,
        start_block,
        scratch=[(rank // 2, rank)],
        flops=900_000_000,
    )
    gram = gram + swap(gram, "tok", 1)
    proj = keep + swap(send, "tok", 1)
    keys_other = swap(after(keys_send, proj), "tok", 1)
    values_own, *values_send = call(
        split_kernel,
        [vmem(tokens, half)] + [vmem(tokens, HD)] * 2,
        after(values, proj),
    )
    values_other = []
    lower = None
    for step in range(ITERS + 1):
        gram = gram + swap(gram, "tok", 2)
        last = step == ITERS
        if last:
            proj = after(proj, gram)
        first, second = proj, swap(proj, "tok", 2)
        if step > 0 and len(values_other) < 2:
            values_other.append(swap(after(values_send[len(values_other)], proj), "tok", 1))
        parts = gathered(gram)
        lower = inverse_factor(*parts)
        if last:
            break
        if step == 0:
            first = after(first, lower, values_own)
        else:
            first = after(first, *parts, *values_other)
        z_keep, z_send = call(
            mix_kernel,
            [vmem(tokens, rank)] * 2,
            keys_own,
            keys_other,
            first,
            second,
            scratch=[(half, rank)],
            flops=900_000_000,
        )
        near, far = summed_streams(z_keep, z_send, lower)
        block, proj, gram = call(
            block_kernel,
            [vmem(2 * tokens, rank), vmem(half, rank), vmem(share, rank)],
            keys_own,
            keys_other,
            near,
            far,
            lower,
            scratch=[(2 * tokens, rank), (rank // 2, rank)],
            flops=1_500_000_000,
        )
    keep, send = call(
        attend_kernel,
        [vmem(HD + 16, HD)] * 2,
        queries,
        block,
        first,
        second,
        lower,
        values_own,
        *values_other,
        jnp.tile(lengths, QH // KVH)[None, :],
        scratch=[(2 * tokens, rank), (2 * tokens, QH // KVH * rows)],
        flops=3_000_000_000,
    )
    result = call(merge_kernel, vmem(rows, half * 4), keep, swap(send, "tok", 2))
    return result[None, :, None, :]


def solution(mesh):
    paired = (mesh.shape["tok"], mesh.shape["lay"], mesh.shape["head"]) == (4, 2, 2)
    body = paired_body if paired else spread_body
    return jax.shard_map(
        body,
        mesh=mesh,
        in_specs=(
            P("lay", ("groups", "tok"), "head"),
            P("lay", ("groups", "tok"), "head"),
            P("lay", "groups", "head"),
            P(("groups", "tok"), None),
            P("groups"),
        ),
        out_specs=P("lay", "groups", "head", "tok"),
        check_vma=False,
    )
```

profile of v0, /device:TPU:0, one launch (start us, length us, event | category | flops | bytes accessed | tf_op | source)
XLA Modules:
  0.0 173.7 jit_solution(17808023363944685901)
XLA Ops:
  3.8 3.1 %collective-permute-start = (f32[256,256]{1,0:T(8,128)S(1)}, f32[256,256]{1,0:T(8,128)S(1)}, u32[]{:S(2)}, u32[]{:S(2)}) collective-permute-start(f32[256,256]{1,0:T(8,128)S(1)} %get-tuple-element.44), channel_id=1, source_target_pairs={{0,4},{4,0},{8,12},{12,8},{1,5},{5,1},{9,13},{13,9},{2,6},{6,2},{1... | collective-permute-start | bytes 786440 | tf_op jit(solution)/shard_map/ppermute | solution.py:126
  6.9 7.6 %collective-permute-done.2 = f32[64,256]{1,0:T(8,128)S(1)} collective-permute-done((f32[64,256]{1,0:T(8,128)S(1)}, f32[64,256]{1,0:T(8,128)S(1)}, u32[]{:S(2)}, u32[]{:S(2)}) %collective-permute-start.2) | collective-permute-done | bytes 65568 | tf_op jit(solution)/shard_map/ppermute | solution.py:126
  14.6 2.8 %collective-permute-start.3 = (f32[64,256]{1,0:T(8,128)S(1)}, f32[64,256]{1,0:T(8,128)S(1)}, u32[]{:S(2)}, u32[]{:S(2)}) collective-permute-start(f32[64,256]{1,0:T(8,128)S(1)} %add.40), channel_id=1, source_target_pairs={{0,8},{4,12},{8,0},{12,4},{1,9},{5,13},{9,1},{13,5},{2,10},{6,14},... | collective-permute-start | bytes 196616 | tf_op jit(solution)/shard_map/ppermute | solution.py:126
  17.4 2.4 %collective-permute-done.3 = f32[64,256]{1,0:T(8,128)S(1)} collective-permute-done((f32[64,256]{1,0:T(8,128)S(1)}, f32[64,256]{1,0:T(8,128)S(1)}, u32[]{:S(2)}, u32[]{:S(2)}) %collective-permute-start.3) | collective-permute-done | bytes 65568 | tf_op jit(solution)/shard_map/ppermute | solution.py:126
  21.6 2.6 %collective-permute-done.4.refs_0_ = f32[64,256]{1,0:T(8,128)S(1)} collective-permute-done((f32[64,256]{1,0:T(8,128)S(1)}, f32[64,256]{1,0:T(8,128)S(1)}, u32[]{:S(2)}, u32[]{:S(2)}) %collective-permute-start.4) | collective-permute-done | bytes 65568 | tf_op jit(solution)/shard_map/ppermute | solution.py:126
  24.2 2.9 %collective-permute-start.7 = (f32[256,256]{1,0:T(8,128)S(1)}, f32[256,256]{1,0:T(8,128)S(1)}, u32[]{:S(2)}, u32[]{:S(2)}) collective-permute-start(f32[256,256]{1,0:T(8,128)S(1)} %add.39.first_ref), channel_id=1, source_target_pairs={{0,8},{4,12},{8,0},{12,4},{1,9},{5,13},{9,1},{13,5},{2,10},{6,14},... | collective-permute-start | bytes 786440 | tf_op jit(solution)/shard_map/ppermute | solution.py:126
  27.1 2.1 %collective-permute-start.1 = (f32[512,256]{1,0:T(8,128)S(1)}, f32[512,256]{1,0:T(8,128)S(1)}, u32[]{:S(2)}, u32[]{:S(2)}) collective-permute-start(f32[512,256]{1,0:T(8,128)S(1)} %get-tuple-element.45), channel_id=1, source_target_pairs={{0,4},{4,0},{8,12},{12,8},{1,5},{5,1},{9,13},{13,9},{2,6},{6,2},{1... | collective-permute-start | bytes 1572872 | tf_op jit(solution)/shard_map/ppermute | solution.py:126
  29.2 7.8 %shard_map.56.lower_ref = f32[256,256]{1,0:T(8,128)S(1)} custom-call(f32[64,256]{1,0:T(8,128)S(1)} %add.41.own_ref, f32[64,256]{1,0:T(8,128)S(1)} %collective-permute-done.4.refs_0_, f32[64,256]{1,0:T(8,128)S(1)} %collective-permute-done.5.refs_1_, f32[64,256]{1,0:T(8,128)S(1)} %collective-permute-done.6.refs_2_), custom_call_target="tpu_custom_call" | custom-call | flops 10000000000 | bytes 524288 | tf_op jit(solution)/shard_map/pallas_call | solution.py:60
  37.2 2.6 %collective-permute-done.7.second_ref = f32[256,256]{1,0:T(8,128)S(1)} collective-permute-done((f32[256,256]{1,0:T(8,128)S(1)}, f32[256,256]{1,0:T(8,128)S(1)}, u32[]{:S(2)}, u32[]{:S(2)}) %collective-permute-start.7) | collective-permute-done | bytes 262176 | tf_op jit(solution)/shard_map/ppermute | solution.py:126
  39.8 5.7 %collective-permute-done.1.other_ref = f32[512,256]{1,0:T(8,128)S(1)} collective-permute-done((f32[512,256]{1,0:T(8,128)S(1)}, f32[512,256]{1,0:T(8,128)S(1)}, u32[]{:S(2)}, u32[]{:S(2)}) %collective-permute-start.1) | collective-permute-done | bytes 524320 | tf_op jit(solution)/shard_map/ppermute | solution.py:126
  47.2 1.9 %collective-permute-done.8.second_ref = f32[512,256]{1,0:T(8,128)S(1)} collective-permute-done((f32[512,256]{1,0:T(8,128)S(1)}, f32[512,256]{1,0:T(8,128)S(1)}, u32[]{:S(2)}, u32[]{:S(2)}) %collective-permute-start.8) | collective-permute-done | bytes 524320 | tf_op jit(solution)/shard_map/ppermute | solution.py:126
  52.3 2.4 %collective-permute-done.9 = f32[128,256]{1,0:T(8,128)S(1)} collective-permute-done((f32[128,256]{1,0:T(8,128)S(1)}, f32[128,256]{1,0:T(8,128)S(1)}, u32[]{:S(2)}, u32[]{:S(2)}) %collective-permute-start.9) | collective-permute-done | bytes 131104 | tf_op jit(solution)/shard_map/ppermute | solution.py:126
  58.0 1.8 %collective-permute-done.10 = f32[128,256]{1,0:T(8,128)S(1)} collective-permute-done((f32[128,256]{1,0:T(8,128)S(1)}, f32[128,256]{1,0:T(8,128)S(1)}, u32[]{:S(2)}, u32[]{:S(2)}) %collective-permute-start.10) | collective-permute-done | bytes 131104 | tf_op jit(solution)/shard_map/ppermute | solution.py:126
  64.9 2.6 %collective-permute-done.14 = f32[128,256]{1,0:T(8,128)S(1)} collective-permute-done((f32[128,256]{1,0:T(8,128)S(1)}, f32[128,256]{1,0:T(8,128)S(1)}, u32[]{:S(2)}, u32[]{:S(2)}) %collective-permute-start.14) | collective-permute-done | bytes 131104 | tf_op jit(solution)/shard_map/ppermute | solution.py:126
  67.6 1.9 %collective-permute-done.15.far_ref = f32[512,256]{1,0:T(8,128)S(1)} collective-permute-done((f32[512,256]{1,0:T(8,128)S(1)}, f32[512,256]{1,0:T(8,128)S(1)}, u32[]{:S(2)}, u32[]{:S(2)}) %collective-permute-start.15) | collective-permute-done | bytes 524320 | tf_op jit(solution)/shard_map/ppermute | solution.py:126
  69.5 5.4 %shard_map.60 = (f32[1024,256]{1,0:T(8,128)}, f32[256,256]{1,0:T(8,128)S(1)}, f32[64,256]{1,0:T(8,128)S(1)}) custom-call(f32[512,256]{1,0:T(8,128)S(1)} %get-tuple-element.41.own_ref, f32[512,256]{1,0:T(8,128)S(1)} %collective-permute-done.1.other_ref, f32[512,256]{1,0:T(8,128)S(1)} %pad_maximum_fusion.near_ref, ...), custom_call_target="tpu_custom_call" | custom-call | flops 1500000000 | bytes 3735552 | tf_op jit(solution)/shard_map/pallas_call | solution.py:60
  75.5 2.2 %collective-permute-start.21 = (f32[256,256]{1,0:T(8,128)S(1)}, f32[256,256]{1,0:T(8,128)S(1)}, u32[]{:S(2)}, u32[]{:S(2)}) collective-permute-start(f32[256,256]{1,0:T(8,128)S(1)} %get-tuple-element.61.first_ref), channel_id=1, source_target_pairs={{0,8},{4,12},{8,0},{12,4},{1,9},{5,13},{9,1},{13,5},{2,10},{6,14},... | collective-permute-start | bytes 786440 | tf_op jit(solution)/shard_map/ppermute | solution.py:126
  78.4 14.5 %collective-permute-done.16 = f32[64,256]{1,0:T(8,128)S(1)} collective-permute-done((f32[64,256]{1,0:T(8,128)S(1)}, f32[64,256]{1,0:T(8,128)S(1)}, u32[]{:S(2)}, u32[]{:S(2)}) %collective-permute-start.16) | collective-permute-done | bytes 65568 | tf_op jit(solution)/shard_map/ppermute | solution.py:126
  94.2 3.1 %collective-permute-done.17.refs_0_ = f32[64,256]{1,0:T(8,128)S(1)} collective-permute-done((f32[64,256]{1,0:T(8,128)S(1)}, f32[64,256]{1,0:T(8,128)S(1)}, u32[]{:S(2)}, u32[]{:S(2)}) %collective-permute-start.17) | collective-permute-done | bytes 65568 | tf_op jit(solution)/shard_map/ppermute | solution.py:126
  104.1 3.7 %collective-permute-done.23 = f32[128,256]{1,0:T(8,128)S(1)} collective-permute-done((f32[128,256]{1,0:T(8,128)S(1)}, f32[128,256]{1,0:T(8,128)S(1)}, u32[]{:S(2)}, u32[]{:S(2)}) %collective-permute-start.23) | collective-permute-done | bytes 131104 | tf_op jit(solution)/shard_map/ppermute | solution.py:126
  109.9 8.0 %shard_map.63.lower_ref = f32[256,256]{1,0:T(8,128)S(1)} custom-call(f32[64,256]{1,0:T(8,128)S(1)} %add.46.own_ref, f32[64,256]{1,0:T(8,128)S(1)} %collective-permute-done.17.refs_0_, f32[64,256]{1,0:T(8,128)S(1)} %collective-permute-done.18.refs_1_, f32[64,256]{1,0:T(8,128)S(1)} %collective-permute-done.19.refs_2_), custom_call_target="tpu_custom_call" | custom-call | flops 10000000000 | bytes 524288 | tf_op jit(solution)/shard_map/pallas_call | solution.py:60
  120.2 2.7 %collective-permute-done.25 = f32[128,256]{1,0:T(8,128)S(1)} collective-permute-done((f32[128,256]{1,0:T(8,128)S(1)}, f32[128,256]{1,0:T(8,128)S(1)}, u32[]{:S(2)}, u32[]{:S(2)}) %collective-permute-start.25) | collective-permute-done | bytes 131104 | tf_op jit(solution)/shard_map/ppermute | solution.py:126
  124.1 1.9 %collective-permute-done.29.far_ref = f32[512,256]{1,0:T(8,128)S(1)} collective-permute-done((f32[512,256]{1,0:T(8,128)S(1)}, f32[512,256]{1,0:T(8,128)S(1)}, u32[]{:S(2)}, u32[]{:S(2)}) %collective-permute-start.29) | collective-permute-done | bytes 524320 | tf_op jit(solution)/shard_map/ppermute | solution.py:126
  126.0 5.2 %shard_map.64 = (f32[1024,256]{1,0:T(8,128)S(1)}, f32[256,256]{1,0:T(8,128)S(1)}, f32[64,256]{1,0:T(8,128)S(1)}) custom-call(f32[512,256]{1,0:T(8,128)S(1)} %get-tuple-element.41.own_ref, f32[512,256]{1,0:T(8,128)S(1)} %collective-permute-done.1.other_ref, f32[512,256]{1,0:T(8,128)S(1)} %pad_maximum_fusion.1.near_ref, ...), custom_call_target="tpu_custom_call" | custom-call | flops 1500000000 | bytes 3735552 | tf_op jit(solution)/shard_map/pallas_call | solution.py:60
  131.2 3.0 %collective-permute-start.30 = (f32[64,256]{1,0:T(8,128)S(1)}, f32[64,256]{1,0:T(8,128)S(1)}, u32[]{:S(2)}, u32[]{:S(2)}) collective-permute-start(f32[64,256]{1,0:T(8,128)S(1)} %get-tuple-element.71), channel_id=1, source_target_pairs={{0,8},{4,12},{8,0},{12,4},{1,9},{5,13},{9,1},{13,5},{2,10},{6,14},... | collective-permute-start | bytes 196616 | tf_op jit(solution)/shard_map/ppermute | solution.py:126
  134.2 3.8 %collective-permute-done.30 = f32[64,256]{1,0:T(8,128)S(1)} collective-permute-done((f32[64,256]{1,0:T(8,128)S(1)}, f32[64,256]{1,0:T(8,128)S(1)}, u32[]{:S(2)}, u32[]{:S(2)}) %collective-permute-start.30) | collective-permute-done | bytes 65568 | tf_op jit(solution)/shard_map/ppermute | solution.py:126
  139.5 2.8 %collective-permute-done.32.refs_0_ = f32[64,256]{1,0:T(8,128)S(1)} collective-permute-done((f32[64,256]{1,0:T(8,128)S(1)}, f32[64,256]{1,0:T(8,128)S(1)}, u32[]{:S(2)}, u32[]{:S(2)}) %collective-permute-start.32) | collective-permute-done | bytes 65568 | tf_op jit(solution)/shard_map/ppermute | solution.py:126
  143.8 2.4 %collective-permute-start.35 = (f32[512,128]{1,0:T(8,128)S(1)}, f32[512,128]{1,0:T(8,128)S(1)}, u32[]{:S(2)}, u32[]{:S(2)}) collective-permute-start(f32[512,128]{1,0:T(8,128)S(1)} %get-tuple-element.74), channel_id=1, source_target_pairs={{0,4},{4,0},{8,12},{12,8},{1,5},{5,1},{9,13},{13,9},{2,6},{6,2},{1... | collective-permute-start | bytes 786440 | tf_op jit(solution)/shard_map/ppermute | solution.py:126
  146.2 7.8 %shard_map.65.lower_ref = f32[256,256]{1,0:T(8,128)S(1)} custom-call(f32[64,256]{1,0:T(8,128)S(1)} %add.51.own_ref, f32[64,256]{1,0:T(8,128)S(1)} %collective-permute-done.32.refs_0_, f32[64,256]{1,0:T(8,128)S(1)} %collective-permute-done.33.refs_1_, f32[64,256]{1,0:T(8,128)S(1)} %collective-permute-done.34.refs_2_), custom_call_target="tpu_custom_call" | custom-call | flops 10000000000 | bytes 524288 | tf_op jit(solution)/shard_map/pallas_call | solution.py:60
  154.0 3.8 %collective-permute-done.35.high_ref = f32[512,128]{1,0:T(8,128)S(1)} collective-permute-done((f32[512,128]{1,0:T(8,128)S(1)}, f32[512,128]{1,0:T(8,128)S(1)}, u32[]{:S(2)}, u32[]{:S(2)}) %collective-permute-start.35) | collective-permute-done | bytes 262176 | tf_op jit(solution)/shard_map/ppermute | solution.py:126
  157.8 8.8 %shard_map.66 = (f32[144,128]{1,0:T(8,128)S(1)}, f32[144,128]{1,0:T(8,128)S(1)}) custom-call(f32[16,4096]{1,0:T(8,128)S(1)} %bitcast.7, f32[1024,256]{1,0:T(8,128)S(1)} %get-tuple-element.69.block_ref, f32[256,256]{1,0:T(8,128)S(1)} %get-tuple-element.72.first_ref, f32[256,256]{1,0:T(8,128)S(1)} %collective-permute-done.31.second_ref, ...), custom_call_target="tpu_custom_call" | custom-call | flops 3000000000 | bytes 3293696 | tf_op jit(solution)/shard_map/pallas_call | solution.py:60
  167.6 5.2 %collective-permute-done.36.second_ref = f32[144,128]{1,0:T(8,128)S(1)} collective-permute-done((f32[144,128]{1,0:T(8,128)S(1)}, f32[144,128]{1,0:T(8,128)S(1)}, u32[]{:S(2)}, u32[]{:S(2)}) %collective-permute-start.36) | collective-permute-done | bytes 73760 | tf_op jit(solution)/shard_map/ppermute | solution.py:126
  (83 shorter events, 39.0 us)
Async XLA Ops:
  3.8 20.4 %collective-permute-start = (f32[256,256]{1,0:T(8,128)S(1)}, f32[256,256]{1,0:T(8,128)S(1)}, u32[]{:S(2)}, u32[]{:S(2)}) collective-permute-start(f32[256,256]{1,0:T(8,128)S(1)} %get-tuple-element.44), channel_id=1, source_target_pairs={{0,4},{4,0},{8,12},{12,8},{1,5},{5,1},{9,13},{13,9},{2,6},{6,2},{1... | collective-permute-start | bytes 786440 | tf_op jit(solution)/shard_map/ppermute | solution.py:126
  6.9 7.7 %collective-permute-start.2 = (f32[64,256]{1,0:T(8,128)S(1)}, f32[64,256]{1,0:T(8,128)S(1)}, u32[]{:S(2)}, u32[]{:S(2)}) collective-permute-start(f32[64,256]{1,0:T(8,128)S(1)} %get-tuple-element.46), channel_id=1, source_target_pairs={{0,4},{4,0},{8,12},{12,8},{1,5},{5,1},{9,13},{13,9},{2,6},{6,2},{1... | collective-permute-start | bytes 196616 | tf_op jit(solution)/shard_map/ppermute | solution.py:126
  14.6 5.2 %collective-permute-start.3 = (f32[64,256]{1,0:T(8,128)S(1)}, f32[64,256]{1,0:T(8,128)S(1)}, u32[]{:S(2)}, u32[]{:S(2)}) collective-permute-start(f32[64,256]{1,0:T(8,128)S(1)} %add.40), channel_id=1, source_target_pairs={{0,8},{4,12},{8,0},{12,4},{1,9},{5,13},{9,1},{13,5},{2,10},{6,14},... | collective-permute-start | bytes 196616 | tf_op jit(solution)/shard_map/ppermute | solution.py:126
  19.9 4.3 %collective-permute-start.4 = (f32[64,256]{1,0:T(8,128)S(1)}, f32[64,256]{1,0:T(8,128)S(1)}, u32[]{:S(2)}, u32[]{:S(2)}) collective-permute-start(f32[64,256]{1,0:T(8,128)S(1)} %add.41.own_ref), channel_id=1, source_target_pairs={{0,2},{2,0},{1,3},{3,1},{4,6},{6,4},{5,7},{7,5},{8,10},{10,8},{9,1... | collective-permute-start | bytes 196616 | tf_op jit(solution)/shard_map/ppermute | solution.py:126
  21.6 7.6 %collective-permute-start.5 = (f32[64,256]{1,0:T(8,128)S(1)}, f32[64,256]{1,0:T(8,128)S(1)}, u32[]{:S(2)}, u32[]{:S(2)}) collective-permute-start(f32[64,256]{1,0:T(8,128)S(1)} %add.41.own_ref), channel_id=1, source_target_pairs={{0,1},{1,0},{2,3},{3,2},{4,5},{5,4},{6,7},{7,6},{8,9},{9,8},{10,11... | collective-permute-start | bytes 196616 | tf_op jit(solution)/shard_map/ppermute | solution.py:126
  24.2 5.0 %collective-permute-start.6 = (f32[64,256]{1,0:T(8,128)S(1)}, f32[64,256]{1,0:T(8,128)S(1)}, u32[]{:S(2)}, u32[]{:S(2)}) collective-permute-start(f32[64,256]{1,0:T(8,128)S(1)} %collective-permute-done.4.refs_0_), channel_id=1, source_target_pairs={{0,1},{1,0},{2,3},{3,2},{4,5},{5,4},{6,7},{7,6},{8,9},{9,8},{10,11... | collective-permute-start | bytes 196616 | tf_op jit(solution)/shard_map/ppermute | solution.py:126
  24.2 15.6 %collective-permute-start.7 = (f32[256,256]{1,0:T(8,128)S(1)}, f32[256,256]{1,0:T(8,128)S(1)}, u32[]{:S(2)}, u32[]{:S(2)}) collective-permute-start(f32[256,256]{1,0:T(8,128)S(1)} %add.39.first_ref), channel_id=1, source_target_pairs={{0,8},{4,12},{8,0},{12,4},{1,9},{5,13},{9,1},{13,5},{2,10},{6,14},... | collective-permute-start | bytes 786440 | tf_op jit(solution)/shard_map/ppermute | solution.py:126
  27.1 18.4 %collective-permute-start.1 = (f32[512,256]{1,0:T(8,128)S(1)}, f32[512,256]{1,0:T(8,128)S(1)}, u32[]{:S(2)}, u32[]{:S(2)}) collective-permute-start(f32[512,256]{1,0:T(8,128)S(1)} %get-tuple-element.45), channel_id=1, source_target_pairs={{0,4},{4,0},{8,12},{12,8},{1,5},{5,1},{9,13},{13,9},{2,6},{6,2},{1... | collective-permute-start | bytes 1572872 | tf_op jit(solution)/shard_map/ppermute | solution.py:126
  49.1 5.6 %collective-permute-start.9 = (f32[128,256]{1,0:T(8,128)S(1)}, f32[128,256]{1,0:T(8,128)S(1)}, u32[]{:S(2)}, u32[]{:S(2)}) collective-permute-start(f32[128,256]{1,0:T(8,128)S(1)} %get-tuple-element.53), channel_id=1, source_target_pairs={{0,2},{2,0},{1,3},{3,1},{4,6},{6,4},{5,7},{7,5},{8,10},{10,8},{9,1... | collective-permute-start | bytes 393224 | tf_op jit(solution)/shard_map/ppermute | solution.py:126
  50.7 5.7 %collective-permute-start.12 = (f32[128,256]{1,0:T(8,128)S(1)}, f32[128,256]{1,0:T(8,128)S(1)}, u32[]{:S(2)}, u32[]{:S(2)}) collective-permute-start(f32[128,256]{1,0:T(8,128)S(1)} %get-tuple-element.56), channel_id=1, source_target_pairs={{0,4},{4,0},{8,12},{12,8},{1,5},{5,1},{9,13},{13,9},{2,6},{6,2},{1... | collective-permute-start | bytes 393224 | tf_op jit(solution)/shard_map/ppermute | solution.py:126
  54.8 5.0 %collective-permute-start.10 = (f32[128,256]{1,0:T(8,128)S(1)}, f32[128,256]{1,0:T(8,128)S(1)}, u32[]{:S(2)}, u32[]{:S(2)}) collective-permute-start(f32[128,256]{1,0:T(8,128)S(1)} %add.42), channel_id=1, source_target_pairs={{0,4},{4,0},{8,12},{12,8},{1,5},{5,1},{9,13},{13,9},{2,6},{6,2},{1... | collective-permute-start | bytes 393224 | tf_op jit(solution)/shard_map/ppermute | solution.py:126
  56.5 5.9 %collective-permute-start.13 = (f32[128,256]{1,0:T(8,128)S(1)}, f32[128,256]{1,0:T(8,128)S(1)}, u32[]{:S(2)}, u32[]{:S(2)}) collective-permute-start(f32[128,256]{1,0:T(8,128)S(1)} %add.44), channel_id=1, source_target_pairs={{0,2},{2,0},{1,3},{3,1},{4,6},{6,4},{5,7},{7,5},{8,10},{10,8},{9,1... | collective-permute-start | bytes 393224 | tf_op jit(solution)/shard_map/ppermute | solution.py:126
  59.8 5.0 %collective-permute-start.11 = (f32[128,256]{1,0:T(8,128)S(1)}, f32[128,256]{1,0:T(8,128)S(1)}, u32[]{:S(2)}, u32[]{:S(2)}) collective-permute-start(f32[128,256]{1,0:T(8,128)S(1)} %add.43), channel_id=1, source_target_pairs={{0,2},{2,0},{1,3},{3,1},{4,6},{6,4},{5,7},{7,5},{8,10},{10,8},{9,1... | collective-permute-start | bytes 393224 | tf_op jit(solution)/shard_map/ppermute | solution.py:126
  62.4 5.0 %collective-permute-start.14 = (f32[128,256]{1,0:T(8,128)S(1)}, f32[128,256]{1,0:T(8,128)S(1)}, u32[]{:S(2)}, u32[]{:S(2)}) collective-permute-start(f32[128,256]{1,0:T(8,128)S(1)} %add.45), channel_id=1, source_target_pairs={{0,4},{4,0},{8,12},{12,8},{1,5},{5,1},{9,13},{13,9},{2,6},{6,2},{1... | collective-permute-start | bytes 393224 | tf_op jit(solution)/shard_map/ppermute | solution.py:126
  74.9 23.6 %collective-permute-start.20 = (f32[512,128]{1,0:T(8,128)S(1)}, f32[512,128]{1,0:T(8,128)S(1)}, u32[]{:S(2)}, u32[]{:S(2)}) collective-permute-start(f32[512,128]{1,0:T(8,128)S(1)} %get-tuple-element.60), channel_id=1, source_target_pairs={{0,4},{4,0},{8,12},{12,8},{1,5},{5,1},{9,13},{13,9},{2,6},{6,2},{1... | collective-permute-start | bytes 786440 | tf_op jit(solution)/shard_map/ppermute | solution.py:126
  75.5 23.0 %collective-permute-start.21 = (f32[256,256]{1,0:T(8,128)S(1)}, f32[256,256]{1,0:T(8,128)S(1)}, u32[]{:S(2)}, u32[]{:S(2)}) collective-permute-start(f32[256,256]{1,0:T(8,128)S(1)} %get-tuple-element.61.first_ref), channel_id=1, source_target_pairs={{0,8},{4,12},{8,0},{12,4},{1,9},{5,13},{9,1},{13,5},{2,10},{6,14},... | collective-permute-start | bytes 786440 | tf_op jit(solution)/shard_map/ppermute | solution.py:126
  77.7 15.3 %collective-permute-start.16 = (f32[64,256]{1,0:T(8,128)S(1)}, f32[64,256]{1,0:T(8,128)S(1)}, u32[]{:S(2)}, u32[]{:S(2)}) collective-permute-start(f32[64,256]{1,0:T(8,128)S(1)} %get-tuple-element.58), channel_id=1, source_target_pairs={{0,8},{4,12},{8,0},{12,4},{1,9},{5,13},{9,1},{13,5},{2,10},{6,14},... | collective-permute-start | bytes 196616 | tf_op jit(solution)/shard_map/ppermute | solution.py:126
  93.0 4.3 %collective-permute-start.17 = (f32[64,256]{1,0:T(8,128)S(1)}, f32[64,256]{1,0:T(8,128)S(1)}, u32[]{:S(2)}, u32[]{:S(2)}) collective-permute-start(f32[64,256]{1,0:T(8,128)S(1)} %add.46.own_ref), channel_id=1, source_target_pairs={{0,2},{2,0},{1,3},{3,1},{4,6},{6,4},{5,7},{7,5},{8,10},{10,8},{9,1... | collective-permute-start | bytes 196616 | tf_op jit(solution)/shard_map/ppermute | solution.py:126
  94.2 3.1 %collective-permute-start.18 = (f32[64,256]{1,0:T(8,128)S(1)}, f32[64,256]{1,0:T(8,128)S(1)}, u32[]{:S(2)}, u32[]{:S(2)}) collective-permute-start(f32[64,256]{1,0:T(8,128)S(1)} %add.46.own_ref), channel_id=1, source_target_pairs={{0,1},{1,0},{2,3},{3,2},{4,5},{5,4},{6,7},{7,6},{8,9},{9,8},{10,11... | collective-permute-start | bytes 196616 | tf_op jit(solution)/shard_map/ppermute | solution.py:126
  102.2 5.6 %collective-permute-start.23 = (f32[128,256]{1,0:T(8,128)S(1)}, f32[128,256]{1,0:T(8,128)S(1)}, u32[]{:S(2)}, u32[]{:S(2)}) collective-permute-start(f32[128,256]{1,0:T(8,128)S(1)} %get-tuple-element.65), channel_id=1, source_target_pairs={{0,2},{2,0},{1,3},{3,1},{4,6},{6,4},{5,7},{7,5},{8,10},{10,8},{9,1... | collective-permute-start | bytes 393224 | tf_op jit(solution)/shard_map/ppermute | solution.py:126
  103.4 5.3 %collective-permute-start.26 = (f32[128,256]{1,0:T(8,128)S(1)}, f32[128,256]{1,0:T(8,128)S(1)}, u32[]{:S(2)}, u32[]{:S(2)}) collective-permute-start(f32[128,256]{1,0:T(8,128)S(1)} %get-tuple-element.68), channel_id=1, source_target_pairs={{0,4},{4,0},{8,12},{12,8},{1,5},{5,1},{9,13},{13,9},{2,6},{6,2},{1... | collective-permute-start | bytes 393224 | tf_op jit(solution)/shard_map/ppermute | solution.py:126
  107.8 10.0 %collective-permute-start.24 = (f32[128,256]{1,0:T(8,128)S(1)}, f32[128,256]{1,0:T(8,128)S(1)}, u32[]{:S(2)}, u32[]{:S(2)}) collective-permute-start(f32[128,256]{1,0:T(8,128)S(1)} %add.47), channel_id=1, source_target_pairs={{0,4},{4,0},{8,12},{12,8},{1,5},{5,1},{9,13},{13,9},{2,6},{6,2},{1... | collective-permute-start | bytes 393224 | tf_op jit(solution)/shard_map/ppermute | solution.py:126
  108.7 10.2 %collective-permute-start.27 = (f32[128,256]{1,0:T(8,128)S(1)}, f32[128,256]{1,0:T(8,128)S(1)}, u32[]{:S(2)}, u32[]{:S(2)}) collective-permute-start(f32[128,256]{1,0:T(8,128)S(1)} %add.49), channel_id=1, source_target_pairs={{0,2},{2,0},{1,3},{3,1},{4,6},{6,4},{5,7},{7,5},{8,10},{10,8},{9,1... | collective-permute-start | bytes 393224 | tf_op jit(solution)/shard_map/ppermute | solution.py:126
  117.9 5.0 %collective-permute-start.25 = (f32[128,256]{1,0:T(8,128)S(1)}, f32[128,256]{1,0:T(8,128)S(1)}, u32[]{:S(2)}, u32[]{:S(2)}) collective-permute-start(f32[128,256]{1,0:T(8,128)S(1)} %add.48), channel_id=1, source_target_pairs={{0,2},{2,0},{1,3},{3,1},{4,6},{6,4},{5,7},{7,5},{8,10},{10,8},{9,1... | collective-permute-start | bytes 393224 | tf_op jit(solution)/shard_map/ppermute | solution.py:126
  118.9 5.0 %collective-permute-start.28 = (f32[128,256]{1,0:T(8,128)S(1)}, f32[128,256]{1,0:T(8,128)S(1)}, u32[]{:S(2)}, u32[]{:S(2)}) collective-permute-start(f32[128,256]{1,0:T(8,128)S(1)} %add.50), channel_id=1, source_target_pairs={{0,4},{4,0},{8,12},{12,8},{1,5},{5,1},{9,13},{13,9},{2,6},{6,2},{1... | collective-permute-start | bytes 393224 | tf_op jit(solution)/shard_map/ppermute | solution.py:126
  131.2 6.8 %collective-permute-start.30 = (f32[64,256]{1,0:T(8,128)S(1)}, f32[64,256]{1,0:T(8,128)S(1)}, u32[]{:S(2)}, u32[]{:S(2)}) collective-permute-start(f32[64,256]{1,0:T(8,128)S(1)} %get-tuple-element.71), channel_id=1, source_target_pairs={{0,8},{4,12},{8,0},{12,4},{1,9},{5,13},{9,1},{13,5},{2,10},{6,14},... | collective-permute-start | bytes 196616 | tf_op jit(solution)/shard_map/ppermute | solution.py:126
  138.0 4.3 %collective-permute-start.32 = (f32[64,256]{1,0:T(8,128)S(1)}, f32[64,256]{1,0:T(8,128)S(1)}, u32[]{:S(2)}, u32[]{:S(2)}) collective-permute-start(f32[64,256]{1,0:T(8,128)S(1)} %add.51.own_ref), channel_id=1, source_target_pairs={{0,2},{2,0},{1,3},{3,1},{4,6},{6,4},{5,7},{7,5},{8,10},{10,8},{9,1... | collective-permute-start | bytes 196616 | tf_op jit(solution)/shard_map/ppermute | solution.py:126
  139.5 6.6 %collective-permute-start.33 = (f32[64,256]{1,0:T(8,128)S(1)}, f32[64,256]{1,0:T(8,128)S(1)}, u32[]{:S(2)}, u32[]{:S(2)}) collective-permute-start(f32[64,256]{1,0:T(8,128)S(1)} %add.51.own_ref), channel_id=1, source_target_pairs={{0,1},{1,0},{2,3},{3,2},{4,5},{5,4},{6,7},{7,6},{8,9},{9,8},{10,11... | collective-permute-start | bytes 196616 | tf_op jit(solution)/shard_map/ppermute | solution.py:126
  142.3 3.9 %collective-permute-start.34 = (f32[64,256]{1,0:T(8,128)S(1)}, f32[64,256]{1,0:T(8,128)S(1)}, u32[]{:S(2)}, u32[]{:S(2)}) collective-permute-start(f32[64,256]{1,0:T(8,128)S(1)} %collective-permute-done.32.refs_0_), channel_id=1, source_target_pairs={{0,1},{1,0},{2,3},{3,2},{4,5},{5,4},{6,7},{7,6},{8,9},{9,8},{10,11... | collective-permute-start | bytes 196616 | tf_op jit(solution)/shard_map/ppermute | solution.py:126
  142.4 15.4 %collective-permute-start.31 = (f32[256,256]{1,0:T(8,128)S(1)}, f32[256,256]{1,0:T(8,128)S(1)}, u32[]{:S(2)}, u32[]{:S(2)}) collective-permute-start(f32[256,256]{1,0:T(8,128)S(1)} %get-tuple-element.72.first_ref), channel_id=1, source_target_pairs={{0,8},{4,12},{8,0},{12,4},{1,9},{5,13},{9,1},{13,5},{2,10},{6,14},... | collective-permute-start | bytes 786440 | tf_op jit(solution)/shard_map/ppermute | solution.py:126
  143.8 14.0 %collective-permute-start.35 = (f32[512,128]{1,0:T(8,128)S(1)}, f32[512,128]{1,0:T(8,128)S(1)}, u32[]{:S(2)}, u32[]{:S(2)}) collective-permute-start(f32[512,128]{1,0:T(8,128)S(1)} %get-tuple-element.74), channel_id=1, source_target_pairs={{0,4},{4,0},{8,12},{12,8},{1,5},{5,1},{9,13},{13,9},{2,6},{6,2},{1... | collective-permute-start | bytes 786440 | tf_op jit(solution)/shard_map/ppermute | solution.py:126
  166.6 6.3 %collective-permute-start.36 = (f32[144,128]{1,0:T(8,128)S(1)}, f32[144,128]{1,0:T(8,128)S(1)}, u32[]{:S(2)}, u32[]{:S(2)}) collective-permute-start(f32[144,128]{1,0:T(8,128)S(1)} %get-tuple-element.76), channel_id=1, source_target_pairs={{0,8},{4,12},{8,0},{12,4},{1,9},{5,13},{9,1},{13,5},{2,10},{6,14},... | collective-permute-start | bytes 221192 | tf_op jit(solution)/shard_map/ppermute | solution.py:126
  (10 other events, 46.5 us)
where the time goes:
time: 174 us
  waiting for transfers between devices  80.5 us (46%)
  Pallas kernels  48 us (28%)
  starting transfers between devices  41.6 us (24%)
  local copies, waits for them, and re-layouts  3.06 us (2%)
    ppermute x37, waiting for transfers between devices, swap(): return lax.ppermute(x, axis, pairs)  80.5 us
    pallas_call x13, Pallas kernels, call(): pl.pallas_call(kernel, out_shape=out_shape, in_specs=[spec] * len(args),...  48 us
    ppermute x37, starting transfers between devices, swap(): return lax.ppermute(x, axis, pairs)  41.6 us
  transfers between devices with their start and end apart: 37, of which 25 were waited for; matrix products, arithmetic and copies ran while one was open for 0% of the time, Pallas kernels for 14%

commit v1 on v0

--- a/solution.py
+++ b/solution.py
@@ -68,17 +68,20 @@
     )(*args)
 
 
+def whole_gram(own_ref, part_refs, gram_ref):
+    if not part_refs:
+        gram_ref[...] = own_ref[...]
+        return
+    lay, head = lax.axis_index("lay"), lax.axis_index("head")
+    rows = own_ref.shape[0]
+    for i, ref in enumerate((own_ref, *part_refs)):
+        at = (2 * (head ^ (i // 2)) + (lay ^ (i % 2))) * rows
+        gram_ref[pl.ds(pl.multiple_of(at, rows), rows), :] = ref[...]
+
+
 def factor_kernel(own_ref, *refs):
-    *part_refs, out_ref, gram_ref, tile_ref, panel_ref = refs
-    part_refs = (own_ref, *part_refs)
-    if len(part_refs) == 1:
-        gram_ref[...] = own_ref[...]
-    else:
-        lay, head = lax.axis_index("lay"), lax.axis_index("head")
-        rows = own_ref.shape[0]
-        for i, ref in enumerate(part_refs):
-            at = (2 * (head ^ (i // 2)) + (lay ^ (i % 2))) * rows
-            gram_ref[pl.ds(pl.multiple_of(at, rows), rows), :] = ref[...]
+    *part_refs, out_ref, gram_ref, tile_ref, cross_ref = refs
+    whole_gram(own_ref, part_refs, gram_ref)
     half = tile_ref.shape[0]
     low, high = pl.ds(0, half), pl.ds(half, half)
 
@@ -92,12 +95,35 @@
         def _():
             panel = product(tile_ref[...], gram_ref[low, high], ((1,), (0,)))
             gram_ref[high, high] = gram_ref[high, high] - product(panel, panel, ((0,), (0,)))
-            panel_ref[...] = product(panel, tile_ref[...], ((0,), (0,)))
+            cross_ref[...] = product(panel, tile_ref[...], ((0,), (0,)))
             out_ref[low, high] = jnp.zeros((half, half), jnp.float32)
 
         @pl.when(i == 1)
         def _():
-            out_ref[high, low] = -product(tile_ref[...], panel_ref[...], ((1,), (0,)))
+            out_ref[high, low] = -product(tile_ref[...], cross_ref[...], ((1,), (0,)))
+
+
+def factor_low_kernel(own_ref, *refs):
+    *part_refs, tile_ref, cross_ref, left_ref, gram_ref = refs
+    whole_gram(own_ref, part_refs, gram_ref)
+    half = tile_ref.shape[0]
+    low, high = pl.ds(0, half), pl.ds(half, half)
+    tile_ref[...] = diagonal_inverse(gram_ref[low, low])
+    panel = product(tile_ref[...], gram_ref[low, high], ((1,), (0,)))
+    left_ref[...] = gram_ref[high, high] - product(panel, panel, ((0,), (0,)))
+    cross_ref[...] = product(panel, tile_ref[...], ((0,), (0,)))
+
+
+def factor_high_kernel(tile_ref, cross_ref, left_ref, out_ref):
+    half = tile_ref.shape[0]
+    low, high = pl.ds(0, half), pl.ds(half, half)
+    out_ref[low, low] = tile_ref[...]
+    out_ref[low, high] = jnp.zeros((half, half), jnp.float32)
+    out_ref[high, high] = diagonal_inverse(left_ref[...])
+    out_ref[high, low] = -product(out_ref[high, high], cross_ref[...], ((1,), (0,)))
+
+
+FACTOR_FLOPS = 1_000_000_000
 
 
 def inverse_factor(*parts):
@@ -108,8 +134,21 @@
         vmem(rank, rank),
         *parts,
         scratch=[(rank, rank), (half, half), (half, half)],
-        flops=10_000_000_000,
-    )
+        flops=FACTOR_FLOPS,
+    )
+
+
+def inverse_factor_low(*parts):
+    rank = parts[0].shape[1]
+    half = rank // 2
+    return call(
+        factor_low_kernel, [vmem(half, half)] * 3, *parts, scratch=[(rank, rank)], flops=FACTOR_FLOPS
+    )
+
+
+def inverse_factor_high(*halves):
+    rank = 2 * halves[0].shape[0]
+    return call(factor_high_kernel, vmem(rank, rank), *halves, flops=FACTOR_FLOPS)
 
 
 def distances(axis):
@@ -250,47 +289,35 @@
     return pl.ds(pl.multiple_of(index * size, size), size)
 
 
-def share_of(scratch_ref, out_ref):
-    rows = out_ref.shape[0]
-    out_ref[...] = scratch_ref[lanes(lax.axis_index("lay"), rows), :]
-
-
-def start_kernel(
-    keys_ref, block_ref, keep_ref, send_ref, kept_ref, sent_ref, gram_ref, scratch_ref
-):
-    mine, _, _, head = pair_sides()
-    half = block_ref.shape[1] // 2
-
-    @pl.loop(0, 2)
-    def _(i):
-        at = lanes(i)
+def gram_share(block_ref, scratch_ref, out_ref):
+    _, _, lay, head = pair_sides()
+    rows, half = out_ref.shape[0], scratch_ref.shape[0]
+    scratch_ref[...] = product(block_ref[:, lanes(head, half)], block_ref[...], ((0,), (0,)))
+    out_ref[...] = scratch_ref[lanes(lay, rows), :]
+
+
+def gram_kernel(block_ref, out_ref, scratch_ref):
+    gram_share(block_ref, scratch_ref, out_ref)
+
+
+def start_kernel(keys_ref, block_ref, keep_ref, send_ref, kept_ref, sent_ref):
+    mine, _, _, _ = pair_sides()
+    for i in range(2):
+        at = pl.ds(i * HD, HD)
         kept_ref[:, at] = keys_ref[:, lanes(2 * i + mine)]
         sent_ref[:, at] = keys_ref[:, lanes(2 * i + 1 - mine)]
-
     send_ref[...] = product(sent_ref[...], block_ref[...], ((0,), (0,)))
     keep_ref[...] = product(kept_ref[...], block_ref[...], ((0,), (0,)))
-    scratch_ref[...] = product(block_ref[:, lanes(head, half)], block_ref[...], ((0,), (0,)))
-    share_of(scratch_ref, gram_ref)
-
-
-def mix_kernel(own_ref, other_ref, first_ref, second_ref, keep_ref, send_ref, coef_ref):
+
+
+def mix_kernel(own_ref, other_ref, first_ref, second_ref, keep_ref, send_ref):
     mine, _, _, head = pair_sides()
-    coef_ref[...] = first_ref[...] + second_ref[...]
+    coef = first_ref[...] + second_ref[...]
     half = own_ref.shape[0] // 2
     for keys_ref, piece in ((own_ref, mine), (other_ref, 1 - mine)):
         to = lanes(piece, half)
-
-        @pl.loop(0, 2)
-        def _(i):
-            term = product(keys_ref[lanes(i, half), :], coef_ref[...], ((1,), (0,)))
-
-            @pl.when(i == head)
-            def _():
-                keep_ref[to, :] = term
-
-            @pl.when(i != head)
-            def _():
-                send_ref[to, :] = term
+        keep_ref[to, :] = product(keys_ref[lanes(head, half), :], coef, ((1,), (0,)))
+        send_ref[to, :] = product(keys_ref[lanes(1 - head, half), :], coef, ((1,), (0,)))
 
 
 def streams_kernel(first_ref, second_ref, a_keep, a_send, b_keep, b_send):
@@ -322,12 +349,10 @@
     return stack, swap(stack, "head", 1)
 
 
-def block_kernel(
-    own_ref, other_ref, near_ref, far_ref, lower_ref, block_ref, proj_ref, gram_ref, whole_ref, scratch_ref
-):
+def block_kernel(near_ref, far_ref, lower_ref, block_ref, gram_ref, whole_ref, scratch_ref):
     mine, _, lay, head = pair_sides()
     count = near_ref.shape[0] // 4
-    half, eighth = count // 2, count // 2
+    half = count // 2
     piece_rows = near_ref.shape[0]
     for ref, owner in ((near_ref, head), (far_ref, 1 - head)):
         for i in range(2):
@@ -341,21 +366,15 @@
             whole_ref[pl.ds(pl.multiple_of(place, count), count), :] = ref[
                 pl.ds((2 + i) * count, count), :
             ]
-    columns = scratch_ref.shape[0]
-    proj_ref[...] = jnp.zeros(proj_ref.shape, jnp.float32)
-    scratch_ref[...] = jnp.zeros(scratch_ref.shape, jnp.float32)
-    for i, keys_ref in enumerate((own_ref, other_ref)):
-
-        @pl.loop(0, 2)
-        def _(k):
-            rows = piece_rows // 2
-            here = pl.ds(pl.multiple_of(i * piece_rows + k * rows, rows), rows)
-            block_ref[here, :] = product(whole_ref[here, :], lower_ref[...], ((1,), (1,)))
-            block = block_ref[here, :]
-            proj_ref[...] += product(keys_ref[lanes(k, rows), :], block, ((0,), (0,)))
-            scratch_ref[...] += product(block_ref[here, lanes(head, columns)], block, ((0,), (0,)))
-
-    share_of(scratch_ref, gram_ref)
+    block_ref[...] = product(whole_ref[...], lower_ref[...], ((1,), (1,)))
+    gram_share(block_ref, scratch_ref, gram_ref)
+
+
+def project_kernel(own_ref, other_ref, block_ref, proj_ref):
+    rows = own_ref.shape[0]
+    proj_ref[...] = product(own_ref[...], block_ref[pl.ds(0, rows), :], ((0,), (0,))) + product(
+        other_ref[...], block_ref[pl.ds(rows, rows), :], ((0,), (0,))
+    )
 
 
 def attend_kernel(
@@ -371,47 +390,41 @@
     keep_ref,
     send_ref,
     basis_ref,
-    score_ref,
 ):
     mine, upper, _, _ = pair_sides()
     group = QH // KVH
     tokens = own_ref.shape[0]
-    width = score_ref.shape[1]
-
-    @pl.loop(0, 4)
-    def _(i):
-        here = lanes(i, tokens // 2)
-        basis_ref[here, :] = product(block_ref[here, :], lower_ref[...], ((1,), (1,)))
-
-    first = lax.axis_index("tok") * tokens
-    second = (lax.axis_index("tok") ^ 1) * tokens
-    at = lax.broadcasted_iota(jnp.int32, (2 * tokens, width), 0)
-    valid = jnp.where(at < tokens, first + at, second + at - tokens) < length_ref[...]
-
-    @pl.loop(0, 2)
-    def _(which):
-        local = lanes(which)
-        coef = product(first_ref[local, :] + second_ref[local, :], lower_ref[...], ((1,), (1,)))
+    width = length_ref.shape[1]
+    basis_ref[...] = product(block_ref[...], lower_ref[...], ((1,), (1,)))
+    coef = product(first_ref[...] + second_ref[...], lower_ref[...], ((1,), (1,)))
+    reduced = []
+    for which in range(2):
         quer = jnp.concatenate(
             [query_ref[:, lanes((2 * which + mine) * group + i)] for i in range(group)]
         )
-        reduced = product(quer, coef, ((1,), (0,))) / math.sqrt(HD)
-        score_ref[...] = product(basis_ref[...], reduced, ((1,), (1,)))
-        peak = jnp.max(jnp.where(valid, score_ref[...], NEG), axis=0, keepdims=True)
-        weight = jnp.where(valid, jnp.exp(score_ref[...] - peak), 0.0)
-        total = jnp.sum(weight, axis=0, keepdims=True)
-        other = jnp.where(which == 0, low_ref[...], high_ref[...])
-        acc = product(own_ref[:, local], weight[:tokens], ((0,), (0,))) + product(
-            other, weight[tokens:], ((0,), (0,))
-        )
+        factor = coef[which * HD : (which + 1) * HD]
+        reduced.append(product(quer, factor, ((1,), (0,))) / math.sqrt(HD))
+    scores = product(basis_ref[...], jnp.concatenate(reduced), ((1,), (1,)))
+    first = lax.axis_index("tok") * tokens
+    second = (lax.axis_index("tok") ^ 1) * tokens
+    at = lax.broadcasted_iota(jnp.int32, scores.shape, 0)
+    valid = jnp.where(at < tokens, first + at, second + at - tokens) < length_ref[...]
+    peak = jnp.max(jnp.where(valid, scores, NEG), axis=0, keepdims=True)
+    weight = jnp.where(valid, jnp.exp(scores - peak), 0.0)
+    total = jnp.sum(weight, axis=0, keepdims=True)
+    half = width // 2
+    for which, there_ref in enumerate((low_ref, high_ref)):
+        here = slice(which * half, (which + 1) * half)
+        acc = product(own_ref[:, pl.ds(which * HD, HD)], weight[:tokens, here], ((0,), (0,)))
+        acc = acc + product(there_ref[...], weight[tokens:, here], ((0,), (0,)))
 
         def give(ref):
             ref[pl.ds(0, HD), :] = acc
-            ref[pl.ds(HD, 8), :] = jnp.broadcast_to(peak, (8, width))
-            ref[pl.ds(HD + 8, 8), :] = jnp.broadcast_to(total, (8, width))
-
-        pl.when(which == upper)(lambda: give(keep_ref))
-        pl.when(which != upper)(lambda: give(send_ref))
+            ref[pl.ds(HD, 8), :] = jnp.broadcast_to(peak[:, here], (8, half))
+            ref[pl.ds(HD + 8, 8), :] = jnp.broadcast_to(total[:, here], (8, half))
+
+        pl.when(upper == which)(lambda: give(keep_ref))
+        pl.when(upper != which)(lambda: give(send_ref))
 
 
 def merge_kernel(first_ref, second_ref, out_ref):
@@ -449,16 +462,22 @@
     rows = queries.shape[0]
     half, share = width // 2, rank // 4
 
-    keep, send, keys_own, keys_send, gram = call(
-        start_kernel,
-        [vmem(half, rank)] * 2 + [vmem(tokens, half)] * 2 + [vmem(share, rank)],
-        keys,
+    gram = call(
+        gram_kernel,
+        vmem(share, rank),
         start_block,
         scratch=[(rank // 2, rank)],
+        flops=400_000_000,
+    )
+    keep, send, keys_own, keys_send = call(
+        start_kernel,
+        [vmem(half, rank)] * 2 + [vmem(tokens, half)] * 2,
+        keys,
+        after(start_block, gram),
         flops=900_000_000,
     )
     gram = gram + swap(gram, "tok", 1)
-    proj = keep + swap(send, "tok", 1)
+    proj = keep + swap(after(send, gram), "tok", 1)
     keys_other = swap(after(keys_send, proj), "tok", 1)
     values_own, *values_send = call(
         split_kernel,
@@ -470,19 +489,19 @@
     for step in range(ITERS + 1):
         gram = gram + swap(gram, "tok", 2)
         last = step == ITERS
-        if last:
-            proj = after(proj, gram)
         first, second = proj, swap(proj, "tok", 2)
         if step > 0 and len(values_other) < 2:
-            values_other.append(swap(after(values_send[len(values_other)], proj), "tok", 1))
+            values_other.append(swap(after(values_send[len(values_other)], proj, gram), "tok", 1))
         parts = gathered(gram)
-        lower = inverse_factor(*parts)
+        if step == 0 or last:
+            lower = inverse_factor(*parts)
+            first = after(first, lower, values_own)
+        else:
+            halves = inverse_factor_low(*parts)
+            first = after(first, halves[0], *values_other)
+            lower = inverse_factor_high(*halves)
         if last:
             break
-        if step == 0:
-            first = after(first, lower, values_own)
-        else:
-            first = after(first, *parts, *values_other)
         z_keep, z_send = call(
             mix_kernel,
             [vmem(tokens, rank)] * 2,
@@ -490,20 +509,25 @@
             keys_other,
             first,
             second,
-            scratch=[(half, rank)],
             flops=900_000_000,
         )
         near, far = summed_streams(z_keep, z_send, lower)
-        block, proj, gram = call(
+        block, gram = call(
             block_kernel,
-            [vmem(2 * tokens, rank), vmem(half, rank), vmem(share, rank)],
-            keys_own,
-            keys_other,
+            [vmem(2 * tokens, rank), vmem(share, rank)],
             near,
             far,
             lower,
             scratch=[(2 * tokens, rank), (rank // 2, rank)],
-            flops=1_500_000_000,
+            flops=1_200_000_000,
+        )
+        proj = call(
+            project_kernel,
+            vmem(half, rank),
+            keys_own,
+            keys_other,
+            block,
+            flops=900_000_000,
         )
     keep, send = call(
         attend_kernel,
@@ -515,8 +539,8 @@
         lower,
         values_own,
         *values_other,
-        jnp.tile(lengths, QH // KVH)[None, :],
-        scratch=[(2 * tokens, rank), (2 * tokens, QH // KVH * rows)],
+        jnp.tile(lengths, 2 * (QH // KVH))[None, :],
+        scratch=[(2 * tokens, rank)],
         flops=3_000_000_000,
     )
     result = call(merge_kernel, vmem(rows, half * 4), keep, swap(send, "tok", 2))

time: 174 us -> 157 us (0.902)
  Pallas kernels: 48 us -> 40.6 us
  starting transfers between devices: 41.6 us -> 37.3 us
  waiting for transfers between devices: 80.5 us -> 76.2 us
    pallas_call x13 -> x17, Pallas kernels: 48 us -> 40.6 us  [call(): pl.pallas_call(kernel, out_shape=out_shape, in_specs=[spec] * len(args),...]
    ppermute x37, waiting for transfers between devices: 80.5 us -> 76.2 us  [swap(): return lax.ppermute(x, axis, pairs)]
    ppermute x37, starting transfers between devices: 41.6 us -> 37.3 us  [swap(): return lax.ppermute(x, axis, pairs)]
  transfers between devices with their start and end apart: 37 -> 37, of which waited for: 25 -> 27; matrix products, arithmetic and copies ran while one was open for 0% -> 0% of each run, Pallas kernels for 14% -> 18%
where the time goes in v1:
time: 157 us
  waiting for transfers between devices  76.2 us (49%)
  Pallas kernels  40.6 us (26%)
  starting transfers between devices  37.3 us (24%)
  local copies, waits for them, and re-layouts  1.94 us (1%)
    ppermute x37, waiting for transfers between devices, swap(): return lax.ppermute(x, axis, pairs)  76.2 us
    pallas_call x17, Pallas kernels, call(): pl.pallas_call(kernel, out_shape=out_shape, in_specs=[spec] * len(args),...  40.6 us
    ppermute x37, starting transfers between devices, swap(): return lax.ppermute(x, axis, pairs)  37.3 us
  transfers between devices with their start and end apart: 37, of which 27 were waited for; matrix products, arithmetic and copies ran while one was open for 0% of the time, Pallas kernels for 18%

profile of v1, /device:TPU:0, one launch (start us, length us, event | category | flops | bytes accessed | tf_op | source)
XLA Modules:
  0.0 156.7 jit_solution(3108809448446367802)
XLA Ops:
  1.6 3.1 %collective-permute-start = (f32[64,256]{1,0:T(8,128)S(1)}, f32[64,256]{1,0:T(8,128)S(1)}, u32[]{:S(2)}, u32[]{:S(2)}) collective-permute-start(f32[64,256]{1,0:T(8,128)S(1)} %shard_map.55), channel_id=1, source_target_pairs={{0,4},{4,0},{8,12},{12,8},{1,5},{5,1},{9,13},{13,9},{2,6},{6,2},{1... | collective-permute-start | bytes 196616 | tf_op jit(solution)/shard_map/ppermute | solution.py:165
  7.0 2.1 %collective-permute-start.1 = (f32[256,256]{1,0:T(8,128)S(1)}, f32[256,256]{1,0:T(8,128)S(1)}, u32[]{:S(2)}, u32[]{:S(2)}) collective-permute-start(f32[256,256]{1,0:T(8,128)S(1)} %get-tuple-element.49), channel_id=1, source_target_pairs={{0,4},{4,0},{8,12},{12,8},{1,5},{5,1},{9,13},{13,9},{2,6},{6,2},{1... | collective-permute-start | bytes 786440 | tf_op jit(solution)/shard_map/ppermute | solution.py:165
  9.1 5.2 %collective-permute-done.1 = f32[256,256]{1,0:T(8,128)S(1)} collective-permute-done((f32[256,256]{1,0:T(8,128)S(1)}, f32[256,256]{1,0:T(8,128)S(1)}, u32[]{:S(2)}, u32[]{:S(2)}) %collective-permute-start.1) | collective-permute-done | bytes 262176 | tf_op jit(solution)/shard_map/ppermute | solution.py:165
  14.2 1.8 %collective-permute-start.2 = (f32[512,256]{1,0:T(8,128)S(1)}, f32[512,256]{1,0:T(8,128)S(1)}, u32[]{:S(2)}, u32[]{:S(2)}) collective-permute-start(f32[512,256]{1,0:T(8,128)S(1)} %get-tuple-element.50), channel_id=1, source_target_pairs={{0,4},{4,0},{8,12},{12,8},{1,5},{5,1},{9,13},{13,9},{2,6},{6,2},{1... | collective-permute-start | bytes 1572872 | tf_op jit(solution)/shard_map/ppermute | solution.py:165
  16.1 2.6 %collective-permute-start.3 = (f32[64,256]{1,0:T(8,128)S(1)}, f32[64,256]{1,0:T(8,128)S(1)}, u32[]{:S(2)}, u32[]{:S(2)}) collective-permute-start(f32[64,256]{1,0:T(8,128)S(1)} %add.39), channel_id=1, source_target_pairs={{0,8},{4,12},{8,0},{12,4},{1,9},{5,13},{9,1},{13,5},{2,10},{6,14},... | collective-permute-start | bytes 196616 | tf_op jit(solution)/shard_map/ppermute | solution.py:165
  19.0 10.4 %collective-permute-done.3 = f32[64,256]{1,0:T(8,128)S(1)} collective-permute-done((f32[64,256]{1,0:T(8,128)S(1)}, f32[64,256]{1,0:T(8,128)S(1)}, u32[]{:S(2)}, u32[]{:S(2)}) %collective-permute-start.3) | collective-permute-done | bytes 65568 | tf_op jit(solution)/shard_map/ppermute | solution.py:165
  31.0 2.8 %collective-permute-done.4.refs_0_ = f32[64,256]{1,0:T(8,128)S(1)} collective-permute-done((f32[64,256]{1,0:T(8,128)S(1)}, f32[64,256]{1,0:T(8,128)S(1)}, u32[]{:S(2)}, u32[]{:S(2)}) %collective-permute-start.4) | collective-permute-done | bytes 65568 | tf_op jit(solution)/shard_map/ppermute | solution.py:165
  35.0 8.0 %shard_map.57.lower_ref = f32[256,256]{1,0:T(8,128)S(1)} custom-call(f32[64,256]{1,0:T(8,128)S(1)} %add.41.own_ref, f32[64,256]{1,0:T(8,128)S(1)} %collective-permute-done.4.refs_0_, f32[64,256]{1,0:T(8,128)S(1)} %collective-permute-done.5.refs_1_, f32[64,256]{1,0:T(8,128)S(1)} %collective-permute-done.6.refs_2_), custom_call_target="tpu_custom_call" | custom-call | flops 1000000000 | bytes 524288 | tf_op jit(solution)/shard_map/pallas_call | solution.py:60
  44.4 1.8 %collective-permute-done.8.second_ref = f32[512,256]{1,0:T(8,128)S(1)} collective-permute-done((f32[512,256]{1,0:T(8,128)S(1)}, f32[512,256]{1,0:T(8,128)S(1)}, u32[]{:S(2)}, u32[]{:S(2)}) %collective-permute-start.8) | collective-permute-done | bytes 524320 | tf_op jit(solution)/shard_map/ppermute | solution.py:165
  47.8 3.5 %collective-permute-start.12 = (f32[128,256]{1,0:T(8,128)S(1)}, f32[128,256]{1,0:T(8,128)S(1)}, u32[]{:S(2)}, u32[]{:S(2)}) collective-permute-start(f32[128,256]{1,0:T(8,128)S(1)} %get-tuple-element.60), channel_id=1, source_target_pairs={{0,4},{4,0},{8,12},{12,8},{1,5},{5,1},{9,13},{13,9},{2,6},{6,2},{1... | collective-permute-start | bytes 393224 | tf_op jit(solution)/shard_map/ppermute | solution.py:165
  51.9 3.6 %collective-permute-start.10 = (f32[128,256]{1,0:T(8,128)S(1)}, f32[128,256]{1,0:T(8,128)S(1)}, u32[]{:S(2)}, u32[]{:S(2)}) collective-permute-start(f32[128,256]{1,0:T(8,128)S(1)} %add.42), channel_id=1, source_target_pairs={{0,4},{4,0},{8,12},{12,8},{1,5},{5,1},{9,13},{13,9},{2,6},{6,2},{1... | collective-permute-start | bytes 393224 | tf_op jit(solution)/shard_map/ppermute | solution.py:165
  60.0 1.6 collective-permute-done.13
  63.5 3.1 %collective-permute-done.14 = f32[128,256]{1,0:T(8,128)S(1)} collective-permute-done((f32[128,256]{1,0:T(8,128)S(1)}, f32[128,256]{1,0:T(8,128)S(1)}, u32[]{:S(2)}, u32[]{:S(2)}) %collective-permute-start.14) | collective-permute-done | bytes 131104 | tf_op jit(solution)/shard_map/ppermute | solution.py:165
  66.7 1.9 %collective-permute-done.15.far_ref = f32[512,256]{1,0:T(8,128)S(1)} collective-permute-done((f32[512,256]{1,0:T(8,128)S(1)}, f32[512,256]{1,0:T(8,128)S(1)}, u32[]{:S(2)}, u32[]{:S(2)}) %collective-permute-start.15) | collective-permute-done | bytes 524320 | tf_op jit(solution)/shard_map/ppermute | solution.py:165
  68.6 2.5 %shard_map.61 = (f32[1024,256]{1,0:T(8,128)S(1)}, f32[64,256]{1,0:T(8,128)S(1)}) custom-call(f32[512,256]{1,0:T(8,128)S(1)} %pad_maximum_fusion.near_ref, f32[512,256]{1,0:T(8,128)S(1)} %collective-permute-done.15.far_ref, f32[256,256]{1,0:T(8,128)S(1)} %shard_map.57.lower_ref), custom_call_target="tpu_custom_call" | custom-call | flops 1200000000 | bytes 2424832 | tf_op jit(solution)/shard_map/pallas_call | solution.py:60
  72.7 4.8 %collective-permute-done.16 = f32[64,256]{1,0:T(8,128)S(1)} collective-permute-done((f32[64,256]{1,0:T(8,128)S(1)}, f32[64,256]{1,0:T(8,128)S(1)}, u32[]{:S(2)}, u32[]{:S(2)}) %collective-permute-start.16) | collective-permute-done | bytes 65568 | tf_op jit(solution)/shard_map/ppermute | solution.py:165
  77.6 1.9 %collective-permute-start.21 = (f32[256,256]{1,0:T(8,128)S(1)}, f32[256,256]{1,0:T(8,128)S(1)}, u32[]{:S(2)}, u32[]{:S(2)}) collective-permute-start(f32[256,256]{1,0:T(8,128)S(1)} %shard_map.62.first_ref), channel_id=1, source_target_pairs={{0,8},{4,12},{8,0},{12,4},{1,9},{5,13},{9,1},{13,5},{2,10},{6,14},... | collective-permute-start | bytes 786440 | tf_op jit(solution)/shard_map/ppermute | solution.py:165
  81.0 2.8 %collective-permute-done.17.refs_0_ = f32[64,256]{1,0:T(8,128)S(1)} collective-permute-done((f32[64,256]{1,0:T(8,128)S(1)}, f32[64,256]{1,0:T(8,128)S(1)}, u32[]{:S(2)}, u32[]{:S(2)}) %collective-permute-start.17) | collective-permute-done | bytes 65568 | tf_op jit(solution)/shard_map/ppermute | solution.py:165
  85.1 4.0 %shard_map.63 = (f32[128,128]{1,0:T(8,128)S(1)}, f32[128,128]{1,0:T(8,128)S(1)}, f32[128,128]{1,0:T(8,128)S(1)}) custom-call(f32[64,256]{1,0:T(8,128)S(1)} %add.46.own_ref, f32[64,256]{1,0:T(8,128)S(1)} %collective-permute-done.17.refs_0_, f32[64,256]{1,0:T(8,128)S(1)} %collective-permute-done.18.refs_1_, f32[64,256]{1,0:T(8,128)S(1)} %collective-permute-done.19.refs_2_), custom_call_target="tpu_custom_call" | custom-call | flops 1000000000 | bytes 458752 | tf_op jit(solution)/shard_map/pallas_call | solution.py:60
  90.1 2.3 %collective-permute-done.21.second_ref = f32[256,256]{1,0:T(8,128)S(1)} collective-permute-done((f32[256,256]{1,0:T(8,128)S(1)}, f32[256,256]{1,0:T(8,128)S(1)}, u32[]{:S(2)}, u32[]{:S(2)}) %collective-permute-start.21) | collective-permute-done | bytes 262176 | tf_op jit(solution)/shard_map/ppermute | solution.py:165
  93.6 1.9 %collective-permute-done.22.second_ref = f32[512,256]{1,0:T(8,128)S(1)} collective-permute-done((f32[512,256]{1,0:T(8,128)S(1)}, f32[512,256]{1,0:T(8,128)S(1)}, u32[]{:S(2)}, u32[]{:S(2)}) %collective-permute-start.22) | collective-permute-done | bytes 524320 | tf_op jit(solution)/shard_map/ppermute | solution.py:165
  96.7 4.5 %collective-permute-done.23 = f32[128,256]{1,0:T(8,128)S(1)} collective-permute-done((f32[128,256]{1,0:T(8,128)S(1)}, f32[128,256]{1,0:T(8,128)S(1)}, u32[]{:S(2)}, u32[]{:S(2)}) %collective-permute-start.23) | collective-permute-done | bytes 131104 | tf_op jit(solution)/shard_map/ppermute | solution.py:165
  103.0 3.9 %shard_map.66.lower_ref = f32[256,256]{1,0:T(8,128)S(1)} custom-call(f32[128,128]{1,0:T(8,128)S(1)} %get-tuple-element.63.tile_ref, f32[128,128]{1,0:T(8,128)S(1)} %get-tuple-element.71.cross_ref, f32[128,128]{1,0:T(8,128)S(1)} %get-tuple-element.72.left_ref), custom_call_target="tpu_custom_call" | custom-call | flops 1000000000 | bytes 458752 | tf_op jit(solution)/shard_map/pallas_call | solution.py:60
  109.4 2.5 %collective-permute-done.25 = f32[128,256]{1,0:T(8,128)S(1)} collective-permute-done((f32[128,256]{1,0:T(8,128)S(1)}, f32[128,256]{1,0:T(8,128)S(1)}, u32[]{:S(2)}, u32[]{:S(2)}) %collective-permute-start.25) | collective-permute-done | bytes 131104 | tf_op jit(solution)/shard_map/ppermute | solution.py:165
  113.2 1.9 %collective-permute-done.29.far_ref = f32[512,256]{1,0:T(8,128)S(1)} collective-permute-done((f32[512,256]{1,0:T(8,128)S(1)}, f32[512,256]{1,0:T(8,128)S(1)}, u32[]{:S(2)}, u32[]{:S(2)}) %collective-permute-start.29) | collective-permute-done | bytes 524320 | tf_op jit(solution)/shard_map/ppermute | solution.py:165
  115.1 2.5 %shard_map.67 = (f32[1024,256]{1,0:T(8,128)S(1)}, f32[64,256]{1,0:T(8,128)S(1)}) custom-call(f32[512,256]{1,0:T(8,128)S(1)} %pad_maximum_fusion.1.near_ref, f32[512,256]{1,0:T(8,128)S(1)} %collective-permute-done.29.far_ref, f32[256,256]{1,0:T(8,128)S(1)} %shard_map.66.lower_ref), custom_call_target="tpu_custom_call" | custom-call | flops 1200000000 | bytes 2424832 | tf_op jit(solution)/shard_map/pallas_call | solution.py:60
  120.1 1.7 %collective-permute-start.34 = (f32[256,256]{1,0:T(8,128)S(1)}, f32[256,256]{1,0:T(8,128)S(1)}, u32[]{:S(2)}, u32[]{:S(2)}) collective-permute-start(f32[256,256]{1,0:T(8,128)S(1)} %shard_map.68.first_ref), channel_id=1, source_target_pairs={{0,8},{4,12},{8,0},{12,4},{1,9},{5,13},{9,1},{13,5},{2,10},{6,14},... | collective-permute-start | bytes 786440 | tf_op jit(solution)/shard_map/ppermute | solution.py:165
  121.9 8.1 %collective-permute-done.30 = f32[64,256]{1,0:T(8,128)S(1)} collective-permute-done((f32[64,256]{1,0:T(8,128)S(1)}, f32[64,256]{1,0:T(8,128)S(1)}, u32[]{:S(2)}, u32[]{:S(2)}) %collective-permute-start.30) | collective-permute-done | bytes 65568 | tf_op jit(solution)/shard_map/ppermute | solution.py:165
  131.5 2.9 %collective-permute-done.31.refs_0_ = f32[64,256]{1,0:T(8,128)S(1)} collective-permute-done((f32[64,256]{1,0:T(8,128)S(1)}, f32[64,256]{1,0:T(8,128)S(1)}, u32[]{:S(2)}, u32[]{:S(2)}) %collective-permute-start.31) | collective-permute-done | bytes 65568 | tf_op jit(solution)/shard_map/ppermute | solution.py:165
  135.7 8.0 %shard_map.69.lower_ref = f32[256,256]{1,0:T(8,128)S(1)} custom-call(f32[64,256]{1,0:T(8,128)S(1)} %add.51.own_ref, f32[64,256]{1,0:T(8,128)S(1)} %collective-permute-done.31.refs_0_, f32[64,256]{1,0:T(8,128)S(1)} %collective-permute-done.32.refs_1_, f32[64,256]{1,0:T(8,128)S(1)} %collective-permute-done.33.refs_2_), custom_call_target="tpu_custom_call" | custom-call | flops 1000000000 | bytes 524288 | tf_op jit(solution)/shard_map/pallas_call | solution.py:60
  143.7 5.2 %shard_map.70 = (f32[144,128]{1,0:T(8,128)S(1)}, f32[144,128]{1,0:T(8,128)S(1)}) custom-call(f32[16,4096]{1,0:T(8,128)S(1)} %bitcast.7, f32[1024,256]{1,0:T(8,128)S(1)} %get-tuple-element.76.block_ref, f32[256,256]{1,0:T(8,128)S(1)} %shard_map.68.first_ref, f32[256,256]{1,0:T(8,128)S(1)} %collective-permute-done.34.second_ref, ...), custom_call_target="tpu_custom_call" | custom-call | flops 3000000000 | bytes 3294208 | tf_op jit(solution)/shard_map/pallas_call | solution.py:60
  149.0 6.8 %collective-permute-done.36.second_ref = f32[144,128]{1,0:T(8,128)S(1)} collective-permute-done((f32[144,128]{1,0:T(8,128)S(1)}, f32[144,128]{1,0:T(8,128)S(1)}, u32[]{:S(2)}, u32[]{:S(2)}) %collective-permute-start.36) | collective-permute-done | bytes 73760 | tf_op jit(solution)/shard_map/ppermute | solution.py:165
  (87 shorter events, 36.7 us)
Async XLA Ops:
  1.6 5.3 %collective-permute-start = (f32[64,256]{1,0:T(8,128)S(1)}, f32[64,256]{1,0:T(8,128)S(1)}, u32[]{:S(2)}, u32[]{:S(2)}) collective-permute-start(f32[64,256]{1,0:T(8,128)S(1)} %shard_map.55), channel_id=1, source_target_pairs={{0,4},{4,0},{8,12},{12,8},{1,5},{5,1},{9,13},{13,9},{2,6},{6,2},{1... | collective-permute-start | bytes 196616 | tf_op jit(solution)/shard_map/ppermute | solution.py:165
  7.0 7.2 %collective-permute-start.1 = (f32[256,256]{1,0:T(8,128)S(1)}, f32[256,256]{1,0:T(8,128)S(1)}, u32[]{:S(2)}, u32[]{:S(2)}) collective-permute-start(f32[256,256]{1,0:T(8,128)S(1)} %get-tuple-element.49), channel_id=1, source_target_pairs={{0,4},{4,0},{8,12},{12,8},{1,5},{5,1},{9,13},{13,9},{2,6},{6,2},{1... | collective-permute-start | bytes 786440 | tf_op jit(solution)/shard_map/ppermute | solution.py:165
  14.2 28.9 %collective-permute-start.2 = (f32[512,256]{1,0:T(8,128)S(1)}, f32[512,256]{1,0:T(8,128)S(1)}, u32[]{:S(2)}, u32[]{:S(2)}) collective-permute-start(f32[512,256]{1,0:T(8,128)S(1)} %get-tuple-element.50), channel_id=1, source_target_pairs={{0,4},{4,0},{8,12},{12,8},{1,5},{5,1},{9,13},{13,9},{2,6},{6,2},{1... | collective-permute-start | bytes 1572872 | tf_op jit(solution)/shard_map/ppermute | solution.py:165
  16.1 13.3 %collective-permute-start.3 = (f32[64,256]{1,0:T(8,128)S(1)}, f32[64,256]{1,0:T(8,128)S(1)}, u32[]{:S(2)}, u32[]{:S(2)}) collective-permute-start(f32[64,256]{1,0:T(8,128)S(1)} %add.39), channel_id=1, source_target_pairs={{0,8},{4,12},{8,0},{12,4},{1,9},{5,13},{9,1},{13,5},{2,10},{6,14},... | collective-permute-start | bytes 196616 | tf_op jit(solution)/shard_map/ppermute | solution.py:165
  18.6 24.5 %collective-permute-start.7 = (f32[256,256]{1,0:T(8,128)S(1)}, f32[256,256]{1,0:T(8,128)S(1)}, u32[]{:S(2)}, u32[]{:S(2)}) collective-permute-start(f32[256,256]{1,0:T(8,128)S(1)} %add.40.first_ref), channel_id=1, source_target_pairs={{0,8},{4,12},{8,0},{12,4},{1,9},{5,13},{9,1},{13,5},{2,10},{6,14},... | collective-permute-start | bytes 786440 | tf_op jit(solution)/shard_map/ppermute | solution.py:165
  29.4 4.3 %collective-permute-start.4 = (f32[64,256]{1,0:T(8,128)S(1)}, f32[64,256]{1,0:T(8,128)S(1)}, u32[]{:S(2)}, u32[]{:S(2)}) collective-permute-start(f32[64,256]{1,0:T(8,128)S(1)} %add.41.own_ref), channel_id=1, source_target_pairs={{0,2},{2,0},{1,3},{3,1},{4,6},{6,4},{5,7},{7,5},{8,10},{10,8},{9,1... | collective-permute-start | bytes 196616 | tf_op jit(solution)/shard_map/ppermute | solution.py:165
  31.0 2.8 %collective-permute-start.5 = (f32[64,256]{1,0:T(8,128)S(1)}, f32[64,256]{1,0:T(8,128)S(1)}, u32[]{:S(2)}, u32[]{:S(2)}) collective-permute-start(f32[64,256]{1,0:T(8,128)S(1)} %add.41.own_ref), channel_id=1, source_target_pairs={{0,1},{1,0},{2,3},{3,2},{4,5},{5,4},{6,7},{7,6},{8,9},{9,8},{10,11... | collective-permute-start | bytes 196616 | tf_op jit(solution)/shard_map/ppermute | solution.py:165
  44.2 2.0 %collective-permute-start.8 = (f32[512,256]{1,0:T(8,128)S(1)}, f32[512,256]{1,0:T(8,128)S(1)}, u32[]{:S(2)}, u32[]{:S(2)}) collective-permute-start(f32[512,256]{1,0:T(8,128)S(1)} %get-tuple-element.55), channel_id=1, source_target_pairs={{0,1},{1,0},{2,3},{3,2},{4,5},{5,4},{6,7},{7,6},{8,9},{9,8},{10,11... | collective-permute-start | bytes 1572872 | tf_op jit(solution)/shard_map/ppermute | solution.py:165
  46.2 5.6 %collective-permute-start.9 = (f32[128,256]{1,0:T(8,128)S(1)}, f32[128,256]{1,0:T(8,128)S(1)}, u32[]{:S(2)}, u32[]{:S(2)}) collective-permute-start(f32[128,256]{1,0:T(8,128)S(1)} %get-tuple-element.57), channel_id=1, source_target_pairs={{0,2},{2,0},{1,3},{3,1},{4,6},{6,4},{5,7},{7,5},{8,10},{10,8},{9,1... | collective-permute-start | bytes 393224 | tf_op jit(solution)/shard_map/ppermute | solution.py:165
  47.8 7.7 %collective-permute-start.12 = (f32[128,256]{1,0:T(8,128)S(1)}, f32[128,256]{1,0:T(8,128)S(1)}, u32[]{:S(2)}, u32[]{:S(2)}) collective-permute-start(f32[128,256]{1,0:T(8,128)S(1)} %get-tuple-element.60), channel_id=1, source_target_pairs={{0,4},{4,0},{8,12},{12,8},{1,5},{5,1},{9,13},{13,9},{2,6},{6,2},{1... | collective-permute-start | bytes 393224 | tf_op jit(solution)/shard_map/ppermute | solution.py:165
  51.9 6.5 %collective-permute-start.10 = (f32[128,256]{1,0:T(8,128)S(1)}, f32[128,256]{1,0:T(8,128)S(1)}, u32[]{:S(2)}, u32[]{:S(2)}) collective-permute-start(f32[128,256]{1,0:T(8,128)S(1)} %add.42), channel_id=1, source_target_pairs={{0,4},{4,0},{8,12},{12,8},{1,5},{5,1},{9,13},{13,9},{2,6},{6,2},{1... | collective-permute-start | bytes 393224 | tf_op jit(solution)/shard_map/ppermute | solution.py:165
  55.5 6.1 %collective-permute-start.13 = (f32[128,256]{1,0:T(8,128)S(1)}, f32[128,256]{1,0:T(8,128)S(1)}, u32[]{:S(2)}, u32[]{:S(2)}) collective-permute-start(f32[128,256]{1,0:T(8,128)S(1)} %add.44), channel_id=1, source_target_pairs={{0,2},{2,0},{1,3},{3,1},{4,6},{6,4},{5,7},{7,5},{8,10},{10,8},{9,1... | collective-permute-start | bytes 393224 | tf_op jit(solution)/shard_map/ppermute | solution.py:165
  58.5 5.0 %collective-permute-start.11 = (f32[128,256]{1,0:T(8,128)S(1)}, f32[128,256]{1,0:T(8,128)S(1)}, u32[]{:S(2)}, u32[]{:S(2)}) collective-permute-start(f32[128,256]{1,0:T(8,128)S(1)} %add.43), channel_id=1, source_target_pairs={{0,2},{2,0},{1,3},{3,1},{4,6},{6,4},{5,7},{7,5},{8,10},{10,8},{9,1... | collective-permute-start | bytes 393224 | tf_op jit(solution)/shard_map/ppermute | solution.py:165
  61.6 5.0 %collective-permute-start.14 = (f32[128,256]{1,0:T(8,128)S(1)}, f32[128,256]{1,0:T(8,128)S(1)}, u32[]{:S(2)}, u32[]{:S(2)}) collective-permute-start(f32[128,256]{1,0:T(8,128)S(1)} %add.45), channel_id=1, source_target_pairs={{0,4},{4,0},{8,12},{12,8},{1,5},{5,1},{9,13},{13,9},{2,6},{6,2},{1... | collective-permute-start | bytes 393224 | tf_op jit(solution)/shard_map/ppermute | solution.py:165
  71.2 6.4 %collective-permute-start.16 = (f32[64,256]{1,0:T(8,128)S(1)}, f32[64,256]{1,0:T(8,128)S(1)}, u32[]{:S(2)}, u32[]{:S(2)}) collective-permute-start(f32[64,256]{1,0:T(8,128)S(1)} %get-tuple-element.62), channel_id=1, source_target_pairs={{0,8},{4,12},{8,0},{12,4},{1,9},{5,13},{9,1},{13,5},{2,10},{6,14},... | collective-permute-start | bytes 196616 | tf_op jit(solution)/shard_map/ppermute | solution.py:165
  77.6 12.6 %collective-permute-start.20 = (f32[512,128]{1,0:T(8,128)S(1)}, f32[512,128]{1,0:T(8,128)S(1)}, u32[]{:S(2)}, u32[]{:S(2)}) collective-permute-start(f32[512,128]{1,0:T(8,128)S(1)} %get-tuple-element.65), channel_id=1, source_target_pairs={{0,4},{4,0},{8,12},{12,8},{1,5},{5,1},{9,13},{13,9},{2,6},{6,2},{1... | collective-permute-start | bytes 786440 | tf_op jit(solution)/shard_map/ppermute | solution.py:165
  77.6 14.8 %collective-permute-start.21 = (f32[256,256]{1,0:T(8,128)S(1)}, f32[256,256]{1,0:T(8,128)S(1)}, u32[]{:S(2)}, u32[]{:S(2)}) collective-permute-start(f32[256,256]{1,0:T(8,128)S(1)} %shard_map.62.first_ref), channel_id=1, source_target_pairs={{0,8},{4,12},{8,0},{12,4},{1,9},{5,13},{9,1},{13,5},{2,10},{6,14},... | collective-permute-start | bytes 786440 | tf_op jit(solution)/shard_map/ppermute | solution.py:165
  79.5 4.3 %collective-permute-start.17 = (f32[64,256]{1,0:T(8,128)S(1)}, f32[64,256]{1,0:T(8,128)S(1)}, u32[]{:S(2)}, u32[]{:S(2)}) collective-permute-start(f32[64,256]{1,0:T(8,128)S(1)} %add.46.own_ref), channel_id=1, source_target_pairs={{0,2},{2,0},{1,3},{3,1},{4,6},{6,4},{5,7},{7,5},{8,10},{10,8},{9,1... | collective-permute-start | bytes 196616 | tf_op jit(solution)/shard_map/ppermute | solution.py:165
  81.0 2.8 %collective-permute-start.18 = (f32[64,256]{1,0:T(8,128)S(1)}, f32[64,256]{1,0:T(8,128)S(1)}, u32[]{:S(2)}, u32[]{:S(2)}) collective-permute-start(f32[64,256]{1,0:T(8,128)S(1)} %add.46.own_ref), channel_id=1, source_target_pairs={{0,1},{1,0},{2,3},{3,2},{4,5},{5,4},{6,7},{7,6},{8,9},{9,8},{10,11... | collective-permute-start | bytes 196616 | tf_op jit(solution)/shard_map/ppermute | solution.py:165
  93.5 2.0 %collective-permute-start.22 = (f32[512,256]{1,0:T(8,128)S(1)}, f32[512,256]{1,0:T(8,128)S(1)}, u32[]{:S(2)}, u32[]{:S(2)}) collective-permute-start(f32[512,256]{1,0:T(8,128)S(1)} %get-tuple-element.68), channel_id=1, source_target_pairs={{0,1},{1,0},{2,3},{3,2},{4,5},{5,4},{6,7},{7,6},{8,9},{9,8},{10,11... | collective-permute-start | bytes 1572872 | tf_op jit(solution)/shard_map/ppermute | solution.py:165
  95.5 5.6 %collective-permute-start.23 = (f32[128,256]{1,0:T(8,128)S(1)}, f32[128,256]{1,0:T(8,128)S(1)}, u32[]{:S(2)}, u32[]{:S(2)}) collective-permute-start(f32[128,256]{1,0:T(8,128)S(1)} %get-tuple-element.70), channel_id=1, source_target_pairs={{0,2},{2,0},{1,3},{3,1},{4,6},{6,4},{5,7},{7,5},{8,10},{10,8},{9,1... | collective-permute-start | bytes 393224 | tf_op jit(solution)/shard_map/ppermute | solution.py:165
  96.7 5.3 %collective-permute-start.26 = (f32[128,256]{1,0:T(8,128)S(1)}, f32[128,256]{1,0:T(8,128)S(1)}, u32[]{:S(2)}, u32[]{:S(2)}) collective-permute-start(f32[128,256]{1,0:T(8,128)S(1)} %get-tuple-element.75), channel_id=1, source_target_pairs={{0,4},{4,0},{8,12},{12,8},{1,5},{5,1},{9,13},{13,9},{2,6},{6,2},{1... | collective-permute-start | bytes 393224 | tf_op jit(solution)/shard_map/ppermute | solution.py:165
  101.2 5.7 %collective-permute-start.24 = (f32[128,256]{1,0:T(8,128)S(1)}, f32[128,256]{1,0:T(8,128)S(1)}, u32[]{:S(2)}, u32[]{:S(2)}) collective-permute-start(f32[128,256]{1,0:T(8,128)S(1)} %add.47), channel_id=1, source_target_pairs={{0,4},{4,0},{8,12},{12,8},{1,5},{5,1},{9,13},{13,9},{2,6},{6,2},{1... | collective-permute-start | bytes 393224 | tf_op jit(solution)/shard_map/ppermute | solution.py:165
  102.0 6.1 %collective-permute-start.27 = (f32[128,256]{1,0:T(8,128)S(1)}, f32[128,256]{1,0:T(8,128)S(1)}, u32[]{:S(2)}, u32[]{:S(2)}) collective-permute-start(f32[128,256]{1,0:T(8,128)S(1)} %add.49), channel_id=1, source_target_pairs={{0,2},{2,0},{1,3},{3,1},{4,6},{6,4},{5,7},{7,5},{8,10},{10,8},{9,1... | collective-permute-start | bytes 393224 | tf_op jit(solution)/shard_map/ppermute | solution.py:165
  106.9 5.0 %collective-permute-start.25 = (f32[128,256]{1,0:T(8,128)S(1)}, f32[128,256]{1,0:T(8,128)S(1)}, u32[]{:S(2)}, u32[]{:S(2)}) collective-permute-start(f32[128,256]{1,0:T(8,128)S(1)} %add.48), channel_id=1, source_target_pairs={{0,2},{2,0},{1,3},{3,1},{4,6},{6,4},{5,7},{7,5},{8,10},{10,8},{9,1... | collective-permute-start | bytes 393224 | tf_op jit(solution)/shard_map/ppermute | solution.py:165
  108.0 5.0 %collective-permute-start.28 = (f32[128,256]{1,0:T(8,128)S(1)}, f32[128,256]{1,0:T(8,128)S(1)}, u32[]{:S(2)}, u32[]{:S(2)}) collective-permute-start(f32[128,256]{1,0:T(8,128)S(1)} %add.50), channel_id=1, source_target_pairs={{0,4},{4,0},{8,12},{12,8},{1,5},{5,1},{9,13},{13,9},{2,6},{6,2},{1... | collective-permute-start | bytes 393224 | tf_op jit(solution)/shard_map/ppermute | solution.py:165
  117.6 12.3 %collective-permute-start.30 = (f32[64,256]{1,0:T(8,128)S(1)}, f32[64,256]{1,0:T(8,128)S(1)}, u32[]{:S(2)}, u32[]{:S(2)}) collective-permute-start(f32[64,256]{1,0:T(8,128)S(1)} %get-tuple-element.77), channel_id=1, source_target_pairs={{0,8},{4,12},{8,0},{12,4},{1,9},{5,13},{9,1},{13,5},{2,10},{6,14},... | collective-permute-start | bytes 196616 | tf_op jit(solution)/shard_map/ppermute | solution.py:165
  120.1 23.6 %collective-permute-start.34 = (f32[256,256]{1,0:T(8,128)S(1)}, f32[256,256]{1,0:T(8,128)S(1)}, u32[]{:S(2)}, u32[]{:S(2)}) collective-permute-start(f32[256,256]{1,0:T(8,128)S(1)} %shard_map.68.first_ref), channel_id=1, source_target_pairs={{0,8},{4,12},{8,0},{12,4},{1,9},{5,13},{9,1},{13,5},{2,10},{6,14},... | collective-permute-start | bytes 786440 | tf_op jit(solution)/shard_map/ppermute | solution.py:165
  130.0 13.7 %collective-permute-start.35 = (f32[512,128]{1,0:T(8,128)S(1)}, f32[512,128]{1,0:T(8,128)S(1)}, u32[]{:S(2)}, u32[]{:S(2)}) collective-permute-start(f32[512,128]{1,0:T(8,128)S(1)} %get-tuple-element.80), channel_id=1, source_target_pairs={{0,4},{4,0},{8,12},{12,8},{1,5},{5,1},{9,13},{13,9},{2,6},{6,2},{1... | collective-permute-start | bytes 786440 | tf_op jit(solution)/shard_map/ppermute | solution.py:165
  130.1 4.3 %collective-permute-start.31 = (f32[64,256]{1,0:T(8,128)S(1)}, f32[64,256]{1,0:T(8,128)S(1)}, u32[]{:S(2)}, u32[]{:S(2)}) collective-permute-start(f32[64,256]{1,0:T(8,128)S(1)} %add.51.own_ref), channel_id=1, source_target_pairs={{0,2},{2,0},{1,3},{3,1},{4,6},{6,4},{5,7},{7,5},{8,10},{10,8},{9,1... | collective-permute-start | bytes 196616 | tf_op jit(solution)/shard_map/ppermute | solution.py:165
  131.5 3.0 %collective-permute-start.32 = (f32[64,256]{1,0:T(8,128)S(1)}, f32[64,256]{1,0:T(8,128)S(1)}, u32[]{:S(2)}, u32[]{:S(2)}) collective-permute-start(f32[64,256]{1,0:T(8,128)S(1)} %add.51.own_ref), channel_id=1, source_target_pairs={{0,1},{1,0},{2,3},{3,2},{4,5},{5,4},{6,7},{7,6},{8,9},{9,8},{10,11... | collective-permute-start | bytes 196616 | tf_op jit(solution)/shard_map/ppermute | solution.py:165
  149.0 6.9 %collective-permute-start.36 = (f32[144,128]{1,0:T(8,128)S(1)}, f32[144,128]{1,0:T(8,128)S(1)}, u32[]{:S(2)}, u32[]{:S(2)}) collective-permute-start(f32[144,128]{1,0:T(8,128)S(1)} %get-tuple-element.82), channel_id=1, source_target_pairs={{0,8},{4,12},{8,0},{12,4},{1,9},{5,13},{9,1},{13,5},{2,10},{6,14},... | collective-permute-start | bytes 221192 | tf_op jit(solution)/shard_map/ppermute | solution.py:165
  (10 other events, 40.8 us)

commit v2 on v1

--- a/solution.py
+++ b/solution.py
@@ -310,14 +310,13 @@
     keep_ref[...] = product(kept_ref[...], block_ref[...], ((0,), (0,)))
 
 
-def mix_kernel(own_ref, other_ref, first_ref, second_ref, keep_ref, send_ref):
+def mix_kernel(sent, own_ref, other_ref, first_ref, second_ref, out_ref):
     mine, _, _, head = pair_sides()
     coef = first_ref[...] + second_ref[...]
     half = own_ref.shape[0] // 2
+    rows = lanes(head ^ int(sent), half)
     for keys_ref, piece in ((own_ref, mine), (other_ref, 1 - mine)):
-        to = lanes(piece, half)
-        keep_ref[to, :] = product(keys_ref[lanes(head, half), :], coef, ((1,), (0,)))
-        send_ref[to, :] = product(keys_ref[lanes(1 - head, half), :], coef, ((1,), (0,)))
+        out_ref[lanes(piece, half), :] = product(keys_ref[rows, :], coef, ((1,), (0,)))
 
 
 def streams_kernel(first_ref, second_ref, a_keep, a_send, b_keep, b_send):
@@ -349,37 +348,49 @@
     return stack, swap(stack, "head", 1)
 
 
-def block_kernel(near_ref, far_ref, lower_ref, block_ref, gram_ref, whole_ref, scratch_ref):
-    mine, _, lay, head = pair_sides()
-    count = near_ref.shape[0] // 4
+def place_block(stack_ref, lower_ref, block_ref):
+    mine, _, lay, _ = pair_sides()
+    count = stack_ref.shape[0] // 4
     half = count // 2
-    piece_rows = near_ref.shape[0]
-    for ref, owner in ((near_ref, head), (far_ref, 1 - head)):
-        for i in range(2):
-            for piece in range(2):
-                place = (piece ^ mine) * piece_rows + owner * (piece_rows // 2)
-                to = place + (lay ^ i) * half
-                whole_ref[pl.ds(pl.multiple_of(to, half), half), :] = ref[
-                    pl.ds(i * count + piece * half, half), :
-                ]
-            place = i * piece_rows + owner * (piece_rows // 2) + count
-            whole_ref[pl.ds(pl.multiple_of(place, count), count), :] = ref[
-                pl.ds((2 + i) * count, count), :
-            ]
-    block_ref[...] = product(whole_ref[...], lower_ref[...], ((1,), (1,)))
+    block = product(stack_ref[...], lower_ref[...], ((1,), (1,)))
+    for i in range(2):
+        for piece in range(2):
+            to = (piece ^ mine) * 2 * count + (lay ^ i) * half
+            at = i * count + piece * half
+            block_ref[pl.ds(pl.multiple_of(to, half), half), :] = block[at : at + half]
+        at = (2 + i) * count
+        block_ref[pl.ds((2 * i + 1) * count, count), :] = block[at : at + count]
+
+
+def half_projection(far, own_ref, other_ref, block_ref):
+    _, _, _, head = pair_sides()
+    half = own_ref.shape[0] // 2
+    rows = lanes(head ^ int(far), half)
+    return product(own_ref[rows, :], block_ref[pl.ds(0, half), :], ((0,), (0,))) + product(
+        other_ref[rows, :], block_ref[pl.ds(half, half), :], ((0,), (0,))
+    )
+
+
+def near_kernel(stack_ref, lower_ref, own_ref, other_ref, block_ref, gram_ref, proj_ref, scratch_ref):
+    place_block(stack_ref, lower_ref, block_ref)
     gram_share(block_ref, scratch_ref, gram_ref)
-
-
-def project_kernel(own_ref, other_ref, block_ref, proj_ref):
-    rows = own_ref.shape[0]
-    proj_ref[...] = product(own_ref[...], block_ref[pl.ds(0, rows), :], ((0,), (0,))) + product(
-        other_ref[...], block_ref[pl.ds(rows, rows), :], ((0,), (0,))
-    )
+    proj_ref[...] = half_projection(False, own_ref, other_ref, block_ref)
+
+
+def far_kernel(stack_ref, lower_ref, part_ref, block_ref, gram_ref, scratch_ref):
+    place_block(stack_ref, lower_ref, block_ref)
+    gram_share(block_ref, scratch_ref, gram_ref)
+    gram_ref[...] += part_ref[...]
+
+
+def project_kernel(own_ref, other_ref, block_ref, part_ref, proj_ref):
+    proj_ref[...] = part_ref[...] + half_projection(True, own_ref, other_ref, block_ref)
 
 
 def attend_kernel(
     query_ref,
-    block_ref,
+    near_ref,
+    far_ref,
     first_ref,
     second_ref,
     lower_ref,
@@ -391,11 +402,14 @@
     send_ref,
     basis_ref,
 ):
-    mine, upper, _, _ = pair_sides()
+    mine, upper, _, head = pair_sides()
     group = QH // KVH
     tokens = own_ref.shape[0]
-    width = length_ref.shape[1]
-    basis_ref[...] = product(block_ref[...], lower_ref[...], ((1,), (1,)))
+    half, width = tokens // 2, length_ref.shape[1]
+    for i, block_ref in enumerate((near_ref, far_ref)):
+        basis_ref[pl.ds(i * tokens, tokens), :] = product(
+            block_ref[...], lower_ref[...], ((1,), (1,))
+        )
     coef = product(first_ref[...] + second_ref[...], lower_ref[...], ((1,), (1,)))
     reduced = []
     for which in range(2):
@@ -405,30 +419,42 @@
         factor = coef[which * HD : (which + 1) * HD]
         reduced.append(product(quer, factor, ((1,), (0,))) / math.sqrt(HD))
     scores = product(basis_ref[...], jnp.concatenate(reduced), ((1,), (1,)))
-    first = lax.axis_index("tok") * tokens
-    second = (lax.axis_index("tok") ^ 1) * tokens
-    at = lax.broadcasted_iota(jnp.int32, scores.shape, 0)
-    valid = jnp.where(at < tokens, first + at, second + at - tokens) < length_ref[...]
+    at = lax.broadcasted_iota(jnp.int32, (half, width), 0)
+    tok = lax.axis_index("tok")
+    valid = jnp.concatenate(
+        [
+            (tok ^ piece) * tokens + (head ^ far) * half + at < length_ref[...]
+            for far in range(2)
+            for piece in range(2)
+        ]
+    )
     peak = jnp.max(jnp.where(valid, scores, NEG), axis=0, keepdims=True)
     weight = jnp.where(valid, jnp.exp(scores - peak), 0.0)
     total = jnp.sum(weight, axis=0, keepdims=True)
-    half = width // 2
+    lane = width // 2
     for which, there_ref in enumerate((low_ref, high_ref)):
-        here = slice(which * half, (which + 1) * half)
-        acc = product(own_ref[:, pl.ds(which * HD, HD)], weight[:tokens, here], ((0,), (0,)))
-        acc = acc + product(there_ref[...], weight[tokens:, here], ((0,), (0,)))
+        here = slice(which * lane, (which + 1) * lane)
+        parts = []
+        for i in range(4):
+            rows = lanes(head ^ (i // 2), half)
+            if i % 2 == 0:
+                value = own_ref[rows, pl.ds(which * HD, HD)]
+            else:
+                value = there_ref[rows, :]
+            parts.append(product(value, weight[i * half : (i + 1) * half, here], ((0,), (0,))))
+        acc = parts[0] + parts[1] + parts[2] + parts[3]
 
         def give(ref):
             ref[pl.ds(0, HD), :] = acc
-            ref[pl.ds(HD, 8), :] = jnp.broadcast_to(peak[:, here], (8, half))
-            ref[pl.ds(HD + 8, 8), :] = jnp.broadcast_to(total[:, here], (8, half))
+            ref[pl.ds(HD, 8), :] = jnp.broadcast_to(peak[:, here], (8, lane))
+            ref[pl.ds(HD + 8, 8), :] = jnp.broadcast_to(total[:, here], (8, lane))
 
         pl.when(upper == which)(lambda: give(keep_ref))
         pl.when(upper != which)(lambda: give(send_ref))
 
 
 def merge_kernel(first_ref, second_ref, out_ref):
-    rows = out_ref.shape[0]
+    rows = out_ref.shape[1]
     top = jnp.maximum(first_ref[pl.ds(HD, 1), :], second_ref[pl.ds(HD, 1), :])
     one = jnp.exp(first_ref[pl.ds(HD, 1), :] - top)
     two = jnp.exp(second_ref[pl.ds(HD, 1), :] - top)
@@ -436,7 +462,7 @@
     acc = first_ref[pl.ds(0, HD), :] * one + second_ref[pl.ds(0, HD), :] * two
     result = (acc / total).T
     for i in range(QH // KVH):
-        out_ref[:, pl.ds(i * HD, HD)] = result[i * rows : (i + 1) * rows, :]
+        out_ref[0, :, 0, pl.ds(i * HD, HD)] = result[i * rows : (i + 1) * rows, :]
 
 
 def gathered(share):
@@ -478,7 +504,6 @@
     )
     gram = gram + swap(gram, "tok", 1)
     proj = keep + swap(after(send, gram), "tok", 1)
-    keys_other = swap(after(keys_send, proj), "tok", 1)
     values_own, *values_send = call(
         split_kernel,
         [vmem(tokens, half)] + [vmem(tokens, HD)] * 2,
@@ -489,6 +514,10 @@
     for step in range(ITERS + 1):
         gram = gram + swap(gram, "tok", 2)
         last = step == ITERS
+        if step != 1:
+            proj = after(proj, gram)
+            if step == 0:
+                keys_other = swap(after(keys_send, proj), "tok", 1)
         first, second = proj, swap(proj, "tok", 2)
         if step > 0 and len(values_other) < 2:
             values_other.append(swap(after(values_send[len(values_other)], proj, gram), "tok", 1))
@@ -502,38 +531,46 @@
             lower = inverse_factor_high(*halves)
         if last:
             break
-        z_keep, z_send = call(
-            mix_kernel,
-            [vmem(tokens, rank)] * 2,
+        mix = (keys_own, keys_other, first, second)
+        z_send, z_keep = (
+            call(functools.partial(mix_kernel, sent), vmem(tokens, rank), *mix, flops=400_000_000)
+            for sent in (True, False)
+        )
+        stack, far = summed_streams(z_keep, z_send, lower)
+        near_block, gram, proj = call(
+            near_kernel,
+            [vmem(tokens, rank), vmem(share, rank), vmem(half, rank)],
+            stack,
+            lower,
             keys_own,
             keys_other,
-            first,
-            second,
+            scratch=[(rank // 2, rank)],
             flops=900_000_000,
         )
-        near, far = summed_streams(z_keep, z_send, lower)
-        block, gram = call(
-            block_kernel,
-            [vmem(2 * tokens, rank), vmem(share, rank)],
-            near,
+        far_block, gram = call(
+            far_kernel,
+            [vmem(tokens, rank), vmem(share, rank)],
             far,
             lower,
-            scratch=[(2 * tokens, rank), (rank // 2, rank)],
-            flops=1_200_000_000,
+            gram,
+            scratch=[(rank // 2, rank)],
+            flops=600_000_000,
         )
         proj = call(
             project_kernel,
             vmem(half, rank),
             keys_own,
             keys_other,
-            block,
-            flops=900_000_000,
+            far_block,
+            proj,
+            flops=400_000_000,
         )
     keep, send = call(
         attend_kernel,
         [vmem(HD + 16, HD)] * 2,
         queries,
-        block,
+        near_block,
+        far_block,
         first,
         second,
         lower,
@@ -543,8 +580,7 @@
         scratch=[(2 * tokens, rank)],
         flops=3_000_000_000,
     )
-    result = call(merge_kernel, vmem(rows, half * 4), keep, swap(send, "tok", 2))
-    return result[None, :, None, :]
+    return call(merge_kernel, vmem(1, rows, 1, half * 4), keep, swap(send, "tok", 2))
 
 
 def solution(mesh):

time: 157 us -> 142 us (0.904)
  waiting for transfers between devices: 76.2 us -> 58.3 us
  Pallas kernels: 40.6 us -> 44 us
    ppermute x37, waiting for transfers between devices: 76.2 us -> 58.3 us  [swap(): return lax.ppermute(x, axis, pairs)]
    pallas_call x17 -> x21, Pallas kernels: 40.6 us -> 44 us  [call(): pl.pallas_call(kernel, out_shape=out_shape, in_specs=[spec] * len(args),...]
  transfers between devices with their start and end apart: 37 -> 37, of which waited for: 27 -> 25; matrix products, arithmetic and copies ran while one was open for 0% -> 0% of each run, Pallas kernels for 18% -> 23%
where the time goes in v2:
time: 142 us
  waiting for transfers between devices  58.3 us (41%)
  Pallas kernels  44 us (31%)
  starting transfers between devices  36.7 us (26%)
  local copies, waits for them, and re-layouts  2.27 us (2%)
    ppermute x37, waiting for transfers between devices, swap(): return lax.ppermute(x, axis, pairs)  58.3 us
    pallas_call x21, Pallas kernels, call(): pl.pallas_call(kernel, out_shape=out_shape, in_specs=[spec] * len(args),...  44 us
    ppermute x37, starting transfers between devices, swap(): return lax.ppermute(x, axis, pairs)  36.7 us
  transfers between devices with their start and end apart: 37, of which 25 were waited for; matrix products, arithmetic and copies ran while one was open for 0% of the time, Pallas kernels for 23%

profile of v2, /device:TPU:0, one launch (start us, length us, event | category | flops | bytes accessed | tf_op | source)
XLA Modules:
  0.0 142.0 jit_solution(17126907912350252067)
XLA Ops:
  1.6 3.1 %collective-permute-start = (f32[64,256]{1,0:T(8,128)S(1)}, f32[64,256]{1,0:T(8,128)S(1)}, u32[]{:S(2)}, u32[]{:S(2)}) collective-permute-start(f32[64,256]{1,0:T(8,128)S(1)} %shard_map.55), channel_id=1, source_target_pairs={{0,4},{4,0},{8,12},{12,8},{1,5},{5,1},{9,13},{13,9},{2,6},{6,2},{1... | collective-permute-start | bytes 196616 | tf_op jit(solution)/shard_map/ppermute | solution.py:165
  7.0 2.1 %collective-permute-start.1 = (f32[256,256]{1,0:T(8,128)S(1)}, f32[256,256]{1,0:T(8,128)S(1)}, u32[]{:S(2)}, u32[]{:S(2)}) collective-permute-start(f32[256,256]{1,0:T(8,128)S(1)} %get-tuple-element.52), channel_id=1, source_target_pairs={{0,4},{4,0},{8,12},{12,8},{1,5},{5,1},{9,13},{13,9},{2,6},{6,2},{1... | collective-permute-start | bytes 786440 | tf_op jit(solution)/shard_map/ppermute | solution.py:165
  9.1 2.6 %collective-permute-start.2 = (f32[64,256]{1,0:T(8,128)S(1)}, f32[64,256]{1,0:T(8,128)S(1)}, u32[]{:S(2)}, u32[]{:S(2)}) collective-permute-start(f32[64,256]{1,0:T(8,128)S(1)} %add.39), channel_id=1, source_target_pairs={{0,8},{4,12},{8,0},{12,4},{1,9},{5,13},{9,1},{13,5},{2,10},{6,14},... | collective-permute-start | bytes 196616 | tf_op jit(solution)/shard_map/ppermute | solution.py:165
  11.6 3.2 %collective-permute-done.2 = f32[64,256]{1,0:T(8,128)S(1)} collective-permute-done((f32[64,256]{1,0:T(8,128)S(1)}, f32[64,256]{1,0:T(8,128)S(1)}, u32[]{:S(2)}, u32[]{:S(2)}) %collective-permute-start.2) | collective-permute-done | bytes 65568 | tf_op jit(solution)/shard_map/ppermute | solution.py:165
  16.2 2.7 %collective-permute-start.3 = (f32[512,256]{1,0:T(8,128)S(1)}, f32[512,256]{1,0:T(8,128)S(1)}, u32[]{:S(2)}, u32[]{:S(2)}) collective-permute-start(f32[512,256]{1,0:T(8,128)S(1)} %get-tuple-element.54), channel_id=1, source_target_pairs={{0,4},{4,0},{8,12},{12,8},{1,5},{5,1},{9,13},{13,9},{2,6},{6,2},{1... | collective-permute-start | bytes 1572872 | tf_op jit(solution)/shard_map/ppermute | solution.py:165
  21.6 2.8 %collective-permute-done.4.refs_0_ = f32[64,256]{1,0:T(8,128)S(1)} collective-permute-done((f32[64,256]{1,0:T(8,128)S(1)}, f32[64,256]{1,0:T(8,128)S(1)}, u32[]{:S(2)}, u32[]{:S(2)}) %collective-permute-start.4) | collective-permute-done | bytes 65568 | tf_op jit(solution)/shard_map/ppermute | solution.py:165
  25.6 8.0 %shard_map.57.lower_ref = f32[256,256]{1,0:T(8,128)S(1)} custom-call(f32[64,256]{1,0:T(8,128)S(1)} %add.41.own_ref, f32[64,256]{1,0:T(8,128)S(1)} %collective-permute-done.4.refs_0_, f32[64,256]{1,0:T(8,128)S(1)} %collective-permute-done.5.refs_1_, f32[64,256]{1,0:T(8,128)S(1)} %collective-permute-done.6.refs_2_), custom_call_target="tpu_custom_call" | custom-call | flops 1000000000 | bytes 524288 | tf_op jit(solution)/shard_map/pallas_call | solution.py:60
  37.2 1.5 %collective-permute-start.9 = (f32[128,256]{1,0:T(8,128)S(1)}, f32[128,256]{1,0:T(8,128)S(1)}, u32[]{:S(2)}, u32[]{:S(2)}) collective-permute-start(f32[128,256]{1,0:T(8,128)S(1)} %get-tuple-element.59), channel_id=1, source_target_pairs={{0,2},{2,0},{1,3},{3,1},{4,6},{6,4},{5,7},{7,5},{8,10},{10,8},{9,1... | collective-permute-start | bytes 393224 | tf_op jit(solution)/shard_map/ppermute | solution.py:165
  38.7 1.8 %collective-permute-start.12 = (f32[128,256]{1,0:T(8,128)S(1)}, f32[128,256]{1,0:T(8,128)S(1)}, u32[]{:S(2)}, u32[]{:S(2)}) collective-permute-start(f32[128,256]{1,0:T(8,128)S(1)} %get-tuple-element.62), channel_id=1, source_target_pairs={{0,4},{4,0},{8,12},{12,8},{1,5},{5,1},{9,13},{13,9},{2,6},{6,2},{1... | collective-permute-start | bytes 393224 | tf_op jit(solution)/shard_map/ppermute | solution.py:165
  40.5 2.3 %collective-permute-done.9 = f32[128,256]{1,0:T(8,128)S(1)} collective-permute-done((f32[128,256]{1,0:T(8,128)S(1)}, f32[128,256]{1,0:T(8,128)S(1)}, u32[]{:S(2)}, u32[]{:S(2)}) %collective-permute-start.9) | collective-permute-done | bytes 131104 | tf_op jit(solution)/shard_map/ppermute | solution.py:165
  42.8 1.8 %collective-permute-start.10 = (f32[128,256]{1,0:T(8,128)S(1)}, f32[128,256]{1,0:T(8,128)S(1)}, u32[]{:S(2)}, u32[]{:S(2)}) collective-permute-start(f32[128,256]{1,0:T(8,128)S(1)} %add.42), channel_id=1, source_target_pairs={{0,4},{4,0},{8,12},{12,8},{1,5},{5,1},{9,13},{13,9},{2,6},{6,2},{1... | collective-permute-start | bytes 393224 | tf_op jit(solution)/shard_map/ppermute | solution.py:165
  44.6 1.6 %collective-permute-start.13 = (f32[128,256]{1,0:T(8,128)S(1)}, f32[128,256]{1,0:T(8,128)S(1)}, u32[]{:S(2)}, u32[]{:S(2)}) collective-permute-start(f32[128,256]{1,0:T(8,128)S(1)} %add.44), channel_id=1, source_target_pairs={{0,2},{2,0},{1,3},{3,1},{4,6},{6,4},{5,7},{7,5},{8,10},{10,8},{9,1... | collective-permute-start | bytes 393224 | tf_op jit(solution)/shard_map/ppermute | solution.py:165
  46.2 1.6 %collective-permute-done.10 = f32[128,256]{1,0:T(8,128)S(1)} collective-permute-done((f32[128,256]{1,0:T(8,128)S(1)}, f32[128,256]{1,0:T(8,128)S(1)}, u32[]{:S(2)}, u32[]{:S(2)}) %collective-permute-start.10) | collective-permute-done | bytes 131104 | tf_op jit(solution)/shard_map/ppermute | solution.py:165
  47.8 1.5 %collective-permute-start.11 = (f32[128,256]{1,0:T(8,128)S(1)}, f32[128,256]{1,0:T(8,128)S(1)}, u32[]{:S(2)}, u32[]{:S(2)}) collective-permute-start(f32[128,256]{1,0:T(8,128)S(1)} %add.43), channel_id=1, source_target_pairs={{0,2},{2,0},{1,3},{3,1},{4,6},{6,4},{5,7},{7,5},{8,10},{10,8},{9,1... | collective-permute-start | bytes 393224 | tf_op jit(solution)/shard_map/ppermute | solution.py:165
  51.2 1.6 %collective-permute-done.11 = f32[128,256]{1,0:T(8,128)S(1)} collective-permute-done((f32[128,256]{1,0:T(8,128)S(1)}, f32[128,256]{1,0:T(8,128)S(1)}, u32[]{:S(2)}, u32[]{:S(2)}) %collective-permute-start.11) | collective-permute-done | bytes 131104 | tf_op jit(solution)/shard_map/ppermute | solution.py:165
  52.9 2.9 %collective-permute-done.14 = f32[128,256]{1,0:T(8,128)S(1)} collective-permute-done((f32[128,256]{1,0:T(8,128)S(1)}, f32[128,256]{1,0:T(8,128)S(1)}, u32[]{:S(2)}, u32[]{:S(2)}) %collective-permute-start.14) | collective-permute-done | bytes 131104 | tf_op jit(solution)/shard_map/ppermute | solution.py:165
  55.9 2.3 %shard_map.62 = (f32[512,256]{1,0:T(8,128)}, f32[64,256]{1,0:T(8,128)S(1)}, f32[256,256]{1,0:T(8,128)S(1)}) custom-call(f32[512,256]{1,0:T(8,128)S(1)} %pad_maximum_fusion.stack_ref, f32[256,256]{1,0:T(8,128)S(1)} %shard_map.57.lower_ref, f32[512,256]{1,0:T(8,128)S(1)} %get-tuple-element.48.own_ref, f32[512,256]{1,0:T(8,128)S(1)} %collective-permute-done.3.other_ref), custom_call_target="tpu_custom_call" | custom-call | flops 900000000 | bytes 2686976 | tf_op jit(solution)/shard_map/pallas_call | solution.py:60
  61.8 4.6 %collective-permute-done.16 = f32[64,256]{1,0:T(8,128)S(1)} collective-permute-done((f32[64,256]{1,0:T(8,128)S(1)}, f32[64,256]{1,0:T(8,128)S(1)}, u32[]{:S(2)}, u32[]{:S(2)}) %collective-permute-start.16) | collective-permute-done | bytes 65568 | tf_op jit(solution)/shard_map/ppermute | solution.py:165
  66.5 2.4 %collective-permute-start.21 = (f32[256,256]{1,0:T(8,128)S(1)}, f32[256,256]{1,0:T(8,128)S(1)}, u32[]{:S(2)}, u32[]{:S(2)}) collective-permute-start(f32[256,256]{1,0:T(8,128)S(1)} %shard_map.64.first_ref), channel_id=1, source_target_pairs={{0,8},{4,12},{8,0},{12,4},{1,9},{5,13},{9,1},{13,5},{2,10},{6,14},... | collective-permute-start | bytes 786440 | tf_op jit(solution)/shard_map/ppermute | solution.py:165
  70.3 2.9 %collective-permute-done.17.refs_0_ = f32[64,256]{1,0:T(8,128)S(1)} collective-permute-done((f32[64,256]{1,0:T(8,128)S(1)}, f32[64,256]{1,0:T(8,128)S(1)}, u32[]{:S(2)}, u32[]{:S(2)}) %collective-permute-start.17) | collective-permute-done | bytes 65568 | tf_op jit(solution)/shard_map/ppermute | solution.py:165
  74.4 4.0 %shard_map.65 = (f32[128,128]{1,0:T(8,128)S(1)}, f32[128,128]{1,0:T(8,128)S(1)}, f32[128,128]{1,0:T(8,128)S(1)}) custom-call(f32[64,256]{1,0:T(8,128)S(1)} %add.46.own_ref, f32[64,256]{1,0:T(8,128)S(1)} %collective-permute-done.17.refs_0_, f32[64,256]{1,0:T(8,128)S(1)} %collective-permute-done.18.refs_1_, f32[64,256]{1,0:T(8,128)S(1)} %collective-permute-done.19.refs_2_), custom_call_target="tpu_custom_call" | custom-call | flops 1000000000 | bytes 458752 | tf_op jit(solution)/shard_map/pallas_call | solution.py:60
  79.2 2.2 %collective-permute-done.21.second_ref = f32[256,256]{1,0:T(8,128)S(1)} collective-permute-done((f32[256,256]{1,0:T(8,128)S(1)}, f32[256,256]{1,0:T(8,128)S(1)}, u32[]{:S(2)}, u32[]{:S(2)}) %collective-permute-start.21) | collective-permute-done | bytes 262176 | tf_op jit(solution)/shard_map/ppermute | solution.py:165
  85.3 4.4 %collective-permute-done.23 = f32[128,256]{1,0:T(8,128)S(1)} collective-permute-done((f32[128,256]{1,0:T(8,128)S(1)}, f32[128,256]{1,0:T(8,128)S(1)}, u32[]{:S(2)}, u32[]{:S(2)}) %collective-permute-start.23) | collective-permute-done | bytes 131104 | tf_op jit(solution)/shard_map/ppermute | solution.py:165
  91.5 3.9 %shard_map.69.lower_ref = f32[256,256]{1,0:T(8,128)S(1)} custom-call(f32[128,128]{1,0:T(8,128)S(1)} %get-tuple-element.67.tile_ref, f32[128,128]{1,0:T(8,128)S(1)} %get-tuple-element.73.cross_ref, f32[128,128]{1,0:T(8,128)S(1)} %get-tuple-element.74.left_ref), custom_call_target="tpu_custom_call" | custom-call | flops 1000000000 | bytes 458752 | tf_op jit(solution)/shard_map/pallas_call | solution.py:60
  98.0 2.5 %collective-permute-done.25 = f32[128,256]{1,0:T(8,128)S(1)} collective-permute-done((f32[128,256]{1,0:T(8,128)S(1)}, f32[128,256]{1,0:T(8,128)S(1)}, u32[]{:S(2)}, u32[]{:S(2)}) %collective-permute-start.25) | collective-permute-done | bytes 131104 | tf_op jit(solution)/shard_map/ppermute | solution.py:165
  101.8 2.3 %shard_map.70 = (f32[512,256]{1,0:T(8,128)S(1)}, f32[64,256]{1,0:T(8,128)S(1)}, f32[256,256]{1,0:T(8,128)S(1)}) custom-call(f32[512,256]{1,0:T(8,128)S(1)} %pad_maximum_fusion.1.stack_ref, f32[256,256]{1,0:T(8,128)S(1)} %shard_map.69.lower_ref, f32[512,256]{1,0:T(8,128)S(1)} %get-tuple-element.48.own_ref, f32[512,256]{1,0:T(8,128)S(1)} %collective-permute-done.3.other_ref), custom_call_target="tpu_custom_call" | custom-call | flops 900000000 | bytes 2686976 | tf_op jit(solution)/shard_map/pallas_call | solution.py:60
  107.7 4.7 %collective-permute-done.30 = f32[64,256]{1,0:T(8,128)S(1)} collective-permute-done((f32[64,256]{1,0:T(8,128)S(1)}, f32[64,256]{1,0:T(8,128)S(1)}, u32[]{:S(2)}, u32[]{:S(2)}) %collective-permute-start.30) | collective-permute-done | bytes 65568 | tf_op jit(solution)/shard_map/ppermute | solution.py:165
  112.5 2.7 %collective-permute-start.34 = (f32[256,256]{1,0:T(8,128)S(1)}, f32[256,256]{1,0:T(8,128)S(1)}, u32[]{:S(2)}, u32[]{:S(2)}) collective-permute-start(f32[256,256]{1,0:T(8,128)S(1)} %shard_map.72.first_ref), channel_id=1, source_target_pairs={{0,8},{4,12},{8,0},{12,4},{1,9},{5,13},{9,1},{13,5},{2,10},{6,14},... | collective-permute-start | bytes 786440 | tf_op jit(solution)/shard_map/ppermute | solution.py:165
  115.3 4.3 %collective-permute-done.31.refs_0_ = f32[64,256]{1,0:T(8,128)S(1)} collective-permute-done((f32[64,256]{1,0:T(8,128)S(1)}, f32[64,256]{1,0:T(8,128)S(1)}, u32[]{:S(2)}, u32[]{:S(2)}) %collective-permute-start.31) | collective-permute-done | bytes 65568 | tf_op jit(solution)/shard_map/ppermute | solution.py:165
  120.8 8.0 %shard_map.73.lower_ref = f32[256,256]{1,0:T(8,128)S(1)} custom-call(f32[64,256]{1,0:T(8,128)S(1)} %add.51.own_ref, f32[64,256]{1,0:T(8,128)S(1)} %collective-permute-done.31.refs_0_, f32[64,256]{1,0:T(8,128)S(1)} %collective-permute-done.32.refs_1_, f32[64,256]{1,0:T(8,128)S(1)} %collective-permute-done.33.refs_2_), custom_call_target="tpu_custom_call" | custom-call | flops 1000000000 | bytes 524288 | tf_op jit(solution)/shard_map/pallas_call | solution.py:60
  128.9 6.0 %shard_map.74 = (f32[144,128]{1,0:T(8,128)S(1)}, f32[144,128]{1,0:T(8,128)S(1)}) custom-call(f32[16,4096]{1,0:T(8,128)S(1)} %bitcast.5, f32[512,256]{1,0:T(8,128)S(1)} %get-tuple-element.78.near_ref, f32[512,256]{1,0:T(8,128)S(1)} %get-tuple-element.80.block_ref.far_ref, f32[256,256]{1,0:T(8,128)S(1)} %shard_map.72.first_ref, ...), custom_call_target="tpu_custom_call" | custom-call | flops 3000000000 | bytes 3294208 | tf_op jit(solution)/shard_map/pallas_call | solution.py:60
  135.2 6.1 %collective-permute-done.36.second_ref = f32[144,128]{1,0:T(8,128)S(1)} collective-permute-done((f32[144,128]{1,0:T(8,128)S(1)}, f32[144,128]{1,0:T(8,128)S(1)}, u32[]{:S(2)}, u32[]{:S(2)}) %collective-permute-start.36) | collective-permute-done | bytes 73760 | tf_op jit(solution)/shard_map/ppermute | solution.py:165
  (92 shorter events, 37.2 us)
Async XLA Ops:
  1.6 5.3 %collective-permute-start = (f32[64,256]{1,0:T(8,128)S(1)}, f32[64,256]{1,0:T(8,128)S(1)}, u32[]{:S(2)}, u32[]{:S(2)}) collective-permute-start(f32[64,256]{1,0:T(8,128)S(1)} %shard_map.55), channel_id=1, source_target_pairs={{0,4},{4,0},{8,12},{12,8},{1,5},{5,1},{9,13},{13,9},{2,6},{6,2},{1... | collective-permute-start | bytes 196616 | tf_op jit(solution)/shard_map/ppermute | solution.py:165
  7.0 9.2 %collective-permute-start.1 = (f32[256,256]{1,0:T(8,128)S(1)}, f32[256,256]{1,0:T(8,128)S(1)}, u32[]{:S(2)}, u32[]{:S(2)}) collective-permute-start(f32[256,256]{1,0:T(8,128)S(1)} %get-tuple-element.52), channel_id=1, source_target_pairs={{0,4},{4,0},{8,12},{12,8},{1,5},{5,1},{9,13},{13,9},{2,6},{6,2},{1... | collective-permute-start | bytes 786440 | tf_op jit(solution)/shard_map/ppermute | solution.py:165
  9.1 5.8 %collective-permute-start.2 = (f32[64,256]{1,0:T(8,128)S(1)}, f32[64,256]{1,0:T(8,128)S(1)}, u32[]{:S(2)}, u32[]{:S(2)}) collective-permute-start(f32[64,256]{1,0:T(8,128)S(1)} %add.39), channel_id=1, source_target_pairs={{0,8},{4,12},{8,0},{12,4},{1,9},{5,13},{9,1},{13,5},{2,10},{6,14},... | collective-permute-start | bytes 196616 | tf_op jit(solution)/shard_map/ppermute | solution.py:165
  16.2 18.3 %collective-permute-start.3 = (f32[512,256]{1,0:T(8,128)S(1)}, f32[512,256]{1,0:T(8,128)S(1)}, u32[]{:S(2)}, u32[]{:S(2)}) collective-permute-start(f32[512,256]{1,0:T(8,128)S(1)} %get-tuple-element.54), channel_id=1, source_target_pairs={{0,4},{4,0},{8,12},{12,8},{1,5},{5,1},{9,13},{13,9},{2,6},{6,2},{1... | collective-permute-start | bytes 1572872 | tf_op jit(solution)/shard_map/ppermute | solution.py:165
  18.9 14.8 %collective-permute-start.7 = (f32[256,256]{1,0:T(8,128)S(1)}, f32[256,256]{1,0:T(8,128)S(1)}, u32[]{:S(2)}, u32[]{:S(2)}) collective-permute-start(f32[256,256]{1,0:T(8,128)S(1)} %add.40.first_ref), channel_id=1, source_target_pairs={{0,8},{4,12},{8,0},{12,4},{1,9},{5,13},{9,1},{13,5},{2,10},{6,14},... | collective-permute-start | bytes 786440 | tf_op jit(solution)/shard_map/ppermute | solution.py:165
  20.1 4.3 %collective-permute-start.4 = (f32[64,256]{1,0:T(8,128)S(1)}, f32[64,256]{1,0:T(8,128)S(1)}, u32[]{:S(2)}, u32[]{:S(2)}) collective-permute-start(f32[64,256]{1,0:T(8,128)S(1)} %add.41.own_ref), channel_id=1, source_target_pairs={{0,2},{2,0},{1,3},{3,1},{4,6},{6,4},{5,7},{7,5},{8,10},{10,8},{9,1... | collective-permute-start | bytes 196616 | tf_op jit(solution)/shard_map/ppermute | solution.py:165
  21.6 2.8 %collective-permute-start.5 = (f32[64,256]{1,0:T(8,128)S(1)}, f32[64,256]{1,0:T(8,128)S(1)}, u32[]{:S(2)}, u32[]{:S(2)}) collective-permute-start(f32[64,256]{1,0:T(8,128)S(1)} %add.41.own_ref), channel_id=1, source_target_pairs={{0,1},{1,0},{2,3},{3,2},{4,5},{5,4},{6,7},{7,6},{8,9},{9,8},{10,11... | collective-permute-start | bytes 196616 | tf_op jit(solution)/shard_map/ppermute | solution.py:165
  37.2 5.6 %collective-permute-start.9 = (f32[128,256]{1,0:T(8,128)S(1)}, f32[128,256]{1,0:T(8,128)S(1)}, u32[]{:S(2)}, u32[]{:S(2)}) collective-permute-start(f32[128,256]{1,0:T(8,128)S(1)} %get-tuple-element.59), channel_id=1, source_target_pairs={{0,2},{2,0},{1,3},{3,1},{4,6},{6,4},{5,7},{7,5},{8,10},{10,8},{9,1... | collective-permute-start | bytes 393224 | tf_op jit(solution)/shard_map/ppermute | solution.py:165
  38.7 5.9 %collective-permute-start.12 = (f32[128,256]{1,0:T(8,128)S(1)}, f32[128,256]{1,0:T(8,128)S(1)}, u32[]{:S(2)}, u32[]{:S(2)}) collective-permute-start(f32[128,256]{1,0:T(8,128)S(1)} %get-tuple-element.62), channel_id=1, source_target_pairs={{0,4},{4,0},{8,12},{12,8},{1,5},{5,1},{9,13},{13,9},{2,6},{6,2},{1... | collective-permute-start | bytes 393224 | tf_op jit(solution)/shard_map/ppermute | solution.py:165
  42.8 5.0 %collective-permute-start.10 = (f32[128,256]{1,0:T(8,128)S(1)}, f32[128,256]{1,0:T(8,128)S(1)}, u32[]{:S(2)}, u32[]{:S(2)}) collective-permute-start(f32[128,256]{1,0:T(8,128)S(1)} %add.42), channel_id=1, source_target_pairs={{0,4},{4,0},{8,12},{12,8},{1,5},{5,1},{9,13},{13,9},{2,6},{6,2},{1... | collective-permute-start | bytes 393224 | tf_op jit(solution)/shard_map/ppermute | solution.py:165
  44.6 6.1 %collective-permute-start.13 = (f32[128,256]{1,0:T(8,128)S(1)}, f32[128,256]{1,0:T(8,128)S(1)}, u32[]{:S(2)}, u32[]{:S(2)}) collective-permute-start(f32[128,256]{1,0:T(8,128)S(1)} %add.44), channel_id=1, source_target_pairs={{0,2},{2,0},{1,3},{3,1},{4,6},{6,4},{5,7},{7,5},{8,10},{10,8},{9,1... | collective-permute-start | bytes 393224 | tf_op jit(solution)/shard_map/ppermute | solution.py:165
  47.8 5.0 %collective-permute-start.11 = (f32[128,256]{1,0:T(8,128)S(1)}, f32[128,256]{1,0:T(8,128)S(1)}, u32[]{:S(2)}, u32[]{:S(2)}) collective-permute-start(f32[128,256]{1,0:T(8,128)S(1)} %add.43), channel_id=1, source_target_pairs={{0,2},{2,0},{1,3},{3,1},{4,6},{6,4},{5,7},{7,5},{8,10},{10,8},{9,1... | collective-permute-start | bytes 393224 | tf_op jit(solution)/shard_map/ppermute | solution.py:165
  50.7 5.0 %collective-permute-start.14 = (f32[128,256]{1,0:T(8,128)S(1)}, f32[128,256]{1,0:T(8,128)S(1)}, u32[]{:S(2)}, u32[]{:S(2)}) collective-permute-start(f32[128,256]{1,0:T(8,128)S(1)} %add.45), channel_id=1, source_target_pairs={{0,4},{4,0},{8,12},{12,8},{1,5},{5,1},{9,13},{13,9},{2,6},{6,2},{1... | collective-permute-start | bytes 393224 | tf_op jit(solution)/shard_map/ppermute | solution.py:165
  55.8 2.4 %collective-permute-start.15 = (f32[512,256]{1,0:T(8,128)S(1)}, f32[512,256]{1,0:T(8,128)S(1)}, u32[]{:S(2)}, u32[]{:S(2)}) collective-permute-start(f32[512,256]{1,0:T(8,128)S(1)} %pad_maximum_fusion.stack_ref), channel_id=1, source_target_pairs={{0,1},{1,0},{2,3},{3,2},{4,5},{5,4},{6,7},{7,6},{8,9},{9,8},{10,11... | collective-permute-start | bytes 1572872 | tf_op jit(solution)/shard_map/ppermute | solution.py:165
  59.7 6.7 %collective-permute-start.16 = (f32[64,256]{1,0:T(8,128)S(1)}, f32[64,256]{1,0:T(8,128)S(1)}, u32[]{:S(2)}, u32[]{:S(2)}) collective-permute-start(f32[64,256]{1,0:T(8,128)S(1)} %get-tuple-element.66), channel_id=1, source_target_pairs={{0,8},{4,12},{8,0},{12,4},{1,9},{5,13},{9,1},{13,5},{2,10},{6,14},... | collective-permute-start | bytes 196616 | tf_op jit(solution)/shard_map/ppermute | solution.py:165
  66.4 12.8 %collective-permute-start.20 = (f32[512,128]{1,0:T(8,128)S(1)}, f32[512,128]{1,0:T(8,128)S(1)}, u32[]{:S(2)}, u32[]{:S(2)}) collective-permute-start(f32[512,128]{1,0:T(8,128)S(1)} %get-tuple-element.69), channel_id=1, source_target_pairs={{0,4},{4,0},{8,12},{12,8},{1,5},{5,1},{9,13},{13,9},{2,6},{6,2},{1... | collective-permute-start | bytes 786440 | tf_op jit(solution)/shard_map/ppermute | solution.py:165
  66.5 14.9 %collective-permute-start.21 = (f32[256,256]{1,0:T(8,128)S(1)}, f32[256,256]{1,0:T(8,128)S(1)}, u32[]{:S(2)}, u32[]{:S(2)}) collective-permute-start(f32[256,256]{1,0:T(8,128)S(1)} %shard_map.64.first_ref), channel_id=1, source_target_pairs={{0,8},{4,12},{8,0},{12,4},{1,9},{5,13},{9,1},{13,5},{2,10},{6,14},... | collective-permute-start | bytes 786440 | tf_op jit(solution)/shard_map/ppermute | solution.py:165
  68.9 4.3 %collective-permute-start.17 = (f32[64,256]{1,0:T(8,128)S(1)}, f32[64,256]{1,0:T(8,128)S(1)}, u32[]{:S(2)}, u32[]{:S(2)}) collective-permute-start(f32[64,256]{1,0:T(8,128)S(1)} %add.46.own_ref), channel_id=1, source_target_pairs={{0,2},{2,0},{1,3},{3,1},{4,6},{6,4},{5,7},{7,5},{8,10},{10,8},{9,1... | collective-permute-start | bytes 196616 | tf_op jit(solution)/shard_map/ppermute | solution.py:165
  70.3 2.9 %collective-permute-start.18 = (f32[64,256]{1,0:T(8,128)S(1)}, f32[64,256]{1,0:T(8,128)S(1)}, u32[]{:S(2)}, u32[]{:S(2)}) collective-permute-start(f32[64,256]{1,0:T(8,128)S(1)} %add.46.own_ref), channel_id=1, source_target_pairs={{0,1},{1,0},{2,3},{3,2},{4,5},{5,4},{6,7},{7,6},{8,9},{9,8},{10,11... | collective-permute-start | bytes 196616 | tf_op jit(solution)/shard_map/ppermute | solution.py:165
  84.1 5.6 %collective-permute-start.23 = (f32[128,256]{1,0:T(8,128)S(1)}, f32[128,256]{1,0:T(8,128)S(1)}, u32[]{:S(2)}, u32[]{:S(2)}) collective-permute-start(f32[128,256]{1,0:T(8,128)S(1)} %get-tuple-element.72), channel_id=1, source_target_pairs={{0,2},{2,0},{1,3},{3,1},{4,6},{6,4},{5,7},{7,5},{8,10},{10,8},{9,1... | collective-permute-start | bytes 393224 | tf_op jit(solution)/shard_map/ppermute | solution.py:165
  85.2 5.3 %collective-permute-start.26 = (f32[128,256]{1,0:T(8,128)S(1)}, f32[128,256]{1,0:T(8,128)S(1)}, u32[]{:S(2)}, u32[]{:S(2)}) collective-permute-start(f32[128,256]{1,0:T(8,128)S(1)} %get-tuple-element.77), channel_id=1, source_target_pairs={{0,4},{4,0},{8,12},{12,8},{1,5},{5,1},{9,13},{13,9},{2,6},{6,2},{1... | collective-permute-start | bytes 393224 | tf_op jit(solution)/shard_map/ppermute | solution.py:165
  89.7 5.7 %collective-permute-start.24 = (f32[128,256]{1,0:T(8,128)S(1)}, f32[128,256]{1,0:T(8,128)S(1)}, u32[]{:S(2)}, u32[]{:S(2)}) collective-permute-start(f32[128,256]{1,0:T(8,128)S(1)} %add.47), channel_id=1, source_target_pairs={{0,4},{4,0},{8,12},{12,8},{1,5},{5,1},{9,13},{13,9},{2,6},{6,2},{1... | collective-permute-start | bytes 393224 | tf_op jit(solution)/shard_map/ppermute | solution.py:165
  90.5 6.1 %collective-permute-start.27 = (f32[128,256]{1,0:T(8,128)S(1)}, f32[128,256]{1,0:T(8,128)S(1)}, u32[]{:S(2)}, u32[]{:S(2)}) collective-permute-start(f32[128,256]{1,0:T(8,128)S(1)} %add.49), channel_id=1, source_target_pairs={{0,2},{2,0},{1,3},{3,1},{4,6},{6,4},{5,7},{7,5},{8,10},{10,8},{9,1... | collective-permute-start | bytes 393224 | tf_op jit(solution)/shard_map/ppermute | solution.py:165
  95.4 5.0 %collective-permute-start.25 = (f32[128,256]{1,0:T(8,128)S(1)}, f32[128,256]{1,0:T(8,128)S(1)}, u32[]{:S(2)}, u32[]{:S(2)}) collective-permute-start(f32[128,256]{1,0:T(8,128)S(1)} %add.48), channel_id=1, source_target_pairs={{0,2},{2,0},{1,3},{3,1},{4,6},{6,4},{5,7},{7,5},{8,10},{10,8},{9,1... | collective-permute-start | bytes 393224 | tf_op jit(solution)/shard_map/ppermute | solution.py:165
  96.6 5.0 %collective-permute-start.28 = (f32[128,256]{1,0:T(8,128)S(1)}, f32[128,256]{1,0:T(8,128)S(1)}, u32[]{:S(2)}, u32[]{:S(2)}) collective-permute-start(f32[128,256]{1,0:T(8,128)S(1)} %add.50), channel_id=1, source_target_pairs={{0,4},{4,0},{8,12},{12,8},{1,5},{5,1},{9,13},{13,9},{2,6},{6,2},{1... | collective-permute-start | bytes 393224 | tf_op jit(solution)/shard_map/ppermute | solution.py:165
  101.7 2.4 %collective-permute-start.29 = (f32[512,256]{1,0:T(8,128)S(1)}, f32[512,256]{1,0:T(8,128)S(1)}, u32[]{:S(2)}, u32[]{:S(2)}) collective-permute-start(f32[512,256]{1,0:T(8,128)S(1)} %pad_maximum_fusion.1.stack_ref), channel_id=1, source_target_pairs={{0,1},{1,0},{2,3},{3,2},{4,5},{5,4},{6,7},{7,6},{8,9},{9,8},{10,11... | collective-permute-start | bytes 1572872 | tf_op jit(solution)/shard_map/ppermute | solution.py:165
  105.6 6.9 %collective-permute-start.30 = (f32[64,256]{1,0:T(8,128)S(1)}, f32[64,256]{1,0:T(8,128)S(1)}, u32[]{:S(2)}, u32[]{:S(2)}) collective-permute-start(f32[64,256]{1,0:T(8,128)S(1)} %get-tuple-element.82), channel_id=1, source_target_pairs={{0,8},{4,12},{8,0},{12,4},{1,9},{5,13},{9,1},{13,5},{2,10},{6,14},... | collective-permute-start | bytes 196616 | tf_op jit(solution)/shard_map/ppermute | solution.py:165
  112.5 16.4 %collective-permute-start.35 = (f32[512,128]{1,0:T(8,128)S(1)}, f32[512,128]{1,0:T(8,128)S(1)}, u32[]{:S(2)}, u32[]{:S(2)}) collective-permute-start(f32[512,128]{1,0:T(8,128)S(1)} %get-tuple-element.86), channel_id=1, source_target_pairs={{0,4},{4,0},{8,12},{12,8},{1,5},{5,1},{9,13},{13,9},{2,6},{6,2},{1... | collective-permute-start | bytes 786440 | tf_op jit(solution)/shard_map/ppermute | solution.py:165
  112.5 16.3 %collective-permute-start.34 = (f32[256,256]{1,0:T(8,128)S(1)}, f32[256,256]{1,0:T(8,128)S(1)}, u32[]{:S(2)}, u32[]{:S(2)}) collective-permute-start(f32[256,256]{1,0:T(8,128)S(1)} %shard_map.72.first_ref), channel_id=1, source_target_pairs={{0,8},{4,12},{8,0},{12,4},{1,9},{5,13},{9,1},{13,5},{2,10},{6,14},... | collective-permute-start | bytes 786440 | tf_op jit(solution)/shard_map/ppermute | solution.py:165
  115.3 4.3 %collective-permute-start.31 = (f32[64,256]{1,0:T(8,128)S(1)}, f32[64,256]{1,0:T(8,128)S(1)}, u32[]{:S(2)}, u32[]{:S(2)}) collective-permute-start(f32[64,256]{1,0:T(8,128)S(1)} %add.51.own_ref), channel_id=1, source_target_pairs={{0,2},{2,0},{1,3},{3,1},{4,6},{6,4},{5,7},{7,5},{8,10},{10,8},{9,1... | collective-permute-start | bytes 196616 | tf_op jit(solution)/shard_map/ppermute | solution.py:165
  115.3 4.4 %collective-permute-start.32 = (f32[64,256]{1,0:T(8,128)S(1)}, f32[64,256]{1,0:T(8,128)S(1)}, u32[]{:S(2)}, u32[]{:S(2)}) collective-permute-start(f32[64,256]{1,0:T(8,128)S(1)} %add.51.own_ref), channel_id=1, source_target_pairs={{0,1},{1,0},{2,3},{3,2},{4,5},{5,4},{6,7},{7,6},{8,9},{9,8},{10,11... | collective-permute-start | bytes 196616 | tf_op jit(solution)/shard_map/ppermute | solution.py:165
  134.8 6.4 %collective-permute-start.36 = (f32[144,128]{1,0:T(8,128)S(1)}, f32[144,128]{1,0:T(8,128)S(1)}, u32[]{:S(2)}, u32[]{:S(2)}) collective-permute-start(f32[144,128]{1,0:T(8,128)S(1)} %get-tuple-element.88), channel_id=1, source_target_pairs={{0,8},{4,12},{8,0},{12,4},{1,9},{5,13},{9,1},{13,5},{2,10},{6,14},... | collective-permute-start | bytes 221192 | tf_op jit(solution)/shard_map/ppermute | solution.py:165
  (11 other events, 48.3 us)

commit v3 on v2

--- a/solution.py
+++ b/solution.py
@@ -300,7 +300,8 @@
     gram_share(block_ref, scratch_ref, out_ref)
 
 
-def start_kernel(keys_ref, block_ref, keep_ref, send_ref, kept_ref, sent_ref):
+def start_kernel(keys_ref, block_ref, gram_ref, keep_ref, send_ref, kept_ref, sent_ref):
+    del gram_ref
     mine, _, _, _ = pair_sides()
     for i in range(2):
         at = pl.ds(i * HD, HD)
@@ -400,16 +401,12 @@
     length_ref,
     keep_ref,
     send_ref,
-    basis_ref,
+    score_ref,
 ):
     mine, upper, _, head = pair_sides()
     group = QH // KVH
-    tokens = own_ref.shape[0]
+    tokens = own_ref.shape[1]
     half, width = tokens // 2, length_ref.shape[1]
-    for i, block_ref in enumerate((near_ref, far_ref)):
-        basis_ref[pl.ds(i * tokens, tokens), :] = product(
-            block_ref[...], lower_ref[...], ((1,), (1,))
-        )
     coef = product(first_ref[...] + second_ref[...], lower_ref[...], ((1,), (1,)))
     reduced = []
     for which in range(2):
@@ -418,15 +415,17 @@
         )
         factor = coef[which * HD : (which + 1) * HD]
         reduced.append(product(quer, factor, ((1,), (0,))) / math.sqrt(HD))
-    scores = product(basis_ref[...], jnp.concatenate(reduced), ((1,), (1,)))
-    at = lax.broadcasted_iota(jnp.int32, (half, width), 0)
+    reduced = product(jnp.concatenate(reduced), lower_ref[...], ((1,), (0,)))
+    for i, block_ref in enumerate((near_ref, far_ref)):
+        part = product(block_ref[...], reduced, ((1,), (1,)))
+        for piece in range(2):
+            to = pl.multiple_of(piece * tokens + (head ^ i) * half, half)
+            score_ref[pl.ds(to, half), :] = part[piece * half : (piece + 1) * half]
+    scores = score_ref[...]
+    at = lax.broadcasted_iota(jnp.int32, (tokens, width), 0)
     tok = lax.axis_index("tok")
     valid = jnp.concatenate(
-        [
-            (tok ^ piece) * tokens + (head ^ far) * half + at < length_ref[...]
-            for far in range(2)
-            for piece in range(2)
-        ]
+        [(tok ^ piece) * tokens + at < length_ref[...] for piece in range(2)]
     )
     peak = jnp.max(jnp.where(valid, scores, NEG), axis=0, keepdims=True)
     weight = jnp.where(valid, jnp.exp(scores - peak), 0.0)
@@ -434,15 +433,9 @@
     lane = width // 2
     for which, there_ref in enumerate((low_ref, high_ref)):
         here = slice(which * lane, (which + 1) * lane)
-        parts = []
-        for i in range(4):
-            rows = lanes(head ^ (i // 2), half)
-            if i % 2 == 0:
-                value = own_ref[rows, pl.ds(which * HD, HD)]
-            else:
-                value = there_ref[rows, :]
-            parts.append(product(value, weight[i * half : (i + 1) * half, here], ((0,), (0,))))
-        acc = parts[0] + parts[1] + parts[2] + parts[3]
+        own = own_ref[pl.ds(which * HD, HD), :]
+        acc = product(own, weight[:tokens, here], ((1,), (0,)))
+        acc = acc + product(there_ref[...], weight[tokens:, here], ((1,), (0,)))
 
         def give(ref):
             ref[pl.ds(0, HD), :] = acc
@@ -477,8 +470,8 @@
 def split_kernel(values_ref, kept_ref, first_ref, second_ref):
     mine, _, _, _ = pair_sides()
     for i, ref in enumerate((first_ref, second_ref)):
-        kept_ref[:, pl.ds(i * HD, HD)] = values_ref[:, lanes(2 * i + mine)]
-        ref[...] = values_ref[:, lanes(2 * i + 1 - mine)]
+        kept_ref[pl.ds(i * HD, HD), :] = values_ref[:, lanes(2 * i + mine)].T
+        ref[...] = values_ref[:, lanes(2 * i + 1 - mine)].T
 
 
 def paired_body(keys, values, queries, start_block, lengths):
@@ -499,14 +492,15 @@
         start_kernel,
         [vmem(half, rank)] * 2 + [vmem(tokens, half)] * 2,
         keys,
-        after(start_block, gram),
+        start_block,
+        gram,
         flops=900_000_000,
     )
     gram = gram + swap(gram, "tok", 1)
     proj = keep + swap(after(send, gram), "tok", 1)
     values_own, *values_send = call(
         split_kernel,
-        [vmem(tokens, half)] + [vmem(tokens, HD)] * 2,
+        [vmem(half, tokens)] + [vmem(HD, tokens)] * 2,
         after(values, proj),
     )
     values_other = []
@@ -577,7 +571,7 @@
         values_own,
         *values_other,
         jnp.tile(lengths, 2 * (QH // KVH))[None, :],
-        scratch=[(2 * tokens, rank)],
+        scratch=[(2 * tokens, 2 * (QH // KVH) * rows)],
         flops=3_000_000_000,
     )
     return call(merge_kernel, vmem(1, rows, 1, half * 4), keep, swap(send, "tok", 2))

time: 142 us -> 140 us (0.986)
  no operation moved by 1% of the time
where the time goes in v3:
time: 140 us
  waiting for transfers between devices  57.5 us (41%)
  Pallas kernels  42.6 us (30%)
  starting transfers between devices  37.9 us (27%)
    ppermute x37, waiting for transfers between devices, swap(): return lax.ppermute(x, axis, pairs)  57.5 us
    pallas_call x21, Pallas kernels, call(): pl.pallas_call(kernel, out_shape=out_shape, in_specs=[spec] * len(args),...  42.6 us
    ppermute x37, starting transfers between devices, swap(): return lax.ppermute(x, axis, pairs)  37.9 us
  transfers between devices with their start and end apart: 37, of which 25 were waited for; matrix products, arithmetic and copies ran while one was open for 0% of the time, Pallas kernels for 23%

profile of v3, /device:TPU:0, one launch (start us, length us, event | category | flops | bytes accessed | tf_op | source)
XLA Modules:
  0.0 139.9 jit_solution(7048096568968030600)
XLA Ops:
  1.6 3.1 %collective-permute-start = (f32[64,256]{1,0:T(8,128)S(1)}, f32[64,256]{1,0:T(8,128)S(1)}, u32[]{:S(2)}, u32[]{:S(2)}) collective-permute-start(f32[64,256]{1,0:T(8,128)S(1)} %shard_map.55.gram_ref), channel_id=1, source_target_pairs={{0,4},{4,0},{8,12},{12,8},{1,5},{5,1},{9,13},{13,9},{2,6},{6,2},{1... | collective-permute-start | bytes 196616 | tf_op jit(solution)/shard_map/ppermute | solution.py:165
  7.0 2.1 %collective-permute-start.1 = (f32[256,256]{1,0:T(8,128)S(1)}, f32[256,256]{1,0:T(8,128)S(1)}, u32[]{:S(2)}, u32[]{:S(2)}) collective-permute-start(f32[256,256]{1,0:T(8,128)S(1)} %get-tuple-element.50), channel_id=1, source_target_pairs={{0,4},{4,0},{8,12},{12,8},{1,5},{5,1},{9,13},{13,9},{2,6},{6,2},{1... | collective-permute-start | bytes 786440 | tf_op jit(solution)/shard_map/ppermute | solution.py:165
  9.1 2.6 %collective-permute-start.2 = (f32[64,256]{1,0:T(8,128)S(1)}, f32[64,256]{1,0:T(8,128)S(1)}, u32[]{:S(2)}, u32[]{:S(2)}) collective-permute-start(f32[64,256]{1,0:T(8,128)S(1)} %add.39), channel_id=1, source_target_pairs={{0,8},{4,12},{8,0},{12,4},{1,9},{5,13},{9,1},{13,5},{2,10},{6,14},... | collective-permute-start | bytes 196616 | tf_op jit(solution)/shard_map/ppermute | solution.py:165
  11.6 3.2 %collective-permute-done.2 = f32[64,256]{1,0:T(8,128)S(1)} collective-permute-done((f32[64,256]{1,0:T(8,128)S(1)}, f32[64,256]{1,0:T(8,128)S(1)}, u32[]{:S(2)}, u32[]{:S(2)}) %collective-permute-start.2) | collective-permute-done | bytes 65568 | tf_op jit(solution)/shard_map/ppermute | solution.py:165
  15.7 2.8 %collective-permute-start.3 = (f32[512,256]{1,0:T(8,128)S(1)}, f32[512,256]{1,0:T(8,128)S(1)}, u32[]{:S(2)}, u32[]{:S(2)}) collective-permute-start(f32[512,256]{1,0:T(8,128)S(1)} %get-tuple-element.52), channel_id=1, source_target_pairs={{0,4},{4,0},{8,12},{12,8},{1,5},{5,1},{9,13},{13,9},{2,6},{6,2},{1... | collective-permute-start | bytes 1572872 | tf_op jit(solution)/shard_map/ppermute | solution.py:165
  21.6 2.8 %collective-permute-done.4.refs_0_ = f32[64,256]{1,0:T(8,128)S(1)} collective-permute-done((f32[64,256]{1,0:T(8,128)S(1)}, f32[64,256]{1,0:T(8,128)S(1)}, u32[]{:S(2)}, u32[]{:S(2)}) %collective-permute-start.4) | collective-permute-done | bytes 65568 | tf_op jit(solution)/shard_map/ppermute | solution.py:165
  25.6 8.0 %shard_map.57.lower_ref = f32[256,256]{1,0:T(8,128)S(1)} custom-call(f32[64,256]{1,0:T(8,128)S(1)} %add.41.own_ref, f32[64,256]{1,0:T(8,128)S(1)} %collective-permute-done.4.refs_0_, f32[64,256]{1,0:T(8,128)S(1)} %collective-permute-done.5.refs_1_, f32[64,256]{1,0:T(8,128)S(1)} %collective-permute-done.6.refs_2_), custom_call_target="tpu_custom_call" | custom-call | flops 1000000000 | bytes 524288 | tf_op jit(solution)/shard_map/pallas_call | solution.py:60
  36.6 1.6 %collective-permute-start.9 = (f32[128,256]{1,0:T(8,128)S(1)}, f32[128,256]{1,0:T(8,128)S(1)}, u32[]{:S(2)}, u32[]{:S(2)}) collective-permute-start(f32[128,256]{1,0:T(8,128)S(1)} %get-tuple-element.57), channel_id=1, source_target_pairs={{0,2},{2,0},{1,3},{3,1},{4,6},{6,4},{5,7},{7,5},{8,10},{10,8},{9,1... | collective-permute-start | bytes 393224 | tf_op jit(solution)/shard_map/ppermute | solution.py:165
  38.2 2.3 %collective-permute-start.12 = (f32[128,256]{1,0:T(8,128)S(1)}, f32[128,256]{1,0:T(8,128)S(1)}, u32[]{:S(2)}, u32[]{:S(2)}) collective-permute-start(f32[128,256]{1,0:T(8,128)S(1)} %get-tuple-element.60), channel_id=1, source_target_pairs={{0,4},{4,0},{8,12},{12,8},{1,5},{5,1},{9,13},{13,9},{2,6},{6,2},{1... | collective-permute-start | bytes 393224 | tf_op jit(solution)/shard_map/ppermute | solution.py:165
  40.5 1.8 %collective-permute-done.9 = f32[128,256]{1,0:T(8,128)S(1)} collective-permute-done((f32[128,256]{1,0:T(8,128)S(1)}, f32[128,256]{1,0:T(8,128)S(1)}, u32[]{:S(2)}, u32[]{:S(2)}) %collective-permute-start.9) | collective-permute-done | bytes 131104 | tf_op jit(solution)/shard_map/ppermute | solution.py:165
  42.3 2.3 %collective-permute-start.10 = (f32[128,256]{1,0:T(8,128)S(1)}, f32[128,256]{1,0:T(8,128)S(1)}, u32[]{:S(2)}, u32[]{:S(2)}) collective-permute-start(f32[128,256]{1,0:T(8,128)S(1)} %add.42), channel_id=1, source_target_pairs={{0,4},{4,0},{8,12},{12,8},{1,5},{5,1},{9,13},{13,9},{2,6},{6,2},{1... | collective-permute-start | bytes 393224 | tf_op jit(solution)/shard_map/ppermute | solution.py:165
  44.6 1.6 %collective-permute-start.13 = (f32[128,256]{1,0:T(8,128)S(1)}, f32[128,256]{1,0:T(8,128)S(1)}, u32[]{:S(2)}, u32[]{:S(2)}) collective-permute-start(f32[128,256]{1,0:T(8,128)S(1)} %add.44), channel_id=1, source_target_pairs={{0,2},{2,0},{1,3},{3,1},{4,6},{6,4},{5,7},{7,5},{8,10},{10,8},{9,1... | collective-permute-start | bytes 393224 | tf_op jit(solution)/shard_map/ppermute | solution.py:165
  47.6 1.6 %collective-permute-start.11 = (f32[128,256]{1,0:T(8,128)S(1)}, f32[128,256]{1,0:T(8,128)S(1)}, u32[]{:S(2)}, u32[]{:S(2)}) collective-permute-start(f32[128,256]{1,0:T(8,128)S(1)} %add.43), channel_id=1, source_target_pairs={{0,2},{2,0},{1,3},{3,1},{4,6},{6,4},{5,7},{7,5},{8,10},{10,8},{9,1... | collective-permute-start | bytes 393224 | tf_op jit(solution)/shard_map/ppermute | solution.py:165
  49.1 1.6 %collective-permute-done.13 = f32[128,256]{1,0:T(8,128)S(1)} collective-permute-done((f32[128,256]{1,0:T(8,128)S(1)}, f32[128,256]{1,0:T(8,128)S(1)}, u32[]{:S(2)}, u32[]{:S(2)}) %collective-permute-start.13) | collective-permute-done | bytes 131104 | tf_op jit(solution)/shard_map/ppermute | solution.py:165
  52.6 3.2 %collective-permute-done.14 = f32[128,256]{1,0:T(8,128)S(1)} collective-permute-done((f32[128,256]{1,0:T(8,128)S(1)}, f32[128,256]{1,0:T(8,128)S(1)}, u32[]{:S(2)}, u32[]{:S(2)}) %collective-permute-start.14) | collective-permute-done | bytes 131104 | tf_op jit(solution)/shard_map/ppermute | solution.py:165
  55.9 2.3 %shard_map.62 = (f32[512,256]{1,0:T(8,128)}, f32[64,256]{1,0:T(8,128)S(1)}, f32[256,256]{1,0:T(8,128)S(1)}) custom-call(f32[512,256]{1,0:T(8,128)S(1)} %pad_maximum_fusion.stack_ref, f32[256,256]{1,0:T(8,128)S(1)} %shard_map.57.lower_ref, f32[512,256]{1,0:T(8,128)S(1)} %get-tuple-element.46.own_ref, f32[512,256]{1,0:T(8,128)S(1)} %collective-permute-done.3.other_ref), custom_call_target="tpu_custom_call" | custom-call | flops 900000000 | bytes 2686976 | tf_op jit(solution)/shard_map/pallas_call | solution.py:60
  59.7 1.7 %collective-permute-start.16 = (f32[64,256]{1,0:T(8,128)S(1)}, f32[64,256]{1,0:T(8,128)S(1)}, u32[]{:S(2)}, u32[]{:S(2)}) collective-permute-start(f32[64,256]{1,0:T(8,128)S(1)} %get-tuple-element.64), channel_id=1, source_target_pairs={{0,8},{4,12},{8,0},{12,4},{1,9},{5,13},{9,1},{13,5},{2,10},{6,14},... | collective-permute-start | bytes 196616 | tf_op jit(solution)/shard_map/ppermute | solution.py:165
  62.1 4.3 %collective-permute-done.16 = f32[64,256]{1,0:T(8,128)S(1)} collective-permute-done((f32[64,256]{1,0:T(8,128)S(1)}, f32[64,256]{1,0:T(8,128)S(1)}, u32[]{:S(2)}, u32[]{:S(2)}) %collective-permute-start.16) | collective-permute-done | bytes 65568 | tf_op jit(solution)/shard_map/ppermute | solution.py:165
  66.5 2.3 %collective-permute-start.21 = (f32[256,256]{1,0:T(8,128)S(1)}, f32[256,256]{1,0:T(8,128)S(1)}, u32[]{:S(2)}, u32[]{:S(2)}) collective-permute-start(f32[256,256]{1,0:T(8,128)S(1)} %shard_map.64.first_ref), channel_id=1, source_target_pairs={{0,8},{4,12},{8,0},{12,4},{1,9},{5,13},{9,1},{13,5},{2,10},{6,14},... | collective-permute-start | bytes 786440 | tf_op jit(solution)/shard_map/ppermute | solution.py:165
  68.8 4.3 %collective-permute-done.17.refs_0_ = f32[64,256]{1,0:T(8,128)S(1)} collective-permute-done((f32[64,256]{1,0:T(8,128)S(1)}, f32[64,256]{1,0:T(8,128)S(1)}, u32[]{:S(2)}, u32[]{:S(2)}) %collective-permute-start.17) | collective-permute-done | bytes 65568 | tf_op jit(solution)/shard_map/ppermute | solution.py:165
  74.3 4.0 %shard_map.65 = (f32[128,128]{1,0:T(8,128)S(1)}, f32[128,128]{1,0:T(8,128)S(1)}, f32[128,128]{1,0:T(8,128)S(1)}) custom-call(f32[64,256]{1,0:T(8,128)S(1)} %add.46.own_ref, f32[64,256]{1,0:T(8,128)S(1)} %collective-permute-done.17.refs_0_, f32[64,256]{1,0:T(8,128)S(1)} %collective-permute-done.18.refs_1_, f32[64,256]{1,0:T(8,128)S(1)} %collective-permute-done.19.refs_2_), custom_call_target="tpu_custom_call" | custom-call | flops 1000000000 | bytes 458752 | tf_op jit(solution)/shard_map/pallas_call | solution.py:60
  79.0 2.5 %collective-permute-done.21.second_ref = f32[256,256]{1,0:T(8,128)S(1)} collective-permute-done((f32[256,256]{1,0:T(8,128)S(1)}, f32[256,256]{1,0:T(8,128)S(1)}, u32[]{:S(2)}, u32[]{:S(2)}) %collective-permute-start.21) | collective-permute-done | bytes 262176 | tf_op jit(solution)/shard_map/ppermute | solution.py:165
  85.2 4.5 %collective-permute-done.23 = f32[128,256]{1,0:T(8,128)S(1)} collective-permute-done((f32[128,256]{1,0:T(8,128)S(1)}, f32[128,256]{1,0:T(8,128)S(1)}, u32[]{:S(2)}, u32[]{:S(2)}) %collective-permute-start.23) | collective-permute-done | bytes 131104 | tf_op jit(solution)/shard_map/ppermute | solution.py:165
  91.5 3.9 %shard_map.69.lower_ref = f32[256,256]{1,0:T(8,128)S(1)} custom-call(f32[128,128]{1,0:T(8,128)S(1)} %get-tuple-element.65.tile_ref, f32[128,128]{1,0:T(8,128)S(1)} %get-tuple-element.71.cross_ref, f32[128,128]{1,0:T(8,128)S(1)} %get-tuple-element.72.left_ref), custom_call_target="tpu_custom_call" | custom-call | flops 1000000000 | bytes 458752 | tf_op jit(solution)/shard_map/pallas_call | solution.py:60
  98.0 2.5 %collective-permute-done.25 = f32[128,256]{1,0:T(8,128)S(1)} collective-permute-done((f32[128,256]{1,0:T(8,128)S(1)}, f32[128,256]{1,0:T(8,128)S(1)}, u32[]{:S(2)}, u32[]{:S(2)}) %collective-permute-start.25) | collective-permute-done | bytes 131104 | tf_op jit(solution)/shard_map/ppermute | solution.py:165
  101.8 2.3 %shard_map.70 = (f32[512,256]{1,0:T(8,128)S(1)}, f32[64,256]{1,0:T(8,128)S(1)}, f32[256,256]{1,0:T(8,128)S(1)}) custom-call(f32[512,256]{1,0:T(8,128)S(1)} %pad_maximum_fusion.1.stack_ref, f32[256,256]{1,0:T(8,128)S(1)} %shard_map.69.lower_ref, f32[512,256]{1,0:T(8,128)S(1)} %get-tuple-element.46.own_ref, f32[512,256]{1,0:T(8,128)S(1)} %collective-permute-done.3.other_ref), custom_call_target="tpu_custom_call" | custom-call | flops 900000000 | bytes 2686976 | tf_op jit(solution)/shard_map/pallas_call | solution.py:60
  107.6 4.8 %collective-permute-done.30 = f32[64,256]{1,0:T(8,128)S(1)} collective-permute-done((f32[64,256]{1,0:T(8,128)S(1)}, f32[64,256]{1,0:T(8,128)S(1)}, u32[]{:S(2)}, u32[]{:S(2)}) %collective-permute-start.30) | collective-permute-done | bytes 65568 | tf_op jit(solution)/shard_map/ppermute | solution.py:165
  112.5 2.1 %collective-permute-start.34 = (f32[256,256]{1,0:T(8,128)S(1)}, f32[256,256]{1,0:T(8,128)S(1)}, u32[]{:S(2)}, u32[]{:S(2)}) collective-permute-start(f32[256,256]{1,0:T(8,128)S(1)} %shard_map.72.first_ref), channel_id=1, source_target_pairs={{0,8},{4,12},{8,0},{12,4},{1,9},{5,13},{9,1},{13,5},{2,10},{6,14},... | collective-permute-start | bytes 786440 | tf_op jit(solution)/shard_map/ppermute | solution.py:165
  115.4 3.5 %collective-permute-done.31.refs_0_ = f32[64,256]{1,0:T(8,128)S(1)} collective-permute-done((f32[64,256]{1,0:T(8,128)S(1)}, f32[64,256]{1,0:T(8,128)S(1)}, u32[]{:S(2)}, u32[]{:S(2)}) %collective-permute-start.31) | collective-permute-done | bytes 65568 | tf_op jit(solution)/shard_map/ppermute | solution.py:165
  120.1 8.0 %shard_map.73.lower_ref = f32[256,256]{1,0:T(8,128)S(1)} custom-call(f32[64,256]{1,0:T(8,128)S(1)} %add.51.own_ref, f32[64,256]{1,0:T(8,128)S(1)} %collective-permute-done.31.refs_0_, f32[64,256]{1,0:T(8,128)S(1)} %collective-permute-done.32.refs_1_, f32[64,256]{1,0:T(8,128)S(1)} %collective-permute-done.33.refs_2_), custom_call_target="tpu_custom_call" | custom-call | flops 1000000000 | bytes 524288 | tf_op jit(solution)/shard_map/pallas_call | solution.py:60
  128.2 4.4 %shard_map.74 = (f32[144,128]{1,0:T(8,128)S(1)}, f32[144,128]{1,0:T(8,128)S(1)}) custom-call(f32[16,4096]{1,0:T(8,128)S(1)} %bitcast.5, f32[512,256]{1,0:T(8,128)S(1)} %get-tuple-element.76.near_ref, f32[512,256]{1,0:T(8,128)S(1)} %get-tuple-element.78.block_ref.far_ref, f32[256,256]{1,0:T(8,128)S(1)} %shard_map.72.first_ref, ...), custom_call_target="tpu_custom_call" | custom-call | flops 3000000000 | bytes 3294208 | tf_op jit(solution)/shard_map/pallas_call | solution.py:60
  133.6 5.6 %collective-permute-done.36.second_ref = f32[144,128]{1,0:T(8,128)S(1)} collective-permute-done((f32[144,128]{1,0:T(8,128)S(1)}, f32[144,128]{1,0:T(8,128)S(1)}, u32[]{:S(2)}, u32[]{:S(2)}) %collective-permute-start.36) | collective-permute-done | bytes 73760 | tf_op jit(solution)/shard_map/ppermute | solution.py:165
  (90 shorter events, 36.2 us)
Async XLA Ops:
  1.6 5.3 %collective-permute-start = (f32[64,256]{1,0:T(8,128)S(1)}, f32[64,256]{1,0:T(8,128)S(1)}, u32[]{:S(2)}, u32[]{:S(2)}) collective-permute-start(f32[64,256]{1,0:T(8,128)S(1)} %shard_map.55.gram_ref), channel_id=1, source_target_pairs={{0,4},{4,0},{8,12},{12,8},{1,5},{5,1},{9,13},{13,9},{2,6},{6,2},{1... | collective-permute-start | bytes 196616 | tf_op jit(solution)/shard_map/ppermute | solution.py:165
  7.0 8.7 %collective-permute-start.1 = (f32[256,256]{1,0:T(8,128)S(1)}, f32[256,256]{1,0:T(8,128)S(1)}, u32[]{:S(2)}, u32[]{:S(2)}) collective-permute-start(f32[256,256]{1,0:T(8,128)S(1)} %get-tuple-element.50), channel_id=1, source_target_pairs={{0,4},{4,0},{8,12},{12,8},{1,5},{5,1},{9,13},{13,9},{2,6},{6,2},{1... | collective-permute-start | bytes 786440 | tf_op jit(solution)/shard_map/ppermute | solution.py:165
  9.1 5.8 %collective-permute-start.2 = (f32[64,256]{1,0:T(8,128)S(1)}, f32[64,256]{1,0:T(8,128)S(1)}, u32[]{:S(2)}, u32[]{:S(2)}) collective-permute-start(f32[64,256]{1,0:T(8,128)S(1)} %add.39), channel_id=1, source_target_pairs={{0,8},{4,12},{8,0},{12,4},{1,9},{5,13},{9,1},{13,5},{2,10},{6,14},... | collective-permute-start | bytes 196616 | tf_op jit(solution)/shard_map/ppermute | solution.py:165
  15.7 18.3 %collective-permute-start.3 = (f32[512,256]{1,0:T(8,128)S(1)}, f32[512,256]{1,0:T(8,128)S(1)}, u32[]{:S(2)}, u32[]{:S(2)}) collective-permute-start(f32[512,256]{1,0:T(8,128)S(1)} %get-tuple-element.52), channel_id=1, source_target_pairs={{0,4},{4,0},{8,12},{12,8},{1,5},{5,1},{9,13},{13,9},{2,6},{6,2},{1... | collective-permute-start | bytes 1572872 | tf_op jit(solution)/shard_map/ppermute | solution.py:165
  18.5 15.4 %collective-permute-start.7 = (f32[256,256]{1,0:T(8,128)S(1)}, f32[256,256]{1,0:T(8,128)S(1)}, u32[]{:S(2)}, u32[]{:S(2)}) collective-permute-start(f32[256,256]{1,0:T(8,128)S(1)} %add.40.first_ref), channel_id=1, source_target_pairs={{0,8},{4,12},{8,0},{12,4},{1,9},{5,13},{9,1},{13,5},{2,10},{6,14},... | collective-permute-start | bytes 786440 | tf_op jit(solution)/shard_map/ppermute | solution.py:165
  20.1 4.3 %collective-permute-start.4 = (f32[64,256]{1,0:T(8,128)S(1)}, f32[64,256]{1,0:T(8,128)S(1)}, u32[]{:S(2)}, u32[]{:S(2)}) collective-permute-start(f32[64,256]{1,0:T(8,128)S(1)} %add.41.own_ref), channel_id=1, source_target_pairs={{0,2},{2,0},{1,3},{3,1},{4,6},{6,4},{5,7},{7,5},{8,10},{10,8},{9,1... | collective-permute-start | bytes 196616 | tf_op jit(solution)/shard_map/ppermute | solution.py:165
  21.6 2.8 %collective-permute-start.5 = (f32[64,256]{1,0:T(8,128)S(1)}, f32[64,256]{1,0:T(8,128)S(1)}, u32[]{:S(2)}, u32[]{:S(2)}) collective-permute-start(f32[64,256]{1,0:T(8,128)S(1)} %add.41.own_ref), channel_id=1, source_target_pairs={{0,1},{1,0},{2,3},{3,2},{4,5},{5,4},{6,7},{7,6},{8,9},{9,8},{10,11... | collective-permute-start | bytes 196616 | tf_op jit(solution)/shard_map/ppermute | solution.py:165
  36.6 5.6 %collective-permute-start.9 = (f32[128,256]{1,0:T(8,128)S(1)}, f32[128,256]{1,0:T(8,128)S(1)}, u32[]{:S(2)}, u32[]{:S(2)}) collective-permute-start(f32[128,256]{1,0:T(8,128)S(1)} %get-tuple-element.57), channel_id=1, source_target_pairs={{0,2},{2,0},{1,3},{3,1},{4,6},{6,4},{5,7},{7,5},{8,10},{10,8},{9,1... | collective-permute-start | bytes 393224 | tf_op jit(solution)/shard_map/ppermute | solution.py:165
  38.2 6.4 %collective-permute-start.12 = (f32[128,256]{1,0:T(8,128)S(1)}, f32[128,256]{1,0:T(8,128)S(1)}, u32[]{:S(2)}, u32[]{:S(2)}) collective-permute-start(f32[128,256]{1,0:T(8,128)S(1)} %get-tuple-element.60), channel_id=1, source_target_pairs={{0,4},{4,0},{8,12},{12,8},{1,5},{5,1},{9,13},{13,9},{2,6},{6,2},{1... | collective-permute-start | bytes 393224 | tf_op jit(solution)/shard_map/ppermute | solution.py:165
  42.3 5.3 %collective-permute-start.10 = (f32[128,256]{1,0:T(8,128)S(1)}, f32[128,256]{1,0:T(8,128)S(1)}, u32[]{:S(2)}, u32[]{:S(2)}) collective-permute-start(f32[128,256]{1,0:T(8,128)S(1)} %add.42), channel_id=1, source_target_pairs={{0,4},{4,0},{8,12},{12,8},{1,5},{5,1},{9,13},{13,9},{2,6},{6,2},{1... | collective-permute-start | bytes 393224 | tf_op jit(solution)/shard_map/ppermute | solution.py:165
  44.6 6.1 %collective-permute-start.13 = (f32[128,256]{1,0:T(8,128)S(1)}, f32[128,256]{1,0:T(8,128)S(1)}, u32[]{:S(2)}, u32[]{:S(2)}) collective-permute-start(f32[128,256]{1,0:T(8,128)S(1)} %add.44), channel_id=1, source_target_pairs={{0,2},{2,0},{1,3},{3,1},{4,6},{6,4},{5,7},{7,5},{8,10},{10,8},{9,1... | collective-permute-start | bytes 393224 | tf_op jit(solution)/shard_map/ppermute | solution.py:165
  47.6 5.0 %collective-permute-start.11 = (f32[128,256]{1,0:T(8,128)S(1)}, f32[128,256]{1,0:T(8,128)S(1)}, u32[]{:S(2)}, u32[]{:S(2)}) collective-permute-start(f32[128,256]{1,0:T(8,128)S(1)} %add.43), channel_id=1, source_target_pairs={{0,2},{2,0},{1,3},{3,1},{4,6},{6,4},{5,7},{7,5},{8,10},{10,8},{9,1... | collective-permute-start | bytes 393224 | tf_op jit(solution)/shard_map/ppermute | solution.py:165
  50.7 5.0 %collective-permute-start.14 = (f32[128,256]{1,0:T(8,128)S(1)}, f32[128,256]{1,0:T(8,128)S(1)}, u32[]{:S(2)}, u32[]{:S(2)}) collective-permute-start(f32[128,256]{1,0:T(8,128)S(1)} %add.45), channel_id=1, source_target_pairs={{0,4},{4,0},{8,12},{12,8},{1,5},{5,1},{9,13},{13,9},{2,6},{6,2},{1... | collective-permute-start | bytes 393224 | tf_op jit(solution)/shard_map/ppermute | solution.py:165
  55.8 2.4 %collective-permute-start.15 = (f32[512,256]{1,0:T(8,128)S(1)}, f32[512,256]{1,0:T(8,128)S(1)}, u32[]{:S(2)}, u32[]{:S(2)}) collective-permute-start(f32[512,256]{1,0:T(8,128)S(1)} %pad_maximum_fusion.stack_ref), channel_id=1, source_target_pairs={{0,1},{1,0},{2,3},{3,2},{4,5},{5,4},{6,7},{7,6},{8,9},{9,8},{10,11... | collective-permute-start | bytes 1572872 | tf_op jit(solution)/shard_map/ppermute | solution.py:165
  59.7 6.7 %collective-permute-start.16 = (f32[64,256]{1,0:T(8,128)S(1)}, f32[64,256]{1,0:T(8,128)S(1)}, u32[]{:S(2)}, u32[]{:S(2)}) collective-permute-start(f32[64,256]{1,0:T(8,128)S(1)} %get-tuple-element.64), channel_id=1, source_target_pairs={{0,8},{4,12},{8,0},{12,4},{1,9},{5,13},{9,1},{13,5},{2,10},{6,14},... | collective-permute-start | bytes 196616 | tf_op jit(solution)/shard_map/ppermute | solution.py:165
  66.4 12.5 %collective-permute-start.20 = (f32[128,512]{1,0:T(8,128)S(1)}, f32[128,512]{1,0:T(8,128)S(1)}, u32[]{:S(2)}, u32[]{:S(2)}) collective-permute-start(f32[128,512]{1,0:T(8,128)S(1)} %get-tuple-element.67), channel_id=1, source_target_pairs={{0,4},{4,0},{8,12},{12,8},{1,5},{5,1},{9,13},{13,9},{2,6},{6,2},{1... | collective-permute-start | bytes 786440 | tf_op jit(solution)/shard_map/ppermute | solution.py:165
  66.5 14.9 %collective-permute-start.21 = (f32[256,256]{1,0:T(8,128)S(1)}, f32[256,256]{1,0:T(8,128)S(1)}, u32[]{:S(2)}, u32[]{:S(2)}) collective-permute-start(f32[256,256]{1,0:T(8,128)S(1)} %shard_map.64.first_ref), channel_id=1, source_target_pairs={{0,8},{4,12},{8,0},{12,4},{1,9},{5,13},{9,1},{13,5},{2,10},{6,14},... | collective-permute-start | bytes 786440 | tf_op jit(solution)/shard_map/ppermute | solution.py:165
  68.8 4.3 %collective-permute-start.17 = (f32[64,256]{1,0:T(8,128)S(1)}, f32[64,256]{1,0:T(8,128)S(1)}, u32[]{:S(2)}, u32[]{:S(2)}) collective-permute-start(f32[64,256]{1,0:T(8,128)S(1)} %add.46.own_ref), channel_id=1, source_target_pairs={{0,2},{2,0},{1,3},{3,1},{4,6},{6,4},{5,7},{7,5},{8,10},{10,8},{9,1... | collective-permute-start | bytes 196616 | tf_op jit(solution)/shard_map/ppermute | solution.py:165
  68.8 4.3 %collective-permute-start.18 = (f32[64,256]{1,0:T(8,128)S(1)}, f32[64,256]{1,0:T(8,128)S(1)}, u32[]{:S(2)}, u32[]{:S(2)}) collective-permute-start(f32[64,256]{1,0:T(8,128)S(1)} %add.46.own_ref), channel_id=1, source_target_pairs={{0,1},{1,0},{2,3},{3,2},{4,5},{5,4},{6,7},{7,6},{8,9},{9,8},{10,11... | collective-permute-start | bytes 196616 | tf_op jit(solution)/shard_map/ppermute | solution.py:165
  84.1 5.6 %collective-permute-start.23 = (f32[128,256]{1,0:T(8,128)S(1)}, f32[128,256]{1,0:T(8,128)S(1)}, u32[]{:S(2)}, u32[]{:S(2)}) collective-permute-start(f32[128,256]{1,0:T(8,128)S(1)} %get-tuple-element.70), channel_id=1, source_target_pairs={{0,2},{2,0},{1,3},{3,1},{4,6},{6,4},{5,7},{7,5},{8,10},{10,8},{9,1... | collective-permute-start | bytes 393224 | tf_op jit(solution)/shard_map/ppermute | solution.py:165
  85.2 5.3 %collective-permute-start.26 = (f32[128,256]{1,0:T(8,128)S(1)}, f32[128,256]{1,0:T(8,128)S(1)}, u32[]{:S(2)}, u32[]{:S(2)}) collective-permute-start(f32[128,256]{1,0:T(8,128)S(1)} %get-tuple-element.75), channel_id=1, source_target_pairs={{0,4},{4,0},{8,12},{12,8},{1,5},{5,1},{9,13},{13,9},{2,6},{6,2},{1... | collective-permute-start | bytes 393224 | tf_op jit(solution)/shard_map/ppermute | solution.py:165
  89.7 5.7 %collective-permute-start.24 = (f32[128,256]{1,0:T(8,128)S(1)}, f32[128,256]{1,0:T(8,128)S(1)}, u32[]{:S(2)}, u32[]{:S(2)}) collective-permute-start(f32[128,256]{1,0:T(8,128)S(1)} %add.47), channel_id=1, source_target_pairs={{0,4},{4,0},{8,12},{12,8},{1,5},{5,1},{9,13},{13,9},{2,6},{6,2},{1... | collective-permute-start | bytes 393224 | tf_op jit(solution)/shard_map/ppermute | solution.py:165
  90.5 6.1 %collective-permute-start.27 = (f32[128,256]{1,0:T(8,128)S(1)}, f32[128,256]{1,0:T(8,128)S(1)}, u32[]{:S(2)}, u32[]{:S(2)}) collective-permute-start(f32[128,256]{1,0:T(8,128)S(1)} %add.49), channel_id=1, source_target_pairs={{0,2},{2,0},{1,3},{3,1},{4,6},{6,4},{5,7},{7,5},{8,10},{10,8},{9,1... | collective-permute-start | bytes 393224 | tf_op jit(solution)/shard_map/ppermute | solution.py:165
  95.4 5.0 %collective-permute-start.25 = (f32[128,256]{1,0:T(8,128)S(1)}, f32[128,256]{1,0:T(8,128)S(1)}, u32[]{:S(2)}, u32[]{:S(2)}) collective-permute-start(f32[128,256]{1,0:T(8,128)S(1)} %add.48), channel_id=1, source_target_pairs={{0,2},{2,0},{1,3},{3,1},{4,6},{6,4},{5,7},{7,5},{8,10},{10,8},{9,1... | collective-permute-start | bytes 393224 | tf_op jit(solution)/shard_map/ppermute | solution.py:165
  96.6 5.0 %collective-permute-start.28 = (f32[128,256]{1,0:T(8,128)S(1)}, f32[128,256]{1,0:T(8,128)S(1)}, u32[]{:S(2)}, u32[]{:S(2)}) collective-permute-start(f32[128,256]{1,0:T(8,128)S(1)} %add.50), channel_id=1, source_target_pairs={{0,4},{4,0},{8,12},{12,8},{1,5},{5,1},{9,13},{13,9},{2,6},{6,2},{1... | collective-permute-start | bytes 393224 | tf_op jit(solution)/shard_map/ppermute | solution.py:165
  101.7 2.4 %collective-permute-start.29 = (f32[512,256]{1,0:T(8,128)S(1)}, f32[512,256]{1,0:T(8,128)S(1)}, u32[]{:S(2)}, u32[]{:S(2)}) collective-permute-start(f32[512,256]{1,0:T(8,128)S(1)} %pad_maximum_fusion.1.stack_ref), channel_id=1, source_target_pairs={{0,1},{1,0},{2,3},{3,2},{4,5},{5,4},{6,7},{7,6},{8,9},{9,8},{10,11... | collective-permute-start | bytes 1572872 | tf_op jit(solution)/shard_map/ppermute | solution.py:165
  105.6 6.9 %collective-permute-start.30 = (f32[64,256]{1,0:T(8,128)S(1)}, f32[64,256]{1,0:T(8,128)S(1)}, u32[]{:S(2)}, u32[]{:S(2)}) collective-permute-start(f32[64,256]{1,0:T(8,128)S(1)} %get-tuple-element.80), channel_id=1, source_target_pairs={{0,8},{4,12},{8,0},{12,4},{1,9},{5,13},{9,1},{13,5},{2,10},{6,14},... | collective-permute-start | bytes 196616 | tf_op jit(solution)/shard_map/ppermute | solution.py:165
  112.5 15.7 %collective-permute-start.35 = (f32[128,512]{1,0:T(8,128)S(1)}, f32[128,512]{1,0:T(8,128)S(1)}, u32[]{:S(2)}, u32[]{:S(2)}) collective-permute-start(f32[128,512]{1,0:T(8,128)S(1)} %get-tuple-element.84), channel_id=1, source_target_pairs={{0,4},{4,0},{8,12},{12,8},{1,5},{5,1},{9,13},{13,9},{2,6},{6,2},{1... | collective-permute-start | bytes 786440 | tf_op jit(solution)/shard_map/ppermute | solution.py:165
  112.5 15.7 %collective-permute-start.34 = (f32[256,256]{1,0:T(8,128)S(1)}, f32[256,256]{1,0:T(8,128)S(1)}, u32[]{:S(2)}, u32[]{:S(2)}) collective-permute-start(f32[256,256]{1,0:T(8,128)S(1)} %shard_map.72.first_ref), channel_id=1, source_target_pairs={{0,8},{4,12},{8,0},{12,4},{1,9},{5,13},{9,1},{13,5},{2,10},{6,14},... | collective-permute-start | bytes 786440 | tf_op jit(solution)/shard_map/ppermute | solution.py:165
  114.6 4.3 %collective-permute-start.31 = (f32[64,256]{1,0:T(8,128)S(1)}, f32[64,256]{1,0:T(8,128)S(1)}, u32[]{:S(2)}, u32[]{:S(2)}) collective-permute-start(f32[64,256]{1,0:T(8,128)S(1)} %add.51.own_ref), channel_id=1, source_target_pairs={{0,2},{2,0},{1,3},{3,1},{4,6},{6,4},{5,7},{7,5},{8,10},{10,8},{9,1... | collective-permute-start | bytes 196616 | tf_op jit(solution)/shard_map/ppermute | solution.py:165
  115.4 3.6 %collective-permute-start.32 = (f32[64,256]{1,0:T(8,128)S(1)}, f32[64,256]{1,0:T(8,128)S(1)}, u32[]{:S(2)}, u32[]{:S(2)}) collective-permute-start(f32[64,256]{1,0:T(8,128)S(1)} %add.51.own_ref), channel_id=1, source_target_pairs={{0,1},{1,0},{2,3},{3,2},{4,5},{5,4},{6,7},{7,6},{8,9},{9,8},{10,11... | collective-permute-start | bytes 196616 | tf_op jit(solution)/shard_map/ppermute | solution.py:165
  132.6 6.5 %collective-permute-start.36 = (f32[144,128]{1,0:T(8,128)S(1)}, f32[144,128]{1,0:T(8,128)S(1)}, u32[]{:S(2)}, u32[]{:S(2)}) collective-permute-start(f32[144,128]{1,0:T(8,128)S(1)} %get-tuple-element.86), channel_id=1, source_target_pairs={{0,8},{4,12},{8,0},{12,4},{1,9},{5,13},{9,1},{13,5},{2,10},{6,14},... | collective-permute-start | bytes 221192 | tf_op jit(solution)/shard_map/ppermute | solution.py:165
  (10 other events, 47.2 us)

commit v4 on v3

--- a/solution.py
+++ b/solution.py
@@ -345,65 +345,56 @@
     b = b_keep + swap(b_send, "tok", 1)
     a, b = a + swap(a, "tok", 1), b + swap(b, "lay", 1)
     a = after(a, lower)
-    stack = jnp.concatenate([a, swap(a, "lay", 1), b, swap(b, "tok", 1)])
-    return stack, swap(stack, "head", 1)
-
-
-def place_block(stack_ref, lower_ref, block_ref):
-    mine, _, lay, _ = pair_sides()
-    count = stack_ref.shape[0] // 4
-    half = count // 2
-    block = product(stack_ref[...], lower_ref[...], ((1,), (1,)))
-    for i in range(2):
-        for piece in range(2):
-            to = (piece ^ mine) * 2 * count + (lay ^ i) * half
-            at = i * count + piece * half
-            block_ref[pl.ds(pl.multiple_of(to, half), half), :] = block[at : at + half]
-        at = (2 + i) * count
-        block_ref[pl.ds((2 * i + 1) * count, count), :] = block[at : at + count]
-
-
-def half_projection(far, own_ref, other_ref, block_ref):
-    _, _, _, head = pair_sides()
-    half = own_ref.shape[0] // 2
-    rows = lanes(head ^ int(far), half)
-    return product(own_ref[rows, :], block_ref[pl.ds(0, half), :], ((0,), (0,))) + product(
-        other_ref[rows, :], block_ref[pl.ds(half, half), :], ((0,), (0,))
-    )
-
-
-def near_kernel(stack_ref, lower_ref, own_ref, other_ref, block_ref, gram_ref, proj_ref, scratch_ref):
-    place_block(stack_ref, lower_ref, block_ref)
+    here = jnp.concatenate([a, b])
+    return here, (swap(a, "lay", 1), swap(b, "tok", 1))
+
+
+def stack_rows(far, beside, size):
+    _, _, lay, head = pair_sides()
+    count = size // 2
+    first = (head ^ far) * size
+    return first + (lay ^ beside) * (count // 2), first + count
+
+
+def project_stack(far, beside, own_ref, other_ref, block_ref, rows_ref):
+    mine, _, _, _ = pair_sides()
+    size = block_ref.shape[0]
+    half, quarter = size // 2, size // 4
+    low, high = stack_rows(far, beside, size)
+    low = pl.ds(pl.multiple_of(low, quarter), quarter)
+    rows_ref[lanes(mine, quarter), :] = own_ref[low, :]
+    rows_ref[lanes(1 - mine, quarter), :] = other_ref[low, :]
+    high = pl.ds(pl.multiple_of(high, half), half)
+    rows_ref[pl.ds(half, half), :] = (other_ref if beside else own_ref)[high, :]
+    return product(rows_ref[...], block_ref[...], ((0,), (0,)))
+
+
+def stack_kernel(far, beside, stack_ref, lower_ref, own_ref, other_ref, *refs):
+    *part_refs, block_ref, gram_ref, proj_ref, rows_ref, scratch_ref = refs
+    block_ref[...] = product(stack_ref[...], lower_ref[...], ((1,), (1,)))
     gram_share(block_ref, scratch_ref, gram_ref)
-    proj_ref[...] = half_projection(False, own_ref, other_ref, block_ref)
-
-
-def far_kernel(stack_ref, lower_ref, part_ref, block_ref, gram_ref, scratch_ref):
-    place_block(stack_ref, lower_ref, block_ref)
+    proj_ref[...] = project_stack(far, beside, own_ref, other_ref, block_ref, rows_ref)
+    for part_ref, ref in zip(part_refs, (gram_ref, proj_ref)):
+        ref[...] += part_ref[...]
+
+
+def last_stack_kernel(stack_ref, lower_ref, part_ref, block_ref, gram_ref, scratch_ref):
+    block_ref[...] = product(stack_ref[...], lower_ref[...], ((1,), (1,)))
     gram_share(block_ref, scratch_ref, gram_ref)
     gram_ref[...] += part_ref[...]
 
 
-def project_kernel(own_ref, other_ref, block_ref, part_ref, proj_ref):
-    proj_ref[...] = part_ref[...] + half_projection(True, own_ref, other_ref, block_ref)
+def project_kernel(own_ref, other_ref, block_ref, part_ref, proj_ref, rows_ref):
+    proj_ref[...] = part_ref[...] + project_stack(1, 1, own_ref, other_ref, block_ref, rows_ref)
 
 
 def attend_kernel(
     query_ref,
-    near_ref,
-    far_ref,
-    first_ref,
-    second_ref,
-    lower_ref,
-    own_ref,
-    low_ref,
-    high_ref,
-    length_ref,
-    keep_ref,
-    send_ref,
-    score_ref,
+    *refs,
 ):
-    mine, upper, _, head = pair_sides()
+    *block_refs, first_ref, second_ref, lower_ref, own_ref, low_ref, high_ref, length_ref = refs[:-3]
+    keep_ref, send_ref, score_ref = refs[-3:]
+    mine, upper, _, _ = pair_sides()
     group = QH // KVH
     tokens = own_ref.shape[1]
     half, width = tokens // 2, length_ref.shape[1]
@@ -416,11 +407,16 @@
         factor = coef[which * HD : (which + 1) * HD]
         reduced.append(product(quer, factor, ((1,), (0,))) / math.sqrt(HD))
     reduced = product(jnp.concatenate(reduced), lower_ref[...], ((1,), (0,)))
-    for i, block_ref in enumerate((near_ref, far_ref)):
+    for i, block_ref in enumerate(block_refs):
+        far, beside = i % 2, i // 2
         part = product(block_ref[...], reduced, ((1,), (1,)))
+        low, high = stack_rows(far, beside, half)
+        quarter = half // 4
         for piece in range(2):
-            to = pl.multiple_of(piece * tokens + (head ^ i) * half, half)
-            score_ref[pl.ds(to, half), :] = part[piece * half : (piece + 1) * half]
+            to = pl.multiple_of((piece ^ mine) * tokens + low, quarter)
+            score_ref[pl.ds(to, quarter), :] = part[piece * quarter : (piece + 1) * quarter]
+        to = pl.multiple_of(beside * tokens + high, half // 2)
+        score_ref[pl.ds(to, half // 2), :] = part[half // 2 :]
     scores = score_ref[...]
     at = lax.broadcasted_iota(jnp.int32, (tokens, width), 0)
     tok = lax.axis_index("tok")
@@ -530,41 +526,51 @@
             call(functools.partial(mix_kernel, sent), vmem(tokens, rank), *mix, flops=400_000_000)
             for sent in (True, False)
         )
-        stack, far = summed_streams(z_keep, z_send, lower)
-        near_block, gram, proj = call(
-            near_kernel,
-            [vmem(tokens, rank), vmem(share, rank), vmem(half, rank)],
-            stack,
+        here, there = summed_streams(z_keep, z_send, lower)
+        block, parts = vmem(tokens // 2, rank), ()
+        blocks = []
+        stacks = [here, swap(here, "head", 1)]
+        for i in range(3):
+            if i == 2:
+                there = jnp.concatenate([after(x, *parts) for x in there])
+                stacks += [there, swap(there, "head", 1)]
+            done, *parts = call(
+                functools.partial(stack_kernel, i % 2, i // 2),
+                [block, vmem(share, rank), vmem(half, rank)],
+                stacks[i],
+                lower,
+                keys_own,
+                keys_other,
+                *parts,
+                scratch=[(tokens // 2, half), (rank // 2, rank)],
+                flops=900_000_000,
+            )
+            blocks.append(done)
+        done, gram = call(
+            last_stack_kernel,
+            [block, vmem(share, rank)],
+            stacks[3],
             lower,
-            keys_own,
-            keys_other,
-            scratch=[(rank // 2, rank)],
-            flops=900_000_000,
-        )
-        far_block, gram = call(
-            far_kernel,
-            [vmem(tokens, rank), vmem(share, rank)],
-            far,
-            lower,
-            gram,
+            parts[0],
             scratch=[(rank // 2, rank)],
             flops=600_000_000,
         )
+        blocks.append(done)
         proj = call(
             project_kernel,
             vmem(half, rank),
             keys_own,
             keys_other,
-            far_block,
-            proj,
+            done,
+            parts[1],
+            scratch=[(tokens // 2, half)],
             flops=400_000_000,
         )
     keep, send = call(
         attend_kernel,
         [vmem(HD + 16, HD)] * 2,
         queries,
-        near_block,
-        far_block,
+        *blocks,
         first,
         second,
         lower,

time: 140 us -> 139 us (level)
  waiting for transfers between devices: 57.5 us -> 51.5 us
  Pallas kernels: 42.6 us -> 45.1 us
  starting transfers between devices: 37.9 us -> 40.1 us
    ppermute x37 -> x39, waiting for transfers between devices: 57.5 us -> 51.5 us  [swap(): return lax.ppermute(x, axis, pairs)]
    pallas_call x21 -> x25, Pallas kernels: 42.6 us -> 45.1 us  [call(): pl.pallas_call(kernel, out_shape=out_shape, in_specs=[spec] * len(args),...]
    ppermute x37 -> x39, starting transfers between devices: 37.9 us -> 40.1 us  [swap(): return lax.ppermute(x, axis, pairs)]
  transfers between devices with their start and end apart: 37 -> 39, of which waited for: 25 -> 26; matrix products, arithmetic and copies ran while one was open for 0% -> 0% of each run, Pallas kernels for 23% -> 26%
where the time goes in v4:
time: 139 us
  waiting for transfers between devices  51.5 us (37%)
  Pallas kernels  45.1 us (32%)
  starting transfers between devices  40.1 us (29%)
    ppermute x39, waiting for transfers between devices, swap(): return lax.ppermute(x, axis, pairs)  51.5 us
    pallas_call x25, Pallas kernels, call(): pl.pallas_call(kernel, out_shape=out_shape, in_specs=[spec] * len(args),...  45.1 us
    ppermute x39, starting transfers between devices, swap(): return lax.ppermute(x, axis, pairs)  40.1 us
  transfers between devices with their start and end apart: 39, of which 26 were waited for; matrix products, arithmetic and copies ran while one was open for 0% of the time, Pallas kernels for 26%

profile of v4, /device:TPU:0, one launch (start us, length us, event | category | flops | bytes accessed | tf_op | source)
XLA Modules:
  0.0 138.6 jit_solution(13050567055089977595)
XLA Ops:
  1.6 3.1 %collective-permute-start = (f32[64,256]{1,0:T(8,128)S(1)}, f32[64,256]{1,0:T(8,128)S(1)}, u32[]{:S(2)}, u32[]{:S(2)}) collective-permute-start(f32[64,256]{1,0:T(8,128)S(1)} %shard_map.55.gram_ref), channel_id=1, source_target_pairs={{0,4},{4,0},{8,12},{12,8},{1,5},{5,1},{9,13},{13,9},{2,6},{6,2},{1... | collective-permute-start | bytes 196616 | tf_op jit(solution)/shard_map/ppermute | solution.py:165
  7.0 2.1 %collective-permute-start.1 = (f32[256,256]{1,0:T(8,128)S(1)}, f32[256,256]{1,0:T(8,128)S(1)}, u32[]{:S(2)}, u32[]{:S(2)}) collective-permute-start(f32[256,256]{1,0:T(8,128)S(1)} %get-tuple-element.64), channel_id=1, source_target_pairs={{0,4},{4,0},{8,12},{12,8},{1,5},{5,1},{9,13},{13,9},{2,6},{6,2},{1... | collective-permute-start | bytes 786440 | tf_op jit(solution)/shard_map/ppermute | solution.py:165
  9.1 2.6 %collective-permute-start.2 = (f32[64,256]{1,0:T(8,128)S(1)}, f32[64,256]{1,0:T(8,128)S(1)}, u32[]{:S(2)}, u32[]{:S(2)}) collective-permute-start(f32[64,256]{1,0:T(8,128)S(1)} %add.39), channel_id=1, source_target_pairs={{0,8},{4,12},{8,0},{12,4},{1,9},{5,13},{9,1},{13,5},{2,10},{6,14},... | collective-permute-start | bytes 196616 | tf_op jit(solution)/shard_map/ppermute | solution.py:165
  11.6 3.2 %collective-permute-done.2 = f32[64,256]{1,0:T(8,128)S(1)} collective-permute-done((f32[64,256]{1,0:T(8,128)S(1)}, f32[64,256]{1,0:T(8,128)S(1)}, u32[]{:S(2)}, u32[]{:S(2)}) %collective-permute-start.2) | collective-permute-done | bytes 65568 | tf_op jit(solution)/shard_map/ppermute | solution.py:165
  15.7 2.8 %collective-permute-start.3 = (f32[512,256]{1,0:T(8,128)S(1)}, f32[512,256]{1,0:T(8,128)S(1)}, u32[]{:S(2)}, u32[]{:S(2)}) collective-permute-start(f32[512,256]{1,0:T(8,128)S(1)} %get-tuple-element.66), channel_id=1, source_target_pairs={{0,4},{4,0},{8,12},{12,8},{1,5},{5,1},{9,13},{13,9},{2,6},{6,2},{1... | collective-permute-start | bytes 1572872 | tf_op jit(solution)/shard_map/ppermute | solution.py:165
  18.5 1.5 %collective-permute-start.7 = (f32[256,256]{1,0:T(8,128)S(1)}, f32[256,256]{1,0:T(8,128)S(1)}, u32[]{:S(2)}, u32[]{:S(2)}) collective-permute-start(f32[256,256]{1,0:T(8,128)S(1)} %add.40.first_ref), channel_id=1, source_target_pairs={{0,8},{4,12},{8,0},{12,4},{1,9},{5,13},{9,1},{13,5},{2,10},{6,14},... | collective-permute-start | bytes 786440 | tf_op jit(solution)/shard_map/ppermute | solution.py:165
  21.6 2.8 %collective-permute-done.4.refs_0_ = f32[64,256]{1,0:T(8,128)S(1)} collective-permute-done((f32[64,256]{1,0:T(8,128)S(1)}, f32[64,256]{1,0:T(8,128)S(1)}, u32[]{:S(2)}, u32[]{:S(2)}) %collective-permute-start.4) | collective-permute-done | bytes 65568 | tf_op jit(solution)/shard_map/ppermute | solution.py:165
  25.6 8.0 %shard_map.57.lower_ref = f32[256,256]{1,0:T(8,128)S(1)} custom-call(f32[64,256]{1,0:T(8,128)S(1)} %add.41.own_ref, f32[64,256]{1,0:T(8,128)S(1)} %collective-permute-done.4.refs_0_, f32[64,256]{1,0:T(8,128)S(1)} %collective-permute-done.5.refs_1_, f32[64,256]{1,0:T(8,128)S(1)} %collective-permute-done.6.refs_2_), custom_call_target="tpu_custom_call" | custom-call | flops 1000000000 | bytes 524288 | tf_op jit(solution)/shard_map/pallas_call | solution.py:60
  36.6 1.6 %collective-permute-start.9 = (f32[128,256]{1,0:T(8,128)S(1)}, f32[128,256]{1,0:T(8,128)S(1)}, u32[]{:S(2)}, u32[]{:S(2)}) collective-permute-start(f32[128,256]{1,0:T(8,128)S(1)} %get-tuple-element.71), channel_id=1, source_target_pairs={{0,2},{2,0},{1,3},{3,1},{4,6},{6,4},{5,7},{7,5},{8,10},{10,8},{9,1... | collective-permute-start | bytes 393224 | tf_op jit(solution)/shard_map/ppermute | solution.py:165
  38.2 2.3 %collective-permute-start.12 = (f32[128,256]{1,0:T(8,128)S(1)}, f32[128,256]{1,0:T(8,128)S(1)}, u32[]{:S(2)}, u32[]{:S(2)}) collective-permute-start(f32[128,256]{1,0:T(8,128)S(1)} %get-tuple-element.74), channel_id=1, source_target_pairs={{0,4},{4,0},{8,12},{12,8},{1,5},{5,1},{9,13},{13,9},{2,6},{6,2},{1... | collective-permute-start | bytes 393224 | tf_op jit(solution)/shard_map/ppermute | solution.py:165
  40.5 1.8 %collective-permute-done.9 = f32[128,256]{1,0:T(8,128)S(1)} collective-permute-done((f32[128,256]{1,0:T(8,128)S(1)}, f32[128,256]{1,0:T(8,128)S(1)}, u32[]{:S(2)}, u32[]{:S(2)}) %collective-permute-start.9) | collective-permute-done | bytes 131104 | tf_op jit(solution)/shard_map/ppermute | solution.py:165
  42.3 2.3 %collective-permute-start.10 = (f32[128,256]{1,0:T(8,128)S(1)}, f32[128,256]{1,0:T(8,128)S(1)}, u32[]{:S(2)}, u32[]{:S(2)}) collective-permute-start(f32[128,256]{1,0:T(8,128)S(1)} %add.42), channel_id=1, source_target_pairs={{0,4},{4,0},{8,12},{12,8},{1,5},{5,1},{9,13},{13,9},{2,6},{6,2},{1... | collective-permute-start | bytes 393224 | tf_op jit(solution)/shard_map/ppermute | solution.py:165
  44.6 1.6 %collective-permute-start.13 = (f32[128,256]{1,0:T(8,128)S(1)}, f32[128,256]{1,0:T(8,128)S(1)}, u32[]{:S(2)}, u32[]{:S(2)}) collective-permute-start(f32[128,256]{1,0:T(8,128)S(1)} %add.44), channel_id=1, source_target_pairs={{0,2},{2,0},{1,3},{3,1},{4,6},{6,4},{5,7},{7,5},{8,10},{10,8},{9,1... | collective-permute-start | bytes 393224 | tf_op jit(solution)/shard_map/ppermute | solution.py:165
  47.6 2.1 %collective-permute-done.13 = f32[128,256]{1,0:T(8,128)S(1)} collective-permute-done((f32[128,256]{1,0:T(8,128)S(1)}, f32[128,256]{1,0:T(8,128)S(1)}, u32[]{:S(2)}, u32[]{:S(2)}) %collective-permute-start.13) | collective-permute-done | bytes 131104 | tf_op jit(solution)/shard_map/ppermute | solution.py:165
  49.8 1.6 %collective-permute-start.11 = (f32[128,256]{1,0:T(8,128)S(1)}, f32[128,256]{1,0:T(8,128)S(1)}, u32[]{:S(2)}, u32[]{:S(2)}) collective-permute-start(f32[128,256]{1,0:T(8,128)S(1)} %add.43), channel_id=1, source_target_pairs={{0,2},{2,0},{1,3},{3,1},{4,6},{6,4},{5,7},{7,5},{8,10},{10,8},{9,1... | collective-permute-start | bytes 393224 | tf_op jit(solution)/shard_map/ppermute | solution.py:165
  51.5 1.7 %shard_map.62 = (f32[256,256]{1,0:T(8,128)}, f32[64,256]{1,0:T(8,128)S(1)}, f32[256,256]{1,0:T(8,128)S(1)}) custom-call(f32[256,256]{1,0:T(8,128)S(1)} %pad_maximum_fusion.stack_ref, f32[256,256]{1,0:T(8,128)S(1)} %shard_map.57.lower_ref, f32[512,256]{1,0:T(8,128)S(1)} %get-tuple-element.60.own_ref, f32[512,256]{1,0:T(8,128)S(1)} %collective-permute-done.3.other_ref), custom_call_target="tpu_custom_call" | custom-call | flops 900000000 | bytes 2162688 | tf_op jit(solution)/shard_map/pallas_call | solution.py:60
  59.4 1.8 %collective-permute-start.17 = (f32[64,256]{1,0:T(8,128)S(1)}, f32[64,256]{1,0:T(8,128)S(1)}, u32[]{:S(2)}, u32[]{:S(2)}) collective-permute-start(f32[64,256]{1,0:T(8,128)S(1)} %get-tuple-element.84), channel_id=1, source_target_pairs={{0,8},{4,12},{8,0},{12,4},{1,9},{5,13},{9,1},{13,5},{2,10},{6,14},... | collective-permute-start | bytes 196616 | tf_op jit(solution)/shard_map/ppermute | solution.py:165
  61.7 4.2 %collective-permute-done.17 = f32[64,256]{1,0:T(8,128)S(1)} collective-permute-done((f32[64,256]{1,0:T(8,128)S(1)}, f32[64,256]{1,0:T(8,128)S(1)}, u32[]{:S(2)}, u32[]{:S(2)}) %collective-permute-start.17) | collective-permute-done | bytes 65568 | tf_op jit(solution)/shard_map/ppermute | solution.py:165
  66.1 2.4 %collective-permute-start.22 = (f32[256,256]{1,0:T(8,128)S(1)}, f32[256,256]{1,0:T(8,128)S(1)}, u32[]{:S(2)}, u32[]{:S(2)}) collective-permute-start(f32[256,256]{1,0:T(8,128)S(1)} %shard_map.66.first_ref), channel_id=1, source_target_pairs={{0,8},{4,12},{8,0},{12,4},{1,9},{5,13},{9,1},{13,5},{2,10},{6,14},... | collective-permute-start | bytes 786440 | tf_op jit(solution)/shard_map/ppermute | solution.py:165
  69.7 3.0 %collective-permute-done.18.refs_0_ = f32[64,256]{1,0:T(8,128)S(1)} collective-permute-done((f32[64,256]{1,0:T(8,128)S(1)}, f32[64,256]{1,0:T(8,128)S(1)}, u32[]{:S(2)}, u32[]{:S(2)}) %collective-permute-start.18) | collective-permute-done | bytes 65568 | tf_op jit(solution)/shard_map/ppermute | solution.py:165
  74.0 4.0 %shard_map.67 = (f32[128,128]{1,0:T(8,128)S(1)}, f32[128,128]{1,0:T(8,128)S(1)}, f32[128,128]{1,0:T(8,128)S(1)}) custom-call(f32[64,256]{1,0:T(8,128)S(1)} %add.46.own_ref, f32[64,256]{1,0:T(8,128)S(1)} %collective-permute-done.18.refs_0_, f32[64,256]{1,0:T(8,128)S(1)} %collective-permute-done.19.refs_1_, f32[64,256]{1,0:T(8,128)S(1)} %collective-permute-done.20.refs_2_), custom_call_target="tpu_custom_call" | custom-call | flops 1000000000 | bytes 458752 | tf_op jit(solution)/shard_map/pallas_call | solution.py:60
  78.6 2.3 %collective-permute-done.22.second_ref = f32[256,256]{1,0:T(8,128)S(1)} collective-permute-done((f32[256,256]{1,0:T(8,128)S(1)}, f32[256,256]{1,0:T(8,128)S(1)}, u32[]{:S(2)}, u32[]{:S(2)}) %collective-permute-start.22) | collective-permute-done | bytes 262176 | tf_op jit(solution)/shard_map/ppermute | solution.py:165
  84.4 4.8 %collective-permute-done.24 = f32[128,256]{1,0:T(8,128)S(1)} collective-permute-done((f32[128,256]{1,0:T(8,128)S(1)}, f32[128,256]{1,0:T(8,128)S(1)}, u32[]{:S(2)}, u32[]{:S(2)}) %collective-permute-start.24) | collective-permute-done | bytes 131104 | tf_op jit(solution)/shard_map/ppermute | solution.py:165
  89.4 1.7 %collective-permute-start.27 = (f32[128,256]{1,0:T(8,128)S(1)}, f32[128,256]{1,0:T(8,128)S(1)}, u32[]{:S(2)}, u32[]{:S(2)}) collective-permute-start(f32[128,256]{1,0:T(8,128)S(1)} %add.49), channel_id=1, source_target_pairs={{0,2},{2,0},{1,3},{3,1},{4,6},{6,4},{5,7},{7,5},{8,10},{10,8},{9,1... | collective-permute-start | bytes 393224 | tf_op jit(solution)/shard_map/ppermute | solution.py:165
  91.1 3.9 %shard_map.71.lower_ref = f32[256,256]{1,0:T(8,128)S(1)} custom-call(f32[128,128]{1,0:T(8,128)S(1)} %get-tuple-element.85.tile_ref, f32[128,128]{1,0:T(8,128)S(1)} %get-tuple-element.91.cross_ref, f32[128,128]{1,0:T(8,128)S(1)} %get-tuple-element.92.left_ref), custom_call_target="tpu_custom_call" | custom-call | flops 1000000000 | bytes 458752 | tf_op jit(solution)/shard_map/pallas_call | solution.py:60
  104.3 1.8 %collective-permute-start.32 = (f32[64,256]{1,0:T(8,128)S(1)}, f32[64,256]{1,0:T(8,128)S(1)}, u32[]{:S(2)}, u32[]{:S(2)}) collective-permute-start(f32[64,256]{1,0:T(8,128)S(1)} %get-tuple-element.108), channel_id=1, source_target_pairs={{0,8},{4,12},{8,0},{12,4},{1,9},{5,13},{9,1},{13,5},{2,10},{6,14},... | collective-permute-start | bytes 196616 | tf_op jit(solution)/shard_map/ppermute | solution.py:165
  106.6 4.5 %collective-permute-done.32 = f32[64,256]{1,0:T(8,128)S(1)} collective-permute-done((f32[64,256]{1,0:T(8,128)S(1)}, f32[64,256]{1,0:T(8,128)S(1)}, u32[]{:S(2)}, u32[]{:S(2)}) %collective-permute-start.32) | collective-permute-done | bytes 65568 | tf_op jit(solution)/shard_map/ppermute | solution.py:165
  111.5 1.9 %collective-permute-start.37 = (f32[128,512]{1,0:T(8,128)S(1)}, f32[128,512]{1,0:T(8,128)S(1)}, u32[]{:S(2)}, u32[]{:S(2)}) collective-permute-start(f32[128,512]{1,0:T(8,128)S(1)} %get-tuple-element.112), channel_id=1, source_target_pairs={{0,4},{4,0},{8,12},{12,8},{1,5},{5,1},{9,13},{13,9},{2,6},{6,2},{1... | collective-permute-start | bytes 786440 | tf_op jit(solution)/shard_map/ppermute | solution.py:165
  114.5 3.2 %collective-permute-done.33.refs_0_ = f32[64,256]{1,0:T(8,128)S(1)} collective-permute-done((f32[64,256]{1,0:T(8,128)S(1)}, f32[64,256]{1,0:T(8,128)S(1)}, u32[]{:S(2)}, u32[]{:S(2)}) %collective-permute-start.33) | collective-permute-done | bytes 65568 | tf_op jit(solution)/shard_map/ppermute | solution.py:165
  119.0 8.0 %shard_map.77.refs_6_ = f32[256,256]{1,0:T(8,128)S(1)} custom-call(f32[64,256]{1,0:T(8,128)S(1)} %add.51.own_ref, f32[64,256]{1,0:T(8,128)S(1)} %collective-permute-done.33.refs_0_, f32[64,256]{1,0:T(8,128)S(1)} %collective-permute-done.34.refs_1_, f32[64,256]{1,0:T(8,128)S(1)} %collective-permute-done.35.refs_2_), custom_call_target="tpu_custom_call" | custom-call | flops 1000000000 | bytes 524288 | tf_op jit(solution)/shard_map/pallas_call | solution.py:60
  127.1 4.4 %shard_map.78 = (f32[144,128]{1,0:T(8,128)S(1)}, f32[144,128]{1,0:T(8,128)S(1)}) custom-call(f32[16,4096]{1,0:T(8,128)S(1)} %bitcast.5, f32[256,256]{1,0:T(8,128)S(1)} %get-tuple-element.96.refs_0_, f32[256,256]{1,0:T(8,128)S(1)} %get-tuple-element.99.refs_1_, f32[256,256]{1,0:T(8,128)S(1)} %get-tuple-element.104.refs_2_, ...), custom_call_target="tpu_custom_call" | custom-call | flops 3000000000 | bytes 3294208 | tf_op jit(solution)/shard_map/pallas_call | solution.py:60
  132.2 5.7 %collective-permute-done.38.second_ref = f32[144,128]{1,0:T(8,128)S(1)} collective-permute-done((f32[144,128]{1,0:T(8,128)S(1)}, f32[144,128]{1,0:T(8,128)S(1)}, u32[]{:S(2)}, u32[]{:S(2)}) %collective-permute-start.38) | collective-permute-done | bytes 73760 | tf_op jit(solution)/shard_map/ppermute | solution.py:165
  (102 shorter events, 39.5 us)
Async XLA Ops:
  1.6 5.3 %collective-permute-start = (f32[64,256]{1,0:T(8,128)S(1)}, f32[64,256]{1,0:T(8,128)S(1)}, u32[]{:S(2)}, u32[]{:S(2)}) collective-permute-start(f32[64,256]{1,0:T(8,128)S(1)} %shard_map.55.gram_ref), channel_id=1, source_target_pairs={{0,4},{4,0},{8,12},{12,8},{1,5},{5,1},{9,13},{13,9},{2,6},{6,2},{1... | collective-permute-start | bytes 196616 | tf_op jit(solution)/shard_map/ppermute | solution.py:165
  7.0 8.7 %collective-permute-start.1 = (f32[256,256]{1,0:T(8,128)S(1)}, f32[256,256]{1,0:T(8,128)S(1)}, u32[]{:S(2)}, u32[]{:S(2)}) collective-permute-start(f32[256,256]{1,0:T(8,128)S(1)} %get-tuple-element.64), channel_id=1, source_target_pairs={{0,4},{4,0},{8,12},{12,8},{1,5},{5,1},{9,13},{13,9},{2,6},{6,2},{1... | collective-permute-start | bytes 786440 | tf_op jit(solution)/shard_map/ppermute | solution.py:165
  9.1 5.8 %collective-permute-start.2 = (f32[64,256]{1,0:T(8,128)S(1)}, f32[64,256]{1,0:T(8,128)S(1)}, u32[]{:S(2)}, u32[]{:S(2)}) collective-permute-start(f32[64,256]{1,0:T(8,128)S(1)} %add.39), channel_id=1, source_target_pairs={{0,8},{4,12},{8,0},{12,4},{1,9},{5,13},{9,1},{13,5},{2,10},{6,14},... | collective-permute-start | bytes 196616 | tf_op jit(solution)/shard_map/ppermute | solution.py:165
  15.7 18.3 %collective-permute-start.3 = (f32[512,256]{1,0:T(8,128)S(1)}, f32[512,256]{1,0:T(8,128)S(1)}, u32[]{:S(2)}, u32[]{:S(2)}) collective-permute-start(f32[512,256]{1,0:T(8,128)S(1)} %get-tuple-element.66), channel_id=1, source_target_pairs={{0,4},{4,0},{8,12},{12,8},{1,5},{5,1},{9,13},{13,9},{2,6},{6,2},{1... | collective-permute-start | bytes 1572872 | tf_op jit(solution)/shard_map/ppermute | solution.py:165
  18.5 15.4 %collective-permute-start.7 = (f32[256,256]{1,0:T(8,128)S(1)}, f32[256,256]{1,0:T(8,128)S(1)}, u32[]{:S(2)}, u32[]{:S(2)}) collective-permute-start(f32[256,256]{1,0:T(8,128)S(1)} %add.40.first_ref), channel_id=1, source_target_pairs={{0,8},{4,12},{8,0},{12,4},{1,9},{5,13},{9,1},{13,5},{2,10},{6,14},... | collective-permute-start | bytes 786440 | tf_op jit(solution)/shard_map/ppermute | solution.py:165
  20.1 4.3 %collective-permute-start.4 = (f32[64,256]{1,0:T(8,128)S(1)}, f32[64,256]{1,0:T(8,128)S(1)}, u32[]{:S(2)}, u32[]{:S(2)}) collective-permute-start(f32[64,256]{1,0:T(8,128)S(1)} %add.41.own_ref), channel_id=1, source_target_pairs={{0,2},{2,0},{1,3},{3,1},{4,6},{6,4},{5,7},{7,5},{8,10},{10,8},{9,1... | collective-permute-start | bytes 196616 | tf_op jit(solution)/shard_map/ppermute | solution.py:165
  21.6 2.8 %collective-permute-start.5 = (f32[64,256]{1,0:T(8,128)S(1)}, f32[64,256]{1,0:T(8,128)S(1)}, u32[]{:S(2)}, u32[]{:S(2)}) collective-permute-start(f32[64,256]{1,0:T(8,128)S(1)} %add.41.own_ref), channel_id=1, source_target_pairs={{0,1},{1,0},{2,3},{3,2},{4,5},{5,4},{6,7},{7,6},{8,9},{9,8},{10,11... | collective-permute-start | bytes 196616 | tf_op jit(solution)/shard_map/ppermute | solution.py:165
  36.6 5.6 %collective-permute-start.9 = (f32[128,256]{1,0:T(8,128)S(1)}, f32[128,256]{1,0:T(8,128)S(1)}, u32[]{:S(2)}, u32[]{:S(2)}) collective-permute-start(f32[128,256]{1,0:T(8,128)S(1)} %get-tuple-element.71), channel_id=1, source_target_pairs={{0,2},{2,0},{1,3},{3,1},{4,6},{6,4},{5,7},{7,5},{8,10},{10,8},{9,1... | collective-permute-start | bytes 393224 | tf_op jit(solution)/shard_map/ppermute | solution.py:165
  38.2 6.4 %collective-permute-start.12 = (f32[128,256]{1,0:T(8,128)S(1)}, f32[128,256]{1,0:T(8,128)S(1)}, u32[]{:S(2)}, u32[]{:S(2)}) collective-permute-start(f32[128,256]{1,0:T(8,128)S(1)} %get-tuple-element.74), channel_id=1, source_target_pairs={{0,4},{4,0},{8,12},{12,8},{1,5},{5,1},{9,13},{13,9},{2,6},{6,2},{1... | collective-permute-start | bytes 393224 | tf_op jit(solution)/shard_map/ppermute | solution.py:165
  42.3 5.3 %collective-permute-start.10 = (f32[128,256]{1,0:T(8,128)S(1)}, f32[128,256]{1,0:T(8,128)S(1)}, u32[]{:S(2)}, u32[]{:S(2)}) collective-permute-start(f32[128,256]{1,0:T(8,128)S(1)} %add.42), channel_id=1, source_target_pairs={{0,4},{4,0},{8,12},{12,8},{1,5},{5,1},{9,13},{13,9},{2,6},{6,2},{1... | collective-permute-start | bytes 393224 | tf_op jit(solution)/shard_map/ppermute | solution.py:165
  44.6 5.0 %collective-permute-start.13 = (f32[128,256]{1,0:T(8,128)S(1)}, f32[128,256]{1,0:T(8,128)S(1)}, u32[]{:S(2)}, u32[]{:S(2)}) collective-permute-start(f32[128,256]{1,0:T(8,128)S(1)} %add.44), channel_id=1, source_target_pairs={{0,2},{2,0},{1,3},{3,1},{4,6},{6,4},{5,7},{7,5},{8,10},{10,8},{9,1... | collective-permute-start | bytes 393224 | tf_op jit(solution)/shard_map/ppermute | solution.py:165
  49.7 3.5 %collective-permute-start.14 = (f32[256,256]{1,0:T(8,128)S(1)}, f32[256,256]{1,0:T(8,128)S(1)}, u32[]{:S(2)}, u32[]{:S(2)}) collective-permute-start(f32[256,256]{1,0:T(8,128)S(1)} %pad_maximum_fusion.stack_ref), channel_id=1, source_target_pairs={{0,1},{1,0},{2,3},{3,2},{4,5},{5,4},{6,7},{7,6},{8,9},{9,8},{10,11... | collective-permute-start | bytes 786440 | tf_op jit(solution)/shard_map/ppermute | solution.py:165
  49.8 5.9 %collective-permute-start.11 = (f32[128,256]{1,0:T(8,128)S(1)}, f32[128,256]{1,0:T(8,128)S(1)}, u32[]{:S(2)}, u32[]{:S(2)}) collective-permute-start(f32[128,256]{1,0:T(8,128)S(1)} %add.43), channel_id=1, source_target_pairs={{0,2},{2,0},{1,3},{3,1},{4,6},{6,4},{5,7},{7,5},{8,10},{10,8},{9,1... | collective-permute-start | bytes 393224 | tf_op jit(solution)/shard_map/ppermute | solution.py:165
  51.3 5.6 %collective-permute-start.15 = (f32[128,256]{1,0:T(8,128)S(1)}, f32[128,256]{1,0:T(8,128)S(1)}, u32[]{:S(2)}, u32[]{:S(2)}) collective-permute-start(f32[128,256]{1,0:T(8,128)S(1)} %add.45), channel_id=1, source_target_pairs={{0,4},{4,0},{8,12},{12,8},{1,5},{5,1},{9,13},{13,9},{2,6},{6,2},{1... | collective-permute-start | bytes 393224 | tf_op jit(solution)/shard_map/ppermute | solution.py:165
  59.4 6.5 %collective-permute-start.17 = (f32[64,256]{1,0:T(8,128)S(1)}, f32[64,256]{1,0:T(8,128)S(1)}, u32[]{:S(2)}, u32[]{:S(2)}) collective-permute-start(f32[64,256]{1,0:T(8,128)S(1)} %get-tuple-element.84), channel_id=1, source_target_pairs={{0,8},{4,12},{8,0},{12,4},{1,9},{5,13},{9,1},{13,5},{2,10},{6,14},... | collective-permute-start | bytes 196616 | tf_op jit(solution)/shard_map/ppermute | solution.py:165
  66.0 12.7 %collective-permute-start.21 = (f32[128,512]{1,0:T(8,128)S(1)}, f32[128,512]{1,0:T(8,128)S(1)}, u32[]{:S(2)}, u32[]{:S(2)}) collective-permute-start(f32[128,512]{1,0:T(8,128)S(1)} %get-tuple-element.87), channel_id=1, source_target_pairs={{0,4},{4,0},{8,12},{12,8},{1,5},{5,1},{9,13},{13,9},{2,6},{6,2},{1... | collective-permute-start | bytes 786440 | tf_op jit(solution)/shard_map/ppermute | solution.py:165
  66.1 14.9 %collective-permute-start.22 = (f32[256,256]{1,0:T(8,128)S(1)}, f32[256,256]{1,0:T(8,128)S(1)}, u32[]{:S(2)}, u32[]{:S(2)}) collective-permute-start(f32[256,256]{1,0:T(8,128)S(1)} %shard_map.66.first_ref), channel_id=1, source_target_pairs={{0,8},{4,12},{8,0},{12,4},{1,9},{5,13},{9,1},{13,5},{2,10},{6,14},... | collective-permute-start | bytes 786440 | tf_op jit(solution)/shard_map/ppermute | solution.py:165
  68.4 4.3 %collective-permute-start.18 = (f32[64,256]{1,0:T(8,128)S(1)}, f32[64,256]{1,0:T(8,128)S(1)}, u32[]{:S(2)}, u32[]{:S(2)}) collective-permute-start(f32[64,256]{1,0:T(8,128)S(1)} %add.46.own_ref), channel_id=1, source_target_pairs={{0,2},{2,0},{1,3},{3,1},{4,6},{6,4},{5,7},{7,5},{8,10},{10,8},{9,1... | collective-permute-start | bytes 196616 | tf_op jit(solution)/shard_map/ppermute | solution.py:165
  69.7 3.0 %collective-permute-start.19 = (f32[64,256]{1,0:T(8,128)S(1)}, f32[64,256]{1,0:T(8,128)S(1)}, u32[]{:S(2)}, u32[]{:S(2)}) collective-permute-start(f32[64,256]{1,0:T(8,128)S(1)} %add.46.own_ref), channel_id=1, source_target_pairs={{0,1},{1,0},{2,3},{3,2},{4,5},{5,4},{6,7},{7,6},{8,9},{9,8},{10,11... | collective-permute-start | bytes 196616 | tf_op jit(solution)/shard_map/ppermute | solution.py:165
  83.6 5.6 %collective-permute-start.24 = (f32[128,256]{1,0:T(8,128)S(1)}, f32[128,256]{1,0:T(8,128)S(1)}, u32[]{:S(2)}, u32[]{:S(2)}) collective-permute-start(f32[128,256]{1,0:T(8,128)S(1)} %get-tuple-element.90), channel_id=1, source_target_pairs={{0,2},{2,0},{1,3},{3,1},{4,6},{6,4},{5,7},{7,5},{8,10},{10,8},{9,1... | collective-permute-start | bytes 393224 | tf_op jit(solution)/shard_map/ppermute | solution.py:165
  84.1 5.3 %collective-permute-start.26 = (f32[128,256]{1,0:T(8,128)S(1)}, f32[128,256]{1,0:T(8,128)S(1)}, u32[]{:S(2)}, u32[]{:S(2)}) collective-permute-start(f32[128,256]{1,0:T(8,128)S(1)} %get-tuple-element.95), channel_id=1, source_target_pairs={{0,4},{4,0},{8,12},{12,8},{1,5},{5,1},{9,13},{13,9},{2,6},{6,2},{1... | collective-permute-start | bytes 393224 | tf_op jit(solution)/shard_map/ppermute | solution.py:165
  89.3 5.7 %collective-permute-start.25 = (f32[128,256]{1,0:T(8,128)S(1)}, f32[128,256]{1,0:T(8,128)S(1)}, u32[]{:S(2)}, u32[]{:S(2)}) collective-permute-start(f32[128,256]{1,0:T(8,128)S(1)} %add.47), channel_id=1, source_target_pairs={{0,4},{4,0},{8,12},{12,8},{1,5},{5,1},{9,13},{13,9},{2,6},{6,2},{1... | collective-permute-start | bytes 393224 | tf_op jit(solution)/shard_map/ppermute | solution.py:165
  89.4 5.6 %collective-permute-start.27 = (f32[128,256]{1,0:T(8,128)S(1)}, f32[128,256]{1,0:T(8,128)S(1)}, u32[]{:S(2)}, u32[]{:S(2)}) collective-permute-start(f32[128,256]{1,0:T(8,128)S(1)} %add.49), channel_id=1, source_target_pairs={{0,2},{2,0},{1,3},{3,1},{4,6},{6,4},{5,7},{7,5},{8,10},{10,8},{9,1... | collective-permute-start | bytes 393224 | tf_op jit(solution)/shard_map/ppermute | solution.py:165
  95.0 3.9 %collective-permute-start.28 = (f32[256,256]{1,0:T(8,128)S(1)}, f32[256,256]{1,0:T(8,128)S(1)}, u32[]{:S(2)}, u32[]{:S(2)}) collective-permute-start(f32[256,256]{1,0:T(8,128)S(1)} %pad_maximum_fusion.1.stack_ref), channel_id=1, source_target_pairs={{0,1},{1,0},{2,3},{3,2},{4,5},{5,4},{6,7},{7,6},{8,9},{9,8},{10,11... | collective-permute-start | bytes 786440 | tf_op jit(solution)/shard_map/ppermute | solution.py:165
  95.1 5.9 %collective-permute-start.29 = (f32[128,256]{1,0:T(8,128)S(1)}, f32[128,256]{1,0:T(8,128)S(1)}, u32[]{:S(2)}, u32[]{:S(2)}) collective-permute-start(f32[128,256]{1,0:T(8,128)S(1)} %add.48), channel_id=1, source_target_pairs={{0,2},{2,0},{1,3},{3,1},{4,6},{6,4},{5,7},{7,5},{8,10},{10,8},{9,1... | collective-permute-start | bytes 393224 | tf_op jit(solution)/shard_map/ppermute | solution.py:165
  96.2 5.6 %collective-permute-start.30 = (f32[128,256]{1,0:T(8,128)S(1)}, f32[128,256]{1,0:T(8,128)S(1)}, u32[]{:S(2)}, u32[]{:S(2)}) collective-permute-start(f32[128,256]{1,0:T(8,128)S(1)} %add.50), channel_id=1, source_target_pairs={{0,4},{4,0},{8,12},{12,8},{1,5},{5,1},{9,13},{13,9},{2,6},{6,2},{1... | collective-permute-start | bytes 393224 | tf_op jit(solution)/shard_map/ppermute | solution.py:165
  104.3 6.7 %collective-permute-start.32 = (f32[64,256]{1,0:T(8,128)S(1)}, f32[64,256]{1,0:T(8,128)S(1)}, u32[]{:S(2)}, u32[]{:S(2)}) collective-permute-start(f32[64,256]{1,0:T(8,128)S(1)} %get-tuple-element.108), channel_id=1, source_target_pairs={{0,8},{4,12},{8,0},{12,4},{1,9},{5,13},{9,1},{13,5},{2,10},{6,14},... | collective-permute-start | bytes 196616 | tf_op jit(solution)/shard_map/ppermute | solution.py:165
  111.1 16.0 %collective-permute-start.36 = (f32[256,256]{1,0:T(8,128)S(1)}, f32[256,256]{1,0:T(8,128)S(1)}, u32[]{:S(2)}, u32[]{:S(2)}) collective-permute-start(f32[256,256]{1,0:T(8,128)S(1)} %shard_map.76.refs_4_), channel_id=1, source_target_pairs={{0,8},{4,12},{8,0},{12,4},{1,9},{5,13},{9,1},{13,5},{2,10},{6,14},... | collective-permute-start | bytes 786440 | tf_op jit(solution)/shard_map/ppermute | solution.py:165
  111.5 15.5 %collective-permute-start.37 = (f32[128,512]{1,0:T(8,128)S(1)}, f32[128,512]{1,0:T(8,128)S(1)}, u32[]{:S(2)}, u32[]{:S(2)}) collective-permute-start(f32[128,512]{1,0:T(8,128)S(1)} %get-tuple-element.112), channel_id=1, source_target_pairs={{0,4},{4,0},{8,12},{12,8},{1,5},{5,1},{9,13},{13,9},{2,6},{6,2},{1... | collective-permute-start | bytes 786440 | tf_op jit(solution)/shard_map/ppermute | solution.py:165
  113.5 4.3 %collective-permute-start.33 = (f32[64,256]{1,0:T(8,128)S(1)}, f32[64,256]{1,0:T(8,128)S(1)}, u32[]{:S(2)}, u32[]{:S(2)}) collective-permute-start(f32[64,256]{1,0:T(8,128)S(1)} %add.51.own_ref), channel_id=1, source_target_pairs={{0,2},{2,0},{1,3},{3,1},{4,6},{6,4},{5,7},{7,5},{8,10},{10,8},{9,1... | collective-permute-start | bytes 196616 | tf_op jit(solution)/shard_map/ppermute | solution.py:165
  114.5 3.3 %collective-permute-start.34 = (f32[64,256]{1,0:T(8,128)S(1)}, f32[64,256]{1,0:T(8,128)S(1)}, u32[]{:S(2)}, u32[]{:S(2)}) collective-permute-start(f32[64,256]{1,0:T(8,128)S(1)} %add.51.own_ref), channel_id=1, source_target_pairs={{0,1},{1,0},{2,3},{3,2},{4,5},{5,4},{6,7},{7,6},{8,9},{9,8},{10,11... | collective-permute-start | bytes 196616 | tf_op jit(solution)/shard_map/ppermute | solution.py:165
  131.5 6.4 %collective-permute-start.38 = (f32[144,128]{1,0:T(8,128)S(1)}, f32[144,128]{1,0:T(8,128)S(1)}, u32[]{:S(2)}, u32[]{:S(2)}) collective-permute-start(f32[144,128]{1,0:T(8,128)S(1)} %get-tuple-element.114), channel_id=1, source_target_pairs={{0,8},{4,12},{8,0},{12,4},{1,9},{5,13},{9,1},{13,5},{2,10},{6,14},... | collective-permute-start | bytes 221192 | tf_op jit(solution)/shard_map/ppermute | solution.py:165
  (12 other events, 50.6 us)

commit v5 on v4

--- a/solution.py
+++ b/solution.py
@@ -313,7 +313,8 @@
 
 def mix_kernel(sent, own_ref, other_ref, first_ref, second_ref, out_ref):
     mine, _, _, head = pair_sides()
-    coef = first_ref[...] + second_ref[...]
+    held = pl.ds(0, own_ref.shape[1])
+    coef = first_ref[held, :] + second_ref[held, :]
     half = own_ref.shape[0] // 2
     rows = lanes(head ^ int(sent), half)
     for keys_ref, piece in ((own_ref, mine), (other_ref, 1 - mine)):
@@ -337,11 +338,11 @@
     b_send[...] = rows(1 - mine, quarter, quarter)
 
 
-def summed_streams(keep, send, lower):
+def summed_streams(keep, send, ready, lower):
     got = swap(send, "head", 1)
     quarter = vmem(keep.shape[0] // 4, keep.shape[1])
     a_keep, a_send, b_keep, b_send = call(streams_kernel, [quarter] * 4, keep, got)
-    a = a_keep + swap(a_send, "lay", 1)
+    a = after(a_keep + swap(a_send, "lay", 1), ready)
     b = b_keep + swap(b_send, "tok", 1)
     a, b = a + swap(a, "tok", 1), b + swap(b, "lay", 1)
     a = after(a, lower)
@@ -386,6 +387,14 @@
 
 def project_kernel(own_ref, other_ref, block_ref, part_ref, proj_ref, rows_ref):
     proj_ref[...] = part_ref[...] + project_stack(1, 1, own_ref, other_ref, block_ref, rows_ref)
+
+
+def project_and_pack_kernel(own_ref, other_ref, block_ref, part_ref, gram_ref, proj_ref, rows_ref):
+    count = part_ref.shape[0]
+    proj_ref[pl.ds(0, count), :] = part_ref[...] + project_stack(
+        1, 1, own_ref, other_ref, block_ref, rows_ref
+    )
+    proj_ref[pl.ds(count, gram_ref.shape[0]), :] = gram_ref[...]
 
 
 def attend_kernel(
@@ -502,23 +511,22 @@
     values_other = []
     lower = None
     for step in range(ITERS + 1):
-        gram = gram + swap(gram, "tok", 2)
         last = step == ITERS
         if step != 1:
+            gram = gram + swap(gram, "tok", 2)
             proj = after(proj, gram)
-            if step == 0:
-                keys_other = swap(after(keys_send, proj), "tok", 1)
+        if step == 0:
+            keys_other = swap(after(keys_send, proj), "tok", 1)
         first, second = proj, swap(proj, "tok", 2)
-        if step > 0 and len(values_other) < 2:
-            values_other.append(swap(after(values_send[len(values_other)], proj, gram), "tok", 1))
-        parts = gathered(gram)
-        if step == 0 or last:
-            lower = inverse_factor(*parts)
+        if step > 0:
+            values_other.append(swap(after(values_send[step - 1], proj), "tok", 1))
+        if step == 1:
+            halves = inverse_factor_low(*gathered(first[half:] + second[half:]))
+            ready, lower = halves[0], inverse_factor_high(*halves)
+            first = after(first, *values_other)
+        else:
+            ready = lower = inverse_factor(*gathered(gram))
             first = after(first, lower, values_own)
-        else:
-            halves = inverse_factor_low(*parts)
-            first = after(first, halves[0], *values_other)
-            lower = inverse_factor_high(*halves)
         if last:
             break
         mix = (keys_own, keys_other, first, second)
@@ -526,7 +534,7 @@
             call(functools.partial(mix_kernel, sent), vmem(tokens, rank), *mix, flops=400_000_000)
             for sent in (True, False)
         )
-        here, there = summed_streams(z_keep, z_send, lower)
+        here, there = summed_streams(z_keep, z_send, ready, lower)
         block, parts = vmem(tokens // 2, rank), ()
         blocks = []
         stacks = [here, swap(here, "head", 1)]
@@ -556,13 +564,15 @@
             flops=600_000_000,
         )
         blocks.append(done)
+        packed = step == 0
         proj = call(
-            project_kernel,
-            vmem(half, rank),
+            project_and_pack_kernel if packed else project_kernel,
+            vmem(half + share if packed else half, rank),
             keys_own,
             keys_other,
             done,
             parts[1],
+            *((gram,) if packed else ()),
             scratch=[(tokens // 2, half)],
             flops=400_000_000,
         )

time: 139 us -> 140 us (level)
  waiting for transfers between devices: 51.5 us -> 55.1 us
  starting transfers between devices: 40.1 us -> 37.8 us
    ppermute x39 -> x38, waiting for transfers between devices: 51.5 us -> 55.1 us  [swap(): return lax.ppermute(x, axis, pairs)]
    ppermute x39 -> x38, starting transfers between devices: 40.1 us -> 37.8 us  [swap(): return lax.ppermute(x, axis, pairs)]
  transfers between devices with their start and end apart: 39 -> 38, of which waited for: 26 -> 21; matrix products, arithmetic and copies ran while one was open for 0% -> 0% of each run, Pallas kernels for 26% -> 26%
where the time goes in v5:
time: 140 us
  waiting for transfers between devices  55.1 us (39%)
  Pallas kernels  45.1 us (32%)
  starting transfers between devices  37.8 us (27%)
    ppermute x38, waiting for transfers between devices, swap(): return lax.ppermute(x, axis, pairs)  55.1 us
    pallas_call x25, Pallas kernels, call(): pl.pallas_call(kernel, out_shape=out_shape, in_specs=[spec] * len(args),...  45.1 us
    ppermute x38, starting transfers between devices, swap(): return lax.ppermute(x, axis, pairs)  37.8 us
  transfers between devices with their start and end apart: 38, of which 21 were waited for; matrix products, arithmetic and copies ran while one was open for 0% of the time, Pallas kernels for 26%

profile of v5, /device:TPU:0, one launch (start us, length us, event | category | flops | bytes accessed | tf_op | source)
XLA Modules:
  0.0 140.0 jit_solution(15404593988585350148)
XLA Ops:
  1.6 3.1 %collective-permute-start = (f32[64,256]{1,0:T(8,128)S(1)}, f32[64,256]{1,0:T(8,128)S(1)}, u32[]{:S(2)}, u32[]{:S(2)}) collective-permute-start(f32[64,256]{1,0:T(8,128)S(1)} %shard_map.55.gram_ref), channel_id=1, source_target_pairs={{0,4},{4,0},{8,12},{12,8},{1,5},{5,1},{9,13},{13,9},{2,6},{6,2},{1... | collective-permute-start | bytes 196616 | tf_op jit(solution)/shard_map/ppermute | solution.py:165
  7.0 2.1 %collective-permute-start.1 = (f32[256,256]{1,0:T(8,128)S(1)}, f32[256,256]{1,0:T(8,128)S(1)}, u32[]{:S(2)}, u32[]{:S(2)}) collective-permute-start(f32[256,256]{1,0:T(8,128)S(1)} %get-tuple-element.66), channel_id=1, source_target_pairs={{0,4},{4,0},{8,12},{12,8},{1,5},{5,1},{9,13},{13,9},{2,6},{6,2},{1... | collective-permute-start | bytes 786440 | tf_op jit(solution)/shard_map/ppermute | solution.py:165
  9.1 2.6 %collective-permute-start.2 = (f32[64,256]{1,0:T(8,128)S(1)}, f32[64,256]{1,0:T(8,128)S(1)}, u32[]{:S(2)}, u32[]{:S(2)}) collective-permute-start(f32[64,256]{1,0:T(8,128)S(1)} %add.39), channel_id=1, source_target_pairs={{0,8},{4,12},{8,0},{12,4},{1,9},{5,13},{9,1},{13,5},{2,10},{6,14},... | collective-permute-start | bytes 196616 | tf_op jit(solution)/shard_map/ppermute | solution.py:165
  11.6 3.2 %collective-permute-done.2 = f32[64,256]{1,0:T(8,128)S(1)} collective-permute-done((f32[64,256]{1,0:T(8,128)S(1)}, f32[64,256]{1,0:T(8,128)S(1)}, u32[]{:S(2)}, u32[]{:S(2)}) %collective-permute-start.2) | collective-permute-done | bytes 65568 | tf_op jit(solution)/shard_map/ppermute | solution.py:165
  15.7 2.8 %collective-permute-start.3 = (f32[512,256]{1,0:T(8,128)S(1)}, f32[512,256]{1,0:T(8,128)S(1)}, u32[]{:S(2)}, u32[]{:S(2)}) collective-permute-start(f32[512,256]{1,0:T(8,128)S(1)} %get-tuple-element.68), channel_id=1, source_target_pairs={{0,4},{4,0},{8,12},{12,8},{1,5},{5,1},{9,13},{13,9},{2,6},{6,2},{1... | collective-permute-start | bytes 1572872 | tf_op jit(solution)/shard_map/ppermute | solution.py:165
  18.5 1.5 %collective-permute-start.7 = (f32[256,256]{1,0:T(8,128)S(1)}, f32[256,256]{1,0:T(8,128)S(1)}, u32[]{:S(2)}, u32[]{:S(2)}) collective-permute-start(f32[256,256]{1,0:T(8,128)S(1)} %add.40.first_ref), channel_id=1, source_target_pairs={{0,8},{4,12},{8,0},{12,4},{1,9},{5,13},{9,1},{13,5},{2,10},{6,14},... | collective-permute-start | bytes 786440 | tf_op jit(solution)/shard_map/ppermute | solution.py:165
  20.1 1.5 %collective-permute-start.4 = (f32[64,256]{1,0:T(8,128)S(1)}, f32[64,256]{1,0:T(8,128)S(1)}, u32[]{:S(2)}, u32[]{:S(2)}) collective-permute-start(f32[64,256]{1,0:T(8,128)S(1)} %add.41.own_ref), channel_id=1, source_target_pairs={{0,2},{2,0},{1,3},{3,1},{4,6},{6,4},{5,7},{7,5},{8,10},{10,8},{9,1... | collective-permute-start | bytes 196616 | tf_op jit(solution)/shard_map/ppermute | solution.py:165
  21.6 2.8 %collective-permute-done.4.refs_0_ = f32[64,256]{1,0:T(8,128)S(1)} collective-permute-done((f32[64,256]{1,0:T(8,128)S(1)}, f32[64,256]{1,0:T(8,128)S(1)}, u32[]{:S(2)}, u32[]{:S(2)}) %collective-permute-start.4) | collective-permute-done | bytes 65568 | tf_op jit(solution)/shard_map/ppermute | solution.py:165
  25.6 8.0 %shard_map.57.lower_ref = f32[256,256]{1,0:T(8,128)S(1)} custom-call(f32[64,256]{1,0:T(8,128)S(1)} %add.41.own_ref, f32[64,256]{1,0:T(8,128)S(1)} %collective-permute-done.4.refs_0_, f32[64,256]{1,0:T(8,128)S(1)} %collective-permute-done.5.refs_1_, f32[64,256]{1,0:T(8,128)S(1)} %collective-permute-done.6.refs_2_), custom_call_target="tpu_custom_call" | custom-call | flops 1000000000 | bytes 524288 | tf_op jit(solution)/shard_map/pallas_call | solution.py:60
  36.6 1.6 %collective-permute-start.9 = (f32[128,256]{1,0:T(8,128)S(1)}, f32[128,256]{1,0:T(8,128)S(1)}, u32[]{:S(2)}, u32[]{:S(2)}) collective-permute-start(f32[128,256]{1,0:T(8,128)S(1)} %get-tuple-element.73), channel_id=1, source_target_pairs={{0,2},{2,0},{1,3},{3,1},{4,6},{6,4},{5,7},{7,5},{8,10},{10,8},{9,1... | collective-permute-start | bytes 393224 | tf_op jit(solution)/shard_map/ppermute | solution.py:165
  38.2 2.3 %collective-permute-start.12 = (f32[128,256]{1,0:T(8,128)S(1)}, f32[128,256]{1,0:T(8,128)S(1)}, u32[]{:S(2)}, u32[]{:S(2)}) collective-permute-start(f32[128,256]{1,0:T(8,128)S(1)} %get-tuple-element.77), channel_id=1, source_target_pairs={{0,4},{4,0},{8,12},{12,8},{1,5},{5,1},{9,13},{13,9},{2,6},{6,2},{1... | collective-permute-start | bytes 393224 | tf_op jit(solution)/shard_map/ppermute | solution.py:165
  40.5 1.8 %collective-permute-done.9 = f32[128,256]{1,0:T(8,128)S(1)} collective-permute-done((f32[128,256]{1,0:T(8,128)S(1)}, f32[128,256]{1,0:T(8,128)S(1)}, u32[]{:S(2)}, u32[]{:S(2)}) %collective-permute-start.9) | collective-permute-done | bytes 131104 | tf_op jit(solution)/shard_map/ppermute | solution.py:165
  42.3 2.3 %collective-permute-start.10 = (f32[128,256]{1,0:T(8,128)S(1)}, f32[128,256]{1,0:T(8,128)S(1)}, u32[]{:S(2)}, u32[]{:S(2)}) collective-permute-start(f32[128,256]{1,0:T(8,128)S(1)} %add.42), channel_id=1, source_target_pairs={{0,4},{4,0},{8,12},{12,8},{1,5},{5,1},{9,13},{13,9},{2,6},{6,2},{1... | collective-permute-start | bytes 393224 | tf_op jit(solution)/shard_map/ppermute | solution.py:165
  44.6 1.6 %collective-permute-start.13 = (f32[128,256]{1,0:T(8,128)S(1)}, f32[128,256]{1,0:T(8,128)S(1)}, u32[]{:S(2)}, u32[]{:S(2)}) collective-permute-start(f32[128,256]{1,0:T(8,128)S(1)} %add.44), channel_id=1, source_target_pairs={{0,2},{2,0},{1,3},{3,1},{4,6},{6,4},{5,7},{7,5},{8,10},{10,8},{9,1... | collective-permute-start | bytes 393224 | tf_op jit(solution)/shard_map/ppermute | solution.py:165
  47.6 2.1 %collective-permute-done.13 = f32[128,256]{1,0:T(8,128)S(1)} collective-permute-done((f32[128,256]{1,0:T(8,128)S(1)}, f32[128,256]{1,0:T(8,128)S(1)}, u32[]{:S(2)}, u32[]{:S(2)}) %collective-permute-start.13) | collective-permute-done | bytes 131104 | tf_op jit(solution)/shard_map/ppermute | solution.py:165
  49.8 1.6 %collective-permute-start.11 = (f32[128,256]{1,0:T(8,128)S(1)}, f32[128,256]{1,0:T(8,128)S(1)}, u32[]{:S(2)}, u32[]{:S(2)}) collective-permute-start(f32[128,256]{1,0:T(8,128)S(1)} %add.43), channel_id=1, source_target_pairs={{0,2},{2,0},{1,3},{3,1},{4,6},{6,4},{5,7},{7,5},{8,10},{10,8},{9,1... | collective-permute-start | bytes 393224 | tf_op jit(solution)/shard_map/ppermute | solution.py:165
  51.5 1.7 %shard_map.62 = (f32[256,256]{1,0:T(8,128)}, f32[64,256]{1,0:T(8,128)S(1)}, f32[256,256]{1,0:T(8,128)S(1)}) custom-call(f32[256,256]{1,0:T(8,128)S(1)} %pad_maximum_fusion.stack_ref, f32[256,256]{1,0:T(8,128)S(1)} %shard_map.57.lower_ref, f32[512,256]{1,0:T(8,128)S(1)} %get-tuple-element.62.own_ref, f32[512,256]{1,0:T(8,128)S(1)} %collective-permute-done.3.other_ref), custom_call_target="tpu_custom_call" | custom-call | flops 900000000 | bytes 2162688 | tf_op jit(solution)/shard_map/pallas_call | solution.py:60
  54.7 2.2 %collective-permute-done.15 = f32[128,256]{1,0:T(8,128)S(1)} collective-permute-done((f32[128,256]{1,0:T(8,128)S(1)}, f32[128,256]{1,0:T(8,128)S(1)}, u32[]{:S(2)}, u32[]{:S(2)}) %collective-permute-start.15) | collective-permute-done | bytes 131104 | tf_op jit(solution)/shard_map/ppermute | solution.py:165
  59.9 1.8 %collective-permute-start.18 = (f32[320,256]{1,0:T(8,128)S(1)}, f32[320,256]{1,0:T(8,128)S(1)}, u32[]{:S(2)}, u32[]{:S(2)}) collective-permute-start(f32[320,256]{1,0:T(8,128)S(1)} %shard_map.66.first_ref), channel_id=1, source_target_pairs={{0,8},{4,12},{8,0},{12,4},{1,9},{5,13},{9,1},{13,5},{2,10},{6,14},... | collective-permute-start | bytes 983048 | tf_op jit(solution)/shard_map/ppermute | solution.py:165
  62.1 12.8 %collective-permute-done.17.refs_8_ = f32[128,512]{1,0:T(8,128)S(1)} collective-permute-done((f32[128,512]{1,0:T(8,128)S(1)}, f32[128,512]{1,0:T(8,128)S(1)}, u32[]{:S(2)}, u32[]{:S(2)}) %collective-permute-start.17) | collective-permute-done | bytes 262176 | tf_op jit(solution)/shard_map/ppermute | solution.py:165
  75.0 2.7 %collective-permute-done.18.second_ref = f32[320,256]{1,0:T(8,128)S(1)} collective-permute-done((f32[320,256]{1,0:T(8,128)S(1)}, f32[320,256]{1,0:T(8,128)S(1)}, u32[]{:S(2)}, u32[]{:S(2)}) %collective-permute-start.18) | collective-permute-done | bytes 327712 | tf_op jit(solution)/shard_map/ppermute | solution.py:165
  79.5 3.5 %collective-permute-done.21.refs_0_ = f32[64,256]{1,0:T(8,128)S(1)} collective-permute-done((f32[64,256]{1,0:T(8,128)S(1)}, f32[64,256]{1,0:T(8,128)S(1)}, u32[]{:S(2)}, u32[]{:S(2)}) %collective-permute-start.21) | collective-permute-done | bytes 65568 | tf_op jit(solution)/shard_map/ppermute | solution.py:165
  84.6 4.0 %shard_map.70 = (f32[128,128]{1,0:T(8,128)S(1)}, f32[128,128]{1,0:T(8,128)S(1)}, f32[128,128]{1,0:T(8,128)S(1)}) custom-call(f32[64,256]{1,0:T(8,128)S(1)} %slice_add_fusion.own_ref, f32[64,256]{1,0:T(8,128)S(1)} %collective-permute-done.21.refs_0_, f32[64,256]{1,0:T(8,128)S(1)} %collective-permute-done.22.refs_1_, f32[64,256]{1,0:T(8,128)S(1)} %collective-permute-done.23.refs_2_), custom_call_target="tpu_custom_call" | custom-call | flops 1000000000 | bytes 458752 | tf_op jit(solution)/shard_map/pallas_call | solution.py:60
  92.1 3.9 %shard_map.71.lower_ref = f32[256,256]{1,0:T(8,128)S(1)} custom-call(f32[128,128]{1,0:T(8,128)S(1)} %get-tuple-element.93.tile_ref, f32[128,128]{1,0:T(8,128)S(1)} %get-tuple-element.95.cross_ref, f32[128,128]{1,0:T(8,128)S(1)} %get-tuple-element.96.left_ref), custom_call_target="tpu_custom_call" | custom-call | flops 1000000000 | bytes 458752 | tf_op jit(solution)/shard_map/pallas_call | solution.py:60
  100.8 2.1 %collective-permute-done.29 = f32[128,256]{1,0:T(8,128)S(1)} collective-permute-done((f32[128,256]{1,0:T(8,128)S(1)}, f32[128,256]{1,0:T(8,128)S(1)}, u32[]{:S(2)}, u32[]{:S(2)}) %collective-permute-start.29) | collective-permute-done | bytes 131104 | tf_op jit(solution)/shard_map/ppermute | solution.py:165
  105.5 1.4 %collective-permute-start.31 = (f32[64,256]{1,0:T(8,128)S(1)}, f32[64,256]{1,0:T(8,128)S(1)}, u32[]{:S(2)}, u32[]{:S(2)}) collective-permute-start(f32[64,256]{1,0:T(8,128)S(1)} %get-tuple-element.112), channel_id=1, source_target_pairs={{0,8},{4,12},{8,0},{12,4},{1,9},{5,13},{9,1},{13,5},{2,10},{6,14},... | collective-permute-start | bytes 196616 | tf_op jit(solution)/shard_map/ppermute | solution.py:165
  107.4 4.8 %collective-permute-done.31 = f32[64,256]{1,0:T(8,128)S(1)} collective-permute-done((f32[64,256]{1,0:T(8,128)S(1)}, f32[64,256]{1,0:T(8,128)S(1)}, u32[]{:S(2)}, u32[]{:S(2)}) %collective-permute-start.31) | collective-permute-done | bytes 65568 | tf_op jit(solution)/shard_map/ppermute | solution.py:165
  112.3 2.5 %collective-permute-start.35 = (f32[256,256]{1,0:T(8,128)S(1)}, f32[256,256]{1,0:T(8,128)S(1)}, u32[]{:S(2)}, u32[]{:S(2)}) collective-permute-start(f32[256,256]{1,0:T(8,128)S(1)} %shard_map.76.refs_4_), channel_id=1, source_target_pairs={{0,8},{4,12},{8,0},{12,4},{1,9},{5,13},{9,1},{13,5},{2,10},{6,14},... | collective-permute-start | bytes 786440 | tf_op jit(solution)/shard_map/ppermute | solution.py:165
  116.0 3.1 %collective-permute-done.32.refs_0_ = f32[64,256]{1,0:T(8,128)S(1)} collective-permute-done((f32[64,256]{1,0:T(8,128)S(1)}, f32[64,256]{1,0:T(8,128)S(1)}, u32[]{:S(2)}, u32[]{:S(2)}) %collective-permute-start.32) | collective-permute-done | bytes 65568 | tf_op jit(solution)/shard_map/ppermute | solution.py:165
  120.3 8.1 %shard_map.77.refs_6_ = f32[256,256]{1,0:T(8,128)S(1)} custom-call(f32[64,256]{1,0:T(8,128)S(1)} %add.51.own_ref, f32[64,256]{1,0:T(8,128)S(1)} %collective-permute-done.32.refs_0_, f32[64,256]{1,0:T(8,128)S(1)} %collective-permute-done.33.refs_1_, f32[64,256]{1,0:T(8,128)S(1)} %collective-permute-done.34.refs_2_), custom_call_target="tpu_custom_call" | custom-call | flops 1000000000 | bytes 524288 | tf_op jit(solution)/shard_map/pallas_call | solution.py:60
  128.4 4.4 %shard_map.78 = (f32[144,128]{1,0:T(8,128)S(1)}, f32[144,128]{1,0:T(8,128)S(1)}) custom-call(f32[16,4096]{1,0:T(8,128)S(1)} %bitcast.5, f32[256,256]{1,0:T(8,128)S(1)} %get-tuple-element.100.refs_0_, f32[256,256]{1,0:T(8,128)S(1)} %get-tuple-element.103.refs_1_, f32[256,256]{1,0:T(8,128)S(1)} %get-tuple-element.108.refs_2_, ...), custom_call_target="tpu_custom_call" | custom-call | flops 3000000000 | bytes 3294208 | tf_op jit(solution)/shard_map/pallas_call | solution.py:60
  133.3 5.9 %collective-permute-done.37.second_ref = f32[144,128]{1,0:T(8,128)S(1)} collective-permute-done((f32[144,128]{1,0:T(8,128)S(1)}, f32[144,128]{1,0:T(8,128)S(1)}, u32[]{:S(2)}, u32[]{:S(2)}) %collective-permute-start.37) | collective-permute-done | bytes 73760 | tf_op jit(solution)/shard_map/ppermute | solution.py:165
  (100 shorter events, 33.7 us)
Async XLA Ops:
  1.6 5.3 %collective-permute-start = (f32[64,256]{1,0:T(8,128)S(1)}, f32[64,256]{1,0:T(8,128)S(1)}, u32[]{:S(2)}, u32[]{:S(2)}) collective-permute-start(f32[64,256]{1,0:T(8,128)S(1)} %shard_map.55.gram_ref), channel_id=1, source_target_pairs={{0,4},{4,0},{8,12},{12,8},{1,5},{5,1},{9,13},{13,9},{2,6},{6,2},{1... | collective-permute-start | bytes 196616 | tf_op jit(solution)/shard_map/ppermute | solution.py:165
  7.0 8.7 %collective-permute-start.1 = (f32[256,256]{1,0:T(8,128)S(1)}, f32[256,256]{1,0:T(8,128)S(1)}, u32[]{:S(2)}, u32[]{:S(2)}) collective-permute-start(f32[256,256]{1,0:T(8,128)S(1)} %get-tuple-element.66), channel_id=1, source_target_pairs={{0,4},{4,0},{8,12},{12,8},{1,5},{5,1},{9,13},{13,9},{2,6},{6,2},{1... | collective-permute-start | bytes 786440 | tf_op jit(solution)/shard_map/ppermute | solution.py:165
  9.1 5.8 %collective-permute-start.2 = (f32[64,256]{1,0:T(8,128)S(1)}, f32[64,256]{1,0:T(8,128)S(1)}, u32[]{:S(2)}, u32[]{:S(2)}) collective-permute-start(f32[64,256]{1,0:T(8,128)S(1)} %add.39), channel_id=1, source_target_pairs={{0,8},{4,12},{8,0},{12,4},{1,9},{5,13},{9,1},{13,5},{2,10},{6,14},... | collective-permute-start | bytes 196616 | tf_op jit(solution)/shard_map/ppermute | solution.py:165
  15.7 18.3 %collective-permute-start.3 = (f32[512,256]{1,0:T(8,128)S(1)}, f32[512,256]{1,0:T(8,128)S(1)}, u32[]{:S(2)}, u32[]{:S(2)}) collective-permute-start(f32[512,256]{1,0:T(8,128)S(1)} %get-tuple-element.68), channel_id=1, source_target_pairs={{0,4},{4,0},{8,12},{12,8},{1,5},{5,1},{9,13},{13,9},{2,6},{6,2},{1... | collective-permute-start | bytes 1572872 | tf_op jit(solution)/shard_map/ppermute | solution.py:165
  18.5 15.4 %collective-permute-start.7 = (f32[256,256]{1,0:T(8,128)S(1)}, f32[256,256]{1,0:T(8,128)S(1)}, u32[]{:S(2)}, u32[]{:S(2)}) collective-permute-start(f32[256,256]{1,0:T(8,128)S(1)} %add.40.first_ref), channel_id=1, source_target_pairs={{0,8},{4,12},{8,0},{12,4},{1,9},{5,13},{9,1},{13,5},{2,10},{6,14},... | collective-permute-start | bytes 786440 | tf_op jit(solution)/shard_map/ppermute | solution.py:165
  20.1 4.3 %collective-permute-start.4 = (f32[64,256]{1,0:T(8,128)S(1)}, f32[64,256]{1,0:T(8,128)S(1)}, u32[]{:S(2)}, u32[]{:S(2)}) collective-permute-start(f32[64,256]{1,0:T(8,128)S(1)} %add.41.own_ref), channel_id=1, source_target_pairs={{0,2},{2,0},{1,3},{3,1},{4,6},{6,4},{5,7},{7,5},{8,10},{10,8},{9,1... | collective-permute-start | bytes 196616 | tf_op jit(solution)/shard_map/ppermute | solution.py:165
  21.6 2.8 %collective-permute-start.5 = (f32[64,256]{1,0:T(8,128)S(1)}, f32[64,256]{1,0:T(8,128)S(1)}, u32[]{:S(2)}, u32[]{:S(2)}) collective-permute-start(f32[64,256]{1,0:T(8,128)S(1)} %add.41.own_ref), channel_id=1, source_target_pairs={{0,1},{1,0},{2,3},{3,2},{4,5},{5,4},{6,7},{7,6},{8,9},{9,8},{10,11... | collective-permute-start | bytes 196616 | tf_op jit(solution)/shard_map/ppermute | solution.py:165
  36.6 5.6 %collective-permute-start.9 = (f32[128,256]{1,0:T(8,128)S(1)}, f32[128,256]{1,0:T(8,128)S(1)}, u32[]{:S(2)}, u32[]{:S(2)}) collective-permute-start(f32[128,256]{1,0:T(8,128)S(1)} %get-tuple-element.73), channel_id=1, source_target_pairs={{0,2},{2,0},{1,3},{3,1},{4,6},{6,4},{5,7},{7,5},{8,10},{10,8},{9,1... | collective-permute-start | bytes 393224 | tf_op jit(solution)/shard_map/ppermute | solution.py:165
  38.2 6.4 %collective-permute-start.12 = (f32[128,256]{1,0:T(8,128)S(1)}, f32[128,256]{1,0:T(8,128)S(1)}, u32[]{:S(2)}, u32[]{:S(2)}) collective-permute-start(f32[128,256]{1,0:T(8,128)S(1)} %get-tuple-element.77), channel_id=1, source_target_pairs={{0,4},{4,0},{8,12},{12,8},{1,5},{5,1},{9,13},{13,9},{2,6},{6,2},{1... | collective-permute-start | bytes 393224 | tf_op jit(solution)/shard_map/ppermute | solution.py:165
  42.3 5.3 %collective-permute-start.10 = (f32[128,256]{1,0:T(8,128)S(1)}, f32[128,256]{1,0:T(8,128)S(1)}, u32[]{:S(2)}, u32[]{:S(2)}) collective-permute-start(f32[128,256]{1,0:T(8,128)S(1)} %add.42), channel_id=1, source_target_pairs={{0,4},{4,0},{8,12},{12,8},{1,5},{5,1},{9,13},{13,9},{2,6},{6,2},{1... | collective-permute-start | bytes 393224 | tf_op jit(solution)/shard_map/ppermute | solution.py:165
  44.6 5.0 %collective-permute-start.13 = (f32[128,256]{1,0:T(8,128)S(1)}, f32[128,256]{1,0:T(8,128)S(1)}, u32[]{:S(2)}, u32[]{:S(2)}) collective-permute-start(f32[128,256]{1,0:T(8,128)S(1)} %add.44), channel_id=1, source_target_pairs={{0,2},{2,0},{1,3},{3,1},{4,6},{6,4},{5,7},{7,5},{8,10},{10,8},{9,1... | collective-permute-start | bytes 393224 | tf_op jit(solution)/shard_map/ppermute | solution.py:165
  49.7 3.6 %collective-permute-start.14 = (f32[256,256]{1,0:T(8,128)S(1)}, f32[256,256]{1,0:T(8,128)S(1)}, u32[]{:S(2)}, u32[]{:S(2)}) collective-permute-start(f32[256,256]{1,0:T(8,128)S(1)} %pad_maximum_fusion.stack_ref), channel_id=1, source_target_pairs={{0,1},{1,0},{2,3},{3,2},{4,5},{5,4},{6,7},{7,6},{8,9},{9,8},{10,11... | collective-permute-start | bytes 786440 | tf_op jit(solution)/shard_map/ppermute | solution.py:165
  49.8 7.1 %collective-permute-start.11 = (f32[128,256]{1,0:T(8,128)S(1)}, f32[128,256]{1,0:T(8,128)S(1)}, u32[]{:S(2)}, u32[]{:S(2)}) collective-permute-start(f32[128,256]{1,0:T(8,128)S(1)} %add.43), channel_id=1, source_target_pairs={{0,2},{2,0},{1,3},{3,1},{4,6},{6,4},{5,7},{7,5},{8,10},{10,8},{9,1... | collective-permute-start | bytes 393224 | tf_op jit(solution)/shard_map/ppermute | solution.py:165
  51.3 5.6 %collective-permute-start.15 = (f32[128,256]{1,0:T(8,128)S(1)}, f32[128,256]{1,0:T(8,128)S(1)}, u32[]{:S(2)}, u32[]{:S(2)}) collective-permute-start(f32[128,256]{1,0:T(8,128)S(1)} %add.45), channel_id=1, source_target_pairs={{0,4},{4,0},{8,12},{12,8},{1,5},{5,1},{9,13},{13,9},{2,6},{6,2},{1... | collective-permute-start | bytes 393224 | tf_op jit(solution)/shard_map/ppermute | solution.py:165
  59.9 17.8 %collective-permute-start.18 = (f32[320,256]{1,0:T(8,128)S(1)}, f32[320,256]{1,0:T(8,128)S(1)}, u32[]{:S(2)}, u32[]{:S(2)}) collective-permute-start(f32[320,256]{1,0:T(8,128)S(1)} %shard_map.66.first_ref), channel_id=1, source_target_pairs={{0,8},{4,12},{8,0},{12,4},{1,9},{5,13},{9,1},{13,5},{2,10},{6,14},... | collective-permute-start | bytes 983048 | tf_op jit(solution)/shard_map/ppermute | solution.py:165
  61.7 13.2 %collective-permute-start.17 = (f32[128,512]{1,0:T(8,128)S(1)}, f32[128,512]{1,0:T(8,128)S(1)}, u32[]{:S(2)}, u32[]{:S(2)}) collective-permute-start(f32[128,512]{1,0:T(8,128)S(1)} %get-tuple-element.89), channel_id=1, source_target_pairs={{0,4},{4,0},{8,12},{12,8},{1,5},{5,1},{9,13},{13,9},{2,6},{6,2},{1... | collective-permute-start | bytes 786440 | tf_op jit(solution)/shard_map/ppermute | solution.py:165
  78.3 5.3 %collective-permute-start.19 = (f32[512,256]{1,0:T(8,128)S(1)}, f32[512,256]{1,0:T(8,128)S(1)}, u32[]{:S(2)}, u32[]{:S(2)}) collective-permute-start(f32[512,256]{1,0:T(8,128)S(1)} %shard_map.68), channel_id=1, source_target_pairs={{0,1},{1,0},{2,3},{3,2},{4,5},{5,4},{6,7},{7,6},{8,9},{9,8},{10,11... | collective-permute-start | bytes 1572872 | tf_op jit(solution)/shard_map/ppermute | solution.py:165
  78.5 4.5 %collective-permute-start.21 = (f32[64,256]{1,0:T(8,128)S(1)}, f32[64,256]{1,0:T(8,128)S(1)}, u32[]{:S(2)}, u32[]{:S(2)}) collective-permute-start(f32[64,256]{1,0:T(8,128)S(1)} %slice_add_fusion.own_ref), channel_id=1, source_target_pairs={{0,2},{2,0},{1,3},{3,1},{4,6},{6,4},{5,7},{7,5},{8,10},{10,8},{9,1... | collective-permute-start | bytes 196616 | tf_op jit(solution)/shard_map/ppermute | solution.py:165
  79.3 5.3 %collective-permute-start.22 = (f32[64,256]{1,0:T(8,128)S(1)}, f32[64,256]{1,0:T(8,128)S(1)}, u32[]{:S(2)}, u32[]{:S(2)}) collective-permute-start(f32[64,256]{1,0:T(8,128)S(1)} %slice_add_fusion.own_ref), channel_id=1, source_target_pairs={{0,1},{1,0},{2,3},{3,2},{4,5},{5,4},{6,7},{7,6},{8,9},{9,8},{10,11... | collective-permute-start | bytes 196616 | tf_op jit(solution)/shard_map/ppermute | solution.py:165
  83.7 6.0 %collective-permute-start.20 = (f32[128,256]{1,0:T(8,128)S(1)}, f32[128,256]{1,0:T(8,128)S(1)}, u32[]{:S(2)}, u32[]{:S(2)}) collective-permute-start(f32[128,256]{1,0:T(8,128)S(1)} %get-tuple-element.92), channel_id=1, source_target_pairs={{0,2},{2,0},{1,3},{3,1},{4,6},{6,4},{5,7},{7,5},{8,10},{10,8},{9,1... | collective-permute-start | bytes 393224 | tf_op jit(solution)/shard_map/ppermute | solution.py:165
  84.6 6.2 %collective-permute-start.25 = (f32[128,256]{1,0:T(8,128)S(1)}, f32[128,256]{1,0:T(8,128)S(1)}, u32[]{:S(2)}, u32[]{:S(2)}) collective-permute-start(f32[128,256]{1,0:T(8,128)S(1)} %get-tuple-element.99), channel_id=1, source_target_pairs={{0,4},{4,0},{8,12},{12,8},{1,5},{5,1},{9,13},{13,9},{2,6},{6,2},{1... | collective-permute-start | bytes 393224 | tf_op jit(solution)/shard_map/ppermute | solution.py:165
  89.7 6.3 %collective-permute-start.24 = (f32[128,256]{1,0:T(8,128)S(1)}, f32[128,256]{1,0:T(8,128)S(1)}, u32[]{:S(2)}, u32[]{:S(2)}) collective-permute-start(f32[128,256]{1,0:T(8,128)S(1)} %add.46), channel_id=1, source_target_pairs={{0,4},{4,0},{8,12},{12,8},{1,5},{5,1},{9,13},{13,9},{2,6},{6,2},{1... | collective-permute-start | bytes 393224 | tf_op jit(solution)/shard_map/ppermute | solution.py:165
  90.8 5.2 %collective-permute-start.26 = (f32[128,256]{1,0:T(8,128)S(1)}, f32[128,256]{1,0:T(8,128)S(1)}, u32[]{:S(2)}, u32[]{:S(2)}) collective-permute-start(f32[128,256]{1,0:T(8,128)S(1)} %add.49), channel_id=1, source_target_pairs={{0,2},{2,0},{1,3},{3,1},{4,6},{6,4},{5,7},{7,5},{8,10},{10,8},{9,1... | collective-permute-start | bytes 393224 | tf_op jit(solution)/shard_map/ppermute | solution.py:165
  96.0 3.3 %collective-permute-start.27 = (f32[256,256]{1,0:T(8,128)S(1)}, f32[256,256]{1,0:T(8,128)S(1)}, u32[]{:S(2)}, u32[]{:S(2)}) collective-permute-start(f32[256,256]{1,0:T(8,128)S(1)} %pad_maximum_fusion.1.stack_ref), channel_id=1, source_target_pairs={{0,1},{1,0},{2,3},{3,2},{4,5},{5,4},{6,7},{7,6},{8,9},{9,8},{10,11... | collective-permute-start | bytes 786440 | tf_op jit(solution)/shard_map/ppermute | solution.py:165
  96.1 6.8 %collective-permute-start.28 = (f32[128,256]{1,0:T(8,128)S(1)}, f32[128,256]{1,0:T(8,128)S(1)}, u32[]{:S(2)}, u32[]{:S(2)}) collective-permute-start(f32[128,256]{1,0:T(8,128)S(1)} %add.48), channel_id=1, source_target_pairs={{0,2},{2,0},{1,3},{3,1},{4,6},{6,4},{5,7},{7,5},{8,10},{10,8},{9,1... | collective-permute-start | bytes 393224 | tf_op jit(solution)/shard_map/ppermute | solution.py:165
  97.3 5.6 %collective-permute-start.29 = (f32[128,256]{1,0:T(8,128)S(1)}, f32[128,256]{1,0:T(8,128)S(1)}, u32[]{:S(2)}, u32[]{:S(2)}) collective-permute-start(f32[128,256]{1,0:T(8,128)S(1)} %add.50), channel_id=1, source_target_pairs={{0,4},{4,0},{8,12},{12,8},{1,5},{5,1},{9,13},{13,9},{2,6},{6,2},{1... | collective-permute-start | bytes 393224 | tf_op jit(solution)/shard_map/ppermute | solution.py:165
  105.5 6.7 %collective-permute-start.31 = (f32[64,256]{1,0:T(8,128)S(1)}, f32[64,256]{1,0:T(8,128)S(1)}, u32[]{:S(2)}, u32[]{:S(2)}) collective-permute-start(f32[64,256]{1,0:T(8,128)S(1)} %get-tuple-element.112), channel_id=1, source_target_pairs={{0,8},{4,12},{8,0},{12,4},{1,9},{5,13},{9,1},{13,5},{2,10},{6,14},... | collective-permute-start | bytes 196616 | tf_op jit(solution)/shard_map/ppermute | solution.py:165
  112.2 16.2 %collective-permute-start.36 = (f32[128,512]{1,0:T(8,128)S(1)}, f32[128,512]{1,0:T(8,128)S(1)}, u32[]{:S(2)}, u32[]{:S(2)}) collective-permute-start(f32[128,512]{1,0:T(8,128)S(1)} %get-tuple-element.116), channel_id=1, source_target_pairs={{0,4},{4,0},{8,12},{12,8},{1,5},{5,1},{9,13},{13,9},{2,6},{6,2},{1... | collective-permute-start | bytes 786440 | tf_op jit(solution)/shard_map/ppermute | solution.py:165
  112.3 16.1 %collective-permute-start.35 = (f32[256,256]{1,0:T(8,128)S(1)}, f32[256,256]{1,0:T(8,128)S(1)}, u32[]{:S(2)}, u32[]{:S(2)}) collective-permute-start(f32[256,256]{1,0:T(8,128)S(1)} %shard_map.76.refs_4_), channel_id=1, source_target_pairs={{0,8},{4,12},{8,0},{12,4},{1,9},{5,13},{9,1},{13,5},{2,10},{6,14},... | collective-permute-start | bytes 786440 | tf_op jit(solution)/shard_map/ppermute | solution.py:165
  114.8 4.3 %collective-permute-start.32 = (f32[64,256]{1,0:T(8,128)S(1)}, f32[64,256]{1,0:T(8,128)S(1)}, u32[]{:S(2)}, u32[]{:S(2)}) collective-permute-start(f32[64,256]{1,0:T(8,128)S(1)} %add.51.own_ref), channel_id=1, source_target_pairs={{0,2},{2,0},{1,3},{3,1},{4,6},{6,4},{5,7},{7,5},{8,10},{10,8},{9,1... | collective-permute-start | bytes 196616 | tf_op jit(solution)/shard_map/ppermute | solution.py:165
  116.0 3.2 %collective-permute-start.33 = (f32[64,256]{1,0:T(8,128)S(1)}, f32[64,256]{1,0:T(8,128)S(1)}, u32[]{:S(2)}, u32[]{:S(2)}) collective-permute-start(f32[64,256]{1,0:T(8,128)S(1)} %add.51.own_ref), channel_id=1, source_target_pairs={{0,1},{1,0},{2,3},{3,2},{4,5},{5,4},{6,7},{7,6},{8,9},{9,8},{10,11... | collective-permute-start | bytes 196616 | tf_op jit(solution)/shard_map/ppermute | solution.py:165
  132.8 6.4 %collective-permute-start.37 = (f32[144,128]{1,0:T(8,128)S(1)}, f32[144,128]{1,0:T(8,128)S(1)}, u32[]{:S(2)}, u32[]{:S(2)}) collective-permute-start(f32[144,128]{1,0:T(8,128)S(1)} %get-tuple-element.118), channel_id=1, source_target_pairs={{0,8},{4,12},{8,0},{12,4},{1,9},{5,13},{9,1},{13,5},{2,10},{6,14},... | collective-permute-start | bytes 221192 | tf_op jit(solution)/shard_map/ppermute | solution.py:165
  (11 other events, 49.2 us)

commit v6 on v4

--- a/solution.py
+++ b/solution.py
@@ -388,25 +388,21 @@
     proj_ref[...] = part_ref[...] + project_stack(1, 1, own_ref, other_ref, block_ref, rows_ref)
 
 
-def attend_kernel(
-    query_ref,
-    *refs,
-):
-    *block_refs, first_ref, second_ref, lower_ref, own_ref, low_ref, high_ref, length_ref = refs[:-3]
-    keep_ref, send_ref, score_ref = refs[-3:]
+def attend_kernel(sent, query_ref, *refs):
+    *block_refs, first_ref, second_ref, lower_ref, own_ref, low_ref, high_ref, length_ref = refs[:-2]
+    out_ref, score_ref = refs[-2:]
     mine, upper, _, _ = pair_sides()
+    which = upper ^ int(sent)
     group = QH // KVH
     tokens = own_ref.shape[1]
     half, width = tokens // 2, length_ref.shape[1]
-    coef = product(first_ref[...] + second_ref[...], lower_ref[...], ((1,), (1,)))
-    reduced = []
-    for which in range(2):
-        quer = jnp.concatenate(
-            [query_ref[:, lanes((2 * which + mine) * group + i)] for i in range(group)]
-        )
-        factor = coef[which * HD : (which + 1) * HD]
-        reduced.append(product(quer, factor, ((1,), (0,))) / math.sqrt(HD))
-    reduced = product(jnp.concatenate(reduced), lower_ref[...], ((1,), (0,)))
+    local = lanes(which)
+    coef = product(first_ref[local, :] + second_ref[local, :], lower_ref[...], ((1,), (1,)))
+    quer = jnp.concatenate(
+        [query_ref[:, lanes((2 * which + mine) * group + i)] for i in range(group)]
+    )
+    reduced = product(quer, coef, ((1,), (0,))) / math.sqrt(HD)
+    reduced = product(reduced, lower_ref[...], ((1,), (0,)))
     for i, block_ref in enumerate(block_refs):
         far, beside = i % 2, i // 2
         part = product(block_ref[...], reduced, ((1,), (1,)))
@@ -426,20 +422,11 @@
     peak = jnp.max(jnp.where(valid, scores, NEG), axis=0, keepdims=True)
     weight = jnp.where(valid, jnp.exp(scores - peak), 0.0)
     total = jnp.sum(weight, axis=0, keepdims=True)
-    lane = width // 2
-    for which, there_ref in enumerate((low_ref, high_ref)):
-        here = slice(which * lane, (which + 1) * lane)
-        own = own_ref[pl.ds(which * HD, HD), :]
-        acc = product(own, weight[:tokens, here], ((1,), (0,)))
-        acc = acc + product(there_ref[...], weight[tokens:, here], ((1,), (0,)))
-
-        def give(ref):
-            ref[pl.ds(0, HD), :] = acc
-            ref[pl.ds(HD, 8), :] = jnp.broadcast_to(peak[:, here], (8, lane))
-            ref[pl.ds(HD + 8, 8), :] = jnp.broadcast_to(total[:, here], (8, lane))
-
-        pl.when(upper == which)(lambda: give(keep_ref))
-        pl.when(upper != which)(lambda: give(send_ref))
+    other = jnp.where(which == 0, low_ref[...], high_ref[...])
+    acc = product(own_ref[local, :], weight[:tokens], ((1,), (0,)))
+    out_ref[pl.ds(0, HD), :] = acc + product(other, weight[tokens:], ((1,), (0,)))
+    out_ref[pl.ds(HD, 8), :] = jnp.broadcast_to(peak, (8, width))
+    out_ref[pl.ds(HD + 8, 8), :] = jnp.broadcast_to(total, (8, width))
 
 
 def merge_kernel(first_ref, second_ref, out_ref):
@@ -513,8 +500,8 @@
             values_other.append(swap(after(values_send[len(values_other)], proj, gram), "tok", 1))
         parts = gathered(gram)
         if step == 0 or last:
-            lower = inverse_factor(*parts)
-            first = after(first, lower, values_own)
+            lower = inverse_factor(after(parts[0], values_own), *parts[1:])
+            first = after(first, lower)
         else:
             halves = inverse_factor_low(*parts)
             first = after(first, halves[0], *values_other)
@@ -566,9 +553,7 @@
             scratch=[(tokens // 2, half)],
             flops=400_000_000,
         )
-    keep, send = call(
-        attend_kernel,
-        [vmem(HD + 16, HD)] * 2,
+    operands = (
         queries,
         *blocks,
         first,
@@ -576,9 +561,17 @@
         lower,
         values_own,
         *values_other,
-        jnp.tile(lengths, 2 * (QH // KVH))[None, :],
-        scratch=[(2 * tokens, 2 * (QH // KVH) * rows)],
-        flops=3_000_000_000,
+        jnp.tile(lengths, QH // KVH)[None, :],
+    )
+    send, keep = (
+        call(
+            functools.partial(attend_kernel, sent),
+            vmem(HD + 16, HD),
+            *operands,
+            scratch=[(2 * tokens, QH // KVH * rows)],
+            flops=1_500_000_000,
+        )
+        for sent in (True, False)
     )
     return call(merge_kernel, vmem(1, rows, 1, half * 4), keep, swap(send, "tok", 2))
 

time: 139 us -> 137 us (0.986)
  waiting for transfers between devices: 51.5 us -> 48.1 us
  Pallas kernels: 45.1 us -> 46.6 us
    ppermute x39, waiting for transfers between devices: 51.5 us -> 48.1 us  [swap(): return lax.ppermute(x, axis, pairs)]
    pallas_call x25 -> x26, Pallas kernels: 45.1 us -> 46.6 us  [call(): pl.pallas_call(kernel, out_shape=out_shape, in_specs=[spec] * len(args),...]
  transfers between devices with their start and end apart: 39 -> 39, of which waited for: 26 -> 27; matrix products, arithmetic and copies ran while one was open for 0% -> 0% of each run, Pallas kernels for 26% -> 29%
where the time goes in v6:
time: 137 us
  waiting for transfers between devices  48.1 us (35%)
  Pallas kernels  46.6 us (34%)
  starting transfers between devices  40.6 us (30%)
    ppermute x39, waiting for transfers between devices, swap(): return lax.ppermute(x, axis, pairs)  48.1 us
    pallas_call x26, Pallas kernels, call(): pl.pallas_call(kernel, out_shape=out_shape, in_specs=[spec] * len(args),...  46.6 us
    ppermute x39, starting transfers between devices, swap(): return lax.ppermute(x, axis, pairs)  40.6 us
  transfers between devices with their start and end apart: 39, of which 27 were waited for; matrix products, arithmetic and copies ran while one was open for 0% of the time, Pallas kernels for 29%

profile of v6, /device:TPU:0, one launch (start us, length us, event | category | flops | bytes accessed | tf_op | source)
XLA Modules:
  0.0 137.2 jit_solution(9147097565182233851)
XLA Ops:
  1.6 3.1 %collective-permute-start = (f32[64,256]{1,0:T(8,128)S(1)}, f32[64,256]{1,0:T(8,128)S(1)}, u32[]{:S(2)}, u32[]{:S(2)}) collective-permute-start(f32[64,256]{1,0:T(8,128)S(1)} %shard_map.55.gram_ref), channel_id=1, source_target_pairs={{0,4},{4,0},{8,12},{12,8},{1,5},{5,1},{9,13},{13,9},{2,6},{6,2},{1... | collective-permute-start | bytes 196616 | tf_op jit(solution)/shard_map/ppermute | solution.py:165
  7.0 2.1 %collective-permute-start.1 = (f32[256,256]{1,0:T(8,128)S(1)}, f32[256,256]{1,0:T(8,128)S(1)}, u32[]{:S(2)}, u32[]{:S(2)}) collective-permute-start(f32[256,256]{1,0:T(8,128)S(1)} %get-tuple-element.64), channel_id=1, source_target_pairs={{0,4},{4,0},{8,12},{12,8},{1,5},{5,1},{9,13},{13,9},{2,6},{6,2},{1... | collective-permute-start | bytes 786440 | tf_op jit(solution)/shard_map/ppermute | solution.py:165
  9.1 2.6 %collective-permute-start.2 = (f32[64,256]{1,0:T(8,128)S(1)}, f32[64,256]{1,0:T(8,128)S(1)}, u32[]{:S(2)}, u32[]{:S(2)}) collective-permute-start(f32[64,256]{1,0:T(8,128)S(1)} %add.39), channel_id=1, source_target_pairs={{0,8},{4,12},{8,0},{12,4},{1,9},{5,13},{9,1},{13,5},{2,10},{6,14},... | collective-permute-start | bytes 196616 | tf_op jit(solution)/shard_map/ppermute | solution.py:165
  11.6 3.2 %collective-permute-done.2 = f32[64,256]{1,0:T(8,128)S(1)} collective-permute-done((f32[64,256]{1,0:T(8,128)S(1)}, f32[64,256]{1,0:T(8,128)S(1)}, u32[]{:S(2)}, u32[]{:S(2)}) %collective-permute-start.2) | collective-permute-done | bytes 65568 | tf_op jit(solution)/shard_map/ppermute | solution.py:165
  15.7 2.8 %collective-permute-start.3 = (f32[512,256]{1,0:T(8,128)S(1)}, f32[512,256]{1,0:T(8,128)S(1)}, u32[]{:S(2)}, u32[]{:S(2)}) collective-permute-start(f32[512,256]{1,0:T(8,128)S(1)} %get-tuple-element.66), channel_id=1, source_target_pairs={{0,4},{4,0},{8,12},{12,8},{1,5},{5,1},{9,13},{13,9},{2,6},{6,2},{1... | collective-permute-start | bytes 1572872 | tf_op jit(solution)/shard_map/ppermute | solution.py:165
  18.5 1.5 %collective-permute-start.7 = (f32[256,256]{1,0:T(8,128)S(1)}, f32[256,256]{1,0:T(8,128)S(1)}, u32[]{:S(2)}, u32[]{:S(2)}) collective-permute-start(f32[256,256]{1,0:T(8,128)S(1)} %add.40.first_ref), channel_id=1, source_target_pairs={{0,8},{4,12},{8,0},{12,4},{1,9},{5,13},{9,1},{13,5},{2,10},{6,14},... | collective-permute-start | bytes 786440 | tf_op jit(solution)/shard_map/ppermute | solution.py:165
  21.5 2.8 %collective-permute-done.4.refs_0_ = f32[64,256]{1,0:T(8,128)S(1)} collective-permute-done((f32[64,256]{1,0:T(8,128)S(1)}, f32[64,256]{1,0:T(8,128)S(1)}, u32[]{:S(2)}, u32[]{:S(2)}) %collective-permute-start.4) | collective-permute-done | bytes 65568 | tf_op jit(solution)/shard_map/ppermute | solution.py:165
  25.6 8.0 %shard_map.58.lower_ref = f32[256,256]{1,0:T(8,128)S(1)} custom-call(f32[64,256]{1,0:T(8,128)S(1)} %add.41.own_ref, f32[64,256]{1,0:T(8,128)S(1)} %collective-permute-done.4.refs_0_, f32[64,256]{1,0:T(8,128)S(1)} %collective-permute-done.5.refs_1_, f32[64,256]{1,0:T(8,128)S(1)} %collective-permute-done.6.refs_2_), custom_call_target="tpu_custom_call" | custom-call | flops 1000000000 | bytes 524288 | tf_op jit(solution)/shard_map/pallas_call | solution.py:60
  36.3 1.5 %collective-permute-start.9 = (f32[128,256]{1,0:T(8,128)S(1)}, f32[128,256]{1,0:T(8,128)S(1)}, u32[]{:S(2)}, u32[]{:S(2)}) collective-permute-start(f32[128,256]{1,0:T(8,128)S(1)} %get-tuple-element.72), channel_id=1, source_target_pairs={{0,2},{2,0},{1,3},{3,1},{4,6},{6,4},{5,7},{7,5},{8,10},{10,8},{9,1... | collective-permute-start | bytes 393224 | tf_op jit(solution)/shard_map/ppermute | solution.py:165
  37.9 2.6 %collective-permute-start.12 = (f32[128,256]{1,0:T(8,128)S(1)}, f32[128,256]{1,0:T(8,128)S(1)}, u32[]{:S(2)}, u32[]{:S(2)}) collective-permute-start(f32[128,256]{1,0:T(8,128)S(1)} %get-tuple-element.75), channel_id=1, source_target_pairs={{0,4},{4,0},{8,12},{12,8},{1,5},{5,1},{9,13},{13,9},{2,6},{6,2},{1... | collective-permute-start | bytes 393224 | tf_op jit(solution)/shard_map/ppermute | solution.py:165
  42.0 2.6 %collective-permute-start.10 = (f32[128,256]{1,0:T(8,128)S(1)}, f32[128,256]{1,0:T(8,128)S(1)}, u32[]{:S(2)}, u32[]{:S(2)}) collective-permute-start(f32[128,256]{1,0:T(8,128)S(1)} %add.42), channel_id=1, source_target_pairs={{0,4},{4,0},{8,12},{12,8},{1,5},{5,1},{9,13},{13,9},{2,6},{6,2},{1... | collective-permute-start | bytes 393224 | tf_op jit(solution)/shard_map/ppermute | solution.py:165
  44.6 1.6 %collective-permute-start.13 = (f32[128,256]{1,0:T(8,128)S(1)}, f32[128,256]{1,0:T(8,128)S(1)}, u32[]{:S(2)}, u32[]{:S(2)}) collective-permute-start(f32[128,256]{1,0:T(8,128)S(1)} %add.44), channel_id=1, source_target_pairs={{0,2},{2,0},{1,3},{3,1},{4,6},{6,4},{5,7},{7,5},{8,10},{10,8},{9,1... | collective-permute-start | bytes 393224 | tf_op jit(solution)/shard_map/ppermute | solution.py:165
  47.6 2.1 %collective-permute-done.13 = f32[128,256]{1,0:T(8,128)S(1)} collective-permute-done((f32[128,256]{1,0:T(8,128)S(1)}, f32[128,256]{1,0:T(8,128)S(1)}, u32[]{:S(2)}, u32[]{:S(2)}) %collective-permute-start.13) | collective-permute-done | bytes 131104 | tf_op jit(solution)/shard_map/ppermute | solution.py:165
  49.8 1.6 %collective-permute-start.11 = (f32[128,256]{1,0:T(8,128)S(1)}, f32[128,256]{1,0:T(8,128)S(1)}, u32[]{:S(2)}, u32[]{:S(2)}) collective-permute-start(f32[128,256]{1,0:T(8,128)S(1)} %add.43), channel_id=1, source_target_pairs={{0,2},{2,0},{1,3},{3,1},{4,6},{6,4},{5,7},{7,5},{8,10},{10,8},{9,1... | collective-permute-start | bytes 393224 | tf_op jit(solution)/shard_map/ppermute | solution.py:165
  51.5 1.7 %shard_map.62 = (f32[256,256]{1,0:T(8,128)}, f32[64,256]{1,0:T(8,128)S(1)}, f32[256,256]{1,0:T(8,128)S(1)}) custom-call(f32[256,256]{1,0:T(8,128)S(1)} %pad_maximum_fusion.stack_ref, f32[256,256]{1,0:T(8,128)S(1)} %shard_map.58.lower_ref, f32[512,256]{1,0:T(8,128)S(1)} %get-tuple-element.60.own_ref, f32[512,256]{1,0:T(8,128)S(1)} %collective-permute-done.3.other_ref), custom_call_target="tpu_custom_call" | custom-call | flops 900000000 | bytes 2162688 | tf_op jit(solution)/shard_map/pallas_call | solution.py:60
  59.4 1.8 %collective-permute-start.17 = (f32[64,256]{1,0:T(8,128)S(1)}, f32[64,256]{1,0:T(8,128)S(1)}, u32[]{:S(2)}, u32[]{:S(2)}) collective-permute-start(f32[64,256]{1,0:T(8,128)S(1)} %get-tuple-element.85), channel_id=1, source_target_pairs={{0,8},{4,12},{8,0},{12,4},{1,9},{5,13},{9,1},{13,5},{2,10},{6,14},... | collective-permute-start | bytes 196616 | tf_op jit(solution)/shard_map/ppermute | solution.py:165
  61.7 4.2 %collective-permute-done.17 = f32[64,256]{1,0:T(8,128)S(1)} collective-permute-done((f32[64,256]{1,0:T(8,128)S(1)}, f32[64,256]{1,0:T(8,128)S(1)}, u32[]{:S(2)}, u32[]{:S(2)}) %collective-permute-start.17) | collective-permute-done | bytes 65568 | tf_op jit(solution)/shard_map/ppermute | solution.py:165
  66.0 2.4 %collective-permute-start.22 = (f32[256,256]{1,0:T(8,128)S(1)}, f32[256,256]{1,0:T(8,128)S(1)}, u32[]{:S(2)}, u32[]{:S(2)}) collective-permute-start(f32[256,256]{1,0:T(8,128)S(1)} %shard_map.66.first_ref), channel_id=1, source_target_pairs={{0,8},{4,12},{8,0},{12,4},{1,9},{5,13},{9,1},{13,5},{2,10},{6,14},... | collective-permute-start | bytes 786440 | tf_op jit(solution)/shard_map/ppermute | solution.py:165
  69.7 3.0 %collective-permute-done.18.refs_0_ = f32[64,256]{1,0:T(8,128)S(1)} collective-permute-done((f32[64,256]{1,0:T(8,128)S(1)}, f32[64,256]{1,0:T(8,128)S(1)}, u32[]{:S(2)}, u32[]{:S(2)}) %collective-permute-start.18) | collective-permute-done | bytes 65568 | tf_op jit(solution)/shard_map/ppermute | solution.py:165
  73.9 4.0 %shard_map.67 = (f32[128,128]{1,0:T(8,128)S(1)}, f32[128,128]{1,0:T(8,128)S(1)}, f32[128,128]{1,0:T(8,128)S(1)}) custom-call(f32[64,256]{1,0:T(8,128)S(1)} %add.46.own_ref, f32[64,256]{1,0:T(8,128)S(1)} %collective-permute-done.18.refs_0_, f32[64,256]{1,0:T(8,128)S(1)} %collective-permute-done.19.refs_1_, f32[64,256]{1,0:T(8,128)S(1)} %collective-permute-done.20.refs_2_), custom_call_target="tpu_custom_call" | custom-call | flops 1000000000 | bytes 458752 | tf_op jit(solution)/shard_map/pallas_call | solution.py:60
  78.6 2.3 %collective-permute-done.22.second_ref = f32[256,256]{1,0:T(8,128)S(1)} collective-permute-done((f32[256,256]{1,0:T(8,128)S(1)}, f32[256,256]{1,0:T(8,128)S(1)}, u32[]{:S(2)}, u32[]{:S(2)}) %collective-permute-start.22) | collective-permute-done | bytes 262176 | tf_op jit(solution)/shard_map/ppermute | solution.py:165
  84.4 4.9 %collective-permute-done.24 = f32[128,256]{1,0:T(8,128)S(1)} collective-permute-done((f32[128,256]{1,0:T(8,128)S(1)}, f32[128,256]{1,0:T(8,128)S(1)}, u32[]{:S(2)}, u32[]{:S(2)}) %collective-permute-start.24) | collective-permute-done | bytes 131104 | tf_op jit(solution)/shard_map/ppermute | solution.py:165
  89.4 1.7 %collective-permute-start.27 = (f32[128,256]{1,0:T(8,128)S(1)}, f32[128,256]{1,0:T(8,128)S(1)}, u32[]{:S(2)}, u32[]{:S(2)}) collective-permute-start(f32[128,256]{1,0:T(8,128)S(1)} %add.49), channel_id=1, source_target_pairs={{0,2},{2,0},{1,3},{3,1},{4,6},{6,4},{5,7},{7,5},{8,10},{10,8},{9,1... | collective-permute-start | bytes 393224 | tf_op jit(solution)/shard_map/ppermute | solution.py:165
  91.1 3.9 %shard_map.71.lower_ref = f32[256,256]{1,0:T(8,128)S(1)} custom-call(f32[128,128]{1,0:T(8,128)S(1)} %get-tuple-element.86.tile_ref, f32[128,128]{1,0:T(8,128)S(1)} %get-tuple-element.92.cross_ref, f32[128,128]{1,0:T(8,128)S(1)} %get-tuple-element.93.left_ref), custom_call_target="tpu_custom_call" | custom-call | flops 1000000000 | bytes 458752 | tf_op jit(solution)/shard_map/pallas_call | solution.py:60
  104.3 1.8 %collective-permute-start.32 = (f32[64,256]{1,0:T(8,128)S(1)}, f32[64,256]{1,0:T(8,128)S(1)}, u32[]{:S(2)}, u32[]{:S(2)}) collective-permute-start(f32[64,256]{1,0:T(8,128)S(1)} %get-tuple-element.109), channel_id=1, source_target_pairs={{0,8},{4,12},{8,0},{12,4},{1,9},{5,13},{9,1},{13,5},{2,10},{6,14},... | collective-permute-start | bytes 196616 | tf_op jit(solution)/shard_map/ppermute | solution.py:165
  106.6 4.5 %collective-permute-done.32 = f32[64,256]{1,0:T(8,128)S(1)} collective-permute-done((f32[64,256]{1,0:T(8,128)S(1)}, f32[64,256]{1,0:T(8,128)S(1)}, u32[]{:S(2)}, u32[]{:S(2)}) %collective-permute-start.32) | collective-permute-done | bytes 65568 | tf_op jit(solution)/shard_map/ppermute | solution.py:165
  111.5 1.9 %collective-permute-start.37 = (f32[128,512]{1,0:T(8,128)S(1)}, f32[128,512]{1,0:T(8,128)S(1)}, u32[]{:S(2)}, u32[]{:S(2)}) collective-permute-start(f32[128,512]{1,0:T(8,128)S(1)} %get-tuple-element.114), channel_id=1, source_target_pairs={{0,4},{4,0},{8,12},{12,8},{1,5},{5,1},{9,13},{13,9},{2,6},{6,2},{1... | collective-permute-start | bytes 786440 | tf_op jit(solution)/shard_map/ppermute | solution.py:165
  114.5 3.2 %collective-permute-done.33.refs_0_ = f32[64,256]{1,0:T(8,128)S(1)} collective-permute-done((f32[64,256]{1,0:T(8,128)S(1)}, f32[64,256]{1,0:T(8,128)S(1)}, u32[]{:S(2)}, u32[]{:S(2)}) %collective-permute-start.33) | collective-permute-done | bytes 65568 | tf_op jit(solution)/shard_map/ppermute | solution.py:165
  119.0 8.0 %shard_map.77.refs_6_ = f32[256,256]{1,0:T(8,128)S(1)} custom-call(f32[64,256]{1,0:T(8,128)S(1)} %add.51.own_ref, f32[64,256]{1,0:T(8,128)S(1)} %collective-permute-done.33.refs_0_, f32[64,256]{1,0:T(8,128)S(1)} %collective-permute-done.34.refs_1_, f32[64,256]{1,0:T(8,128)S(1)} %collective-permute-done.35.refs_2_), custom_call_target="tpu_custom_call" | custom-call | flops 1000000000 | bytes 524288 | tf_op jit(solution)/shard_map/pallas_call | solution.py:60
  127.1 2.9 %shard_map.79 = f32[144,128]{1,0:T(8,128)S(1)} custom-call(f32[16,4096]{1,0:T(8,128)S(1)} %bitcast.5, f32[256,256]{1,0:T(8,128)S(1)} %get-tuple-element.97.refs_0_, f32[256,256]{1,0:T(8,128)S(1)} %get-tuple-element.100.refs_1_, f32[256,256]{1,0:T(8,128)S(1)} %get-tuple-element.105.refs_2_, f32[256,256]{1,0:T(8,128)S(1)} %get-tuple-element.107.block_ref.refs_3_, ...), custom_call_target="tpu_custom_call" | custom-call | flops 1500000000 | bytes 3219968 | tf_op jit(solution)/shard_map/pallas_call | solution.py:60
  130.7 2.9 %shard_map.78.first_ref = f32[144,128]{1,0:T(8,128)S(1)} custom-call(f32[16,4096]{1,0:T(8,128)S(1)} %bitcast.6, f32[256,256]{1,0:T(8,128)S(1)} %get-tuple-element.97.refs_0_, f32[256,256]{1,0:T(8,128)S(1)} %get-tuple-element.100.refs_1_, f32[256,256]{1,0:T(8,128)S(1)} %get-tuple-element.105.refs_2_, f32[256,256]{1,0:T(8,128)S(1)} %get-tuple-element.107.block_ref.refs_3_, ...), custom_call_target="tpu_custom_call" | custom-call | flops 1500000000 | bytes 3219968 | tf_op jit(solution)/shard_map/pallas_call | solution.py:60
  133.7 2.7 %collective-permute-done.38.second_ref = f32[144,128]{1,0:T(8,128)S(1)} collective-permute-done((f32[144,128]{1,0:T(8,128)S(1)}, f32[144,128]{1,0:T(8,128)S(1)}, u32[]{:S(2)}, u32[]{:S(2)}) %collective-permute-start.38) | collective-permute-done | bytes 73760 | tf_op jit(solution)/shard_map/ppermute | solution.py:165
  (103 shorter events, 40.7 us)
Async XLA Ops:
  1.6 5.3 %collective-permute-start = (f32[64,256]{1,0:T(8,128)S(1)}, f32[64,256]{1,0:T(8,128)S(1)}, u32[]{:S(2)}, u32[]{:S(2)}) collective-permute-start(f32[64,256]{1,0:T(8,128)S(1)} %shard_map.55.gram_ref), channel_id=1, source_target_pairs={{0,4},{4,0},{8,12},{12,8},{1,5},{5,1},{9,13},{13,9},{2,6},{6,2},{1... | collective-permute-start | bytes 196616 | tf_op jit(solution)/shard_map/ppermute | solution.py:165
  7.0 8.7 %collective-permute-start.1 = (f32[256,256]{1,0:T(8,128)S(1)}, f32[256,256]{1,0:T(8,128)S(1)}, u32[]{:S(2)}, u32[]{:S(2)}) collective-permute-start(f32[256,256]{1,0:T(8,128)S(1)} %get-tuple-element.64), channel_id=1, source_target_pairs={{0,4},{4,0},{8,12},{12,8},{1,5},{5,1},{9,13},{13,9},{2,6},{6,2},{1... | collective-permute-start | bytes 786440 | tf_op jit(solution)/shard_map/ppermute | solution.py:165
  9.1 5.8 %collective-permute-start.2 = (f32[64,256]{1,0:T(8,128)S(1)}, f32[64,256]{1,0:T(8,128)S(1)}, u32[]{:S(2)}, u32[]{:S(2)}) collective-permute-start(f32[64,256]{1,0:T(8,128)S(1)} %add.39), channel_id=1, source_target_pairs={{0,8},{4,12},{8,0},{12,4},{1,9},{5,13},{9,1},{13,5},{2,10},{6,14},... | collective-permute-start | bytes 196616 | tf_op jit(solution)/shard_map/ppermute | solution.py:165
  15.7 18.0 %collective-permute-start.3 = (f32[512,256]{1,0:T(8,128)S(1)}, f32[512,256]{1,0:T(8,128)S(1)}, u32[]{:S(2)}, u32[]{:S(2)}) collective-permute-start(f32[512,256]{1,0:T(8,128)S(1)} %get-tuple-element.66), channel_id=1, source_target_pairs={{0,4},{4,0},{8,12},{12,8},{1,5},{5,1},{9,13},{13,9},{2,6},{6,2},{1... | collective-permute-start | bytes 1572872 | tf_op jit(solution)/shard_map/ppermute | solution.py:165
  18.5 15.1 %collective-permute-start.7 = (f32[256,256]{1,0:T(8,128)S(1)}, f32[256,256]{1,0:T(8,128)S(1)}, u32[]{:S(2)}, u32[]{:S(2)}) collective-permute-start(f32[256,256]{1,0:T(8,128)S(1)} %add.40.first_ref), channel_id=1, source_target_pairs={{0,8},{4,12},{8,0},{12,4},{1,9},{5,13},{9,1},{13,5},{2,10},{6,14},... | collective-permute-start | bytes 786440 | tf_op jit(solution)/shard_map/ppermute | solution.py:165
  20.0 4.3 %collective-permute-start.4 = (f32[64,256]{1,0:T(8,128)S(1)}, f32[64,256]{1,0:T(8,128)S(1)}, u32[]{:S(2)}, u32[]{:S(2)}) collective-permute-start(f32[64,256]{1,0:T(8,128)S(1)} %add.41.own_ref), channel_id=1, source_target_pairs={{0,2},{2,0},{1,3},{3,1},{4,6},{6,4},{5,7},{7,5},{8,10},{10,8},{9,1... | collective-permute-start | bytes 196616 | tf_op jit(solution)/shard_map/ppermute | solution.py:165
  21.5 3.1 %collective-permute-start.5 = (f32[64,256]{1,0:T(8,128)S(1)}, f32[64,256]{1,0:T(8,128)S(1)}, u32[]{:S(2)}, u32[]{:S(2)}) collective-permute-start(f32[64,256]{1,0:T(8,128)S(1)} %add.41.own_ref), channel_id=1, source_target_pairs={{0,1},{1,0},{2,3},{3,2},{4,5},{5,4},{6,7},{7,6},{8,9},{9,8},{10,11... | collective-permute-start | bytes 196616 | tf_op jit(solution)/shard_map/ppermute | solution.py:165
  36.3 5.6 %collective-permute-start.9 = (f32[128,256]{1,0:T(8,128)S(1)}, f32[128,256]{1,0:T(8,128)S(1)}, u32[]{:S(2)}, u32[]{:S(2)}) collective-permute-start(f32[128,256]{1,0:T(8,128)S(1)} %get-tuple-element.72), channel_id=1, source_target_pairs={{0,2},{2,0},{1,3},{3,1},{4,6},{6,4},{5,7},{7,5},{8,10},{10,8},{9,1... | collective-permute-start | bytes 393224 | tf_op jit(solution)/shard_map/ppermute | solution.py:165
  37.9 6.7 %collective-permute-start.12 = (f32[128,256]{1,0:T(8,128)S(1)}, f32[128,256]{1,0:T(8,128)S(1)}, u32[]{:S(2)}, u32[]{:S(2)}) collective-permute-start(f32[128,256]{1,0:T(8,128)S(1)} %get-tuple-element.75), channel_id=1, source_target_pairs={{0,4},{4,0},{8,12},{12,8},{1,5},{5,1},{9,13},{13,9},{2,6},{6,2},{1... | collective-permute-start | bytes 393224 | tf_op jit(solution)/shard_map/ppermute | solution.py:165
  42.0 5.6 %collective-permute-start.10 = (f32[128,256]{1,0:T(8,128)S(1)}, f32[128,256]{1,0:T(8,128)S(1)}, u32[]{:S(2)}, u32[]{:S(2)}) collective-permute-start(f32[128,256]{1,0:T(8,128)S(1)} %add.42), channel_id=1, source_target_pairs={{0,4},{4,0},{8,12},{12,8},{1,5},{5,1},{9,13},{13,9},{2,6},{6,2},{1... | collective-permute-start | bytes 393224 | tf_op jit(solution)/shard_map/ppermute | solution.py:165
  44.6 5.0 %collective-permute-start.13 = (f32[128,256]{1,0:T(8,128)S(1)}, f32[128,256]{1,0:T(8,128)S(1)}, u32[]{:S(2)}, u32[]{:S(2)}) collective-permute-start(f32[128,256]{1,0:T(8,128)S(1)} %add.44), channel_id=1, source_target_pairs={{0,2},{2,0},{1,3},{3,1},{4,6},{6,4},{5,7},{7,5},{8,10},{10,8},{9,1... | collective-permute-start | bytes 393224 | tf_op jit(solution)/shard_map/ppermute | solution.py:165
  49.7 3.6 %collective-permute-start.14 = (f32[256,256]{1,0:T(8,128)S(1)}, f32[256,256]{1,0:T(8,128)S(1)}, u32[]{:S(2)}, u32[]{:S(2)}) collective-permute-start(f32[256,256]{1,0:T(8,128)S(1)} %pad_maximum_fusion.stack_ref), channel_id=1, source_target_pairs={{0,1},{1,0},{2,3},{3,2},{4,5},{5,4},{6,7},{7,6},{8,9},{9,8},{10,11... | collective-permute-start | bytes 786440 | tf_op jit(solution)/shard_map/ppermute | solution.py:165
  49.8 5.9 %collective-permute-start.11 = (f32[128,256]{1,0:T(8,128)S(1)}, f32[128,256]{1,0:T(8,128)S(1)}, u32[]{:S(2)}, u32[]{:S(2)}) collective-permute-start(f32[128,256]{1,0:T(8,128)S(1)} %add.43), channel_id=1, source_target_pairs={{0,2},{2,0},{1,3},{3,1},{4,6},{6,4},{5,7},{7,5},{8,10},{10,8},{9,1... | collective-permute-start | bytes 393224 | tf_op jit(solution)/shard_map/ppermute | solution.py:165
  51.3 5.6 %collective-permute-start.15 = (f32[128,256]{1,0:T(8,128)S(1)}, f32[128,256]{1,0:T(8,128)S(1)}, u32[]{:S(2)}, u32[]{:S(2)}) collective-permute-start(f32[128,256]{1,0:T(8,128)S(1)} %add.45), channel_id=1, source_target_pairs={{0,4},{4,0},{8,12},{12,8},{1,5},{5,1},{9,13},{13,9},{2,6},{6,2},{1... | collective-permute-start | bytes 393224 | tf_op jit(solution)/shard_map/ppermute | solution.py:165
  59.4 6.5 %collective-permute-start.17 = (f32[64,256]{1,0:T(8,128)S(1)}, f32[64,256]{1,0:T(8,128)S(1)}, u32[]{:S(2)}, u32[]{:S(2)}) collective-permute-start(f32[64,256]{1,0:T(8,128)S(1)} %get-tuple-element.85), channel_id=1, source_target_pairs={{0,8},{4,12},{8,0},{12,4},{1,9},{5,13},{9,1},{13,5},{2,10},{6,14},... | collective-permute-start | bytes 196616 | tf_op jit(solution)/shard_map/ppermute | solution.py:165
  66.0 12.7 %collective-permute-start.21 = (f32[128,512]{1,0:T(8,128)S(1)}, f32[128,512]{1,0:T(8,128)S(1)}, u32[]{:S(2)}, u32[]{:S(2)}) collective-permute-start(f32[128,512]{1,0:T(8,128)S(1)} %get-tuple-element.88), channel_id=1, source_target_pairs={{0,4},{4,0},{8,12},{12,8},{1,5},{5,1},{9,13},{13,9},{2,6},{6,2},{1... | collective-permute-start | bytes 786440 | tf_op jit(solution)/shard_map/ppermute | solution.py:165
  66.0 14.9 %collective-permute-start.22 = (f32[256,256]{1,0:T(8,128)S(1)}, f32[256,256]{1,0:T(8,128)S(1)}, u32[]{:S(2)}, u32[]{:S(2)}) collective-permute-start(f32[256,256]{1,0:T(8,128)S(1)} %shard_map.66.first_ref), channel_id=1, source_target_pairs={{0,8},{4,12},{8,0},{12,4},{1,9},{5,13},{9,1},{13,5},{2,10},{6,14},... | collective-permute-start | bytes 786440 | tf_op jit(solution)/shard_map/ppermute | solution.py:165
  68.4 4.3 %collective-permute-start.18 = (f32[64,256]{1,0:T(8,128)S(1)}, f32[64,256]{1,0:T(8,128)S(1)}, u32[]{:S(2)}, u32[]{:S(2)}) collective-permute-start(f32[64,256]{1,0:T(8,128)S(1)} %add.46.own_ref), channel_id=1, source_target_pairs={{0,2},{2,0},{1,3},{3,1},{4,6},{6,4},{5,7},{7,5},{8,10},{10,8},{9,1... | collective-permute-start | bytes 196616 | tf_op jit(solution)/shard_map/ppermute | solution.py:165
  69.7 3.0 %collective-permute-start.19 = (f32[64,256]{1,0:T(8,128)S(1)}, f32[64,256]{1,0:T(8,128)S(1)}, u32[]{:S(2)}, u32[]{:S(2)}) collective-permute-start(f32[64,256]{1,0:T(8,128)S(1)} %add.46.own_ref), channel_id=1, source_target_pairs={{0,1},{1,0},{2,3},{3,2},{4,5},{5,4},{6,7},{7,6},{8,9},{9,8},{10,11... | collective-permute-start | bytes 196616 | tf_op jit(solution)/shard_map/ppermute | solution.py:165
  83.6 5.6 %collective-permute-start.24 = (f32[128,256]{1,0:T(8,128)S(1)}, f32[128,256]{1,0:T(8,128)S(1)}, u32[]{:S(2)}, u32[]{:S(2)}) collective-permute-start(f32[128,256]{1,0:T(8,128)S(1)} %get-tuple-element.91), channel_id=1, source_target_pairs={{0,2},{2,0},{1,3},{3,1},{4,6},{6,4},{5,7},{7,5},{8,10},{10,8},{9,1... | collective-permute-start | bytes 393224 | tf_op jit(solution)/shard_map/ppermute | solution.py:165
  84.1 5.3 %collective-permute-start.26 = (f32[128,256]{1,0:T(8,128)S(1)}, f32[128,256]{1,0:T(8,128)S(1)}, u32[]{:S(2)}, u32[]{:S(2)}) collective-permute-start(f32[128,256]{1,0:T(8,128)S(1)} %get-tuple-element.96), channel_id=1, source_target_pairs={{0,4},{4,0},{8,12},{12,8},{1,5},{5,1},{9,13},{13,9},{2,6},{6,2},{1... | collective-permute-start | bytes 393224 | tf_op jit(solution)/shard_map/ppermute | solution.py:165
  89.2 5.7 %collective-permute-start.25 = (f32[128,256]{1,0:T(8,128)S(1)}, f32[128,256]{1,0:T(8,128)S(1)}, u32[]{:S(2)}, u32[]{:S(2)}) collective-permute-start(f32[128,256]{1,0:T(8,128)S(1)} %add.47), channel_id=1, source_target_pairs={{0,4},{4,0},{8,12},{12,8},{1,5},{5,1},{9,13},{13,9},{2,6},{6,2},{1... | collective-permute-start | bytes 393224 | tf_op jit(solution)/shard_map/ppermute | solution.py:165
  89.4 5.6 %collective-permute-start.27 = (f32[128,256]{1,0:T(8,128)S(1)}, f32[128,256]{1,0:T(8,128)S(1)}, u32[]{:S(2)}, u32[]{:S(2)}) collective-permute-start(f32[128,256]{1,0:T(8,128)S(1)} %add.49), channel_id=1, source_target_pairs={{0,2},{2,0},{1,3},{3,1},{4,6},{6,4},{5,7},{7,5},{8,10},{10,8},{9,1... | collective-permute-start | bytes 393224 | tf_op jit(solution)/shard_map/ppermute | solution.py:165
  95.0 3.9 %collective-permute-start.28 = (f32[256,256]{1,0:T(8,128)S(1)}, f32[256,256]{1,0:T(8,128)S(1)}, u32[]{:S(2)}, u32[]{:S(2)}) collective-permute-start(f32[256,256]{1,0:T(8,128)S(1)} %pad_maximum_fusion.1.stack_ref), channel_id=1, source_target_pairs={{0,1},{1,0},{2,3},{3,2},{4,5},{5,4},{6,7},{7,6},{8,9},{9,8},{10,11... | collective-permute-start | bytes 786440 | tf_op jit(solution)/shard_map/ppermute | solution.py:165
  95.1 5.9 %collective-permute-start.29 = (f32[128,256]{1,0:T(8,128)S(1)}, f32[128,256]{1,0:T(8,128)S(1)}, u32[]{:S(2)}, u32[]{:S(2)}) collective-permute-start(f32[128,256]{1,0:T(8,128)S(1)} %add.48), channel_id=1, source_target_pairs={{0,2},{2,0},{1,3},{3,1},{4,6},{6,4},{5,7},{7,5},{8,10},{10,8},{9,1... | collective-permute-start | bytes 393224 | tf_op jit(solution)/shard_map/ppermute | solution.py:165
  96.2 5.6 %collective-permute-start.30 = (f32[128,256]{1,0:T(8,128)S(1)}, f32[128,256]{1,0:T(8,128)S(1)}, u32[]{:S(2)}, u32[]{:S(2)}) collective-permute-start(f32[128,256]{1,0:T(8,128)S(1)} %add.50), channel_id=1, source_target_pairs={{0,4},{4,0},{8,12},{12,8},{1,5},{5,1},{9,13},{13,9},{2,6},{6,2},{1... | collective-permute-start | bytes 393224 | tf_op jit(solution)/shard_map/ppermute | solution.py:165
  104.3 6.7 %collective-permute-start.32 = (f32[64,256]{1,0:T(8,128)S(1)}, f32[64,256]{1,0:T(8,128)S(1)}, u32[]{:S(2)}, u32[]{:S(2)}) collective-permute-start(f32[64,256]{1,0:T(8,128)S(1)} %get-tuple-element.109), channel_id=1, source_target_pairs={{0,8},{4,12},{8,0},{12,4},{1,9},{5,13},{9,1},{13,5},{2,10},{6,14},... | collective-permute-start | bytes 196616 | tf_op jit(solution)/shard_map/ppermute | solution.py:165
  111.1 16.0 %collective-permute-start.36 = (f32[256,256]{1,0:T(8,128)S(1)}, f32[256,256]{1,0:T(8,128)S(1)}, u32[]{:S(2)}, u32[]{:S(2)}) collective-permute-start(f32[256,256]{1,0:T(8,128)S(1)} %shard_map.76.refs_4_), channel_id=1, source_target_pairs={{0,8},{4,12},{8,0},{12,4},{1,9},{5,13},{9,1},{13,5},{2,10},{6,14},... | collective-permute-start | bytes 786440 | tf_op jit(solution)/shard_map/ppermute | solution.py:165
  111.5 15.5 %collective-permute-start.37 = (f32[128,512]{1,0:T(8,128)S(1)}, f32[128,512]{1,0:T(8,128)S(1)}, u32[]{:S(2)}, u32[]{:S(2)}) collective-permute-start(f32[128,512]{1,0:T(8,128)S(1)} %get-tuple-element.114), channel_id=1, source_target_pairs={{0,4},{4,0},{8,12},{12,8},{1,5},{5,1},{9,13},{13,9},{2,6},{6,2},{1... | collective-permute-start | bytes 786440 | tf_op jit(solution)/shard_map/ppermute | solution.py:165
  113.4 4.3 %collective-permute-start.33 = (f32[64,256]{1,0:T(8,128)S(1)}, f32[64,256]{1,0:T(8,128)S(1)}, u32[]{:S(2)}, u32[]{:S(2)}) collective-permute-start(f32[64,256]{1,0:T(8,128)S(1)} %add.51.own_ref), channel_id=1, source_target_pairs={{0,2},{2,0},{1,3},{3,1},{4,6},{6,4},{5,7},{7,5},{8,10},{10,8},{9,1... | collective-permute-start | bytes 196616 | tf_op jit(solution)/shard_map/ppermute | solution.py:165
  114.5 3.3 %collective-permute-start.34 = (f32[64,256]{1,0:T(8,128)S(1)}, f32[64,256]{1,0:T(8,128)S(1)}, u32[]{:S(2)}, u32[]{:S(2)}) collective-permute-start(f32[64,256]{1,0:T(8,128)S(1)} %add.51.own_ref), channel_id=1, source_target_pairs={{0,1},{1,0},{2,3},{3,2},{4,5},{5,4},{6,7},{7,6},{8,9},{9,8},{10,11... | collective-permute-start | bytes 196616 | tf_op jit(solution)/shard_map/ppermute | solution.py:165
  130.0 6.4 %collective-permute-start.38 = (f32[144,128]{1,0:T(8,128)S(1)}, f32[144,128]{1,0:T(8,128)S(1)}, u32[]{:S(2)}, u32[]{:S(2)}) collective-permute-start(f32[144,128]{1,0:T(8,128)S(1)} %shard_map.79), channel_id=1, source_target_pairs={{0,8},{4,12},{8,0},{12,4},{1,9},{5,13},{9,1},{13,5},{2,10},{6,14},... | collective-permute-start | bytes 221192 | tf_op jit(solution)/shard_map/ppermute | solution.py:165
  (12 other events, 51.1 us)

commit v7 on v6

--- a/solution.py
+++ b/solution.py
@@ -393,15 +393,11 @@
     out_ref, score_ref = refs[-2:]
     mine, upper, _, _ = pair_sides()
     which = upper ^ int(sent)
-    group = QH // KVH
     tokens = own_ref.shape[1]
     half, width = tokens // 2, length_ref.shape[1]
     local = lanes(which)
     coef = product(first_ref[local, :] + second_ref[local, :], lower_ref[...], ((1,), (1,)))
-    quer = jnp.concatenate(
-        [query_ref[:, lanes((2 * which + mine) * group + i)] for i in range(group)]
-    )
-    reduced = product(quer, coef, ((1,), (0,))) / math.sqrt(HD)
+    reduced = product(query_ref[lanes(which, width), :], coef, ((1,), (0,))) / math.sqrt(HD)
     reduced = product(reduced, lower_ref[...], ((1,), (0,)))
     for i, block_ref in enumerate(block_refs):
         far, beside = i % 2, i // 2
@@ -430,15 +426,12 @@
 
 
 def merge_kernel(first_ref, second_ref, out_ref):
-    rows = out_ref.shape[1]
     top = jnp.maximum(first_ref[pl.ds(HD, 1), :], second_ref[pl.ds(HD, 1), :])
     one = jnp.exp(first_ref[pl.ds(HD, 1), :] - top)
     two = jnp.exp(second_ref[pl.ds(HD, 1), :] - top)
     total = first_ref[pl.ds(HD + 8, 1), :] * one + second_ref[pl.ds(HD + 8, 1), :] * two
     acc = first_ref[pl.ds(0, HD), :] * one + second_ref[pl.ds(0, HD), :] * two
-    result = (acc / total).T
-    for i in range(QH // KVH):
-        out_ref[0, :, 0, pl.ds(i * HD, HD)] = result[i * rows : (i + 1) * rows, :]
+    out_ref[...] = (acc / total).T
 
 
 def gathered(share):
@@ -450,9 +443,14 @@
     return lax.optimization_barrier((x, *others))[0]
 
 
-def split_kernel(values_ref, kept_ref, first_ref, second_ref):
+def split_kernel(values_ref, query_ref, kept_ref, first_ref, second_ref, order_ref):
     mine, _, _, _ = pair_sides()
+    rows, group = query_ref.shape[0], QH // KVH
     for i, ref in enumerate((first_ref, second_ref)):
+        for k in range(group):
+            order_ref[pl.ds(i * rows * group + k, rows, stride=group), :] = query_ref[
+                :, lanes((2 * i + mine) * group + k)
+            ]
         kept_ref[pl.ds(i * HD, HD), :] = values_ref[:, lanes(2 * i + mine)].T
         ref[...] = values_ref[:, lanes(2 * i + 1 - mine)].T
 
@@ -481,24 +479,29 @@
     )
     gram = gram + swap(gram, "tok", 1)
     proj = keep + swap(after(send, gram), "tok", 1)
-    values_own, *values_send = call(
+    group = QH // KVH
+    values_own, *values_send, ordered = call(
         split_kernel,
-        [vmem(half, tokens)] + [vmem(HD, tokens)] * 2,
+        [vmem(half, tokens)] + [vmem(HD, tokens)] * 2 + [vmem(2 * rows * group, HD)],
         after(values, proj),
+        queries,
     )
     values_other = []
     lower = None
     for step in range(ITERS + 1):
         gram = gram + swap(gram, "tok", 2)
         last = step == ITERS
-        if step != 1:
+        if last:
+            proj, gram = lax.optimization_barrier((proj, gram))
+        elif step == 0:
             proj = after(proj, gram)
             if step == 0:
                 keys_other = swap(after(keys_send, proj), "tok", 1)
         first, second = proj, swap(proj, "tok", 2)
-        if step > 0 and len(values_other) < 2:
-            values_other.append(swap(after(values_send[len(values_other)], proj, gram), "tok", 1))
         parts = gathered(gram)
+        if step > 0:
+            ready = parts[1] if last else gram
+            values_other.append(swap(after(values_send[step - 1], proj, ready), "tok", 1))
         if step == 0 or last:
             lower = inverse_factor(after(parts[0], values_own), *parts[1:])
             first = after(first, lower)
@@ -554,26 +557,27 @@
             flops=400_000_000,
         )
     operands = (
-        queries,
+        ordered,
         *blocks,
         first,
         second,
         lower,
         values_own,
         *values_other,
-        jnp.tile(lengths, QH // KVH)[None, :],
+        jnp.repeat(lengths, group)[None, :],
     )
     send, keep = (
         call(
             functools.partial(attend_kernel, sent),
             vmem(HD + 16, HD),
             *operands,
-            scratch=[(2 * tokens, QH // KVH * rows)],
+            scratch=[(2 * tokens, group * rows)],
             flops=1_500_000_000,
         )
         for sent in (True, False)
     )
-    return call(merge_kernel, vmem(1, rows, 1, half * 4), keep, swap(send, "tok", 2))
+    result = call(merge_kernel, vmem(group * rows, HD), keep, swap(send, "tok", 2))
+    return result.reshape(1, rows, 1, group * HD)
 
 
 def solution(mesh):

time: 137 us -> 136 us (level)
  transfers between devices with their start and end apart: 39 -> 39, of which waited for: 27 -> 29; matrix products, arithmetic and copies ran while one was open for 0% -> 0% of each run, Pallas kernels for 29% -> 29%
where the time goes in v7:
time: 136 us
  waiting for transfers between devices  48.1 us (35%)
  Pallas kernels  46.6 us (34%)
  starting transfers between devices  39.6 us (29%)
    ppermute x39, waiting for transfers between devices, swap(): return lax.ppermute(x, axis, pairs)  48.1 us
    pallas_call x26, Pallas kernels, call(): pl.pallas_call(kernel, out_shape=out_shape, in_specs=[spec] * len(args),...  46.6 us
    ppermute x39, starting transfers between devices, swap(): return lax.ppermute(x, axis, pairs)  39.6 us
  transfers between devices with their start and end apart: 39, of which 29 were waited for; matrix products, arithmetic and copies ran while one was open for 0% of the time, Pallas kernels for 29%

profile of v7, /device:TPU:0, one launch (start us, length us, event | category | flops | bytes accessed | tf_op | source)
XLA Modules:
  0.0 136.3 jit_solution(2171174087563865221)
XLA Ops:
  1.6 3.1 %collective-permute-start = (f32[64,256]{1,0:T(8,128)S(1)}, f32[64,256]{1,0:T(8,128)S(1)}, u32[]{:S(2)}, u32[]{:S(2)}) collective-permute-start(f32[64,256]{1,0:T(8,128)S(1)} %shard_map.55.gram_ref), channel_id=1, source_target_pairs={{0,4},{4,0},{8,12},{12,8},{1,5},{5,1},{9,13},{13,9},{2,6},{6,2},{1... | collective-permute-start | bytes 196616 | tf_op jit(solution)/shard_map/ppermute | solution.py:165
  7.0 2.1 %collective-permute-start.1 = (f32[256,256]{1,0:T(8,128)S(1)}, f32[256,256]{1,0:T(8,128)S(1)}, u32[]{:S(2)}, u32[]{:S(2)}) collective-permute-start(f32[256,256]{1,0:T(8,128)S(1)} %get-tuple-element.64), channel_id=1, source_target_pairs={{0,4},{4,0},{8,12},{12,8},{1,5},{5,1},{9,13},{13,9},{2,6},{6,2},{1... | collective-permute-start | bytes 786440 | tf_op jit(solution)/shard_map/ppermute | solution.py:165
  9.1 2.6 %collective-permute-start.2 = (f32[64,256]{1,0:T(8,128)S(1)}, f32[64,256]{1,0:T(8,128)S(1)}, u32[]{:S(2)}, u32[]{:S(2)}) collective-permute-start(f32[64,256]{1,0:T(8,128)S(1)} %add.39), channel_id=1, source_target_pairs={{0,8},{4,12},{8,0},{12,4},{1,9},{5,13},{9,1},{13,5},{2,10},{6,14},... | collective-permute-start | bytes 196616 | tf_op jit(solution)/shard_map/ppermute | solution.py:165
  11.6 3.2 %collective-permute-done.2 = f32[64,256]{1,0:T(8,128)S(1)} collective-permute-done((f32[64,256]{1,0:T(8,128)S(1)}, f32[64,256]{1,0:T(8,128)S(1)}, u32[]{:S(2)}, u32[]{:S(2)}) %collective-permute-start.2) | collective-permute-done | bytes 65568 | tf_op jit(solution)/shard_map/ppermute | solution.py:165
  15.7 2.8 %collective-permute-start.3 = (f32[512,256]{1,0:T(8,128)S(1)}, f32[512,256]{1,0:T(8,128)S(1)}, u32[]{:S(2)}, u32[]{:S(2)}) collective-permute-start(f32[512,256]{1,0:T(8,128)S(1)} %get-tuple-element.70), channel_id=1, source_target_pairs={{0,4},{4,0},{8,12},{12,8},{1,5},{5,1},{9,13},{13,9},{2,6},{6,2},{1... | collective-permute-start | bytes 1572872 | tf_op jit(solution)/shard_map/ppermute | solution.py:165
  18.5 1.5 %collective-permute-start.7 = (f32[256,256]{1,0:T(8,128)S(1)}, f32[256,256]{1,0:T(8,128)S(1)}, u32[]{:S(2)}, u32[]{:S(2)}) collective-permute-start(f32[256,256]{1,0:T(8,128)S(1)} %add.40.first_ref), channel_id=1, source_target_pairs={{0,8},{4,12},{8,0},{12,4},{1,9},{5,13},{9,1},{13,5},{2,10},{6,14},... | collective-permute-start | bytes 786440 | tf_op jit(solution)/shard_map/ppermute | solution.py:165
  21.5 2.8 %collective-permute-done.4.refs_0_ = f32[64,256]{1,0:T(8,128)S(1)} collective-permute-done((f32[64,256]{1,0:T(8,128)S(1)}, f32[64,256]{1,0:T(8,128)S(1)}, u32[]{:S(2)}, u32[]{:S(2)}) %collective-permute-start.4) | collective-permute-done | bytes 65568 | tf_op jit(solution)/shard_map/ppermute | solution.py:165
  25.6 8.0 %shard_map.58.lower_ref = f32[256,256]{1,0:T(8,128)S(1)} custom-call(f32[64,256]{1,0:T(8,128)S(1)} %add.41.own_ref, f32[64,256]{1,0:T(8,128)S(1)} %collective-permute-done.4.refs_0_, f32[64,256]{1,0:T(8,128)S(1)} %collective-permute-done.5.refs_1_, f32[64,256]{1,0:T(8,128)S(1)} %collective-permute-done.6.refs_2_), custom_call_target="tpu_custom_call" | custom-call | flops 1000000000 | bytes 524288 | tf_op jit(solution)/shard_map/pallas_call | solution.py:60
  36.3 1.5 %collective-permute-start.9 = (f32[128,256]{1,0:T(8,128)S(1)}, f32[128,256]{1,0:T(8,128)S(1)}, u32[]{:S(2)}, u32[]{:S(2)}) collective-permute-start(f32[128,256]{1,0:T(8,128)S(1)} %get-tuple-element.75), channel_id=1, source_target_pairs={{0,2},{2,0},{1,3},{3,1},{4,6},{6,4},{5,7},{7,5},{8,10},{10,8},{9,1... | collective-permute-start | bytes 393224 | tf_op jit(solution)/shard_map/ppermute | solution.py:165
  37.9 2.6 %collective-permute-start.12 = (f32[128,256]{1,0:T(8,128)S(1)}, f32[128,256]{1,0:T(8,128)S(1)}, u32[]{:S(2)}, u32[]{:S(2)}) collective-permute-start(f32[128,256]{1,0:T(8,128)S(1)} %get-tuple-element.78), channel_id=1, source_target_pairs={{0,4},{4,0},{8,12},{12,8},{1,5},{5,1},{9,13},{13,9},{2,6},{6,2},{1... | collective-permute-start | bytes 393224 | tf_op jit(solution)/shard_map/ppermute | solution.py:165
  40.5 1.5 %collective-permute-done.9 = f32[128,256]{1,0:T(8,128)S(1)} collective-permute-done((f32[128,256]{1,0:T(8,128)S(1)}, f32[128,256]{1,0:T(8,128)S(1)}, u32[]{:S(2)}, u32[]{:S(2)}) %collective-permute-start.9) | collective-permute-done | bytes 131104 | tf_op jit(solution)/shard_map/ppermute | solution.py:165
  42.0 2.6 %collective-permute-start.10 = (f32[128,256]{1,0:T(8,128)S(1)}, f32[128,256]{1,0:T(8,128)S(1)}, u32[]{:S(2)}, u32[]{:S(2)}) collective-permute-start(f32[128,256]{1,0:T(8,128)S(1)} %add.42), channel_id=1, source_target_pairs={{0,4},{4,0},{8,12},{12,8},{1,5},{5,1},{9,13},{13,9},{2,6},{6,2},{1... | collective-permute-start | bytes 393224 | tf_op jit(solution)/shard_map/ppermute | solution.py:165
  44.6 1.6 %collective-permute-start.13 = (f32[128,256]{1,0:T(8,128)S(1)}, f32[128,256]{1,0:T(8,128)S(1)}, u32[]{:S(2)}, u32[]{:S(2)}) collective-permute-start(f32[128,256]{1,0:T(8,128)S(1)} %add.44), channel_id=1, source_target_pairs={{0,2},{2,0},{1,3},{3,1},{4,6},{6,4},{5,7},{7,5},{8,10},{10,8},{9,1... | collective-permute-start | bytes 393224 | tf_op jit(solution)/shard_map/ppermute | solution.py:165
  47.6 2.1 %collective-permute-done.13 = f32[128,256]{1,0:T(8,128)S(1)} collective-permute-done((f32[128,256]{1,0:T(8,128)S(1)}, f32[128,256]{1,0:T(8,128)S(1)}, u32[]{:S(2)}, u32[]{:S(2)}) %collective-permute-start.13) | collective-permute-done | bytes 131104 | tf_op jit(solution)/shard_map/ppermute | solution.py:165
  49.8 1.6 %collective-permute-start.11 = (f32[128,256]{1,0:T(8,128)S(1)}, f32[128,256]{1,0:T(8,128)S(1)}, u32[]{:S(2)}, u32[]{:S(2)}) collective-permute-start(f32[128,256]{1,0:T(8,128)S(1)} %add.43), channel_id=1, source_target_pairs={{0,2},{2,0},{1,3},{3,1},{4,6},{6,4},{5,7},{7,5},{8,10},{10,8},{9,1... | collective-permute-start | bytes 393224 | tf_op jit(solution)/shard_map/ppermute | solution.py:165
  51.5 1.7 %shard_map.62 = (f32[256,256]{1,0:T(8,128)}, f32[64,256]{1,0:T(8,128)S(1)}, f32[256,256]{1,0:T(8,128)S(1)}) custom-call(f32[256,256]{1,0:T(8,128)S(1)} %pad_maximum_fusion.stack_ref, f32[256,256]{1,0:T(8,128)S(1)} %shard_map.58.lower_ref, f32[512,256]{1,0:T(8,128)S(1)} %get-tuple-element.67.own_ref, f32[512,256]{1,0:T(8,128)S(1)} %collective-permute-done.3.other_ref), custom_call_target="tpu_custom_call" | custom-call | flops 900000000 | bytes 2162688 | tf_op jit(solution)/shard_map/pallas_call | solution.py:60
  59.4 1.8 %collective-permute-start.17 = (f32[64,256]{1,0:T(8,128)S(1)}, f32[64,256]{1,0:T(8,128)S(1)}, u32[]{:S(2)}, u32[]{:S(2)}) collective-permute-start(f32[64,256]{1,0:T(8,128)S(1)} %get-tuple-element.88), channel_id=1, source_target_pairs={{0,8},{4,12},{8,0},{12,4},{1,9},{5,13},{9,1},{13,5},{2,10},{6,14},... | collective-permute-start | bytes 196616 | tf_op jit(solution)/shard_map/ppermute | solution.py:165
  61.7 4.2 %collective-permute-done.17 = f32[64,256]{1,0:T(8,128)S(1)} collective-permute-done((f32[64,256]{1,0:T(8,128)S(1)}, f32[64,256]{1,0:T(8,128)S(1)}, u32[]{:S(2)}, u32[]{:S(2)}) %collective-permute-start.17) | collective-permute-done | bytes 65568 | tf_op jit(solution)/shard_map/ppermute | solution.py:165
  66.0 2.4 %collective-permute-start.22 = (f32[256,256]{1,0:T(8,128)S(1)}, f32[256,256]{1,0:T(8,128)S(1)}, u32[]{:S(2)}, u32[]{:S(2)}) collective-permute-start(f32[256,256]{1,0:T(8,128)S(1)} %shard_map.66.first_ref), channel_id=1, source_target_pairs={{0,8},{4,12},{8,0},{12,4},{1,9},{5,13},{9,1},{13,5},{2,10},{6,14},... | collective-permute-start | bytes 786440 | tf_op jit(solution)/shard_map/ppermute | solution.py:165
  69.7 3.0 %collective-permute-done.18.refs_0_ = f32[64,256]{1,0:T(8,128)S(1)} collective-permute-done((f32[64,256]{1,0:T(8,128)S(1)}, f32[64,256]{1,0:T(8,128)S(1)}, u32[]{:S(2)}, u32[]{:S(2)}) %collective-permute-start.18) | collective-permute-done | bytes 65568 | tf_op jit(solution)/shard_map/ppermute | solution.py:165
  73.9 4.0 %shard_map.67 = (f32[128,128]{1,0:T(8,128)S(1)}, f32[128,128]{1,0:T(8,128)S(1)}, f32[128,128]{1,0:T(8,128)S(1)}) custom-call(f32[64,256]{1,0:T(8,128)S(1)} %add.46.own_ref, f32[64,256]{1,0:T(8,128)S(1)} %collective-permute-done.18.refs_0_, f32[64,256]{1,0:T(8,128)S(1)} %collective-permute-done.19.refs_1_, f32[64,256]{1,0:T(8,128)S(1)} %collective-permute-done.20.refs_2_), custom_call_target="tpu_custom_call" | custom-call | flops 1000000000 | bytes 458752 | tf_op jit(solution)/shard_map/pallas_call | solution.py:60
  78.6 2.3 %collective-permute-done.22.second_ref = f32[256,256]{1,0:T(8,128)S(1)} collective-permute-done((f32[256,256]{1,0:T(8,128)S(1)}, f32[256,256]{1,0:T(8,128)S(1)}, u32[]{:S(2)}, u32[]{:S(2)}) %collective-permute-start.22) | collective-permute-done | bytes 262176 | tf_op jit(solution)/shard_map/ppermute | solution.py:165
  84.4 4.9 %collective-permute-done.24 = f32[128,256]{1,0:T(8,128)S(1)} collective-permute-done((f32[128,256]{1,0:T(8,128)S(1)}, f32[128,256]{1,0:T(8,128)S(1)}, u32[]{:S(2)}, u32[]{:S(2)}) %collective-permute-start.24) | collective-permute-done | bytes 131104 | tf_op jit(solution)/shard_map/ppermute | solution.py:165
  89.4 1.7 %collective-permute-start.27 = (f32[128,256]{1,0:T(8,128)S(1)}, f32[128,256]{1,0:T(8,128)S(1)}, u32[]{:S(2)}, u32[]{:S(2)}) collective-permute-start(f32[128,256]{1,0:T(8,128)S(1)} %add.49), channel_id=1, source_target_pairs={{0,2},{2,0},{1,3},{3,1},{4,6},{6,4},{5,7},{7,5},{8,10},{10,8},{9,1... | collective-permute-start | bytes 393224 | tf_op jit(solution)/shard_map/ppermute | solution.py:165
  91.1 3.9 %shard_map.71.lower_ref = f32[256,256]{1,0:T(8,128)S(1)} custom-call(f32[128,128]{1,0:T(8,128)S(1)} %get-tuple-element.89.tile_ref, f32[128,128]{1,0:T(8,128)S(1)} %get-tuple-element.95.cross_ref, f32[128,128]{1,0:T(8,128)S(1)} %get-tuple-element.96.left_ref), custom_call_target="tpu_custom_call" | custom-call | flops 1000000000 | bytes 458752 | tf_op jit(solution)/shard_map/pallas_call | solution.py:60
  104.3 1.8 %collective-permute-start.32 = (f32[64,256]{1,0:T(8,128)S(1)}, f32[64,256]{1,0:T(8,128)S(1)}, u32[]{:S(2)}, u32[]{:S(2)}) collective-permute-start(f32[64,256]{1,0:T(8,128)S(1)} %get-tuple-element.112), channel_id=1, source_target_pairs={{0,8},{4,12},{8,0},{12,4},{1,9},{5,13},{9,1},{13,5},{2,10},{6,14},... | collective-permute-start | bytes 196616 | tf_op jit(solution)/shard_map/ppermute | solution.py:165
  106.6 4.5 %collective-permute-done.32 = f32[64,256]{1,0:T(8,128)S(1)} collective-permute-done((f32[64,256]{1,0:T(8,128)S(1)}, f32[64,256]{1,0:T(8,128)S(1)}, u32[]{:S(2)}, u32[]{:S(2)}) %collective-permute-start.32) | collective-permute-done | bytes 65568 | tf_op jit(solution)/shard_map/ppermute | solution.py:165
  112.5 2.9 %collective-permute-done.33.refs_0_ = f32[64,256]{1,0:T(8,128)S(1)} collective-permute-done((f32[64,256]{1,0:T(8,128)S(1)}, f32[64,256]{1,0:T(8,128)S(1)}, u32[]{:S(2)}, u32[]{:S(2)}) %collective-permute-start.33) | collective-permute-done | bytes 65568 | tf_op jit(solution)/shard_map/ppermute | solution.py:165
  116.9 8.0 %shard_map.77.refs_6_ = f32[256,256]{1,0:T(8,128)S(1)} custom-call(f32[64,256]{1,0:T(8,128)S(1)} %add.51.own_ref, f32[64,256]{1,0:T(8,128)S(1)} %collective-permute-done.33.refs_0_, f32[64,256]{1,0:T(8,128)S(1)} %collective-permute-done.34.refs_1_, f32[64,256]{1,0:T(8,128)S(1)} %collective-permute-done.35.refs_2_), custom_call_target="tpu_custom_call" | custom-call | flops 1000000000 | bytes 524288 | tf_op jit(solution)/shard_map/pallas_call | solution.py:60
  126.1 2.9 %shard_map.79 = f32[144,128]{1,0:T(8,128)S(1)} custom-call(f32[256,128]{1,0:T(8,128)S(1)} %get-tuple-element.66.query_ref, f32[256,256]{1,0:T(8,128)S(1)} %get-tuple-element.100.refs_0_, f32[256,256]{1,0:T(8,128)S(1)} %get-tuple-element.103.refs_1_, f32[256,256]{1,0:T(8,128)S(1)} %get-tuple-element.108.refs_2_, ...), custom_call_target="tpu_custom_call" | custom-call | flops 1500000000 | bytes 3088896 | tf_op jit(solution)/shard_map/pallas_call | solution.py:60
  130.2 2.9 %shard_map.78.first_ref = f32[144,128]{1,0:T(8,128)S(1)} custom-call(f32[256,128]{1,0:T(8,128)S(1)} %get-tuple-element.66.query_ref, f32[256,256]{1,0:T(8,128)S(1)} %get-tuple-element.100.refs_0_, f32[256,256]{1,0:T(8,128)S(1)} %get-tuple-element.103.refs_1_, f32[256,256]{1,0:T(8,128)S(1)} %get-tuple-element.108.refs_2_, ...), custom_call_target="tpu_custom_call" | custom-call | flops 1500000000 | bytes 3088896 | tf_op jit(solution)/shard_map/pallas_call | solution.py:60
  133.2 2.4 %collective-permute-done.38.second_ref = f32[144,128]{1,0:T(8,128)S(1)} collective-permute-done((f32[144,128]{1,0:T(8,128)S(1)}, f32[144,128]{1,0:T(8,128)S(1)}, u32[]{:S(2)}, u32[]{:S(2)}) %collective-permute-start.38) | collective-permute-done | bytes 73760 | tf_op jit(solution)/shard_map/ppermute | solution.py:165
  (103 shorter events, 40.9 us)
Async XLA Ops:
  1.6 5.3 %collective-permute-start = (f32[64,256]{1,0:T(8,128)S(1)}, f32[64,256]{1,0:T(8,128)S(1)}, u32[]{:S(2)}, u32[]{:S(2)}) collective-permute-start(f32[64,256]{1,0:T(8,128)S(1)} %shard_map.55.gram_ref), channel_id=1, source_target_pairs={{0,4},{4,0},{8,12},{12,8},{1,5},{5,1},{9,13},{13,9},{2,6},{6,2},{1... | collective-permute-start | bytes 196616 | tf_op jit(solution)/shard_map/ppermute | solution.py:165
  7.0 8.7 %collective-permute-start.1 = (f32[256,256]{1,0:T(8,128)S(1)}, f32[256,256]{1,0:T(8,128)S(1)}, u32[]{:S(2)}, u32[]{:S(2)}) collective-permute-start(f32[256,256]{1,0:T(8,128)S(1)} %get-tuple-element.64), channel_id=1, source_target_pairs={{0,4},{4,0},{8,12},{12,8},{1,5},{5,1},{9,13},{13,9},{2,6},{6,2},{1... | collective-permute-start | bytes 786440 | tf_op jit(solution)/shard_map/ppermute | solution.py:165
  9.1 5.8 %collective-permute-start.2 = (f32[64,256]{1,0:T(8,128)S(1)}, f32[64,256]{1,0:T(8,128)S(1)}, u32[]{:S(2)}, u32[]{:S(2)}) collective-permute-start(f32[64,256]{1,0:T(8,128)S(1)} %add.39), channel_id=1, source_target_pairs={{0,8},{4,12},{8,0},{12,4},{1,9},{5,13},{9,1},{13,5},{2,10},{6,14},... | collective-permute-start | bytes 196616 | tf_op jit(solution)/shard_map/ppermute | solution.py:165
  15.7 18.0 %collective-permute-start.3 = (f32[512,256]{1,0:T(8,128)S(1)}, f32[512,256]{1,0:T(8,128)S(1)}, u32[]{:S(2)}, u32[]{:S(2)}) collective-permute-start(f32[512,256]{1,0:T(8,128)S(1)} %get-tuple-element.70), channel_id=1, source_target_pairs={{0,4},{4,0},{8,12},{12,8},{1,5},{5,1},{9,13},{13,9},{2,6},{6,2},{1... | collective-permute-start | bytes 1572872 | tf_op jit(solution)/shard_map/ppermute | solution.py:165
  18.5 15.1 %collective-permute-start.7 = (f32[256,256]{1,0:T(8,128)S(1)}, f32[256,256]{1,0:T(8,128)S(1)}, u32[]{:S(2)}, u32[]{:S(2)}) collective-permute-start(f32[256,256]{1,0:T(8,128)S(1)} %add.40.first_ref), channel_id=1, source_target_pairs={{0,8},{4,12},{8,0},{12,4},{1,9},{5,13},{9,1},{13,5},{2,10},{6,14},... | collective-permute-start | bytes 786440 | tf_op jit(solution)/shard_map/ppermute | solution.py:165
  20.0 4.3 %collective-permute-start.4 = (f32[64,256]{1,0:T(8,128)S(1)}, f32[64,256]{1,0:T(8,128)S(1)}, u32[]{:S(2)}, u32[]{:S(2)}) collective-permute-start(f32[64,256]{1,0:T(8,128)S(1)} %add.41.own_ref), channel_id=1, source_target_pairs={{0,2},{2,0},{1,3},{3,1},{4,6},{6,4},{5,7},{7,5},{8,10},{10,8},{9,1... | collective-permute-start | bytes 196616 | tf_op jit(solution)/shard_map/ppermute | solution.py:165
  21.5 3.2 %collective-permute-start.5 = (f32[64,256]{1,0:T(8,128)S(1)}, f32[64,256]{1,0:T(8,128)S(1)}, u32[]{:S(2)}, u32[]{:S(2)}) collective-permute-start(f32[64,256]{1,0:T(8,128)S(1)} %add.41.own_ref), channel_id=1, source_target_pairs={{0,1},{1,0},{2,3},{3,2},{4,5},{5,4},{6,7},{7,6},{8,9},{9,8},{10,11... | collective-permute-start | bytes 196616 | tf_op jit(solution)/shard_map/ppermute | solution.py:165
  34.3 2.0 %collective-permute-start.8 = (f32[512,256]{1,0:T(8,128)S(1)}, f32[512,256]{1,0:T(8,128)S(1)}, u32[]{:S(2)}, u32[]{:S(2)}) collective-permute-start(f32[512,256]{1,0:T(8,128)S(1)} %shard_map.60), channel_id=1, source_target_pairs={{0,1},{1,0},{2,3},{3,2},{4,5},{5,4},{6,7},{7,6},{8,9},{9,8},{10,11... | collective-permute-start | bytes 1572872 | tf_op jit(solution)/shard_map/ppermute | solution.py:165
  36.3 5.6 %collective-permute-start.9 = (f32[128,256]{1,0:T(8,128)S(1)}, f32[128,256]{1,0:T(8,128)S(1)}, u32[]{:S(2)}, u32[]{:S(2)}) collective-permute-start(f32[128,256]{1,0:T(8,128)S(1)} %get-tuple-element.75), channel_id=1, source_target_pairs={{0,2},{2,0},{1,3},{3,1},{4,6},{6,4},{5,7},{7,5},{8,10},{10,8},{9,1... | collective-permute-start | bytes 393224 | tf_op jit(solution)/shard_map/ppermute | solution.py:165
  37.9 6.7 %collective-permute-start.12 = (f32[128,256]{1,0:T(8,128)S(1)}, f32[128,256]{1,0:T(8,128)S(1)}, u32[]{:S(2)}, u32[]{:S(2)}) collective-permute-start(f32[128,256]{1,0:T(8,128)S(1)} %get-tuple-element.78), channel_id=1, source_target_pairs={{0,4},{4,0},{8,12},{12,8},{1,5},{5,1},{9,13},{13,9},{2,6},{6,2},{1... | collective-permute-start | bytes 393224 | tf_op jit(solution)/shard_map/ppermute | solution.py:165
  42.0 5.6 %collective-permute-start.10 = (f32[128,256]{1,0:T(8,128)S(1)}, f32[128,256]{1,0:T(8,128)S(1)}, u32[]{:S(2)}, u32[]{:S(2)}) collective-permute-start(f32[128,256]{1,0:T(8,128)S(1)} %add.42), channel_id=1, source_target_pairs={{0,4},{4,0},{8,12},{12,8},{1,5},{5,1},{9,13},{13,9},{2,6},{6,2},{1... | collective-permute-start | bytes 393224 | tf_op jit(solution)/shard_map/ppermute | solution.py:165
  44.6 5.0 %collective-permute-start.13 = (f32[128,256]{1,0:T(8,128)S(1)}, f32[128,256]{1,0:T(8,128)S(1)}, u32[]{:S(2)}, u32[]{:S(2)}) collective-permute-start(f32[128,256]{1,0:T(8,128)S(1)} %add.44), channel_id=1, source_target_pairs={{0,2},{2,0},{1,3},{3,1},{4,6},{6,4},{5,7},{7,5},{8,10},{10,8},{9,1... | collective-permute-start | bytes 393224 | tf_op jit(solution)/shard_map/ppermute | solution.py:165
  49.7 3.6 %collective-permute-start.14 = (f32[256,256]{1,0:T(8,128)S(1)}, f32[256,256]{1,0:T(8,128)S(1)}, u32[]{:S(2)}, u32[]{:S(2)}) collective-permute-start(f32[256,256]{1,0:T(8,128)S(1)} %pad_maximum_fusion.stack_ref), channel_id=1, source_target_pairs={{0,1},{1,0},{2,3},{3,2},{4,5},{5,4},{6,7},{7,6},{8,9},{9,8},{10,11... | collective-permute-start | bytes 786440 | tf_op jit(solution)/shard_map/ppermute | solution.py:165
  49.8 5.9 %collective-permute-start.11 = (f32[128,256]{1,0:T(8,128)S(1)}, f32[128,256]{1,0:T(8,128)S(1)}, u32[]{:S(2)}, u32[]{:S(2)}) collective-permute-start(f32[128,256]{1,0:T(8,128)S(1)} %add.43), channel_id=1, source_target_pairs={{0,2},{2,0},{1,3},{3,1},{4,6},{6,4},{5,7},{7,5},{8,10},{10,8},{9,1... | collective-permute-start | bytes 393224 | tf_op jit(solution)/shard_map/ppermute | solution.py:165
  51.3 5.6 %collective-permute-start.15 = (f32[128,256]{1,0:T(8,128)S(1)}, f32[128,256]{1,0:T(8,128)S(1)}, u32[]{:S(2)}, u32[]{:S(2)}) collective-permute-start(f32[128,256]{1,0:T(8,128)S(1)} %add.45), channel_id=1, source_target_pairs={{0,4},{4,0},{8,12},{12,8},{1,5},{5,1},{9,13},{13,9},{2,6},{6,2},{1... | collective-permute-start | bytes 393224 | tf_op jit(solution)/shard_map/ppermute | solution.py:165
  59.4 6.5 %collective-permute-start.17 = (f32[64,256]{1,0:T(8,128)S(1)}, f32[64,256]{1,0:T(8,128)S(1)}, u32[]{:S(2)}, u32[]{:S(2)}) collective-permute-start(f32[64,256]{1,0:T(8,128)S(1)} %get-tuple-element.88), channel_id=1, source_target_pairs={{0,8},{4,12},{8,0},{12,4},{1,9},{5,13},{9,1},{13,5},{2,10},{6,14},... | collective-permute-start | bytes 196616 | tf_op jit(solution)/shard_map/ppermute | solution.py:165
  66.0 12.7 %collective-permute-start.21 = (f32[128,512]{1,0:T(8,128)S(1)}, f32[128,512]{1,0:T(8,128)S(1)}, u32[]{:S(2)}, u32[]{:S(2)}) collective-permute-start(f32[128,512]{1,0:T(8,128)S(1)} %get-tuple-element.91), channel_id=1, source_target_pairs={{0,4},{4,0},{8,12},{12,8},{1,5},{5,1},{9,13},{13,9},{2,6},{6,2},{1... | collective-permute-start | bytes 786440 | tf_op jit(solution)/shard_map/ppermute | solution.py:165
  66.0 14.9 %collective-permute-start.22 = (f32[256,256]{1,0:T(8,128)S(1)}, f32[256,256]{1,0:T(8,128)S(1)}, u32[]{:S(2)}, u32[]{:S(2)}) collective-permute-start(f32[256,256]{1,0:T(8,128)S(1)} %shard_map.66.first_ref), channel_id=1, source_target_pairs={{0,8},{4,12},{8,0},{12,4},{1,9},{5,13},{9,1},{13,5},{2,10},{6,14},... | collective-permute-start | bytes 786440 | tf_op jit(solution)/shard_map/ppermute | solution.py:165
  68.4 4.3 %collective-permute-start.18 = (f32[64,256]{1,0:T(8,128)S(1)}, f32[64,256]{1,0:T(8,128)S(1)}, u32[]{:S(2)}, u32[]{:S(2)}) collective-permute-start(f32[64,256]{1,0:T(8,128)S(1)} %add.46.own_ref), channel_id=1, source_target_pairs={{0,2},{2,0},{1,3},{3,1},{4,6},{6,4},{5,7},{7,5},{8,10},{10,8},{9,1... | collective-permute-start | bytes 196616 | tf_op jit(solution)/shard_map/ppermute | solution.py:165
  69.7 3.0 %collective-permute-start.19 = (f32[64,256]{1,0:T(8,128)S(1)}, f32[64,256]{1,0:T(8,128)S(1)}, u32[]{:S(2)}, u32[]{:S(2)}) collective-permute-start(f32[64,256]{1,0:T(8,128)S(1)} %add.46.own_ref), channel_id=1, source_target_pairs={{0,1},{1,0},{2,3},{3,2},{4,5},{5,4},{6,7},{7,6},{8,9},{9,8},{10,11... | collective-permute-start | bytes 196616 | tf_op jit(solution)/shard_map/ppermute | solution.py:165
  83.6 5.6 %collective-permute-start.24 = (f32[128,256]{1,0:T(8,128)S(1)}, f32[128,256]{1,0:T(8,128)S(1)}, u32[]{:S(2)}, u32[]{:S(2)}) collective-permute-start(f32[128,256]{1,0:T(8,128)S(1)} %get-tuple-element.94), channel_id=1, source_target_pairs={{0,2},{2,0},{1,3},{3,1},{4,6},{6,4},{5,7},{7,5},{8,10},{10,8},{9,1... | collective-permute-start | bytes 393224 | tf_op jit(solution)/shard_map/ppermute | solution.py:165
  84.1 5.3 %collective-permute-start.26 = (f32[128,256]{1,0:T(8,128)S(1)}, f32[128,256]{1,0:T(8,128)S(1)}, u32[]{:S(2)}, u32[]{:S(2)}) collective-permute-start(f32[128,256]{1,0:T(8,128)S(1)} %get-tuple-element.99), channel_id=1, source_target_pairs={{0,4},{4,0},{8,12},{12,8},{1,5},{5,1},{9,13},{13,9},{2,6},{6,2},{1... | collective-permute-start | bytes 393224 | tf_op jit(solution)/shard_map/ppermute | solution.py:165
  89.2 5.7 %collective-permute-start.25 = (f32[128,256]{1,0:T(8,128)S(1)}, f32[128,256]{1,0:T(8,128)S(1)}, u32[]{:S(2)}, u32[]{:S(2)}) collective-permute-start(f32[128,256]{1,0:T(8,128)S(1)} %add.47), channel_id=1, source_target_pairs={{0,4},{4,0},{8,12},{12,8},{1,5},{5,1},{9,13},{13,9},{2,6},{6,2},{1... | collective-permute-start | bytes 393224 | tf_op jit(solution)/shard_map/ppermute | solution.py:165
  89.4 5.6 %collective-permute-start.27 = (f32[128,256]{1,0:T(8,128)S(1)}, f32[128,256]{1,0:T(8,128)S(1)}, u32[]{:S(2)}, u32[]{:S(2)}) collective-permute-start(f32[128,256]{1,0:T(8,128)S(1)} %add.49), channel_id=1, source_target_pairs={{0,2},{2,0},{1,3},{3,1},{4,6},{6,4},{5,7},{7,5},{8,10},{10,8},{9,1... | collective-permute-start | bytes 393224 | tf_op jit(solution)/shard_map/ppermute | solution.py:165
  95.0 3.9 %collective-permute-start.28 = (f32[256,256]{1,0:T(8,128)S(1)}, f32[256,256]{1,0:T(8,128)S(1)}, u32[]{:S(2)}, u32[]{:S(2)}) collective-permute-start(f32[256,256]{1,0:T(8,128)S(1)} %pad_maximum_fusion.1.stack_ref), channel_id=1, source_target_pairs={{0,1},{1,0},{2,3},{3,2},{4,5},{5,4},{6,7},{7,6},{8,9},{9,8},{10,11... | collective-permute-start | bytes 786440 | tf_op jit(solution)/shard_map/ppermute | solution.py:165
  95.1 5.9 %collective-permute-start.29 = (f32[128,256]{1,0:T(8,128)S(1)}, f32[128,256]{1,0:T(8,128)S(1)}, u32[]{:S(2)}, u32[]{:S(2)}) collective-permute-start(f32[128,256]{1,0:T(8,128)S(1)} %add.48), channel_id=1, source_target_pairs={{0,2},{2,0},{1,3},{3,1},{4,6},{6,4},{5,7},{7,5},{8,10},{10,8},{9,1... | collective-permute-start | bytes 393224 | tf_op jit(solution)/shard_map/ppermute | solution.py:165
  96.2 5.6 %collective-permute-start.30 = (f32[128,256]{1,0:T(8,128)S(1)}, f32[128,256]{1,0:T(8,128)S(1)}, u32[]{:S(2)}, u32[]{:S(2)}) collective-permute-start(f32[128,256]{1,0:T(8,128)S(1)} %add.50), channel_id=1, source_target_pairs={{0,4},{4,0},{8,12},{12,8},{1,5},{5,1},{9,13},{13,9},{2,6},{6,2},{1... | collective-permute-start | bytes 393224 | tf_op jit(solution)/shard_map/ppermute | solution.py:165
  104.3 6.7 %collective-permute-start.32 = (f32[64,256]{1,0:T(8,128)S(1)}, f32[64,256]{1,0:T(8,128)S(1)}, u32[]{:S(2)}, u32[]{:S(2)}) collective-permute-start(f32[64,256]{1,0:T(8,128)S(1)} %get-tuple-element.112), channel_id=1, source_target_pairs={{0,8},{4,12},{8,0},{12,4},{1,9},{5,13},{9,1},{13,5},{2,10},{6,14},... | collective-permute-start | bytes 196616 | tf_op jit(solution)/shard_map/ppermute | solution.py:165
  111.1 4.3 %collective-permute-start.33 = (f32[64,256]{1,0:T(8,128)S(1)}, f32[64,256]{1,0:T(8,128)S(1)}, u32[]{:S(2)}, u32[]{:S(2)}) collective-permute-start(f32[64,256]{1,0:T(8,128)S(1)} %add.51.own_ref), channel_id=1, source_target_pairs={{0,2},{2,0},{1,3},{3,1},{4,6},{6,4},{5,7},{7,5},{8,10},{10,8},{9,1... | collective-permute-start | bytes 196616 | tf_op jit(solution)/shard_map/ppermute | solution.py:165
  112.1 12.8 %collective-permute-start.36 = (f32[256,256]{1,0:T(8,128)S(1)}, f32[256,256]{1,0:T(8,128)S(1)}, u32[]{:S(2)}, u32[]{:S(2)}) collective-permute-start(f32[256,256]{1,0:T(8,128)S(1)} %shard_map.76.refs_4_), channel_id=1, source_target_pairs={{0,8},{4,12},{8,0},{12,4},{1,9},{5,13},{9,1},{13,5},{2,10},{6,14},... | collective-permute-start | bytes 786440 | tf_op jit(solution)/shard_map/ppermute | solution.py:165
  115.4 10.7 %collective-permute-start.37 = (f32[128,512]{1,0:T(8,128)S(1)}, f32[128,512]{1,0:T(8,128)S(1)}, u32[]{:S(2)}, u32[]{:S(2)}) collective-permute-start(f32[128,512]{1,0:T(8,128)S(1)} %get-tuple-element.118), channel_id=1, source_target_pairs={{0,4},{4,0},{8,12},{12,8},{1,5},{5,1},{9,13},{13,9},{2,6},{6,2},{1... | collective-permute-start | bytes 786440 | tf_op jit(solution)/shard_map/ppermute | solution.py:165
  129.1 6.5 %collective-permute-start.38 = (f32[144,128]{1,0:T(8,128)S(1)}, f32[144,128]{1,0:T(8,128)S(1)}, u32[]{:S(2)}, u32[]{:S(2)}) collective-permute-start(f32[144,128]{1,0:T(8,128)S(1)} %shard_map.79), channel_id=1, source_target_pairs={{0,8},{4,12},{8,0},{12,4},{1,9},{5,13},{9,1},{13,5},{2,10},{6,14},... | collective-permute-start | bytes 221192 | tf_op jit(solution)/shard_map/ppermute | solution.py:165
  (12 other events, 59.2 us)

commit v8 on v7

--- a/solution.py
+++ b/solution.py
@@ -389,7 +389,7 @@
 
 
 def attend_kernel(sent, query_ref, *refs):
-    *block_refs, first_ref, second_ref, lower_ref, own_ref, low_ref, high_ref, length_ref = refs[:-2]
+    *block_refs, first_ref, second_ref, lower_ref, own_ref, other_ref, length_ref = refs[:-2]
     out_ref, score_ref = refs[-2:]
     mine, upper, _, _ = pair_sides()
     which = upper ^ int(sent)
@@ -418,9 +418,8 @@
     peak = jnp.max(jnp.where(valid, scores, NEG), axis=0, keepdims=True)
     weight = jnp.where(valid, jnp.exp(scores - peak), 0.0)
     total = jnp.sum(weight, axis=0, keepdims=True)
-    other = jnp.where(which == 0, low_ref[...], high_ref[...])
     acc = product(own_ref[local, :], weight[:tokens], ((1,), (0,)))
-    out_ref[pl.ds(0, HD), :] = acc + product(other, weight[tokens:], ((1,), (0,)))
+    out_ref[pl.ds(0, HD), :] = acc + product(other_ref[...], weight[tokens:], ((1,), (0,)))
     out_ref[pl.ds(HD, 8), :] = jnp.broadcast_to(peak, (8, width))
     out_ref[pl.ds(HD + 8, 8), :] = jnp.broadcast_to(total, (8, width))
 
@@ -444,15 +443,16 @@
 
 
 def split_kernel(values_ref, query_ref, kept_ref, first_ref, second_ref, order_ref):
-    mine, _, _, _ = pair_sides()
+    mine, upper, _, _ = pair_sides()
     rows, group = query_ref.shape[0], QH // KVH
     for i, ref in enumerate((first_ref, second_ref)):
+        which = upper ^ 1 ^ i
         for k in range(group):
             order_ref[pl.ds(i * rows * group + k, rows, stride=group), :] = query_ref[
                 :, lanes((2 * i + mine) * group + k)
             ]
         kept_ref[pl.ds(i * HD, HD), :] = values_ref[:, lanes(2 * i + mine)].T
-        ref[...] = values_ref[:, lanes(2 * i + 1 - mine)].T
+        ref[...] = values_ref[:, lanes(2 * which + 1 - mine)].T
 
 
 def paired_body(keys, values, queries, start_block, lengths):
@@ -563,18 +563,19 @@
         second,
         lower,
         values_own,
-        *values_other,
-        jnp.repeat(lengths, group)[None, :],
-    )
+    )
+    row_lengths = jnp.repeat(lengths, group)[None, :]
     send, keep = (
         call(
             functools.partial(attend_kernel, sent),
             vmem(HD + 16, HD),
             *operands,
+            other,
+            row_lengths,
             scratch=[(2 * tokens, group * rows)],
             flops=1_500_000_000,
         )
-        for sent in (True, False)
+        for sent, other in zip((True, False), values_other)
     )
     result = call(merge_kernel, vmem(group * rows, HD), keep, swap(send, "tok", 2))
     return result.reshape(1, rows, 1, group * HD)

time: 136 us -> 137 us (level)
  starting transfers between devices: 39.6 us -> 41.5 us
  waiting for transfers between devices: 48.1 us -> 46.4 us
    ppermute x39, starting transfers between devices: 39.6 us -> 41.5 us  [swap(): return lax.ppermute(x, axis, pairs)]
    ppermute x39, waiting for transfers between devices: 48.1 us -> 46.4 us  [swap(): return lax.ppermute(x, axis, pairs)]
  transfers between devices with their start and end apart: 39 -> 39, of which waited for: 29 -> 26; matrix products, arithmetic and copies ran while one was open for 0% -> 0% of each run, Pallas kernels for 29% -> 31%
where the time goes in v8:
time: 137 us
  Pallas kernels  46.6 us (34%)
  waiting for transfers between devices  46.4 us (34%)
  starting transfers between devices  41.5 us (30%)
    pallas_call x26, Pallas kernels, call(): pl.pallas_call(kernel, out_shape=out_shape, in_specs=[spec] * len(args),...  46.6 us
    ppermute x39, waiting for transfers between devices, swap(): return lax.ppermute(x, axis, pairs)  46.4 us
    ppermute x39, starting transfers between devices, swap(): return lax.ppermute(x, axis, pairs)  41.5 us
  transfers between devices with their start and end apart: 39, of which 26 were waited for; matrix products, arithmetic and copies ran while one was open for 0% of the time, Pallas kernels for 31%

profile of v8, /device:TPU:0, one launch (start us, length us, event | category | flops | bytes accessed | tf_op | source)
XLA Modules:
  0.0 136.6 jit_solution(736280572104253072)
XLA Ops:
  1.6 3.1 %collective-permute-start = (f32[64,256]{1,0:T(8,128)S(1)}, f32[64,256]{1,0:T(8,128)S(1)}, u32[]{:S(2)}, u32[]{:S(2)}) collective-permute-start(f32[64,256]{1,0:T(8,128)S(1)} %shard_map.55.gram_ref), channel_id=1, source_target_pairs={{0,4},{4,0},{8,12},{12,8},{1,5},{5,1},{9,13},{13,9},{2,6},{6,2},{1... | collective-permute-start | bytes 196616 | tf_op jit(solution)/shard_map/ppermute | solution.py:165
  7.0 2.1 %collective-permute-start.1 = (f32[256,256]{1,0:T(8,128)S(1)}, f32[256,256]{1,0:T(8,128)S(1)}, u32[]{:S(2)}, u32[]{:S(2)}) collective-permute-start(f32[256,256]{1,0:T(8,128)S(1)} %get-tuple-element.64), channel_id=1, source_target_pairs={{0,4},{4,0},{8,12},{12,8},{1,5},{5,1},{9,13},{13,9},{2,6},{6,2},{1... | collective-permute-start | bytes 786440 | tf_op jit(solution)/shard_map/ppermute | solution.py:165
  9.1 2.6 %collective-permute-start.2 = (f32[64,256]{1,0:T(8,128)S(1)}, f32[64,256]{1,0:T(8,128)S(1)}, u32[]{:S(2)}, u32[]{:S(2)}) collective-permute-start(f32[64,256]{1,0:T(8,128)S(1)} %add.39), channel_id=1, source_target_pairs={{0,8},{4,12},{8,0},{12,4},{1,9},{5,13},{9,1},{13,5},{2,10},{6,14},... | collective-permute-start | bytes 196616 | tf_op jit(solution)/shard_map/ppermute | solution.py:165
  11.6 3.2 %collective-permute-done.2 = f32[64,256]{1,0:T(8,128)S(1)} collective-permute-done((f32[64,256]{1,0:T(8,128)S(1)}, f32[64,256]{1,0:T(8,128)S(1)}, u32[]{:S(2)}, u32[]{:S(2)}) %collective-permute-start.2) | collective-permute-done | bytes 65568 | tf_op jit(solution)/shard_map/ppermute | solution.py:165
  15.7 2.8 %collective-permute-start.3 = (f32[512,256]{1,0:T(8,128)S(1)}, f32[512,256]{1,0:T(8,128)S(1)}, u32[]{:S(2)}, u32[]{:S(2)}) collective-permute-start(f32[512,256]{1,0:T(8,128)S(1)} %get-tuple-element.70), channel_id=1, source_target_pairs={{0,4},{4,0},{8,12},{12,8},{1,5},{5,1},{9,13},{13,9},{2,6},{6,2},{1... | collective-permute-start | bytes 1572872 | tf_op jit(solution)/shard_map/ppermute | solution.py:165
  21.5 2.8 %collective-permute-done.4.refs_0_ = f32[64,256]{1,0:T(8,128)S(1)} collective-permute-done((f32[64,256]{1,0:T(8,128)S(1)}, f32[64,256]{1,0:T(8,128)S(1)}, u32[]{:S(2)}, u32[]{:S(2)}) %collective-permute-start.4) | collective-permute-done | bytes 65568 | tf_op jit(solution)/shard_map/ppermute | solution.py:165
  25.6 8.0 %shard_map.58.lower_ref = f32[256,256]{1,0:T(8,128)S(1)} custom-call(f32[64,256]{1,0:T(8,128)S(1)} %add.41.own_ref, f32[64,256]{1,0:T(8,128)S(1)} %collective-permute-done.4.refs_0_, f32[64,256]{1,0:T(8,128)S(1)} %collective-permute-done.5.refs_1_, f32[64,256]{1,0:T(8,128)S(1)} %collective-permute-done.6.refs_2_), custom_call_target="tpu_custom_call" | custom-call | flops 1000000000 | bytes 524288 | tf_op jit(solution)/shard_map/pallas_call | solution.py:60
  36.3 1.5 %collective-permute-start.9 = (f32[128,256]{1,0:T(8,128)S(1)}, f32[128,256]{1,0:T(8,128)S(1)}, u32[]{:S(2)}, u32[]{:S(2)}) collective-permute-start(f32[128,256]{1,0:T(8,128)S(1)} %get-tuple-element.75), channel_id=1, source_target_pairs={{0,2},{2,0},{1,3},{3,1},{4,6},{6,4},{5,7},{7,5},{8,10},{10,8},{9,1... | collective-permute-start | bytes 393224 | tf_op jit(solution)/shard_map/ppermute | solution.py:165
  37.9 2.6 %collective-permute-start.12 = (f32[128,256]{1,0:T(8,128)S(1)}, f32[128,256]{1,0:T(8,128)S(1)}, u32[]{:S(2)}, u32[]{:S(2)}) collective-permute-start(f32[128,256]{1,0:T(8,128)S(1)} %get-tuple-element.78), channel_id=1, source_target_pairs={{0,4},{4,0},{8,12},{12,8},{1,5},{5,1},{9,13},{13,9},{2,6},{6,2},{1... | collective-permute-start | bytes 393224 | tf_op jit(solution)/shard_map/ppermute | solution.py:165
  42.0 2.6 %collective-permute-start.10 = (f32[128,256]{1,0:T(8,128)S(1)}, f32[128,256]{1,0:T(8,128)S(1)}, u32[]{:S(2)}, u32[]{:S(2)}) collective-permute-start(f32[128,256]{1,0:T(8,128)S(1)} %add.42), channel_id=1, source_target_pairs={{0,4},{4,0},{8,12},{12,8},{1,5},{5,1},{9,13},{13,9},{2,6},{6,2},{1... | collective-permute-start | bytes 393224 | tf_op jit(solution)/shard_map/ppermute | solution.py:165
  44.6 1.6 %collective-permute-start.13 = (f32[128,256]{1,0:T(8,128)S(1)}, f32[128,256]{1,0:T(8,128)S(1)}, u32[]{:S(2)}, u32[]{:S(2)}) collective-permute-start(f32[128,256]{1,0:T(8,128)S(1)} %add.44), channel_id=1, source_target_pairs={{0,2},{2,0},{1,3},{3,1},{4,6},{6,4},{5,7},{7,5},{8,10},{10,8},{9,1... | collective-permute-start | bytes 393224 | tf_op jit(solution)/shard_map/ppermute | solution.py:165
  47.6 2.1 %collective-permute-done.13 = f32[128,256]{1,0:T(8,128)S(1)} collective-permute-done((f32[128,256]{1,0:T(8,128)S(1)}, f32[128,256]{1,0:T(8,128)S(1)}, u32[]{:S(2)}, u32[]{:S(2)}) %collective-permute-start.13) | collective-permute-done | bytes 131104 | tf_op jit(solution)/shard_map/ppermute | solution.py:165
  49.8 1.6 %collective-permute-start.11 = (f32[128,256]{1,0:T(8,128)S(1)}, f32[128,256]{1,0:T(8,128)S(1)}, u32[]{:S(2)}, u32[]{:S(2)}) collective-permute-start(f32[128,256]{1,0:T(8,128)S(1)} %add.43), channel_id=1, source_target_pairs={{0,2},{2,0},{1,3},{3,1},{4,6},{6,4},{5,7},{7,5},{8,10},{10,8},{9,1... | collective-permute-start | bytes 393224 | tf_op jit(solution)/shard_map/ppermute | solution.py:165
  51.5 1.7 %shard_map.62 = (f32[256,256]{1,0:T(8,128)}, f32[64,256]{1,0:T(8,128)S(1)}, f32[256,256]{1,0:T(8,128)S(1)}) custom-call(f32[256,256]{1,0:T(8,128)S(1)} %pad_maximum_fusion.stack_ref, f32[256,256]{1,0:T(8,128)S(1)} %shard_map.58.lower_ref, f32[512,256]{1,0:T(8,128)S(1)} %get-tuple-element.67.own_ref, f32[512,256]{1,0:T(8,128)S(1)} %collective-permute-done.3.other_ref), custom_call_target="tpu_custom_call" | custom-call | flops 900000000 | bytes 2162688 | tf_op jit(solution)/shard_map/pallas_call | solution.py:60
  59.4 1.8 %collective-permute-start.17 = (f32[64,256]{1,0:T(8,128)S(1)}, f32[64,256]{1,0:T(8,128)S(1)}, u32[]{:S(2)}, u32[]{:S(2)}) collective-permute-start(f32[64,256]{1,0:T(8,128)S(1)} %get-tuple-element.88), channel_id=1, source_target_pairs={{0,8},{4,12},{8,0},{12,4},{1,9},{5,13},{9,1},{13,5},{2,10},{6,14},... | collective-permute-start | bytes 196616 | tf_op jit(solution)/shard_map/ppermute | solution.py:165
  61.7 4.2 %collective-permute-done.17 = f32[64,256]{1,0:T(8,128)S(1)} collective-permute-done((f32[64,256]{1,0:T(8,128)S(1)}, f32[64,256]{1,0:T(8,128)S(1)}, u32[]{:S(2)}, u32[]{:S(2)}) %collective-permute-start.17) | collective-permute-done | bytes 65568 | tf_op jit(solution)/shard_map/ppermute | solution.py:165
  66.0 2.4 %collective-permute-start.22 = (f32[256,256]{1,0:T(8,128)S(1)}, f32[256,256]{1,0:T(8,128)S(1)}, u32[]{:S(2)}, u32[]{:S(2)}) collective-permute-start(f32[256,256]{1,0:T(8,128)S(1)} %shard_map.66.first_ref), channel_id=1, source_target_pairs={{0,8},{4,12},{8,0},{12,4},{1,9},{5,13},{9,1},{13,5},{2,10},{6,14},... | collective-permute-start | bytes 786440 | tf_op jit(solution)/shard_map/ppermute | solution.py:165
  69.7 3.0 %collective-permute-done.18.refs_0_ = f32[64,256]{1,0:T(8,128)S(1)} collective-permute-done((f32[64,256]{1,0:T(8,128)S(1)}, f32[64,256]{1,0:T(8,128)S(1)}, u32[]{:S(2)}, u32[]{:S(2)}) %collective-permute-start.18) | collective-permute-done | bytes 65568 | tf_op jit(solution)/shard_map/ppermute | solution.py:165
  73.9 4.0 %shard_map.67 = (f32[128,128]{1,0:T(8,128)S(1)}, f32[128,128]{1,0:T(8,128)S(1)}, f32[128,128]{1,0:T(8,128)S(1)}) custom-call(f32[64,256]{1,0:T(8,128)S(1)} %add.46.own_ref, f32[64,256]{1,0:T(8,128)S(1)} %collective-permute-done.18.refs_0_, f32[64,256]{1,0:T(8,128)S(1)} %collective-permute-done.19.refs_1_, f32[64,256]{1,0:T(8,128)S(1)} %collective-permute-done.20.refs_2_), custom_call_target="tpu_custom_call" | custom-call | flops 1000000000 | bytes 458752 | tf_op jit(solution)/shard_map/pallas_call | solution.py:60
  78.6 2.3 %collective-permute-done.22.second_ref = f32[256,256]{1,0:T(8,128)S(1)} collective-permute-done((f32[256,256]{1,0:T(8,128)S(1)}, f32[256,256]{1,0:T(8,128)S(1)}, u32[]{:S(2)}, u32[]{:S(2)}) %collective-permute-start.22) | collective-permute-done | bytes 262176 | tf_op jit(solution)/shard_map/ppermute | solution.py:165
  84.4 4.9 %collective-permute-done.24 = f32[128,256]{1,0:T(8,128)S(1)} collective-permute-done((f32[128,256]{1,0:T(8,128)S(1)}, f32[128,256]{1,0:T(8,128)S(1)}, u32[]{:S(2)}, u32[]{:S(2)}) %collective-permute-start.24) | collective-permute-done | bytes 131104 | tf_op jit(solution)/shard_map/ppermute | solution.py:165
  89.4 1.7 %collective-permute-start.27 = (f32[128,256]{1,0:T(8,128)S(1)}, f32[128,256]{1,0:T(8,128)S(1)}, u32[]{:S(2)}, u32[]{:S(2)}) collective-permute-start(f32[128,256]{1,0:T(8,128)S(1)} %add.49), channel_id=1, source_target_pairs={{0,2},{2,0},{1,3},{3,1},{4,6},{6,4},{5,7},{7,5},{8,10},{10,8},{9,1... | collective-permute-start | bytes 393224 | tf_op jit(solution)/shard_map/ppermute | solution.py:165
  91.1 3.9 %shard_map.71.lower_ref = f32[256,256]{1,0:T(8,128)S(1)} custom-call(f32[128,128]{1,0:T(8,128)S(1)} %get-tuple-element.89.tile_ref, f32[128,128]{1,0:T(8,128)S(1)} %get-tuple-element.95.cross_ref, f32[128,128]{1,0:T(8,128)S(1)} %get-tuple-element.96.left_ref), custom_call_target="tpu_custom_call" | custom-call | flops 1000000000 | bytes 458752 | tf_op jit(solution)/shard_map/pallas_call | solution.py:60
  104.3 1.8 %collective-permute-start.32 = (f32[64,256]{1,0:T(8,128)S(1)}, f32[64,256]{1,0:T(8,128)S(1)}, u32[]{:S(2)}, u32[]{:S(2)}) collective-permute-start(f32[64,256]{1,0:T(8,128)S(1)} %get-tuple-element.112), channel_id=1, source_target_pairs={{0,8},{4,12},{8,0},{12,4},{1,9},{5,13},{9,1},{13,5},{2,10},{6,14},... | collective-permute-start | bytes 196616 | tf_op jit(solution)/shard_map/ppermute | solution.py:165
  106.6 4.5 %collective-permute-done.32 = f32[64,256]{1,0:T(8,128)S(1)} collective-permute-done((f32[64,256]{1,0:T(8,128)S(1)}, f32[64,256]{1,0:T(8,128)S(1)}, u32[]{:S(2)}, u32[]{:S(2)}) %collective-permute-start.32) | collective-permute-done | bytes 65568 | tf_op jit(solution)/shard_map/ppermute | solution.py:165
  112.5 3.3 %collective-permute-done.33.refs_0_ = f32[64,256]{1,0:T(8,128)S(1)} collective-permute-done((f32[64,256]{1,0:T(8,128)S(1)}, f32[64,256]{1,0:T(8,128)S(1)}, u32[]{:S(2)}, u32[]{:S(2)}) %collective-permute-start.33) | collective-permute-done | bytes 65568 | tf_op jit(solution)/shard_map/ppermute | solution.py:165
  115.8 1.9 %collective-permute-start.37 = (f32[128,512]{1,0:T(8,128)S(1)}, f32[128,512]{1,0:T(8,128)S(1)}, u32[]{:S(2)}, u32[]{:S(2)}) collective-permute-start(f32[128,512]{1,0:T(8,128)S(1)} %get-tuple-element.118), channel_id=1, source_target_pairs={{0,4},{4,0},{8,12},{12,8},{1,5},{5,1},{9,13},{13,9},{2,6},{6,2},{1... | collective-permute-start | bytes 786440 | tf_op jit(solution)/shard_map/ppermute | solution.py:165
  117.9 8.1 %shard_map.77.refs_6_ = f32[256,256]{1,0:T(8,128)S(1)} custom-call(f32[64,256]{1,0:T(8,128)S(1)} %add.51.own_ref, f32[64,256]{1,0:T(8,128)S(1)} %collective-permute-done.33.refs_0_, f32[64,256]{1,0:T(8,128)S(1)} %collective-permute-done.34.refs_1_, f32[64,256]{1,0:T(8,128)S(1)} %collective-permute-done.35.refs_2_), custom_call_target="tpu_custom_call" | custom-call | flops 1000000000 | bytes 524288 | tf_op jit(solution)/shard_map/pallas_call | solution.py:60
  126.0 2.9 %shard_map.79 = f32[144,128]{1,0:T(8,128)S(1)} custom-call(f32[256,128]{1,0:T(8,128)S(1)} %get-tuple-element.66.query_ref, f32[256,256]{1,0:T(8,128)S(1)} %get-tuple-element.100.refs_0_, f32[256,256]{1,0:T(8,128)S(1)} %get-tuple-element.103.refs_1_, f32[256,256]{1,0:T(8,128)S(1)} %get-tuple-element.108.refs_2_, ...), custom_call_target="tpu_custom_call" | custom-call | flops 1500000000 | bytes 2826752 | tf_op jit(solution)/shard_map/pallas_call | solution.py:60
  128.9 1.8 %collective-permute-start.38 = (f32[144,128]{1,0:T(8,128)S(1)}, f32[144,128]{1,0:T(8,128)S(1)}, u32[]{:S(2)}, u32[]{:S(2)}) collective-permute-start(f32[144,128]{1,0:T(8,128)S(1)} %shard_map.79), channel_id=1, source_target_pairs={{0,8},{4,12},{8,0},{12,4},{1,9},{5,13},{9,1},{13,5},{2,10},{6,14},... | collective-permute-start | bytes 221192 | tf_op jit(solution)/shard_map/ppermute | solution.py:165
  130.7 2.9 %shard_map.78.first_ref = f32[144,128]{1,0:T(8,128)S(1)} custom-call(f32[256,128]{1,0:T(8,128)S(1)} %get-tuple-element.66.query_ref, f32[256,256]{1,0:T(8,128)S(1)} %get-tuple-element.100.refs_0_, f32[256,256]{1,0:T(8,128)S(1)} %get-tuple-element.103.refs_1_, f32[256,256]{1,0:T(8,128)S(1)} %get-tuple-element.108.refs_2_, ...), custom_call_target="tpu_custom_call" | custom-call | flops 1500000000 | bytes 2826752 | tf_op jit(solution)/shard_map/pallas_call | solution.py:60
  133.6 2.2 %collective-permute-done.38.second_ref = f32[144,128]{1,0:T(8,128)S(1)} collective-permute-done((f32[144,128]{1,0:T(8,128)S(1)}, f32[144,128]{1,0:T(8,128)S(1)}, u32[]{:S(2)}, u32[]{:S(2)}) %collective-permute-start.38) | collective-permute-done | bytes 73760 | tf_op jit(solution)/shard_map/ppermute | solution.py:165
  (103 shorter events, 40.4 us)
Async XLA Ops:
  1.6 5.3 %collective-permute-start = (f32[64,256]{1,0:T(8,128)S(1)}, f32[64,256]{1,0:T(8,128)S(1)}, u32[]{:S(2)}, u32[]{:S(2)}) collective-permute-start(f32[64,256]{1,0:T(8,128)S(1)} %shard_map.55.gram_ref), channel_id=1, source_target_pairs={{0,4},{4,0},{8,12},{12,8},{1,5},{5,1},{9,13},{13,9},{2,6},{6,2},{1... | collective-permute-start | bytes 196616 | tf_op jit(solution)/shard_map/ppermute | solution.py:165
  7.0 8.7 %collective-permute-start.1 = (f32[256,256]{1,0:T(8,128)S(1)}, f32[256,256]{1,0:T(8,128)S(1)}, u32[]{:S(2)}, u32[]{:S(2)}) collective-permute-start(f32[256,256]{1,0:T(8,128)S(1)} %get-tuple-element.64), channel_id=1, source_target_pairs={{0,4},{4,0},{8,12},{12,8},{1,5},{5,1},{9,13},{13,9},{2,6},{6,2},{1... | collective-permute-start | bytes 786440 | tf_op jit(solution)/shard_map/ppermute | solution.py:165
  9.1 5.8 %collective-permute-start.2 = (f32[64,256]{1,0:T(8,128)S(1)}, f32[64,256]{1,0:T(8,128)S(1)}, u32[]{:S(2)}, u32[]{:S(2)}) collective-permute-start(f32[64,256]{1,0:T(8,128)S(1)} %add.39), channel_id=1, source_target_pairs={{0,8},{4,12},{8,0},{12,4},{1,9},{5,13},{9,1},{13,5},{2,10},{6,14},... | collective-permute-start | bytes 196616 | tf_op jit(solution)/shard_map/ppermute | solution.py:165
  15.7 18.0 %collective-permute-start.3 = (f32[512,256]{1,0:T(8,128)S(1)}, f32[512,256]{1,0:T(8,128)S(1)}, u32[]{:S(2)}, u32[]{:S(2)}) collective-permute-start(f32[512,256]{1,0:T(8,128)S(1)} %get-tuple-element.70), channel_id=1, source_target_pairs={{0,4},{4,0},{8,12},{12,8},{1,5},{5,1},{9,13},{13,9},{2,6},{6,2},{1... | collective-permute-start | bytes 1572872 | tf_op jit(solution)/shard_map/ppermute | solution.py:165
  18.5 15.1 %collective-permute-start.7 = (f32[256,256]{1,0:T(8,128)S(1)}, f32[256,256]{1,0:T(8,128)S(1)}, u32[]{:S(2)}, u32[]{:S(2)}) collective-permute-start(f32[256,256]{1,0:T(8,128)S(1)} %add.40.first_ref), channel_id=1, source_target_pairs={{0,8},{4,12},{8,0},{12,4},{1,9},{5,13},{9,1},{13,5},{2,10},{6,14},... | collective-permute-start | bytes 786440 | tf_op jit(solution)/shard_map/ppermute | solution.py:165
  20.0 4.3 %collective-permute-start.4 = (f32[64,256]{1,0:T(8,128)S(1)}, f32[64,256]{1,0:T(8,128)S(1)}, u32[]{:S(2)}, u32[]{:S(2)}) collective-permute-start(f32[64,256]{1,0:T(8,128)S(1)} %add.41.own_ref), channel_id=1, source_target_pairs={{0,2},{2,0},{1,3},{3,1},{4,6},{6,4},{5,7},{7,5},{8,10},{10,8},{9,1... | collective-permute-start | bytes 196616 | tf_op jit(solution)/shard_map/ppermute | solution.py:165
  21.5 3.2 %collective-permute-start.5 = (f32[64,256]{1,0:T(8,128)S(1)}, f32[64,256]{1,0:T(8,128)S(1)}, u32[]{:S(2)}, u32[]{:S(2)}) collective-permute-start(f32[64,256]{1,0:T(8,128)S(1)} %add.41.own_ref), channel_id=1, source_target_pairs={{0,1},{1,0},{2,3},{3,2},{4,5},{5,4},{6,7},{7,6},{8,9},{9,8},{10,11... | collective-permute-start | bytes 196616 | tf_op jit(solution)/shard_map/ppermute | solution.py:165
  36.3 5.6 %collective-permute-start.9 = (f32[128,256]{1,0:T(8,128)S(1)}, f32[128,256]{1,0:T(8,128)S(1)}, u32[]{:S(2)}, u32[]{:S(2)}) collective-permute-start(f32[128,256]{1,0:T(8,128)S(1)} %get-tuple-element.75), channel_id=1, source_target_pairs={{0,2},{2,0},{1,3},{3,1},{4,6},{6,4},{5,7},{7,5},{8,10},{10,8},{9,1... | collective-permute-start | bytes 393224 | tf_op jit(solution)/shard_map/ppermute | solution.py:165
  37.9 6.7 %collective-permute-start.12 = (f32[128,256]{1,0:T(8,128)S(1)}, f32[128,256]{1,0:T(8,128)S(1)}, u32[]{:S(2)}, u32[]{:S(2)}) collective-permute-start(f32[128,256]{1,0:T(8,128)S(1)} %get-tuple-element.78), channel_id=1, source_target_pairs={{0,4},{4,0},{8,12},{12,8},{1,5},{5,1},{9,13},{13,9},{2,6},{6,2},{1... | collective-permute-start | bytes 393224 | tf_op jit(solution)/shard_map/ppermute | solution.py:165
  42.0 5.6 %collective-permute-start.10 = (f32[128,256]{1,0:T(8,128)S(1)}, f32[128,256]{1,0:T(8,128)S(1)}, u32[]{:S(2)}, u32[]{:S(2)}) collective-permute-start(f32[128,256]{1,0:T(8,128)S(1)} %add.42), channel_id=1, source_target_pairs={{0,4},{4,0},{8,12},{12,8},{1,5},{5,1},{9,13},{13,9},{2,6},{6,2},{1... | collective-permute-start | bytes 393224 | tf_op jit(solution)/shard_map/ppermute | solution.py:165
  44.6 5.0 %collective-permute-start.13 = (f32[128,256]{1,0:T(8,128)S(1)}, f32[128,256]{1,0:T(8,128)S(1)}, u32[]{:S(2)}, u32[]{:S(2)}) collective-permute-start(f32[128,256]{1,0:T(8,128)S(1)} %add.44), channel_id=1, source_target_pairs={{0,2},{2,0},{1,3},{3,1},{4,6},{6,4},{5,7},{7,5},{8,10},{10,8},{9,1... | collective-permute-start | bytes 393224 | tf_op jit(solution)/shard_map/ppermute | solution.py:165
  49.7 3.6 %collective-permute-start.14 = (f32[256,256]{1,0:T(8,128)S(1)}, f32[256,256]{1,0:T(8,128)S(1)}, u32[]{:S(2)}, u32[]{:S(2)}) collective-permute-start(f32[256,256]{1,0:T(8,128)S(1)} %pad_maximum_fusion.stack_ref), channel_id=1, source_target_pairs={{0,1},{1,0},{2,3},{3,2},{4,5},{5,4},{6,7},{7,6},{8,9},{9,8},{10,11... | collective-permute-start | bytes 786440 | tf_op jit(solution)/shard_map/ppermute | solution.py:165
  49.8 5.9 %collective-permute-start.11 = (f32[128,256]{1,0:T(8,128)S(1)}, f32[128,256]{1,0:T(8,128)S(1)}, u32[]{:S(2)}, u32[]{:S(2)}) collective-permute-start(f32[128,256]{1,0:T(8,128)S(1)} %add.43), channel_id=1, source_target_pairs={{0,2},{2,0},{1,3},{3,1},{4,6},{6,4},{5,7},{7,5},{8,10},{10,8},{9,1... | collective-permute-start | bytes 393224 | tf_op jit(solution)/shard_map/ppermute | solution.py:165
  51.3 5.6 %collective-permute-start.15 = (f32[128,256]{1,0:T(8,128)S(1)}, f32[128,256]{1,0:T(8,128)S(1)}, u32[]{:S(2)}, u32[]{:S(2)}) collective-permute-start(f32[128,256]{1,0:T(8,128)S(1)} %add.45), channel_id=1, source_target_pairs={{0,4},{4,0},{8,12},{12,8},{1,5},{5,1},{9,13},{13,9},{2,6},{6,2},{1... | collective-permute-start | bytes 393224 | tf_op jit(solution)/shard_map/ppermute | solution.py:165
  59.4 6.5 %collective-permute-start.17 = (f32[64,256]{1,0:T(8,128)S(1)}, f32[64,256]{1,0:T(8,128)S(1)}, u32[]{:S(2)}, u32[]{:S(2)}) collective-permute-start(f32[64,256]{1,0:T(8,128)S(1)} %get-tuple-element.88), channel_id=1, source_target_pairs={{0,8},{4,12},{8,0},{12,4},{1,9},{5,13},{9,1},{13,5},{2,10},{6,14},... | collective-permute-start | bytes 196616 | tf_op jit(solution)/shard_map/ppermute | solution.py:165
  66.0 12.7 %collective-permute-start.21 = (f32[128,512]{1,0:T(8,128)S(1)}, f32[128,512]{1,0:T(8,128)S(1)}, u32[]{:S(2)}, u32[]{:S(2)}) collective-permute-start(f32[128,512]{1,0:T(8,128)S(1)} %get-tuple-element.91), channel_id=1, source_target_pairs={{0,4},{4,0},{8,12},{12,8},{1,5},{5,1},{9,13},{13,9},{2,6},{6,2},{1... | collective-permute-start | bytes 786440 | tf_op jit(solution)/shard_map/ppermute | solution.py:165
  66.0 14.9 %collective-permute-start.22 = (f32[256,256]{1,0:T(8,128)S(1)}, f32[256,256]{1,0:T(8,128)S(1)}, u32[]{:S(2)}, u32[]{:S(2)}) collective-permute-start(f32[256,256]{1,0:T(8,128)S(1)} %shard_map.66.first_ref), channel_id=1, source_target_pairs={{0,8},{4,12},{8,0},{12,4},{1,9},{5,13},{9,1},{13,5},{2,10},{6,14},... | collective-permute-start | bytes 786440 | tf_op jit(solution)/shard_map/ppermute | solution.py:165
  68.4 4.3 %collective-permute-start.18 = (f32[64,256]{1,0:T(8,128)S(1)}, f32[64,256]{1,0:T(8,128)S(1)}, u32[]{:S(2)}, u32[]{:S(2)}) collective-permute-start(f32[64,256]{1,0:T(8,128)S(1)} %add.46.own_ref), channel_id=1, source_target_pairs={{0,2},{2,0},{1,3},{3,1},{4,6},{6,4},{5,7},{7,5},{8,10},{10,8},{9,1... | collective-permute-start | bytes 196616 | tf_op jit(solution)/shard_map/ppermute | solution.py:165
  69.7 3.0 %collective-permute-start.19 = (f32[64,256]{1,0:T(8,128)S(1)}, f32[64,256]{1,0:T(8,128)S(1)}, u32[]{:S(2)}, u32[]{:S(2)}) collective-permute-start(f32[64,256]{1,0:T(8,128)S(1)} %add.46.own_ref), channel_id=1, source_target_pairs={{0,1},{1,0},{2,3},{3,2},{4,5},{5,4},{6,7},{7,6},{8,9},{9,8},{10,11... | collective-permute-start | bytes 196616 | tf_op jit(solution)/shard_map/ppermute | solution.py:165
  83.6 5.6 %collective-permute-start.24 = (f32[128,256]{1,0:T(8,128)S(1)}, f32[128,256]{1,0:T(8,128)S(1)}, u32[]{:S(2)}, u32[]{:S(2)}) collective-permute-start(f32[128,256]{1,0:T(8,128)S(1)} %get-tuple-element.94), channel_id=1, source_target_pairs={{0,2},{2,0},{1,3},{3,1},{4,6},{6,4},{5,7},{7,5},{8,10},{10,8},{9,1... | collective-permute-start | bytes 393224 | tf_op jit(solution)/shard_map/ppermute | solution.py:165
  84.1 5.3 %collective-permute-start.26 = (f32[128,256]{1,0:T(8,128)S(1)}, f32[128,256]{1,0:T(8,128)S(1)}, u32[]{:S(2)}, u32[]{:S(2)}) collective-permute-start(f32[128,256]{1,0:T(8,128)S(1)} %get-tuple-element.99), channel_id=1, source_target_pairs={{0,4},{4,0},{8,12},{12,8},{1,5},{5,1},{9,13},{13,9},{2,6},{6,2},{1... | collective-permute-start | bytes 393224 | tf_op jit(solution)/shard_map/ppermute | solution.py:165
  89.2 5.7 %collective-permute-start.25 = (f32[128,256]{1,0:T(8,128)S(1)}, f32[128,256]{1,0:T(8,128)S(1)}, u32[]{:S(2)}, u32[]{:S(2)}) collective-permute-start(f32[128,256]{1,0:T(8,128)S(1)} %add.47), channel_id=1, source_target_pairs={{0,4},{4,0},{8,12},{12,8},{1,5},{5,1},{9,13},{13,9},{2,6},{6,2},{1... | collective-permute-start | bytes 393224 | tf_op jit(solution)/shard_map/ppermute | solution.py:165
  89.4 5.6 %collective-permute-start.27 = (f32[128,256]{1,0:T(8,128)S(1)}, f32[128,256]{1,0:T(8,128)S(1)}, u32[]{:S(2)}, u32[]{:S(2)}) collective-permute-start(f32[128,256]{1,0:T(8,128)S(1)} %add.49), channel_id=1, source_target_pairs={{0,2},{2,0},{1,3},{3,1},{4,6},{6,4},{5,7},{7,5},{8,10},{10,8},{9,1... | collective-permute-start | bytes 393224 | tf_op jit(solution)/shard_map/ppermute | solution.py:165
  95.0 3.9 %collective-permute-start.28 = (f32[256,256]{1,0:T(8,128)S(1)}, f32[256,256]{1,0:T(8,128)S(1)}, u32[]{:S(2)}, u32[]{:S(2)}) collective-permute-start(f32[256,256]{1,0:T(8,128)S(1)} %pad_maximum_fusion.1.stack_ref), channel_id=1, source_target_pairs={{0,1},{1,0},{2,3},{3,2},{4,5},{5,4},{6,7},{7,6},{8,9},{9,8},{10,11... | collective-permute-start | bytes 786440 | tf_op jit(solution)/shard_map/ppermute | solution.py:165
  95.1 5.9 %collective-permute-start.29 = (f32[128,256]{1,0:T(8,128)S(1)}, f32[128,256]{1,0:T(8,128)S(1)}, u32[]{:S(2)}, u32[]{:S(2)}) collective-permute-start(f32[128,256]{1,0:T(8,128)S(1)} %add.48), channel_id=1, source_target_pairs={{0,2},{2,0},{1,3},{3,1},{4,6},{6,4},{5,7},{7,5},{8,10},{10,8},{9,1... | collective-permute-start | bytes 393224 | tf_op jit(solution)/shard_map/ppermute | solution.py:165
  96.2 5.6 %collective-permute-start.30 = (f32[128,256]{1,0:T(8,128)S(1)}, f32[128,256]{1,0:T(8,128)S(1)}, u32[]{:S(2)}, u32[]{:S(2)}) collective-permute-start(f32[128,256]{1,0:T(8,128)S(1)} %add.50), channel_id=1, source_target_pairs={{0,4},{4,0},{8,12},{12,8},{1,5},{5,1},{9,13},{13,9},{2,6},{6,2},{1... | collective-permute-start | bytes 393224 | tf_op jit(solution)/shard_map/ppermute | solution.py:165
  104.3 6.7 %collective-permute-start.32 = (f32[64,256]{1,0:T(8,128)S(1)}, f32[64,256]{1,0:T(8,128)S(1)}, u32[]{:S(2)}, u32[]{:S(2)}) collective-permute-start(f32[64,256]{1,0:T(8,128)S(1)} %get-tuple-element.112), channel_id=1, source_target_pairs={{0,8},{4,12},{8,0},{12,4},{1,9},{5,13},{9,1},{13,5},{2,10},{6,14},... | collective-permute-start | bytes 196616 | tf_op jit(solution)/shard_map/ppermute | solution.py:165
  111.1 14.9 %collective-permute-start.36 = (f32[256,256]{1,0:T(8,128)S(1)}, f32[256,256]{1,0:T(8,128)S(1)}, u32[]{:S(2)}, u32[]{:S(2)}) collective-permute-start(f32[256,256]{1,0:T(8,128)S(1)} %shard_map.76.refs_4_), channel_id=1, source_target_pairs={{0,8},{4,12},{8,0},{12,4},{1,9},{5,13},{9,1},{13,5},{2,10},{6,14},... | collective-permute-start | bytes 786440 | tf_op jit(solution)/shard_map/ppermute | solution.py:165
  111.5 4.3 %collective-permute-start.33 = (f32[64,256]{1,0:T(8,128)S(1)}, f32[64,256]{1,0:T(8,128)S(1)}, u32[]{:S(2)}, u32[]{:S(2)}) collective-permute-start(f32[64,256]{1,0:T(8,128)S(1)} %add.51.own_ref), channel_id=1, source_target_pairs={{0,2},{2,0},{1,3},{3,1},{4,6},{6,4},{5,7},{7,5},{8,10},{10,8},{9,1... | collective-permute-start | bytes 196616 | tf_op jit(solution)/shard_map/ppermute | solution.py:165
  112.5 5.4 %collective-permute-start.34 = (f32[64,256]{1,0:T(8,128)S(1)}, f32[64,256]{1,0:T(8,128)S(1)}, u32[]{:S(2)}, u32[]{:S(2)}) collective-permute-start(f32[64,256]{1,0:T(8,128)S(1)} %add.51.own_ref), channel_id=1, source_target_pairs={{0,1},{1,0},{2,3},{3,2},{4,5},{5,4},{6,7},{7,6},{8,9},{9,8},{10,11... | collective-permute-start | bytes 196616 | tf_op jit(solution)/shard_map/ppermute | solution.py:165
  115.8 14.9 %collective-permute-start.37 = (f32[128,512]{1,0:T(8,128)S(1)}, f32[128,512]{1,0:T(8,128)S(1)}, u32[]{:S(2)}, u32[]{:S(2)}) collective-permute-start(f32[128,512]{1,0:T(8,128)S(1)} %get-tuple-element.118), channel_id=1, source_target_pairs={{0,4},{4,0},{8,12},{12,8},{1,5},{5,1},{9,13},{13,9},{2,6},{6,2},{1... | collective-permute-start | bytes 786440 | tf_op jit(solution)/shard_map/ppermute | solution.py:165
  128.9 7.0 %collective-permute-start.38 = (f32[144,128]{1,0:T(8,128)S(1)}, f32[144,128]{1,0:T(8,128)S(1)}, u32[]{:S(2)}, u32[]{:S(2)}) collective-permute-start(f32[144,128]{1,0:T(8,128)S(1)} %shard_map.79), channel_id=1, source_target_pairs={{0,8},{4,12},{8,0},{12,4},{1,9},{5,13},{9,1},{13,5},{2,10},{6,14},... | collective-permute-start | bytes 221192 | tf_op jit(solution)/shard_map/ppermute | solution.py:165
  (12 other events, 62.3 us)

commit v9 on v8

--- a/solution.py
+++ b/solution.py
@@ -126,7 +126,7 @@
 FACTOR_FLOPS = 1_000_000_000
 
 
-def inverse_factor(*parts):
+def inverse_factor(*parts, flops=FACTOR_FLOPS):
     rank = parts[0].shape[1]
     half = rank // 2
     return call(
@@ -134,7 +134,7 @@
         vmem(rank, rank),
         *parts,
         scratch=[(rank, rank), (half, half), (half, half)],
-        flops=FACTOR_FLOPS,
+        flops=flops,
     )
 
 
@@ -503,7 +503,8 @@
             ready = parts[1] if last else gram
             values_other.append(swap(after(values_send[step - 1], proj, ready), "tok", 1))
         if step == 0 or last:
-            lower = inverse_factor(after(parts[0], values_own), *parts[1:])
+            flops = 1_500_000_000 if last else FACTOR_FLOPS
+            lower = inverse_factor(after(parts[0], values_own), *parts[1:], flops=flops)
             first = after(first, lower)
         else:
             halves = inverse_factor_low(*parts)

time: 137 us -> 135 us (0.985)
  starting transfers between devices: 41.5 us -> 39.2 us
    ppermute x39, starting transfers between devices: 41.5 us -> 39.2 us  [swap(): return lax.ppermute(x, axis, pairs)]
  transfers between devices with their start and end apart: 39 -> 39, of which waited for: 26 -> 28; matrix products, arithmetic and copies ran while one was open for 0% -> 0% of each run, Pallas kernels for 31% -> 31%
where the time goes in v9:
time: 135 us
  waiting for transfers between devices  47.4 us (35%)
  Pallas kernels  46.6 us (35%)
  starting transfers between devices  39.2 us (29%)
  local copies, waits for them, and re-layouts  1.35 us (1%)
    ppermute x39, waiting for transfers between devices, swap(): return lax.ppermute(x, axis, pairs)  47.4 us
    pallas_call x26, Pallas kernels, call(): pl.pallas_call(kernel, out_shape=out_shape, in_specs=[spec] * len(args),...  46.6 us
    ppermute x39, starting transfers between devices, swap(): return lax.ppermute(x, axis, pairs)  39.2 us
  transfers between devices with their start and end apart: 39, of which 28 were waited for; matrix products, arithmetic and copies ran while one was open for 0% of the time, Pallas kernels for 31%

profile of v9, /device:TPU:0, one launch (start us, length us, event | category | flops | bytes accessed | tf_op | source)
XLA Modules:
  0.0 135.3 jit_solution(4165277335922434094)
XLA Ops:
  1.6 3.1 %collective-permute-start = (f32[64,256]{1,0:T(8,128)S(1)}, f32[64,256]{1,0:T(8,128)S(1)}, u32[]{:S(2)}, u32[]{:S(2)}) collective-permute-start(f32[64,256]{1,0:T(8,128)S(1)} %shard_map.55.gram_ref), channel_id=1, source_target_pairs={{0,4},{4,0},{8,12},{12,8},{1,5},{5,1},{9,13},{13,9},{2,6},{6,2},{1... | collective-permute-start | bytes 196616 | tf_op jit(solution)/shard_map/ppermute | solution.py:165
  7.0 2.1 %collective-permute-start.1 = (f32[256,256]{1,0:T(8,128)S(1)}, f32[256,256]{1,0:T(8,128)S(1)}, u32[]{:S(2)}, u32[]{:S(2)}) collective-permute-start(f32[256,256]{1,0:T(8,128)S(1)} %get-tuple-element.64), channel_id=1, source_target_pairs={{0,4},{4,0},{8,12},{12,8},{1,5},{5,1},{9,13},{13,9},{2,6},{6,2},{1... | collective-permute-start | bytes 786440 | tf_op jit(solution)/shard_map/ppermute | solution.py:165
  9.1 2.6 %collective-permute-start.2 = (f32[64,256]{1,0:T(8,128)S(1)}, f32[64,256]{1,0:T(8,128)S(1)}, u32[]{:S(2)}, u32[]{:S(2)}) collective-permute-start(f32[64,256]{1,0:T(8,128)S(1)} %add.39), channel_id=1, source_target_pairs={{0,8},{4,12},{8,0},{12,4},{1,9},{5,13},{9,1},{13,5},{2,10},{6,14},... | collective-permute-start | bytes 196616 | tf_op jit(solution)/shard_map/ppermute | solution.py:165
  11.6 3.2 %collective-permute-done.2 = f32[64,256]{1,0:T(8,128)S(1)} collective-permute-done((f32[64,256]{1,0:T(8,128)S(1)}, f32[64,256]{1,0:T(8,128)S(1)}, u32[]{:S(2)}, u32[]{:S(2)}) %collective-permute-start.2) | collective-permute-done | bytes 65568 | tf_op jit(solution)/shard_map/ppermute | solution.py:165
  15.7 2.8 %collective-permute-start.3 = (f32[512,256]{1,0:T(8,128)S(1)}, f32[512,256]{1,0:T(8,128)S(1)}, u32[]{:S(2)}, u32[]{:S(2)}) collective-permute-start(f32[512,256]{1,0:T(8,128)S(1)} %get-tuple-element.70), channel_id=1, source_target_pairs={{0,4},{4,0},{8,12},{12,8},{1,5},{5,1},{9,13},{13,9},{2,6},{6,2},{1... | collective-permute-start | bytes 1572872 | tf_op jit(solution)/shard_map/ppermute | solution.py:165
  18.5 1.5 %collective-permute-start.7 = (f32[256,256]{1,0:T(8,128)S(1)}, f32[256,256]{1,0:T(8,128)S(1)}, u32[]{:S(2)}, u32[]{:S(2)}) collective-permute-start(f32[256,256]{1,0:T(8,128)S(1)} %add.40.first_ref), channel_id=1, source_target_pairs={{0,8},{4,12},{8,0},{12,4},{1,9},{5,13},{9,1},{13,5},{2,10},{6,14},... | collective-permute-start | bytes 786440 | tf_op jit(solution)/shard_map/ppermute | solution.py:165
  21.5 2.8 %collective-permute-done.4.refs_0_ = f32[64,256]{1,0:T(8,128)S(1)} collective-permute-done((f32[64,256]{1,0:T(8,128)S(1)}, f32[64,256]{1,0:T(8,128)S(1)}, u32[]{:S(2)}, u32[]{:S(2)}) %collective-permute-start.4) | collective-permute-done | bytes 65568 | tf_op jit(solution)/shard_map/ppermute | solution.py:165
  25.6 8.0 %shard_map.58.lower_ref = f32[256,256]{1,0:T(8,128)S(1)} custom-call(f32[64,256]{1,0:T(8,128)S(1)} %add.41.own_ref, f32[64,256]{1,0:T(8,128)S(1)} %collective-permute-done.4.refs_0_, f32[64,256]{1,0:T(8,128)S(1)} %collective-permute-done.5.refs_1_, f32[64,256]{1,0:T(8,128)S(1)} %collective-permute-done.6.refs_2_), custom_call_target="tpu_custom_call" | custom-call | flops 1000000000 | bytes 524288 | tf_op jit(solution)/shard_map/pallas_call | solution.py:60
  36.3 1.5 %collective-permute-start.9 = (f32[128,256]{1,0:T(8,128)S(1)}, f32[128,256]{1,0:T(8,128)S(1)}, u32[]{:S(2)}, u32[]{:S(2)}) collective-permute-start(f32[128,256]{1,0:T(8,128)S(1)} %get-tuple-element.75), channel_id=1, source_target_pairs={{0,2},{2,0},{1,3},{3,1},{4,6},{6,4},{5,7},{7,5},{8,10},{10,8},{9,1... | collective-permute-start | bytes 393224 | tf_op jit(solution)/shard_map/ppermute | solution.py:165
  37.9 2.6 %collective-permute-start.12 = (f32[128,256]{1,0:T(8,128)S(1)}, f32[128,256]{1,0:T(8,128)S(1)}, u32[]{:S(2)}, u32[]{:S(2)}) collective-permute-start(f32[128,256]{1,0:T(8,128)S(1)} %get-tuple-element.78), channel_id=1, source_target_pairs={{0,4},{4,0},{8,12},{12,8},{1,5},{5,1},{9,13},{13,9},{2,6},{6,2},{1... | collective-permute-start | bytes 393224 | tf_op jit(solution)/shard_map/ppermute | solution.py:165
  40.5 1.5 %collective-permute-done.9 = f32[128,256]{1,0:T(8,128)S(1)} collective-permute-done((f32[128,256]{1,0:T(8,128)S(1)}, f32[128,256]{1,0:T(8,128)S(1)}, u32[]{:S(2)}, u32[]{:S(2)}) %collective-permute-start.9) | collective-permute-done | bytes 131104 | tf_op jit(solution)/shard_map/ppermute | solution.py:165
  42.0 2.6 %collective-permute-start.10 = (f32[128,256]{1,0:T(8,128)S(1)}, f32[128,256]{1,0:T(8,128)S(1)}, u32[]{:S(2)}, u32[]{:S(2)}) collective-permute-start(f32[128,256]{1,0:T(8,128)S(1)} %add.42), channel_id=1, source_target_pairs={{0,4},{4,0},{8,12},{12,8},{1,5},{5,1},{9,13},{13,9},{2,6},{6,2},{1... | collective-permute-start | bytes 393224 | tf_op jit(solution)/shard_map/ppermute | solution.py:165
  44.6 1.6 %collective-permute-start.13 = (f32[128,256]{1,0:T(8,128)S(1)}, f32[128,256]{1,0:T(8,128)S(1)}, u32[]{:S(2)}, u32[]{:S(2)}) collective-permute-start(f32[128,256]{1,0:T(8,128)S(1)} %add.44), channel_id=1, source_target_pairs={{0,2},{2,0},{1,3},{3,1},{4,6},{6,4},{5,7},{7,5},{8,10},{10,8},{9,1... | collective-permute-start | bytes 393224 | tf_op jit(solution)/shard_map/ppermute | solution.py:165
  47.6 2.1 %collective-permute-done.13 = f32[128,256]{1,0:T(8,128)S(1)} collective-permute-done((f32[128,256]{1,0:T(8,128)S(1)}, f32[128,256]{1,0:T(8,128)S(1)}, u32[]{:S(2)}, u32[]{:S(2)}) %collective-permute-start.13) | collective-permute-done | bytes 131104 | tf_op jit(solution)/shard_map/ppermute | solution.py:165
  49.8 1.6 %collective-permute-start.11 = (f32[128,256]{1,0:T(8,128)S(1)}, f32[128,256]{1,0:T(8,128)S(1)}, u32[]{:S(2)}, u32[]{:S(2)}) collective-permute-start(f32[128,256]{1,0:T(8,128)S(1)} %add.43), channel_id=1, source_target_pairs={{0,2},{2,0},{1,3},{3,1},{4,6},{6,4},{5,7},{7,5},{8,10},{10,8},{9,1... | collective-permute-start | bytes 393224 | tf_op jit(solution)/shard_map/ppermute | solution.py:165
  51.5 1.7 %shard_map.62 = (f32[256,256]{1,0:T(8,128)}, f32[64,256]{1,0:T(8,128)S(1)}, f32[256,256]{1,0:T(8,128)S(1)}) custom-call(f32[256,256]{1,0:T(8,128)S(1)} %pad_maximum_fusion.stack_ref, f32[256,256]{1,0:T(8,128)S(1)} %shard_map.58.lower_ref, f32[512,256]{1,0:T(8,128)S(1)} %get-tuple-element.67.own_ref, f32[512,256]{1,0:T(8,128)S(1)} %collective-permute-done.3.other_ref), custom_call_target="tpu_custom_call" | custom-call | flops 900000000 | bytes 2162688 | tf_op jit(solution)/shard_map/pallas_call | solution.py:60
  59.4 1.8 %collective-permute-start.17 = (f32[64,256]{1,0:T(8,128)S(1)}, f32[64,256]{1,0:T(8,128)S(1)}, u32[]{:S(2)}, u32[]{:S(2)}) collective-permute-start(f32[64,256]{1,0:T(8,128)S(1)} %get-tuple-element.88), channel_id=1, source_target_pairs={{0,8},{4,12},{8,0},{12,4},{1,9},{5,13},{9,1},{13,5},{2,10},{6,14},... | collective-permute-start | bytes 196616 | tf_op jit(solution)/shard_map/ppermute | solution.py:165
  61.7 4.2 %collective-permute-done.17 = f32[64,256]{1,0:T(8,128)S(1)} collective-permute-done((f32[64,256]{1,0:T(8,128)S(1)}, f32[64,256]{1,0:T(8,128)S(1)}, u32[]{:S(2)}, u32[]{:S(2)}) %collective-permute-start.17) | collective-permute-done | bytes 65568 | tf_op jit(solution)/shard_map/ppermute | solution.py:165
  66.0 2.4 %collective-permute-start.22 = (f32[256,256]{1,0:T(8,128)S(1)}, f32[256,256]{1,0:T(8,128)S(1)}, u32[]{:S(2)}, u32[]{:S(2)}) collective-permute-start(f32[256,256]{1,0:T(8,128)S(1)} %shard_map.66.first_ref), channel_id=1, source_target_pairs={{0,8},{4,12},{8,0},{12,4},{1,9},{5,13},{9,1},{13,5},{2,10},{6,14},... | collective-permute-start | bytes 786440 | tf_op jit(solution)/shard_map/ppermute | solution.py:165
  69.7 3.0 %collective-permute-done.18.refs_0_ = f32[64,256]{1,0:T(8,128)S(1)} collective-permute-done((f32[64,256]{1,0:T(8,128)S(1)}, f32[64,256]{1,0:T(8,128)S(1)}, u32[]{:S(2)}, u32[]{:S(2)}) %collective-permute-start.18) | collective-permute-done | bytes 65568 | tf_op jit(solution)/shard_map/ppermute | solution.py:165
  73.9 4.0 %shard_map.67 = (f32[128,128]{1,0:T(8,128)S(1)}, f32[128,128]{1,0:T(8,128)S(1)}, f32[128,128]{1,0:T(8,128)S(1)}) custom-call(f32[64,256]{1,0:T(8,128)S(1)} %add.46.own_ref, f32[64,256]{1,0:T(8,128)S(1)} %collective-permute-done.18.refs_0_, f32[64,256]{1,0:T(8,128)S(1)} %collective-permute-done.19.refs_1_, f32[64,256]{1,0:T(8,128)S(1)} %collective-permute-done.20.refs_2_), custom_call_target="tpu_custom_call" | custom-call | flops 1000000000 | bytes 458752 | tf_op jit(solution)/shard_map/pallas_call | solution.py:60
  78.6 2.3 %collective-permute-done.22.second_ref = f32[256,256]{1,0:T(8,128)S(1)} collective-permute-done((f32[256,256]{1,0:T(8,128)S(1)}, f32[256,256]{1,0:T(8,128)S(1)}, u32[]{:S(2)}, u32[]{:S(2)}) %collective-permute-start.22) | collective-permute-done | bytes 262176 | tf_op jit(solution)/shard_map/ppermute | solution.py:165
  84.4 4.9 %collective-permute-done.24 = f32[128,256]{1,0:T(8,128)S(1)} collective-permute-done((f32[128,256]{1,0:T(8,128)S(1)}, f32[128,256]{1,0:T(8,128)S(1)}, u32[]{:S(2)}, u32[]{:S(2)}) %collective-permute-start.24) | collective-permute-done | bytes 131104 | tf_op jit(solution)/shard_map/ppermute | solution.py:165
  89.4 1.7 %collective-permute-start.27 = (f32[128,256]{1,0:T(8,128)S(1)}, f32[128,256]{1,0:T(8,128)S(1)}, u32[]{:S(2)}, u32[]{:S(2)}) collective-permute-start(f32[128,256]{1,0:T(8,128)S(1)} %add.49), channel_id=1, source_target_pairs={{0,2},{2,0},{1,3},{3,1},{4,6},{6,4},{5,7},{7,5},{8,10},{10,8},{9,1... | collective-permute-start | bytes 393224 | tf_op jit(solution)/shard_map/ppermute | solution.py:165
  91.1 3.9 %shard_map.71.lower_ref = f32[256,256]{1,0:T(8,128)S(1)} custom-call(f32[128,128]{1,0:T(8,128)S(1)} %get-tuple-element.89.tile_ref, f32[128,128]{1,0:T(8,128)S(1)} %get-tuple-element.95.cross_ref, f32[128,128]{1,0:T(8,128)S(1)} %get-tuple-element.96.left_ref), custom_call_target="tpu_custom_call" | custom-call | flops 1000000000 | bytes 458752 | tf_op jit(solution)/shard_map/pallas_call | solution.py:60
  104.3 1.8 %collective-permute-start.32 = (f32[64,256]{1,0:T(8,128)S(1)}, f32[64,256]{1,0:T(8,128)S(1)}, u32[]{:S(2)}, u32[]{:S(2)}) collective-permute-start(f32[64,256]{1,0:T(8,128)S(1)} %get-tuple-element.112), channel_id=1, source_target_pairs={{0,8},{4,12},{8,0},{12,4},{1,9},{5,13},{9,1},{13,5},{2,10},{6,14},... | collective-permute-start | bytes 196616 | tf_op jit(solution)/shard_map/ppermute | solution.py:165
  106.6 4.5 %collective-permute-done.32 = f32[64,256]{1,0:T(8,128)S(1)} collective-permute-done((f32[64,256]{1,0:T(8,128)S(1)}, f32[64,256]{1,0:T(8,128)S(1)}, u32[]{:S(2)}, u32[]{:S(2)}) %collective-permute-start.32) | collective-permute-done | bytes 65568 | tf_op jit(solution)/shard_map/ppermute | solution.py:165
  112.5 2.9 %collective-permute-done.33.refs_0_ = f32[64,256]{1,0:T(8,128)S(1)} collective-permute-done((f32[64,256]{1,0:T(8,128)S(1)}, f32[64,256]{1,0:T(8,128)S(1)}, u32[]{:S(2)}, u32[]{:S(2)}) %collective-permute-start.33) | collective-permute-done | bytes 65568 | tf_op jit(solution)/shard_map/ppermute | solution.py:165
  116.6 8.0 %shard_map.77.refs_6_ = f32[256,256]{1,0:T(8,128)S(1)} custom-call(f32[64,256]{1,0:T(8,128)S(1)} %add.51.own_ref, f32[64,256]{1,0:T(8,128)S(1)} %collective-permute-done.33.refs_0_, f32[64,256]{1,0:T(8,128)S(1)} %collective-permute-done.34.refs_1_, f32[64,256]{1,0:T(8,128)S(1)} %collective-permute-done.35.refs_2_), custom_call_target="tpu_custom_call" | custom-call | flops 1500000000 | bytes 524288 | tf_op jit(solution)/shard_map/pallas_call | solution.py:60
  124.8 2.9 %shard_map.79 = f32[144,128]{1,0:T(8,128)S(1)} custom-call(f32[256,128]{1,0:T(8,128)S(1)} %get-tuple-element.66.query_ref, f32[256,256]{1,0:T(8,128)S(1)} %get-tuple-element.100.refs_0_, f32[256,256]{1,0:T(8,128)S(1)} %get-tuple-element.103.refs_1_, f32[256,256]{1,0:T(8,128)S(1)} %get-tuple-element.108.refs_2_, ...), custom_call_target="tpu_custom_call" | custom-call | flops 1500000000 | bytes 2826752 | tf_op jit(solution)/shard_map/pallas_call | solution.py:60
  129.0 2.9 %shard_map.78.first_ref = f32[144,128]{1,0:T(8,128)S(1)} custom-call(f32[256,128]{1,0:T(8,128)S(1)} %get-tuple-element.66.query_ref, f32[256,256]{1,0:T(8,128)S(1)} %get-tuple-element.100.refs_0_, f32[256,256]{1,0:T(8,128)S(1)} %get-tuple-element.103.refs_1_, f32[256,256]{1,0:T(8,128)S(1)} %get-tuple-element.108.refs_2_, ...), custom_call_target="tpu_custom_call" | custom-call | flops 1500000000 | bytes 2826752 | tf_op jit(solution)/shard_map/pallas_call | solution.py:60
  132.0 2.6 %collective-permute-done.38.second_ref = f32[144,128]{1,0:T(8,128)S(1)} collective-permute-done((f32[144,128]{1,0:T(8,128)S(1)}, f32[144,128]{1,0:T(8,128)S(1)}, u32[]{:S(2)}, u32[]{:S(2)}) %collective-permute-start.38) | collective-permute-done | bytes 73760 | tf_op jit(solution)/shard_map/ppermute | solution.py:165
  (103 shorter events, 39.8 us)
Async XLA Ops:
  1.6 5.3 %collective-permute-start = (f32[64,256]{1,0:T(8,128)S(1)}, f32[64,256]{1,0:T(8,128)S(1)}, u32[]{:S(2)}, u32[]{:S(2)}) collective-permute-start(f32[64,256]{1,0:T(8,128)S(1)} %shard_map.55.gram_ref), channel_id=1, source_target_pairs={{0,4},{4,0},{8,12},{12,8},{1,5},{5,1},{9,13},{13,9},{2,6},{6,2},{1... | collective-permute-start | bytes 196616 | tf_op jit(solution)/shard_map/ppermute | solution.py:165
  7.0 8.7 %collective-permute-start.1 = (f32[256,256]{1,0:T(8,128)S(1)}, f32[256,256]{1,0:T(8,128)S(1)}, u32[]{:S(2)}, u32[]{:S(2)}) collective-permute-start(f32[256,256]{1,0:T(8,128)S(1)} %get-tuple-element.64), channel_id=1, source_target_pairs={{0,4},{4,0},{8,12},{12,8},{1,5},{5,1},{9,13},{13,9},{2,6},{6,2},{1... | collective-permute-start | bytes 786440 | tf_op jit(solution)/shard_map/ppermute | solution.py:165
  9.1 5.8 %collective-permute-start.2 = (f32[64,256]{1,0:T(8,128)S(1)}, f32[64,256]{1,0:T(8,128)S(1)}, u32[]{:S(2)}, u32[]{:S(2)}) collective-permute-start(f32[64,256]{1,0:T(8,128)S(1)} %add.39), channel_id=1, source_target_pairs={{0,8},{4,12},{8,0},{12,4},{1,9},{5,13},{9,1},{13,5},{2,10},{6,14},... | collective-permute-start | bytes 196616 | tf_op jit(solution)/shard_map/ppermute | solution.py:165
  15.7 18.0 %collective-permute-start.3 = (f32[512,256]{1,0:T(8,128)S(1)}, f32[512,256]{1,0:T(8,128)S(1)}, u32[]{:S(2)}, u32[]{:S(2)}) collective-permute-start(f32[512,256]{1,0:T(8,128)S(1)} %get-tuple-element.70), channel_id=1, source_target_pairs={{0,4},{4,0},{8,12},{12,8},{1,5},{5,1},{9,13},{13,9},{2,6},{6,2},{1... | collective-permute-start | bytes 1572872 | tf_op jit(solution)/shard_map/ppermute | solution.py:165
  18.5 15.1 %collective-permute-start.7 = (f32[256,256]{1,0:T(8,128)S(1)}, f32[256,256]{1,0:T(8,128)S(1)}, u32[]{:S(2)}, u32[]{:S(2)}) collective-permute-start(f32[256,256]{1,0:T(8,128)S(1)} %add.40.first_ref), channel_id=1, source_target_pairs={{0,8},{4,12},{8,0},{12,4},{1,9},{5,13},{9,1},{13,5},{2,10},{6,14},... | collective-permute-start | bytes 786440 | tf_op jit(solution)/shard_map/ppermute | solution.py:165
  20.0 4.3 %collective-permute-start.4 = (f32[64,256]{1,0:T(8,128)S(1)}, f32[64,256]{1,0:T(8,128)S(1)}, u32[]{:S(2)}, u32[]{:S(2)}) collective-permute-start(f32[64,256]{1,0:T(8,128)S(1)} %add.41.own_ref), channel_id=1, source_target_pairs={{0,2},{2,0},{1,3},{3,1},{4,6},{6,4},{5,7},{7,5},{8,10},{10,8},{9,1... | collective-permute-start | bytes 196616 | tf_op jit(solution)/shard_map/ppermute | solution.py:165
  21.5 3.2 %collective-permute-start.5 = (f32[64,256]{1,0:T(8,128)S(1)}, f32[64,256]{1,0:T(8,128)S(1)}, u32[]{:S(2)}, u32[]{:S(2)}) collective-permute-start(f32[64,256]{1,0:T(8,128)S(1)} %add.41.own_ref), channel_id=1, source_target_pairs={{0,1},{1,0},{2,3},{3,2},{4,5},{5,4},{6,7},{7,6},{8,9},{9,8},{10,11... | collective-permute-start | bytes 196616 | tf_op jit(solution)/shard_map/ppermute | solution.py:165
  36.3 5.6 %collective-permute-start.9 = (f32[128,256]{1,0:T(8,128)S(1)}, f32[128,256]{1,0:T(8,128)S(1)}, u32[]{:S(2)}, u32[]{:S(2)}) collective-permute-start(f32[128,256]{1,0:T(8,128)S(1)} %get-tuple-element.75), channel_id=1, source_target_pairs={{0,2},{2,0},{1,3},{3,1},{4,6},{6,4},{5,7},{7,5},{8,10},{10,8},{9,1... | collective-permute-start | bytes 393224 | tf_op jit(solution)/shard_map/ppermute | solution.py:165
  37.9 6.7 %collective-permute-start.12 = (f32[128,256]{1,0:T(8,128)S(1)}, f32[128,256]{1,0:T(8,128)S(1)}, u32[]{:S(2)}, u32[]{:S(2)}) collective-permute-start(f32[128,256]{1,0:T(8,128)S(1)} %get-tuple-element.78), channel_id=1, source_target_pairs={{0,4},{4,0},{8,12},{12,8},{1,5},{5,1},{9,13},{13,9},{2,6},{6,2},{1... | collective-permute-start | bytes 393224 | tf_op jit(solution)/shard_map/ppermute | solution.py:165
  42.0 5.6 %collective-permute-start.10 = (f32[128,256]{1,0:T(8,128)S(1)}, f32[128,256]{1,0:T(8,128)S(1)}, u32[]{:S(2)}, u32[]{:S(2)}) collective-permute-start(f32[128,256]{1,0:T(8,128)S(1)} %add.42), channel_id=1, source_target_pairs={{0,4},{4,0},{8,12},{12,8},{1,5},{5,1},{9,13},{13,9},{2,6},{6,2},{1... | collective-permute-start | bytes 393224 | tf_op jit(solution)/shard_map/ppermute | solution.py:165
  44.6 5.0 %collective-permute-start.13 = (f32[128,256]{1,0:T(8,128)S(1)}, f32[128,256]{1,0:T(8,128)S(1)}, u32[]{:S(2)}, u32[]{:S(2)}) collective-permute-start(f32[128,256]{1,0:T(8,128)S(1)} %add.44), channel_id=1, source_target_pairs={{0,2},{2,0},{1,3},{3,1},{4,6},{6,4},{5,7},{7,5},{8,10},{10,8},{9,1... | collective-permute-start | bytes 393224 | tf_op jit(solution)/shard_map/ppermute | solution.py:165
  49.7 3.6 %collective-permute-start.14 = (f32[256,256]{1,0:T(8,128)S(1)}, f32[256,256]{1,0:T(8,128)S(1)}, u32[]{:S(2)}, u32[]{:S(2)}) collective-permute-start(f32[256,256]{1,0:T(8,128)S(1)} %pad_maximum_fusion.stack_ref), channel_id=1, source_target_pairs={{0,1},{1,0},{2,3},{3,2},{4,5},{5,4},{6,7},{7,6},{8,9},{9,8},{10,11... | collective-permute-start | bytes 786440 | tf_op jit(solution)/shard_map/ppermute | solution.py:165
  49.8 5.9 %collective-permute-start.11 = (f32[128,256]{1,0:T(8,128)S(1)}, f32[128,256]{1,0:T(8,128)S(1)}, u32[]{:S(2)}, u32[]{:S(2)}) collective-permute-start(f32[128,256]{1,0:T(8,128)S(1)} %add.43), channel_id=1, source_target_pairs={{0,2},{2,0},{1,3},{3,1},{4,6},{6,4},{5,7},{7,5},{8,10},{10,8},{9,1... | collective-permute-start | bytes 393224 | tf_op jit(solution)/shard_map/ppermute | solution.py:165
  51.3 5.6 %collective-permute-start.15 = (f32[128,256]{1,0:T(8,128)S(1)}, f32[128,256]{1,0:T(8,128)S(1)}, u32[]{:S(2)}, u32[]{:S(2)}) collective-permute-start(f32[128,256]{1,0:T(8,128)S(1)} %add.45), channel_id=1, source_target_pairs={{0,4},{4,0},{8,12},{12,8},{1,5},{5,1},{9,13},{13,9},{2,6},{6,2},{1... | collective-permute-start | bytes 393224 | tf_op jit(solution)/shard_map/ppermute | solution.py:165
  59.4 6.5 %collective-permute-start.17 = (f32[64,256]{1,0:T(8,128)S(1)}, f32[64,256]{1,0:T(8,128)S(1)}, u32[]{:S(2)}, u32[]{:S(2)}) collective-permute-start(f32[64,256]{1,0:T(8,128)S(1)} %get-tuple-element.88), channel_id=1, source_target_pairs={{0,8},{4,12},{8,0},{12,4},{1,9},{5,13},{9,1},{13,5},{2,10},{6,14},... | collective-permute-start | bytes 196616 | tf_op jit(solution)/shard_map/ppermute | solution.py:165
  66.0 12.7 %collective-permute-start.21 = (f32[128,512]{1,0:T(8,128)S(1)}, f32[128,512]{1,0:T(8,128)S(1)}, u32[]{:S(2)}, u32[]{:S(2)}) collective-permute-start(f32[128,512]{1,0:T(8,128)S(1)} %get-tuple-element.91), channel_id=1, source_target_pairs={{0,4},{4,0},{8,12},{12,8},{1,5},{5,1},{9,13},{13,9},{2,6},{6,2},{1... | collective-permute-start | bytes 786440 | tf_op jit(solution)/shard_map/ppermute | solution.py:165
  66.0 14.9 %collective-permute-start.22 = (f32[256,256]{1,0:T(8,128)S(1)}, f32[256,256]{1,0:T(8,128)S(1)}, u32[]{:S(2)}, u32[]{:S(2)}) collective-permute-start(f32[256,256]{1,0:T(8,128)S(1)} %shard_map.66.first_ref), channel_id=1, source_target_pairs={{0,8},{4,12},{8,0},{12,4},{1,9},{5,13},{9,1},{13,5},{2,10},{6,14},... | collective-permute-start | bytes 786440 | tf_op jit(solution)/shard_map/ppermute | solution.py:165
  68.4 4.3 %collective-permute-start.18 = (f32[64,256]{1,0:T(8,128)S(1)}, f32[64,256]{1,0:T(8,128)S(1)}, u32[]{:S(2)}, u32[]{:S(2)}) collective-permute-start(f32[64,256]{1,0:T(8,128)S(1)} %add.46.own_ref), channel_id=1, source_target_pairs={{0,2},{2,0},{1,3},{3,1},{4,6},{6,4},{5,7},{7,5},{8,10},{10,8},{9,1... | collective-permute-start | bytes 196616 | tf_op jit(solution)/shard_map/ppermute | solution.py:165
  69.7 3.0 %collective-permute-start.19 = (f32[64,256]{1,0:T(8,128)S(1)}, f32[64,256]{1,0:T(8,128)S(1)}, u32[]{:S(2)}, u32[]{:S(2)}) collective-permute-start(f32[64,256]{1,0:T(8,128)S(1)} %add.46.own_ref), channel_id=1, source_target_pairs={{0,1},{1,0},{2,3},{3,2},{4,5},{5,4},{6,7},{7,6},{8,9},{9,8},{10,11... | collective-permute-start | bytes 196616 | tf_op jit(solution)/shard_map/ppermute | solution.py:165
  83.6 5.6 %collective-permute-start.24 = (f32[128,256]{1,0:T(8,128)S(1)}, f32[128,256]{1,0:T(8,128)S(1)}, u32[]{:S(2)}, u32[]{:S(2)}) collective-permute-start(f32[128,256]{1,0:T(8,128)S(1)} %get-tuple-element.94), channel_id=1, source_target_pairs={{0,2},{2,0},{1,3},{3,1},{4,6},{6,4},{5,7},{7,5},{8,10},{10,8},{9,1... | collective-permute-start | bytes 393224 | tf_op jit(solution)/shard_map/ppermute | solution.py:165
  84.1 5.3 %collective-permute-start.26 = (f32[128,256]{1,0:T(8,128)S(1)}, f32[128,256]{1,0:T(8,128)S(1)}, u32[]{:S(2)}, u32[]{:S(2)}) collective-permute-start(f32[128,256]{1,0:T(8,128)S(1)} %get-tuple-element.99), channel_id=1, source_target_pairs={{0,4},{4,0},{8,12},{12,8},{1,5},{5,1},{9,13},{13,9},{2,6},{6,2},{1... | collective-permute-start | bytes 393224 | tf_op jit(solution)/shard_map/ppermute | solution.py:165
  89.2 5.7 %collective-permute-start.25 = (f32[128,256]{1,0:T(8,128)S(1)}, f32[128,256]{1,0:T(8,128)S(1)}, u32[]{:S(2)}, u32[]{:S(2)}) collective-permute-start(f32[128,256]{1,0:T(8,128)S(1)} %add.47), channel_id=1, source_target_pairs={{0,4},{4,0},{8,12},{12,8},{1,5},{5,1},{9,13},{13,9},{2,6},{6,2},{1... | collective-permute-start | bytes 393224 | tf_op jit(solution)/shard_map/ppermute | solution.py:165
  89.4 5.6 %collective-permute-start.27 = (f32[128,256]{1,0:T(8,128)S(1)}, f32[128,256]{1,0:T(8,128)S(1)}, u32[]{:S(2)}, u32[]{:S(2)}) collective-permute-start(f32[128,256]{1,0:T(8,128)S(1)} %add.49), channel_id=1, source_target_pairs={{0,2},{2,0},{1,3},{3,1},{4,6},{6,4},{5,7},{7,5},{8,10},{10,8},{9,1... | collective-permute-start | bytes 393224 | tf_op jit(solution)/shard_map/ppermute | solution.py:165
  95.0 3.9 %collective-permute-start.28 = (f32[256,256]{1,0:T(8,128)S(1)}, f32[256,256]{1,0:T(8,128)S(1)}, u32[]{:S(2)}, u32[]{:S(2)}) collective-permute-start(f32[256,256]{1,0:T(8,128)S(1)} %pad_maximum_fusion.1.stack_ref), channel_id=1, source_target_pairs={{0,1},{1,0},{2,3},{3,2},{4,5},{5,4},{6,7},{7,6},{8,9},{9,8},{10,11... | collective-permute-start | bytes 786440 | tf_op jit(solution)/shard_map/ppermute | solution.py:165
  95.1 5.9 %collective-permute-start.29 = (f32[128,256]{1,0:T(8,128)S(1)}, f32[128,256]{1,0:T(8,128)S(1)}, u32[]{:S(2)}, u32[]{:S(2)}) collective-permute-start(f32[128,256]{1,0:T(8,128)S(1)} %add.48), channel_id=1, source_target_pairs={{0,2},{2,0},{1,3},{3,1},{4,6},{6,4},{5,7},{7,5},{8,10},{10,8},{9,1... | collective-permute-start | bytes 393224 | tf_op jit(solution)/shard_map/ppermute | solution.py:165
  96.2 5.6 %collective-permute-start.30 = (f32[128,256]{1,0:T(8,128)S(1)}, f32[128,256]{1,0:T(8,128)S(1)}, u32[]{:S(2)}, u32[]{:S(2)}) collective-permute-start(f32[128,256]{1,0:T(8,128)S(1)} %add.50), channel_id=1, source_target_pairs={{0,4},{4,0},{8,12},{12,8},{1,5},{5,1},{9,13},{13,9},{2,6},{6,2},{1... | collective-permute-start | bytes 393224 | tf_op jit(solution)/shard_map/ppermute | solution.py:165
  104.3 6.7 %collective-permute-start.32 = (f32[64,256]{1,0:T(8,128)S(1)}, f32[64,256]{1,0:T(8,128)S(1)}, u32[]{:S(2)}, u32[]{:S(2)}) collective-permute-start(f32[64,256]{1,0:T(8,128)S(1)} %get-tuple-element.112), channel_id=1, source_target_pairs={{0,8},{4,12},{8,0},{12,4},{1,9},{5,13},{9,1},{13,5},{2,10},{6,14},... | collective-permute-start | bytes 196616 | tf_op jit(solution)/shard_map/ppermute | solution.py:165
  111.1 4.3 %collective-permute-start.33 = (f32[64,256]{1,0:T(8,128)S(1)}, f32[64,256]{1,0:T(8,128)S(1)}, u32[]{:S(2)}, u32[]{:S(2)}) collective-permute-start(f32[64,256]{1,0:T(8,128)S(1)} %add.51.own_ref), channel_id=1, source_target_pairs={{0,2},{2,0},{1,3},{3,1},{4,6},{6,4},{5,7},{7,5},{8,10},{10,8},{9,1... | collective-permute-start | bytes 196616 | tf_op jit(solution)/shard_map/ppermute | solution.py:165
  112.1 12.7 %collective-permute-start.36 = (f32[256,256]{1,0:T(8,128)S(1)}, f32[256,256]{1,0:T(8,128)S(1)}, u32[]{:S(2)}, u32[]{:S(2)}) collective-permute-start(f32[256,256]{1,0:T(8,128)S(1)} %shard_map.76.refs_4_), channel_id=1, source_target_pairs={{0,8},{4,12},{8,0},{12,4},{1,9},{5,13},{9,1},{13,5},{2,10},{6,14},... | collective-permute-start | bytes 786440 | tf_op jit(solution)/shard_map/ppermute | solution.py:165
  112.5 3.2 %collective-permute-start.34 = (f32[64,256]{1,0:T(8,128)S(1)}, f32[64,256]{1,0:T(8,128)S(1)}, u32[]{:S(2)}, u32[]{:S(2)}) collective-permute-start(f32[64,256]{1,0:T(8,128)S(1)} %add.51.own_ref), channel_id=1, source_target_pairs={{0,1},{1,0},{2,3},{3,2},{4,5},{5,4},{6,7},{7,6},{8,9},{9,8},{10,11... | collective-permute-start | bytes 196616 | tf_op jit(solution)/shard_map/ppermute | solution.py:165
  115.6 13.5 %collective-permute-start.37 = (f32[128,512]{1,0:T(8,128)S(1)}, f32[128,512]{1,0:T(8,128)S(1)}, u32[]{:S(2)}, u32[]{:S(2)}) collective-permute-start(f32[128,512]{1,0:T(8,128)S(1)} %get-tuple-element.118), channel_id=1, source_target_pairs={{0,4},{4,0},{8,12},{12,8},{1,5},{5,1},{9,13},{13,9},{2,6},{6,2},{1... | collective-permute-start | bytes 786440 | tf_op jit(solution)/shard_map/ppermute | solution.py:165
  127.8 6.8 %collective-permute-start.38 = (f32[144,128]{1,0:T(8,128)S(1)}, f32[144,128]{1,0:T(8,128)S(1)}, u32[]{:S(2)}, u32[]{:S(2)}) collective-permute-start(f32[144,128]{1,0:T(8,128)S(1)} %shard_map.79), channel_id=1, source_target_pairs={{0,8},{4,12},{8,0},{12,4},{1,9},{5,13},{9,1},{13,5},{2,10},{6,14},... | collective-permute-start | bytes 221192 | tf_op jit(solution)/shard_map/ppermute | solution.py:165
  (12 other events, 63.7 us)
